TPU v7x, 256 devices: a whole 4x4x8 slice. The times are simulated.
256 devices in a mesh: blk: 32 (over y_lo, z, core), head: 8 (over x, y_hi).
Axes of the slice: x: 4, y: 4 (y_hi: 2, y_lo: 2; y = y_hi * 2 + y_lo), z: 8, core: 2. Of those that a mesh axis runs over, the one named last changes fastest.
Arguments:
- pages: bfloat16 [32, 16, 16, 768], P('blk'), may hold values from -6 to 6
- valid_counts: int32 [32], replicated, may hold values from 32 to 256
- dw_weight: float32 [7, 7, 768], replicated, may hold values from -0.875 to 0.875
- dw_bias: float32 [768], replicated, may hold values from -3 to 3
- norm1_gain: float32 [768], replicated, may hold values from 0.5 to 2
- fc1_w: bfloat16 [768, 3072], P(None, 'head'), may hold values from -0.21875 to 0.21875
- fc1_b: float32 [3072], P('head'), may hold values from -3 to 3
- fc2_w: bfloat16 [3072, 768], P('head'), may hold values from -0.109375 to 0.109375
- fc2_b: float32 [768], replicated, may hold values from -3 to 3
- layer_scale: float32 [768], replicated, may hold values from 0.5 to 2
- norm2_gain: float32 [768], replicated, may hold values from 0.5 to 2
- w_query: bfloat16 [768, 4096], P(None, 'head'), may hold values from -3 to 3
- w_key: bfloat16 [768, 1024], P(None, 'head'), may hold values from -0.21875 to 0.21875
- w_value: bfloat16 [768, 1024], P(None, 'head'), may hold values from -0.21875 to 0.21875
- w_out: bfloat16 [4096, 768], P('head'), may hold values from -0.09375 to 0.09375
Outputs:
- mixed: bfloat16 [8192, 768], P(('blk', 'head'))
All inputs are finite; a program needn't handle non-finite values.
Results may differ from a plain program's by a relative error of at most 0.023.
Values may be sent and summed in bfloat16 or wider, within the bound.
No kernel may reach another device: no remote copies, remote signals or barrier semaphores. Data moves between devices by JAX's collectives and lax.ppermute only.
A program may use at most 128 MiB of HBM per device.

v0:
```python
import jax
import jax.numpy as jnp
from jax import lax
from jax.sharding import PartitionSpec as P

HEADS = 32
KV_HEADS = 8
HD = 128


def depthwise(pages, dw_weight, dw_bias):
    height = pages.shape[1]
    breadth = pages.shape[2]
    padded = jnp.pad(pages.astype(jnp.float32), ((0, 0), (3, 3), (3, 3), (0, 0)))
    total = jnp.zeros(pages.shape, jnp.float32)
    for vertical in range(7):
        for sideways in range(7):
            total = (
                total
                + padded[:, vertical : vertical + height, sideways : sideways + breadth, :]
                * dw_weight[vertical, sideways]
            )
    return total + dw_bias


def layer_norm(values, gain, epsilon):
    centred = values - jnp.mean(values, axis=-1, keepdims=True)
    spread = jnp.mean(centred * centred, axis=-1, keepdims=True)
    return centred * lax.rsqrt(spread + epsilon) * gain


def mlp_partial(pages, dw_weight, dw_bias, norm1_gain, fc1_w, fc1_b, fc2_w):
    convolved = depthwise(pages, dw_weight, dw_bias)
    flattened = convolved.reshape(-1, convolved.shape[-1])
    normed = layer_norm(flattened, norm1_gain, 1e-06).astype(jnp.bfloat16)
    hidden = jax.nn.gelu(
        jnp.dot(normed, fc1_w, preferred_element_type=jnp.float32) + fc1_b, approximate=False
    ).astype(jnp.bfloat16)
    return jnp.dot(hidden, fc2_w, preferred_element_type=jnp.float32)


def fold_keys(carry, keys, values, queries, valid_counts, page_tokens):
    running_top, denominator, weighted = carry
    count = keys.shape[0]
    kv_groups = queries.shape[1]
    key_heads = keys.reshape(count, kv_groups, HD)
    value_heads = values.reshape(count, kv_groups, HD)
    scores = jnp.einsum(
        "rgqd,ngd->gqrn", queries, key_heads, preferred_element_type=jnp.float32
    ) * HD ** (-0.5)
    position = jnp.arange(count, dtype=jnp.int32)
    page_number = position // page_tokens
    matches = page_number[:, None] == jnp.arange(valid_counts.shape[0], dtype=jnp.int32)[None, :]
    page_count = jnp.sum(jnp.where(matches, valid_counts[None, :], 0), axis=1)
    valid = position % page_tokens < page_count
    scores = jnp.where(valid, scores, -1e30)
    new_top = jnp.maximum(running_top, jnp.max(scores, axis=-1))
    exponent = jnp.where(valid, jnp.exp(scores - new_top[..., None]), 0.0)
    denominator = jnp.sum(exponent, axis=-1)
    update = jnp.einsum(
        "gqrn,ngd->gqrd",
        exponent.astype(jnp.bfloat16),
        value_heads,
        preferred_element_type=jnp.float32,
    )
    weighted = update
    return (new_top, denominator, weighted)


def per_device(
    pages,
    valid_counts,
    dw_weight,
    dw_bias,
    norm1_gain,
    fc1_w,
    fc1_b,
    fc2_w,
    fc2_b,
    layer_scale,
    norm2_gain,
    w_query,
    w_key,
    w_value,
    w_out,
):
    channels = pages.shape[-1]
    page_tokens = pages.shape[1] * pages.shape[2]
    rows = pages.shape[0] * page_tokens
    partial_sum = mlp_partial(pages, dw_weight, dw_bias, norm1_gain, fc1_w, fc1_b, fc2_w)
    flat_pages = pages.reshape(rows, channels)
    summed = lax.psum(partial_sum, "head")
    block = flat_pages.astype(jnp.float32) + layer_scale * (summed + fc2_b)
    normed = layer_norm(block, norm2_gain, 1e-05).astype(jnp.bfloat16)
    kv_groups = w_key.shape[1] // HD
    group = HEADS // KV_HEADS
    queries = jnp.dot(normed, w_query, preferred_element_type=jnp.float32).astype(jnp.bfloat16)
    queries = queries.reshape(rows, kv_groups, group, HD)
    initial = (
        jnp.full((kv_groups, group, rows), -1e30, jnp.float32),
        jnp.zeros((kv_groups, group, rows), jnp.float32),
        jnp.zeros((kv_groups, group, rows, HD), jnp.float32),
    )
    own_keys = jnp.dot(normed, w_key, preferred_element_type=jnp.float32).astype(jnp.bfloat16)
    own_values = jnp.dot(normed, w_value, preferred_element_type=jnp.float32).astype(jnp.bfloat16)
    final = fold_keys(
        initial,
        lax.all_gather(own_keys, "blk", axis=0, tiled=True),
        lax.all_gather(own_values, "blk", axis=0, tiled=True),
        queries,
        valid_counts,
        page_tokens,
    )
    attended = (final[2] / final[1][..., None]).astype(jnp.bfloat16)
    attended = attended.transpose(2, 0, 1, 3).reshape(rows, kv_groups * group * HD)
    mixed = lax.psum_scatter(
        jnp.dot(attended, w_out, preferred_element_type=jnp.float32),
        "head",
        scatter_dimension=0,
        tiled=True,
    )
    return mixed.astype(jnp.bfloat16)


def solution(mesh):
    in_specs = (
        P("blk", None, None, None),
        P(),
        P(),
        P(),
        P(),
        P(None, "head"),
        P("head"),
        P("head", None),
        P(),
        P(),
        P(),
        P(None, "head"),
        P(None, "head"),
        P(None, "head"),
        P("head", None),
    )
    out_specs = P(("blk", "head"), None)
    return jax.shard_map(
        per_device, mesh=mesh, in_specs=in_specs, out_specs=out_specs, check_vma=False
    )
```

profile of v0, /device:TPU:32, one launch (start us, length us, event | category | flops | bytes accessed | tf_op | source)
XLA Modules:
  0.0 354.2 jit_solution(8926439461209473395)
XLA Ops:
  6.5 0.0 copy-start
  6.5 0.0 all-reduce.3.cloned.1.call-start
  6.5 1.3 slice_reduce_fusion.48
  7.9 1.4 slice_reduce_fusion.47
  9.3 1.1 slice_reduce_fusion.46
  10.4 1.1 convert_element_type.54
  11.5 7.0 %fusion.207 = (f32[16,16]{1,0:T(8,128)S(1)}, f32[1,16,16,768]{3,2,1,0:T(8,128)S(1)}) fusion(f32[768]{0:T(1024)} %param.18, f32[768]{0:T(1024)S(1)} %get-tuple-element.52, f32[768]{0:T(1024)S(1)} %get-tuple-element.53, f32[768]{0:T(1024)S(1)} %get-tuple-element.6, f32[768]{0:T(1024)S(1)} %get-tuple-element.7, f32[768]{0:T(1024)S(1)} %get-tuple-element.8, ...), kind=kLoop, calls=%fused_computation.328 | loop fusion | flops 19463936 | bytes 1727488 | tf_op jit(solution)/shard_map/reduce_sum | solution.py:27
  18.5 0.1 div.34
  18.6 0.2 multiply_reduce_fusion.1
  18.8 0.1 rsqrt.20
  18.9 0.9 fusion.122
  19.8 3.6 %fusion.133 = f32[256,768]{1,0:T(8,128)} fusion(bf16[384,768]{1,0:T(8,128)(2,1)} %param.22, bf16[256,768]{1,0:T(8,128)(2,1)S(1)} %fusion.122, bf16[768,384]{1,0:T(8,128)(2,1)} %param.20, f32[384]{0:T(512)} %param.21), kind=kOutput, calls=%fused_computation.195 | convolution fusion | flops 308477952 | bytes 2360832 | tf_op jit(solution)/shard_map/dot_general | solution.py:39
  23.4 0.0 all-reduce.3.cloned.1.call-update
  23.4 0.0 all-gather.3.cloned.1.call-start
  23.4 94.7 %all-reduce.3.cloned.1.call-done = f32[256,768]{1,0:T(8,128)} async-done(((f32[256,768]{1,0:T(8,128)}), f32[256,768]{1,0:T(8,128)}) %all-reduce.3.cloned.1.call-update) | async-done | bytes 786448 | tf_op jit(solution)/shard_map/psum | solution.py:92
  118.2 1.5 fusion.167
  119.7 1.5 multiply_reduce_fusion
  121.2 1.5 multiply_convert_fusion
  122.7 1.8 convolution_convert_fusion.2
  124.5 0.0 all-gather.3.cloned.1.call-update
  124.5 0.0 all-gather.5.cloned.1.call-start
  124.6 0.9 select_reduce_fusion
  125.5 1.5 fusion.12
  127.0 1.9 convolution_convert_fusion.1
  128.9 0.0 all-gather.5.cloned.1.call-update
  128.9 0.2 reduce-scatter.2.cloned.1.call-start
  129.2 57.3 %all-gather.3.cloned.1.call-done = bf16[8192,128]{1,0:T(8,128)(2,1)} async-done(((bf16[256,128]{1,0:T(8,128)(2,1)}), bf16[8192,128]{1,0:T(8,128)(2,1)}) %all-gather.3.cloned.1.call-update) | async-done | bytes 2097168 | tf_op jit(solution)/shard_map/all_gather | solution.py:108
  186.5 14.5 %bitcast_reduce_fusion = (f32[4,256]{1,0:T(4,128)S(1)}, f32[8192,256,4]{1,0,2:T(8,128)}) fusion(pred[8192]{0:T(1024)(128)(4,1)S(1)} %fusion.168, bf16[32,4,8,128]{3,2,1,0:T(8,128)(2,1)S(1)} %fusion.12, bf16[8192,128]{1,0:T(8,128)(2,1)} %all-gather.3.cloned.1.call-done), kind=kOutput, calls=%fused_computation.1 | convolution fusion | flops 2172648448 | bytes 35926016 | tf_op jit(solution)/shard_map/rgqd,ngd->gqrn/dot_general | solution.py:48
  201.0 15.1 %fusion.2 = f32[4,256]{1,0:T(4,128)S(1)} fusion(f32[8192,256,4]{1,0,2:T(8,128)} %get-tuple-element.57, f32[4,256]{1,0:T(4,128)S(1)} %broadcast_maximum_fusion, pred[8192]{0:T(1024)(128)(4,1)S(1)} %fusion.168), kind=kLoop, calls=%fused_computation.5 | loop fusion | flops 41942016 | bytes 33570816 | tf_op jit(solution)/shard_map/reduce_sum | solution.py:59
  216.1 38.5 %all-gather.5.cloned.1.call-done = bf16[8192,128]{0,1:T(8,128)(2,1)} async-done(((bf16[256,128]{0,1:T(8,128)(2,1)}), bf16[8192,128]{0,1:T(8,128)(2,1)}) %all-gather.5.cloned.1.call-update) | async-done | bytes 2097168 | tf_op jit(solution)/shard_map/all_gather | solution.py:109
  254.6 14.3 %fusion.18 = bf16[4,256,128]{1,2,0:T(8,128)(2,1)S(1)} fusion(f32[8192,256,4]{1,0,2:T(8,128)} %get-tuple-element.57, f32[4,256]{1,0:T(4,128)S(1)} %broadcast_maximum_fusion, pred[8192]{0:T(1024)(128)(4,1)S(1)} %fusion.168, bf16[8192,128]{0,1:T(8,128)(2,1)} %all-gather.5.cloned.1.call-done, f32[4,256]{1,0:T(4,128)S(1)} %fusion.2), kind=kOutput, calls=%fused_computation.70 | convolution fusion | flops 2189688832 | bytes 35930112 | tf_op jit(solution)/shard_map/gqrn,ngd->gqrd/dot_general | solution.py:60
  268.9 0.0 copy-done
  269.0 1.3 fusion.209
  270.2 0.0 reduce-scatter.2.cloned.1.call-update
  270.3 75.9 %reduce-scatter.2.cloned.1.call-done = f32[32,768]{1,0:T(8,128)} async-done(((f32[256,768]{1,0:T(8,128)}), f32[32,768]{1,0:T(8,128)}) %reduce-scatter.2.cloned.1.call-update) | async-done | bytes 98320 | tf_op jit(solution)/shard_map/reduce_scatter | solution.py:116
  346.2 1.5 convert_element_type.53
  (7 shorter events, 0.0 us)
Async XLA Ops:
  6.5 262.4 %copy-start = (bf16[512,768]{1,0:T(8,128)(2,1)S(1)}, bf16[512,768]{1,0:T(8,128)(2,1)}, u32[]{:S(2)}) copy-start(bf16[512,768]{1,0:T(8,128)(2,1)} %param.29) | copy-start | bytes 2359300
  6.5 111.7 %all-reduce.3.cloned.1.call-start = ((), (), s32[]{:S(2)}) async-start(), calls=%async_computation.1 | async-start | bytes 1572864 | tf_op jit(solution)/shard_map/psum | solution.py:92
  23.4 163.1 %all-gather.3.cloned.1.call-start = ((), (), s32[]{:S(2)}) async-start(), calls=%async_computation.2 | async-start | bytes 2162688 | tf_op jit(solution)/shard_map/all_gather | solution.py:108
  124.5 130.1 %all-gather.5.cloned.1.call-start = ((), (), s32[]{:S(2)}) async-start(), calls=%async_computation.3 | async-start | bytes 2162688 | tf_op jit(solution)/shard_map/all_gather | solution.py:109
  128.9 217.3 %reduce-scatter.2.cloned.1.call-start = ((), (), s32[]{:S(2)}) async-start(), calls=%async_computation.4 | async-start | bytes 884736 | tf_op jit(solution)/shard_map/reduce_scatter | solution.py:116
Sparse Core Ops, SparseCore 0:
  23.5 94.6 all-reduce.2
  124.7 61.7 all-gather.2
  188.4 66.2 all-gather.4
  270.4 75.7 reduce-scatter.1
where the time goes:
time: 355 us; the launch traced here: 354 us
  waiting for transfers between devices  267 us (75%)
  matrix products  38.9 us (11%)
  other arithmetic  31.2 us (9%)
  between operations  13.2 us (4%)
  local copies, waits for them, and re-layouts  4.04 us (1%)
    psum x1, waiting for transfers between devices, per_device(): summed = lax.psum(partial_sum, 'head')  94.7 us
    reduce_scatter x1, waiting for transfers between devices, per_device(): lax.psum_scatter(jnp.dot(attended, w_out, preferred_element_type=jnp.floa...  75.9 us
    all_gather x1, waiting for transfers between devices, per_device(): lax.all_gather(own_keys, 'blk', axis=0, tiled=True)  57.3 us
    all_gather x1, waiting for transfers between devices, per_device(): lax.all_gather(own_values, 'blk', axis=0, tiled=True)  38.5 us
    reduce_sum x1, other arithmetic, fold_keys(): denominator = jnp.sum(exponent, axis=-1)  15.1 us
    dot_general x1, matrix products, fold_keys(): jnp.einsum('rgqd,ngd->gqrn', queries, key_heads, preferred_element_type=j...  14.5 us
    dot_general x1, matrix products, fold_keys(): jnp.einsum('gqrn,ngd->gqrd', exponent.astype(jnp.bfloat16), value_heads,...  14.3 us
    reduce_sum x2, other arithmetic, layer_norm(): centred = values - jnp.mean(values, axis=-1, keepdims=True)  8.47 us
  transfers between devices with their start and end apart: 4, of which 4 were waited for; matrix products, arithmetic and copies ran while one was open for 10% of the time, Pallas kernels for 0%

commit v1 on v0

v1 whole, which is shorter than its diff:
```python
import functools

import jax
import jax.numpy as jnp
from jax import lax
from jax.experimental import pallas as pl
from jax.experimental.pallas import tpu as pltpu
from jax.sharding import PartitionSpec as P

HEADS = 32
KV_HEADS = 8
HD = 128
LOG2E = 1.4426950408889634
NEG = -1e30
BF = jnp.bfloat16
F32 = jnp.float32


def vmem_spec():
    return pl.BlockSpec(memory_space=pltpu.VMEM)


def smem_spec():
    return pl.BlockSpec(memory_space=pltpu.SMEM)


def normalise(values, gain, epsilon):
    centred = values - jnp.mean(values, axis=-1, keepdims=True)
    spread = jnp.mean(centred * centred, axis=-1, keepdims=True)
    return centred * lax.rsqrt(spread + epsilon) * gain


def mlp_kernel(pages, dw, dwb, gain, w1, b1, w2, out, padded, conv):
    height, breadth, channels = pages.shape
    padded[...] = jnp.zeros(padded.shape, F32)
    padded[3 : 3 + height, 8 : 8 + breadth, :] = pages[...].astype(F32)
    half = height // 2
    for start in range(0, channels, 128):
        lanes = slice(start, start + 128)
        for top in range(0, height, half):
            total = jnp.broadcast_to(dwb[0:1, lanes][None], (half, breadth, 128))
            for sideways in range(7):
                window = padded[top : top + half + 6, 5 + sideways : 5 + sideways + breadth, lanes]
                for vertical in range(7):
                    tap = dw[vertical, sideways : sideways + 1, lanes]
                    total = total + window[vertical : vertical + half] * tap[None]
            conv[top * breadth : (top + half) * breadth, lanes] = total.reshape(half * breadth, 128)
    normed = normalise(conv[...], gain[...], 1e-06).astype(BF)
    pre = jnp.dot(normed, w1[...], preferred_element_type=F32) + b1[...]
    hidden = (0.5 * pre * (1.0 + lax.erf(pre * 0.7071067811865476))).astype(BF)
    out[...] = jnp.dot(hidden, w2[...], preferred_element_type=F32).astype(BF)


def mlp(pages, dw, dwb, gain, w1, b1, w2):
    _, height, breadth, channels = pages.shape
    rows = height * breadth
    return pl.pallas_call(
        mlp_kernel,
        out_shape=jax.ShapeDtypeStruct((rows, channels), BF),
        in_specs=[vmem_spec()] * 7,
        out_specs=vmem_spec(),
        scratch_shapes=[
            pltpu.VMEM((height + 6, breadth + 16, channels), F32),
            pltpu.VMEM((rows, channels), F32),
        ],
        name="conv_mlp",
    )(pages[0], dw, dwb[None], gain[None], w1, b1[None], w2)


def block_kernel(place, parts, pages, scale, b2, gain, out):
    count, chunk, _ = parts.shape
    total = parts[0].astype(F32)
    for part in range(1, count):
        total = total + parts[part].astype(F32)
    start = pl.multiple_of(place[0] * chunk, chunk)
    own = pages[pl.ds(start, chunk), :].astype(F32)
    block = own + scale[...] * (total + b2[...])
    normed = normalise(block, gain[...], 1e-05).astype(BF)
    for part in range(count):
        out[part] = normed


def block_norm(place, parts, pages, scale, b2, gain):
    return pl.pallas_call(
        block_kernel,
        out_shape=jax.ShapeDtypeStruct(parts.shape, BF),
        in_specs=[smem_spec()] + [vmem_spec()] * 5,
        out_specs=vmem_spec(),
        name="block_norm",
    )(place, parts, pages, scale[None], b2[None], gain[None])


def kv_kernel(normed, wk, wv, out):
    tokens = normed[...]
    out[0, :, 0:HD] = jnp.dot(tokens, wv[...], preferred_element_type=F32).astype(BF)
    out[0, :, HD : 2 * HD] = jnp.dot(tokens, wk[...], preferred_element_type=F32).astype(BF)


def key_values(normed, wk, wv):
    rows = normed.shape[0]
    return pl.pallas_call(
        kv_kernel,
        out_shape=jax.ShapeDtypeStruct((1, rows, 2 * HD), BF),
        in_specs=[vmem_spec()] * 3,
        out_specs=vmem_spec(),
        name="key_values",
    )(normed, wk, wv)


def query_kernel(normed, wq, out):
    product = jnp.dot(normed[...], wq[...], preferred_element_type=F32) * (HD**-0.5 * LOG2E)
    for head in range(out.shape[0]):
        out[head] = product[:, head * HD : (head + 1) * HD].astype(BF)


def queries_of(normed, wq):
    rows = normed.shape[0]
    return pl.pallas_call(
        query_kernel,
        out_shape=jax.ShapeDtypeStruct((wq.shape[1] // HD, rows, HD), BF),
        in_specs=[vmem_spec()] * 2,
        out_specs=vmem_spec(),
        name="queries",
    )(normed, wq)


def attend_kernel(first, last, offset, sizes, *refs):
    refs = list(refs)
    counts = refs.pop(0)
    query = refs.pop(0)
    chunks = [refs.pop(0) for _ in sizes]
    if not first:
        top_in, sums_in = refs.pop(0), refs.pop(0)
    if last:
        w_out = refs.pop(0)
        mixed = refs.pop(0)
        top_out, sums_out = refs.pop(0), refs.pop(0)
    else:
        top_out, sums_out = refs.pop(0), refs.pop(0)
    heads, rows, _ = query.shape
    pages = []
    for chunk, size in zip(chunks, sizes):
        for index in range(size):
            pages.append((chunk, index, offset + len(pages)))
    tokens = chunks[0].shape[1]
    lane = lax.broadcasted_iota(jnp.int32, (1, tokens), 1)
    lane_kv = lax.broadcasted_iota(jnp.int32, (tokens, 2 * HD), 1)
    fresh = first
    for begin in range(0, len(pages), 4):
        group = pages[begin : begin + 4]
        keys, values, masks = [], [], []
        for chunk, index, number in group:
            both = chunk[index]
            keys.append(both[:, HD : 2 * HD])
            values.append(jnp.where(lane_kv < HD, both, jnp.ones_like(both)))
            masks.append(jnp.where(lane < counts[number], 0.0, NEG).astype(F32))
        for head in range(heads):
            scores = [
                lax.dot_general(query[head], key, (((1,), (1,)), ((), ())), preferred_element_type=F32) + mask
                for key, mask in zip(keys, masks)
            ]
            largest = functools.reduce(jnp.maximum, scores)
            top = jnp.max(largest, axis=1, keepdims=True)
            if not fresh:
                source_top, source_sums = (top_in, sums_in) if begin == 0 else (top_out, sums_out)
                before = source_top[head][:, 0:1]
                top = jnp.maximum(top, before)
                carried = source_sums[head] * jnp.exp2(before - top)
            total = functools.reduce(
                jnp.add,
                [
                    jnp.dot(jnp.exp2(score - top).astype(BF), value, preferred_element_type=F32)
                    for score, value in zip(scores, values)
                ],
            )
            if not fresh:
                total = total + carried
            sums_out[head] = total
            top_out[head] = jnp.broadcast_to(top, (rows, HD))
        fresh = False
    if last:
        attended = jnp.concatenate(
            [(sums_out[head][:, 0:HD] / sums_out[head][:, HD : 2 * HD]).astype(BF) for head in range(heads)], axis=1
        )
        mixed[...] = jnp.dot(attended, w_out[...], preferred_element_type=F32).astype(BF)


def attend(counts, query, chunks, offset, carry=None, w_out=None):
    heads, rows, _ = query.shape
    sizes = tuple(chunk.shape[0] for chunk in chunks)
    state = [jax.ShapeDtypeStruct((heads, rows, HD), F32), jax.ShapeDtypeStruct((heads, rows, 2 * HD), F32)]
    operands = [counts, query, *chunks]
    if carry is not None:
        operands += list(carry)
    scratch = []
    if w_out is not None:
        operands.append(w_out)
        out_shape = [jax.ShapeDtypeStruct((rows, w_out.shape[1]), BF)]
        scratch = [pltpu.VMEM(one.shape, F32) for one in state]
    else:
        out_shape = state
    pairs = sum(sizes) * chunks[0].shape[1] * heads * rows
    return pl.pallas_call(
        functools.partial(attend_kernel, carry is None, w_out is not None, offset, sizes),
        out_shape=out_shape,
        in_specs=[smem_spec()] + [vmem_spec()] * (len(operands) - 1),
        out_specs=[vmem_spec()] * len(out_shape),
        scratch_shapes=scratch,
        cost_estimate=pl.CostEstimate(flops=pairs * 512, transcendentals=pairs, bytes_accessed=4 * 2**20),
        name="attend",
    )(*operands)


def total_kernel(parts, out):
    total = parts[0].astype(F32)
    for part in range(1, parts.shape[0]):
        total = total + parts[part].astype(F32)
    out[...] = total.astype(BF)


def total_of(parts):
    return pl.pallas_call(
        total_kernel,
        out_shape=jax.ShapeDtypeStruct(parts.shape[1:], BF),
        in_specs=[vmem_spec()],
        out_specs=vmem_spec(),
        name="total",
    )(parts)


def per_device(
    pages,
    valid_counts,
    dw_weight,
    dw_bias,
    norm1_gain,
    fc1_w,
    fc1_b,
    fc2_w,
    fc2_b,
    layer_scale,
    norm2_gain,
    w_query,
    w_key,
    w_value,
    w_out,
):
    channels = pages.shape[-1]
    rows = pages.shape[1] * pages.shape[2]
    groups = lax.axis_size("head")
    blocks = lax.axis_size("blk")
    depth = blocks // 4
    share = rows // groups

    def flip_y(array):
        return lax.ppermute(array, "blk", [(i, (i + 2 * depth) % blocks) for i in range(blocks)])

    def flip_core(array):
        return lax.ppermute(array, "blk", [(i, i ^ 1) for i in range(blocks)])

    def along_z(array, step):
        def target(i):
            return i // (2 * depth) * (2 * depth) + (i + 2 * step) % (2 * depth)

        return lax.ppermute(array, "blk", [(i, target(i)) for i in range(blocks)])

    own = lax.axis_index("blk").astype(jnp.int32)
    base_y, base_z, base_core = own // (2 * depth), own // 2 % depth, own % 2

    order = []
    for shifts in ((0,), (-1, 1), (-2, 2), (-3, 3), (4,)):
        for core in (0, 1):
            for side in (0, 1):
                for shift in shifts:
                    order.append((side, shift, core))
    sides = jnp.array([one[0] for one in order], jnp.int32)
    shifts = jnp.array([one[1] for one in order], jnp.int32)
    cores = jnp.array([one[2] for one in order], jnp.int32)
    numbers = (base_y ^ sides) * (2 * depth) + (base_z + shifts) % depth * 2 + (base_core ^ cores)
    counts = valid_counts[numbers]
    place = lax.axis_index("head").astype(jnp.int32)[None]

    partial = mlp(pages, dw_weight, dw_bias, norm1_gain, fc1_w, fc1_b, fc2_w)
    parts = lax.all_to_all(partial.reshape(groups, share, channels), "head", 0, 0, tiled=True)
    copies = block_norm(place, parts, pages.reshape(rows, channels), layer_scale, fc2_b, norm2_gain)
    normed = lax.all_to_all(copies, "head", 0, 0, tiled=True).reshape(rows, channels)

    start = key_values(normed, w_key, w_value)
    up, down = along_z(start, 1), along_z(start, -1)
    query = queries_of(normed, w_query)
    pair = jnp.concatenate([start, flip_y(start)])
    pair_core = flip_core(pair)

    def spread(array):
        both = jnp.concatenate([array, flip_y(array)])
        return both, flip_core(both)

    one = spread(jnp.concatenate([up, down]))
    up, down = along_z(up, 1), along_z(down, -1)
    two = spread(jnp.concatenate([up, down]))
    up, down = along_z(up, 1), along_z(down, -1)
    three = spread(jnp.concatenate([up, down]))
    up, down = along_z(up[:, : rows // 2], 1), along_z(down[:, rows // 2 :], -1)
    four = spread(jnp.concatenate([up, down], axis=1))

    carry = attend(counts, query, [pair, pair_core, *one], 0)
    carry = attend(counts, query, [*two], 12, carry)
    carry = attend(counts, query, [*three], 20, carry)
    (mixed,) = attend(counts, query, [*four], 28, carry, w_out)
    parts = lax.all_to_all(mixed.reshape(groups, share, channels), "head", 0, 0, tiled=True)
    return total_of(parts)


def solution(mesh):
    in_specs = (
        P("blk", None, None, None),
        P(),
        P(),
        P(),
        P(),
        P(None, "head"),
        P("head"),
        P("head", None),
        P(),
        P(),
        P(),
        P(None, "head"),
        P(None, "head"),
        P(None, "head"),
        P("head", None),
    )
    out_specs = P(("blk", "head"), None)
    return jax.shard_map(per_device, mesh=mesh, in_specs=in_specs, out_specs=out_specs, check_vma=False)
```

time: 355 us -> 131 us (0.37)
  waiting for transfers between devices: 267 us -> 27.2 us
  Pallas kernels: 0 us -> 41.5 us
  matrix products: 38.9 us -> 0 us
  other arithmetic: 31.2 us -> 0.15 us
  blocking collectives: 0 us -> 28.4 us
  starting transfers between devices: 0.31 us -> 23.4 us
  between operations: 13.2 us -> 0.3 us
  local copies, waits for them, and re-layouts: 4.04 us -> 9.57 us
    all_gather x2 -> x0, waiting for transfers between devices: 95.8 us -> none  [the longest x1 57.3 us: per_device(): lax.all_gather(own_keys, 'blk', axis=0, tiled=True)]
    psum x1 -> x0, waiting for transfers between devices: 94.7 us -> none  [per_device(): summed = lax.psum(partial_sum, 'head')]
    reduce_scatter x1 -> x0, waiting for transfers between devices: 75.9 us -> none  [per_device(): lax.psum_scatter(jnp.dot(attended, w_out, preferred_element_type=jnp.floa...]
    pallas_call x0 -> x9, Pallas kernels: none -> 41.5 us  [the longest x4 23.4 us: attend(): pl.pallas_call(functools.partial(attend_kernel, carry is None, w_out is n...]
    dot_general x7 -> x0, matrix products: 38.9 us -> none  [the longest x1 14.5 us: fold_keys(): jnp.einsum('rgqd,ngd->gqrn', queries, key_heads, preferred_element_type=j...]
    all_to_all x0 -> x2, blocking collectives: none -> 28.4 us  [the longest x1 15 us: per_device(): lax.all_to_all(mixed.reshape(groups, share, channels), 'head', 0, 0, tile...]
    reduce_sum x6 -> x0, other arithmetic: 26.2 us -> none  [the longest x1 15.1 us: fold_keys(): denominator = jnp.sum(exponent, axis=-1)]
    ppermute x0 -> x18, waiting for transfers between devices: none -> 20.1 us  [the longest x8 19.4 us: along_z(): return lax.ppermute(array, 'blk', [(i, target(i)) for i in range(blocks)])]
  transfers between devices with their start and end apart: 4 -> 19, of which waited for: 4 -> 10; matrix products, arithmetic and copies ran while one was open for 10% -> 2% of each run, Pallas kernels for 0% -> 16%
where the time goes in v1:
time: 131 us; the launch traced here: 130 us
  Pallas kernels  41.5 us (32%)
  blocking collectives  28.4 us (22%)
  waiting for transfers between devices  27.2 us (21%)
  starting transfers between devices  23.4 us (18%)
  local copies, waits for them, and re-layouts  9.57 us (7%)
    pallas_call x4, Pallas kernels, attend(): pl.pallas_call(functools.partial(attend_kernel, carry is None, w_out is n...  23.4 us
    ppermute x8, waiting for transfers between devices, along_z(): return lax.ppermute(array, 'blk', [(i, target(i)) for i in range(blocks)])  19.4 us
    all_to_all x1, blocking collectives, per_device(): lax.all_to_all(mixed.reshape(groups, share, channels), 'head', 0, 0, tile...  15 us
    all_to_all x1, blocking collectives, per_device(): lax.all_to_all(copies, 'head', 0, 0, tiled=True).reshape(rows, channels)  13.4 us
    ppermute x8, starting transfers between devices, along_z(): return lax.ppermute(array, 'blk', [(i, target(i)) for i in range(blocks)])  10.2 us
    pallas_call x1, Pallas kernels, mlp(): pl.pallas_call(mlp_kernel, out_shape=jax.ShapeDtypeStruct((rows, channels...  9.84 us
    all_to_all x1, waiting for transfers between devices, per_device(): lax.all_to_all(partial.reshape(groups, share, channels), 'head', 0, 0, ti...  7.12 us
    all_to_all x1, starting transfers between devices, per_device(): lax.all_to_all(partial.reshape(groups, share, channels), 'head', 0, 0, ti...  6.92 us
  transfers between devices with their start and end apart: 19, of which 10 were waited for; matrix products, arithmetic and copies ran while one was open for 2% of the time, Pallas kernels for 16%

profile of v1, /device:TPU:32, one launch (start us, length us, event | category | flops | bytes accessed | tf_op | source)
XLA Modules:
  0.0 130.4 jit_solution(7317977558697207514)
XLA Ops:
  0.0 1.3 broadcast_in_dim.26.dwb
  1.3 0.6 broadcast_in_dim.27.gain
  2.0 0.6 broadcast_in_dim.28.b1
  2.6 9.8 %conv_mlp.1 = bf16[256,768]{1,0:T(8,128)(2,1)} custom-call(bf16[16,16,768]{2,1,0:T(8,128)(2,1)} %bitcast.8, f32[7,7,768]{2,1,0:T(8,128)} %dw.1, f32[1,768]{1,0:T(1,128)} %broadcast_in_dim.26.dwb, f32[1,768]{1,0:T(1,128)} %broadcast_in_dim.27.gain, bf16[768,384]{1,0:T(8,128)(2,1)} %w1.1, f32[1,384]{1,0:T(1,128)} %broadcast_in_dim.28.b1, bf16[384,768]{1,0:T(8,128)(2,1)} %w2.1), custom_call_target="tpu_custom_call" | custom-call | tf_op jit(solution)/shard_map/conv_mlp/pallas_call | solution.py:57
  12.4 6.9 %all-to-all-start = ((bf16[8,32,768]{2,1,0:T(8,128)(2,1)}), bf16[8,32,768]{2,1,0:T(8,128)(2,1)S(1)}, u32[]{:S(2)}, u32[]{:S(2)}) async-start(bf16[8,32,768]{2,1,0:T(8,128)(2,1)} %bitcast.10), calls=%async_computation | async-start | bytes 786432 | tf_op jit(solution)/shard_map/all_to_all | solution.py:284
  19.3 0.7 copy-done.10
  20.0 0.6 broadcast_in_dim.29.scale
  20.6 0.6 broadcast_in_dim.30.b2
  21.3 0.6 broadcast_in_dim.31.gain
  21.9 7.1 %all-to-all-done.parts = bf16[8,32,768]{2,1,0:T(8,128)(2,1)S(1)} async-done(((bf16[8,32,768]{2,1,0:T(8,128)(2,1)}), bf16[8,32,768]{2,1,0:T(8,128)(2,1)S(1)}, u32[]{:S(2)}, u32[]{:S(2)}) %all-to-all-start) | async-done | bytes 393248 | tf_op jit(solution)/shard_map/all_to_all | solution.py:284
  29.0 0.8 copy-done.1
  29.7 2.1 %block_norm.1 = bf16[8,32,768]{2,1,0:T(8,128)(2,1)} custom-call(s32[1]{0:T(128)} %bitcast.place, bf16[8,32,768]{2,1,0:T(8,128)(2,1)} %copy-done.1, bf16[256,768]{1,0:T(8,128)(2,1)} %bitcast.9, f32[1,768]{1,0:T(1,128)} %broadcast_in_dim.29.scale, f32[1,768]{1,0:T(1,128)} %broadcast_in_dim.30.b2, f32[1,768]{1,0:T(1,128)} %broadcast_in_dim.31.gain), custom_call_target="tpu_custom_call" | custom-call | tf_op jit(solution)/shard_map/block_norm/pallas_call | solution.py:84
  31.9 13.4 %all_to_all.15 = bf16[8,32,768]{2,1,0:T(8,128)(2,1)} all-to-all(bf16[8,32,768]{2,1,0:T(8,128)(2,1)} %block_norm.1), channel_id=1, replica_groups=mesh['blk'=32,'head'=8] {'head'}, dimensions={0} | all-to-all | bytes 786432 | tf_op jit(solution)/shard_map/all_to_all | solution.py:286
  45.3 2.1 %key_values.1 = bf16[1,256,256]{2,1,0:T(8,128)(2,1)} custom-call(bf16[256,768]{1,0:T(8,128)(2,1)} %bitcast.6, bf16[768,128]{1,0:T(8,128)(2,1)} %wk.1, bf16[768,128]{1,0:T(8,128)(2,1)} %wv.1), custom_call_target="tpu_custom_call" | custom-call | tf_op jit(solution)/shard_map/key_values/pallas_call | solution.py:101
  47.4 1.9 %collective-permute-start = (bf16[1,256,256]{2,1,0:T(8,128)(2,1)}, bf16[1,256,256]{2,1,0:T(8,128)(2,1)S(1)}, u32[]{:S(2)}, u32[]{:S(2)}) collective-permute-start(bf16[1,256,256]{2,1,0:T(8,128)(2,1)} %key_values.1), channel_id=1, source_target_pairs={{0,16},{8,24},{16,32},{24,40},{32,48},{40,56},{48,64},{56,72},{64,... | collective-permute-start | bytes 393224 | tf_op jit(solution)/shard_map/ppermute | solution.py:265
  49.4 0.7 collective-permute-start.14
  50.1 2.5 %collective-permute-done = bf16[1,256,256]{2,1,0:T(8,128)(2,1)S(1)} collective-permute-done((bf16[1,256,256]{2,1,0:T(8,128)(2,1)}, bf16[1,256,256]{2,1,0:T(8,128)(2,1)S(1)}, u32[]{:S(2)}, u32[]{:S(2)}) %collective-permute-start) | collective-permute-done | bytes 131104 | tf_op jit(solution)/shard_map/ppermute | solution.py:265
  52.6 1.9 %collective-permute-done.4 = bf16[1,256,256]{2,1,0:T(8,128)(2,1)S(1)} collective-permute-done((bf16[1,256,256]{2,1,0:T(8,128)(2,1)}, bf16[1,256,256]{2,1,0:T(8,128)(2,1)S(1)}, u32[]{:S(2)}, u32[]{:S(2)}) %collective-permute-start.4) | collective-permute-done | bytes 131104 | tf_op jit(solution)/shard_map/ppermute | solution.py:265
  54.5 0.8 collective-permute-start.16
  55.3 0.7 collective-permute-done.14
  56.0 0.3 collective-permute-start.15
  56.3 2.5 %collective-permute-start.1 = (bf16[1,256,256]{2,1,0:T(8,128)(2,1)S(1)}, bf16[1,256,256]{2,1,0:T(8,128)(2,1)S(1)}, u32[]{:S(2)}, u32[]{:S(2)}) collective-permute-start(bf16[1,256,256]{2,1,0:T(8,128)(2,1)S(1)} %collective-permute-done), channel_id=1, source_target_pairs={{0,16},{8,24},{16,32},{24,40},{32,48},{40,56},{48,64},{56,72},{64,... | collective-permute-start | bytes 393224 | tf_op jit(solution)/shard_map/ppermute | solution.py:265
  58.8 1.6 %collective-permute-start.5 = (bf16[1,256,256]{2,1,0:T(8,128)(2,1)S(1)}, bf16[1,256,256]{2,1,0:T(8,128)(2,1)S(1)}, u32[]{:S(2)}, u32[]{:S(2)}) collective-permute-start(bf16[1,256,256]{2,1,0:T(8,128)(2,1)S(1)} %collective-permute-done.4), channel_id=1, source_target_pairs={{0,112},{8,120},{16,0},{24,8},{32,16},{40,24},{48,32},{56,40},{64,... | collective-permute-start | bytes 393224 | tf_op jit(solution)/shard_map/ppermute | solution.py:265
  60.4 3.9 %collective-permute-done.1 = bf16[1,256,256]{2,1,0:T(8,128)(2,1)S(1)} collective-permute-done((bf16[1,256,256]{2,1,0:T(8,128)(2,1)S(1)}, bf16[1,256,256]{2,1,0:T(8,128)(2,1)S(1)}, u32[]{:S(2)}, u32[]{:S(2)}) %collective-permute-start.1) | collective-permute-done | bytes 131104 | tf_op jit(solution)/shard_map/ppermute | solution.py:265
  64.3 1.4 %collective-permute-done.5 = bf16[1,256,256]{2,1,0:T(8,128)(2,1)S(1)} collective-permute-done((bf16[1,256,256]{2,1,0:T(8,128)(2,1)S(1)}, bf16[1,256,256]{2,1,0:T(8,128)(2,1)S(1)}, u32[]{:S(2)}, u32[]{:S(2)}) %collective-permute-start.5) | collective-permute-done | bytes 131104 | tf_op jit(solution)/shard_map/ppermute | solution.py:265
  65.8 1.4 %collective-permute-start.12 = (bf16[2,256,256]{2,1,0:T(8,128)(2,1)S(1)}, bf16[2,256,256]{2,1,0:T(8,128)(2,1)S(1)}, u32[]{:S(2)}, u32[]{:S(2)}) collective-permute-start(bf16[2,256,256]{2,1,0:T(8,128)(2,1)S(1)} %pad_maximum_fusion.2), channel_id=1, source_target_pairs={{0,128},{8,136},{16,144},{24,152},{32,160},{40,168},{48,176},{56,1... | collective-permute-start | bytes 786440 | tf_op jit(solution)/shard_map/ppermute | solution.py:256
  67.2 1.7 %collective-permute-start.2 = (bf16[1,256,256]{2,1,0:T(8,128)(2,1)S(1)}, bf16[1,256,256]{2,1,0:T(8,128)(2,1)S(1)}, u32[]{:S(2)}, u32[]{:S(2)}) collective-permute-start(bf16[1,256,256]{2,1,0:T(8,128)(2,1)S(1)} %collective-permute-done.1), channel_id=1, source_target_pairs={{0,16},{8,24},{16,32},{24,40},{32,48},{40,56},{48,64},{56,72},{64,... | collective-permute-start | bytes 393224 | tf_op jit(solution)/shard_map/ppermute | solution.py:265
  69.0 0.3 collective-permute-start.6
  69.3 2.9 %collective-permute-done.2 = bf16[1,256,256]{2,1,0:T(8,128)(2,1)S(1)} collective-permute-done((bf16[1,256,256]{2,1,0:T(8,128)(2,1)S(1)}, bf16[1,256,256]{2,1,0:T(8,128)(2,1)S(1)}, u32[]{:S(2)}, u32[]{:S(2)}) %collective-permute-start.2) | collective-permute-done | bytes 131104 | tf_op jit(solution)/shard_map/ppermute | solution.py:265
  72.2 2.5 %collective-permute-done.6 = bf16[1,256,256]{2,1,0:T(8,128)(2,1)S(1)} collective-permute-done((bf16[1,256,256]{2,1,0:T(8,128)(2,1)S(1)}, bf16[1,256,256]{2,1,0:T(8,128)(2,1)S(1)}, u32[]{:S(2)}, u32[]{:S(2)}) %collective-permute-start.6) | collective-permute-done | bytes 131104 | tf_op jit(solution)/shard_map/ppermute | solution.py:265
  74.7 1.4 %collective-permute-start.10 = (bf16[2,256,256]{2,1,0:T(8,128)(2,1)S(1)}, bf16[2,256,256]{2,1,0:T(8,128)(2,1)S(1)}, u32[]{:S(2)}, u32[]{:S(2)}) collective-permute-start(bf16[2,256,256]{2,1,0:T(8,128)(2,1)S(1)} %pad_maximum_fusion.1), channel_id=1, source_target_pairs={{0,128},{8,136},{16,144},{24,152},{32,160},{40,168},{48,176},{56,1... | collective-permute-start | bytes 786440 | tf_op jit(solution)/shard_map/ppermute | solution.py:256
  76.2 2.0 %collective-permute-start.3 = (bf16[1,128,256]{2,1,0:T(8,128)(2,1)S(1)}, bf16[1,128,256]{2,1,0:T(8,128)(2,1)S(1)}, u32[]{:S(2)}, u32[]{:S(2)}) collective-permute-start(bf16[1,128,256]{2,1,0:T(8,128)(2,1)S(1)} %slice.10), channel_id=1, source_target_pairs={{0,16},{8,24},{16,32},{24,40},{32,48},{40,56},{48,64},{56,72},{64,... | collective-permute-start | bytes 196616 | tf_op jit(solution)/shard_map/ppermute | solution.py:265
  78.4 2.1 %collective-permute-done.3 = bf16[1,128,256]{2,1,0:T(8,128)(2,1)S(1)} collective-permute-done((bf16[1,128,256]{2,1,0:T(8,128)(2,1)S(1)}, bf16[1,128,256]{2,1,0:T(8,128)(2,1)S(1)}, u32[]{:S(2)}, u32[]{:S(2)}) %collective-permute-start.3) | collective-permute-done | bytes 65568 | tf_op jit(solution)/shard_map/ppermute | solution.py:265
  80.4 2.1 %collective-permute-done.7 = bf16[1,128,256]{2,1,0:T(8,128)(2,1)S(1)} collective-permute-done((bf16[1,128,256]{2,1,0:T(8,128)(2,1)S(1)}, bf16[1,128,256]{2,1,0:T(8,128)(2,1)S(1)}, u32[]{:S(2)}, u32[]{:S(2)}) %collective-permute-start.7) | collective-permute-done | bytes 65568 | tf_op jit(solution)/shard_map/ppermute | solution.py:265
  82.6 0.7 collective-permute-start.8
  83.5 0.6 collective-permute-start.11
  84.2 1.2 gather_fusion
  85.4 2.3 %queries.1.refs_1_ = bf16[4,256,128]{2,1,0:T(8,128)(2,1)} custom-call(bf16[256,768]{1,0:T(8,128)(2,1)} %bitcast.7, bf16[768,512]{1,0:T(8,128)(2,1)} %wq.1), custom_call_target="tpu_custom_call" | custom-call | tf_op jit(solution)/shard_map/queries/pallas_call | solution.py:118
  87.7 0.3 collective-permute-start.9
  88.1 0.8 copy-done.17
  88.9 6.8 %attend.4 = (f32[4,256,128]{2,1,0:T(8,128)}, f32[4,256,256]{2,1,0:T(8,128)}) custom-call(s32[32]{0:T(128)} %gather_fusion, bf16[4,256,128]{2,1,0:T(8,128)(2,1)} %queries.1.refs_1_, bf16[2,256,256]{2,1,0:T(8,128)(2,1)} %copy-done.4, bf16[2,256,256]{2,1,0:T(8,128)(2,1)} %collective-permute-done.15.refs_3_, bf16[4,256,256]{2,1,0:T(8,128)(2,1)} %copy-done.7, ...), custom_call_target="tpu_custom_call" | custom-call | flops 1610612736 | bytes 4194304 | tf_op jit(solution)/shard_map/attend/pallas_call | solution.py:203
  95.7 0.8 copy-done.18
  96.5 5.9 %attend.5 = (f32[4,256,128]{2,1,0:T(8,128)}, f32[4,256,256]{2,1,0:T(8,128)}) custom-call(s32[32]{0:T(128)} %gather_fusion, bf16[4,256,128]{2,1,0:T(8,128)(2,1)} %queries.1.refs_1_, bf16[4,256,256]{2,1,0:T(8,128)(2,1)} %copy-done.8, bf16[4,256,256]{2,1,0:T(8,128)(2,1)} %copy-done.18, f32[4,256,128]{2,1,0:T(8,128)} %get-tuple-element.11.refs_4_, ...), custom_call_target="tpu_custom_call" | custom-call | flops 1073741824 | bytes 4194304 | tf_op jit(solution)/shard_map/attend/pallas_call | solution.py:203
  102.4 5.9 %attend.6 = (f32[4,256,128]{2,1,0:T(8,128)}, f32[4,256,256]{2,1,0:T(8,128)}) custom-call(s32[32]{0:T(128)} %gather_fusion, bf16[4,256,128]{2,1,0:T(8,128)(2,1)} %queries.1.refs_1_, bf16[4,256,256]{2,1,0:T(8,128)(2,1)} %copy-done.6, bf16[4,256,256]{2,1,0:T(8,128)(2,1)} %collective-permute-done.11.refs_3_, f32[4,256,128]{2,1,0:T(8,128)} %get-tuple-element.13.refs_4_, ...), custom_call_target="tpu_custom_call" | custom-call | flops 1073741824 | bytes 4194304 | tf_op jit(solution)/shard_map/attend/pallas_call | solution.py:203
  108.4 0.7 copy-done.5
  109.1 4.7 %attend.7 = bf16[256,768]{1,0:T(8,128)(2,1)} custom-call(s32[32]{0:T(128)} %gather_fusion, bf16[4,256,128]{2,1,0:T(8,128)(2,1)} %queries.1.refs_1_, bf16[2,256,256]{2,1,0:T(8,128)(2,1)} %copy-done.2, bf16[2,256,256]{2,1,0:T(8,128)(2,1)} %copy-done.5, f32[4,256,128]{2,1,0:T(8,128)} %get-tuple-element.15.refs_4_, f32[4,256,256]{2,1,0:T(8,128)} %get-tuple-element.16.refs_5_, ...), custom_call_target="tpu_custom_call" | custom-call | flops 536870912 | bytes 4194304 | tf_op jit(solution)/shard_map/attend/pallas_call | solution.py:203
  113.8 15.0 %all_to_all.16.parts = bf16[8,32,768]{2,1,0:T(8,128)(2,1)} all-to-all(bf16[8,32,768]{2,1,0:T(8,128)(2,1)} %bitcast.11), channel_id=1, replica_groups=mesh['blk'=32,'head'=8] {'head'}, dimensions={0} | all-to-all | bytes 786432 | tf_op jit(solution)/shard_map/all_to_all | solution.py:310
  128.8 1.7 %total.1 = bf16[32,768]{1,0:T(8,128)(2,1)} custom-call(bf16[8,32,768]{2,1,0:T(8,128)(2,1)} %all_to_all.16.parts), custom_call_target="tpu_custom_call" | custom-call | tf_op jit(solution)/shard_map/total/pallas_call | solution.py:222
  (66 shorter events, 0.9 us)
Async XLA Ops:
  0.0 84.1 %copy-start = (s32[32]{0:T(128)S(1)}, s32[32]{0:T(128)}, u32[]{:S(2)}) copy-start(s32[32]{0:T(128)} %param.19) | copy-start | bytes 388
  0.0 1.3 copy-start.9
  1.3 0.7 copy-start.13
  12.4 16.6 %all-to-all-start = ((bf16[8,32,768]{2,1,0:T(8,128)(2,1)}), bf16[8,32,768]{2,1,0:T(8,128)(2,1)S(1)}, u32[]{:S(2)}, u32[]{:S(2)}) async-start(bf16[8,32,768]{2,1,0:T(8,128)(2,1)} %bitcast.10), calls=%async_computation | async-start | bytes 786432 | tf_op jit(solution)/shard_map/all_to_all | solution.py:284
  19.3 0.7 copy-start.10
  19.3 1.3 copy-start.11
  20.6 0.7 copy-start.12
  29.0 0.8 copy-start.1
  47.4 5.2 %collective-permute-start = (bf16[1,256,256]{2,1,0:T(8,128)(2,1)}, bf16[1,256,256]{2,1,0:T(8,128)(2,1)S(1)}, u32[]{:S(2)}, u32[]{:S(2)}) collective-permute-start(bf16[1,256,256]{2,1,0:T(8,128)(2,1)} %key_values.1), channel_id=1, source_target_pairs={{0,16},{8,24},{16,32},{24,40},{32,48},{40,56},{48,64},{56,72},{64,... | collective-permute-start | bytes 393224 | tf_op jit(solution)/shard_map/ppermute | solution.py:265
  49.3 5.2 %collective-permute-start.4 = (bf16[1,256,256]{2,1,0:T(8,128)(2,1)}, bf16[1,256,256]{2,1,0:T(8,128)(2,1)S(1)}, u32[]{:S(2)}, u32[]{:S(2)}) collective-permute-start(bf16[1,256,256]{2,1,0:T(8,128)(2,1)} %key_values.1), channel_id=1, source_target_pairs={{0,112},{8,120},{16,0},{24,8},{32,16},{40,24},{48,32},{56,40},{64,... | collective-permute-start | bytes 393224 | tf_op jit(solution)/shard_map/ppermute | solution.py:265
  49.4 6.5 %collective-permute-start.14 = (bf16[1,256,256]{2,1,0:T(8,128)(2,1)}, bf16[1,256,256]{2,1,0:T(8,128)(2,1)S(1)}, u32[]{:S(2)}, u32[]{:S(2)}) collective-permute-start(bf16[1,256,256]{2,1,0:T(8,128)(2,1)} %key_values.1), channel_id=1, source_target_pairs={{0,128},{8,136},{16,144},{24,152},{32,160},{40,168},{48,176},{56,1... | collective-permute-start | bytes 393224 | tf_op jit(solution)/shard_map/ppermute | solution.py:256
  50.1 5.9 %copy-start.3 = (bf16[1,256,256]{2,1,0:T(8,128)(2,1)S(1)}, bf16[1,256,256]{2,1,0:T(8,128)(2,1)}, u32[]{:S(2)}) copy-start(bf16[1,256,256]{2,1,0:T(8,128)(2,1)} %key_values.1) | copy-start | bytes 393220
  54.5 23.7 %collective-permute-start.16 = (bf16[2,256,256]{2,1,0:T(8,128)(2,1)S(1)}, bf16[2,256,256]{2,1,0:T(8,128)(2,1)S(1)}, u32[]{:S(2)}, u32[]{:S(2)}) collective-permute-start(bf16[2,256,256]{2,1,0:T(8,128)(2,1)S(1)} %pad_maximum_fusion.4), channel_id=1, source_target_pairs={{0,128},{8,136},{16,144},{24,152},{32,160},{40,168},{48,176},{56,1... | collective-permute-start | bytes 786440 | tf_op jit(solution)/shard_map/ppermute | solution.py:256
  56.0 4.4 %copy-start.4 = (bf16[2,256,256]{2,1,0:T(8,128)(2,1)}, bf16[2,256,256]{2,1,0:T(8,128)(2,1)S(1)}, u32[]{:S(2)}) copy-start(bf16[2,256,256]{2,1,0:T(8,128)(2,1)S(1)} %pad_maximum_fusion.3.refs_2_) | copy-start | bytes 786436
  56.0 32.1 %collective-permute-start.15 = (bf16[2,256,256]{2,1,0:T(8,128)(2,1)S(1)}, bf16[2,256,256]{2,1,0:T(8,128)(2,1)}, u32[]{:S(2)}, u32[]{:S(2)}) collective-permute-start(bf16[2,256,256]{2,1,0:T(8,128)(2,1)S(1)} %pad_maximum_fusion.3.refs_2_), channel_id=1, source_target_pairs={{0,8},{8,0},{16,24},{24,16},{32,40},{40,32},{48,56},{56,48},{64,72... | collective-permute-start | bytes 786440 | tf_op jit(solution)/shard_map/ppermute | solution.py:259
  56.3 8.0 %collective-permute-start.1 = (bf16[1,256,256]{2,1,0:T(8,128)(2,1)S(1)}, bf16[1,256,256]{2,1,0:T(8,128)(2,1)S(1)}, u32[]{:S(2)}, u32[]{:S(2)}) collective-permute-start(bf16[1,256,256]{2,1,0:T(8,128)(2,1)S(1)} %collective-permute-done), channel_id=1, source_target_pairs={{0,16},{8,24},{16,32},{24,40},{32,48},{40,56},{48,64},{56,72},{64,... | collective-permute-start | bytes 393224 | tf_op jit(solution)/shard_map/ppermute | solution.py:265
  58.8 7.0 %collective-permute-start.5 = (bf16[1,256,256]{2,1,0:T(8,128)(2,1)S(1)}, bf16[1,256,256]{2,1,0:T(8,128)(2,1)S(1)}, u32[]{:S(2)}, u32[]{:S(2)}) collective-permute-start(bf16[1,256,256]{2,1,0:T(8,128)(2,1)S(1)} %collective-permute-done.4), channel_id=1, source_target_pairs={{0,112},{8,120},{16,0},{24,8},{32,16},{40,24},{48,32},{56,40},{64,... | collective-permute-start | bytes 393224 | tf_op jit(solution)/shard_map/ppermute | solution.py:265
  65.8 17.5 %collective-permute-start.12 = (bf16[2,256,256]{2,1,0:T(8,128)(2,1)S(1)}, bf16[2,256,256]{2,1,0:T(8,128)(2,1)S(1)}, u32[]{:S(2)}, u32[]{:S(2)}) collective-permute-start(bf16[2,256,256]{2,1,0:T(8,128)(2,1)S(1)} %pad_maximum_fusion.2), channel_id=1, source_target_pairs={{0,128},{8,136},{16,144},{24,152},{32,160},{40,168},{48,176},{56,1... | collective-permute-start | bytes 786440 | tf_op jit(solution)/shard_map/ppermute | solution.py:256
  67.2 5.0 %collective-permute-start.2 = (bf16[1,256,256]{2,1,0:T(8,128)(2,1)S(1)}, bf16[1,256,256]{2,1,0:T(8,128)(2,1)S(1)}, u32[]{:S(2)}, u32[]{:S(2)}) collective-permute-start(bf16[1,256,256]{2,1,0:T(8,128)(2,1)S(1)} %collective-permute-done.1), channel_id=1, source_target_pairs={{0,16},{8,24},{16,32},{24,40},{32,48},{40,56},{48,64},{56,72},{64,... | collective-permute-start | bytes 393224 | tf_op jit(solution)/shard_map/ppermute | solution.py:265
  69.0 5.7 %collective-permute-start.6 = (bf16[1,256,256]{2,1,0:T(8,128)(2,1)S(1)}, bf16[1,256,256]{2,1,0:T(8,128)(2,1)S(1)}, u32[]{:S(2)}, u32[]{:S(2)}) collective-permute-start(bf16[1,256,256]{2,1,0:T(8,128)(2,1)S(1)} %collective-permute-done.5), channel_id=1, source_target_pairs={{0,112},{8,120},{16,0},{24,8},{32,16},{40,24},{48,32},{56,40},{64,... | collective-permute-start | bytes 393224 | tf_op jit(solution)/shard_map/ppermute | solution.py:265
  74.7 8.7 %collective-permute-start.10 = (bf16[2,256,256]{2,1,0:T(8,128)(2,1)S(1)}, bf16[2,256,256]{2,1,0:T(8,128)(2,1)S(1)}, u32[]{:S(2)}, u32[]{:S(2)}) collective-permute-start(bf16[2,256,256]{2,1,0:T(8,128)(2,1)S(1)} %pad_maximum_fusion.1), channel_id=1, source_target_pairs={{0,128},{8,136},{16,144},{24,152},{32,160},{40,168},{48,176},{56,1... | collective-permute-start | bytes 786440 | tf_op jit(solution)/shard_map/ppermute | solution.py:256
  76.2 4.3 %collective-permute-start.3 = (bf16[1,128,256]{2,1,0:T(8,128)(2,1)S(1)}, bf16[1,128,256]{2,1,0:T(8,128)(2,1)S(1)}, u32[]{:S(2)}, u32[]{:S(2)}) collective-permute-start(bf16[1,128,256]{2,1,0:T(8,128)(2,1)S(1)} %slice.10), channel_id=1, source_target_pairs={{0,16},{8,24},{16,32},{24,40},{32,48},{40,56},{48,64},{56,72},{64,... | collective-permute-start | bytes 196616 | tf_op jit(solution)/shard_map/ppermute | solution.py:265
  78.2 4.3 %collective-permute-start.7 = (bf16[1,128,256]{2,1,0:T(8,128)(2,1)S(1)}, bf16[1,128,256]{2,1,0:T(8,128)(2,1)S(1)}, u32[]{:S(2)}, u32[]{:S(2)}) collective-permute-start(bf16[1,128,256]{2,1,0:T(8,128)(2,1)S(1)} %slice.11), channel_id=1, source_target_pairs={{0,112},{8,120},{16,0},{24,8},{32,16},{40,24},{48,32},{56,40},{64,... | collective-permute-start | bytes 196616 | tf_op jit(solution)/shard_map/ppermute | solution.py:265
  78.4 5.1 %copy-start.7 = (bf16[4,256,256]{2,1,0:T(8,128)(2,1)}, bf16[4,256,256]{2,1,0:T(8,128)(2,1)S(1)}, u32[]{:S(2)}) copy-start(bf16[4,256,256]{2,1,0:T(8,128)(2,1)S(1)} %constant_dynamic-update-slice_fusion.8.refs_4_) | copy-start | bytes 1572868
  80.4 7.6 %collective-permute-start.17 = (bf16[4,256,256]{2,1,0:T(8,128)(2,1)S(1)}, bf16[4,256,256]{2,1,0:T(8,128)(2,1)S(1)}, u32[]{:S(2)}, u32[]{:S(2)}) collective-permute-start(bf16[4,256,256]{2,1,0:T(8,128)(2,1)S(1)} %constant_dynamic-update-slice_fusion.8.refs_4_), channel_id=1, source_target_pairs={{0,8},{8,0},{16,24},{24,16},{32,40},{40,32},{48,56},{56,48},{64,72... | collective-permute-start | bytes 1572872 | tf_op jit(solution)/shard_map/ppermute | solution.py:259
  82.6 5.1 %collective-permute-start.8 = (bf16[1,256,256]{2,1,0:T(8,128)(2,1)S(1)}, bf16[1,256,256]{2,1,0:T(8,128)(2,1)S(1)}, u32[]{:S(2)}, u32[]{:S(2)}) collective-permute-start(bf16[1,256,256]{2,1,0:T(8,128)(2,1)S(1)} %constant_dynamic-update-slice_fusion), channel_id=1, source_target_pairs={{0,128},{8,136},{16,144},{24,152},{32,160},{40,168},{48,176},{56,1... | collective-permute-start | bytes 393224 | tf_op jit(solution)/shard_map/ppermute | solution.py:256
  83.3 2.1 %copy-start.8 = (bf16[4,256,256]{2,1,0:T(8,128)(2,1)}, bf16[4,256,256]{2,1,0:T(8,128)(2,1)S(1)}, u32[]{:S(2)}) copy-start(bf16[4,256,256]{2,1,0:T(8,128)(2,1)S(1)} %constant_dynamic-update-slice_fusion.5.refs_2_) | copy-start | bytes 1572868
  83.3 0.8 copy-start.14
  83.3 0.8 copy-start.15
  83.3 0.8 copy-start.16
  83.3 12.4 %collective-permute-start.13 = (bf16[4,256,256]{2,1,0:T(8,128)(2,1)S(1)}, bf16[4,256,256]{2,1,0:T(8,128)(2,1)S(1)}, u32[]{:S(2)}, u32[]{:S(2)}) collective-permute-start(bf16[4,256,256]{2,1,0:T(8,128)(2,1)S(1)} %constant_dynamic-update-slice_fusion.5.refs_2_), channel_id=1, source_target_pairs={{0,8},{8,0},{16,24},{24,16},{32,40},{40,32},{48,56},{56,48},{64,72... | collective-permute-start | bytes 1572872 | tf_op jit(solution)/shard_map/ppermute | solution.py:259
  83.5 4.2 %copy-start.6 = (bf16[4,256,256]{2,1,0:T(8,128)(2,1)}, bf16[4,256,256]{2,1,0:T(8,128)(2,1)S(1)}, u32[]{:S(2)}) copy-start(bf16[4,256,256]{2,1,0:T(8,128)(2,1)S(1)} %constant_dynamic-update-slice_fusion.2.refs_2_) | copy-start | bytes 1572868
  83.5 18.9 %collective-permute-start.11 = (bf16[4,256,256]{2,1,0:T(8,128)(2,1)S(1)}, bf16[4,256,256]{2,1,0:T(8,128)(2,1)}, u32[]{:S(2)}, u32[]{:S(2)}) collective-permute-start(bf16[4,256,256]{2,1,0:T(8,128)(2,1)S(1)} %constant_dynamic-update-slice_fusion.2.refs_2_), channel_id=1, source_target_pairs={{0,8},{8,0},{16,24},{24,16},{32,40},{40,32},{48,56},{56,48},{64,72... | collective-permute-start | bytes 1572872 | tf_op jit(solution)/shard_map/ppermute | solution.py:259
  87.7 8.0 %copy-start.2 = (bf16[2,256,256]{2,1,0:T(8,128)(2,1)}, bf16[2,256,256]{2,1,0:T(8,128)(2,1)S(1)}, u32[]{:S(2)}) copy-start(bf16[2,256,256]{2,1,0:T(8,128)(2,1)S(1)} %pad_maximum_fusion.refs_2_) | copy-start | bytes 786436
  87.7 20.6 %collective-permute-start.9 = (bf16[2,256,256]{2,1,0:T(8,128)(2,1)S(1)}, bf16[2,256,256]{2,1,0:T(8,128)(2,1)S(1)}, u32[]{:S(2)}, u32[]{:S(2)}) collective-permute-start(bf16[2,256,256]{2,1,0:T(8,128)(2,1)S(1)} %pad_maximum_fusion.refs_2_), channel_id=1, source_target_pairs={{0,8},{8,0},{16,24},{24,16},{32,40},{40,32},{48,56},{56,48},{64,72... | collective-permute-start | bytes 786440 | tf_op jit(solution)/shard_map/ppermute | solution.py:259
  88.1 0.8 copy-start.17
  95.7 0.8 copy-start.18
  108.4 0.7 copy-start.5

commit v2 on v1

v2 whole, which is shorter than its diff:
```python
import functools

import jax
import jax.numpy as jnp
from jax import lax
from jax.experimental import pallas as pl
from jax.experimental.pallas import tpu as pltpu
from jax.sharding import PartitionSpec as P

HEADS = 32
KV_HEADS = 8
HD = 128
LANES = 128
LOG2E = 1.4426950408889634
NEG = -1e30
BF = jnp.bfloat16
F32 = jnp.float32


def params(mebibytes):
    return pltpu.CompilerParams(vmem_limit_bytes=mebibytes * 2**20)


def vmem_spec():
    return pl.BlockSpec(memory_space=pltpu.VMEM)


def smem_spec():
    return pl.BlockSpec(memory_space=pltpu.SMEM)


def fold_lanes(pieces):
    return jnp.sum(functools.reduce(jnp.add, pieces), axis=-1, keepdims=True)


def normalise(pieces, gain, epsilon):
    width = len(pieces) * pieces[0].shape[-1]
    mean = fold_lanes(pieces) / width
    centred = [piece - mean for piece in pieces]
    spread = fold_lanes([piece * piece for piece in centred]) / width
    factor = lax.rsqrt(spread + epsilon)
    return [(piece * factor * gain[index : index + 1, :]).astype(BF) for index, piece in enumerate(centred)]


def lane_rows(vector):
    return vector.reshape(-1, LANES)


def mlp_kernel(pages, dw, dwb, gain, w1_hbm, b1, w2_hbm, out, padded, conv, w1, w2, arrived):
    loads = [
        pltpu.make_async_copy(w1_hbm, w1, arrived.at[0]),
        pltpu.make_async_copy(w2_hbm, w2, arrived.at[1]),
    ]
    for load in loads:
        load.start()
    height, breadth, channels = pages.shape
    half = height // 2
    column = lax.broadcasted_iota(jnp.int32, (half, breadth, LANES), 1)
    blank = jnp.zeros((3, breadth, LANES), F32)
    for chunk in range(channels // LANES):
        lanes = slice(chunk * LANES, (chunk + 1) * LANES)
        padded[chunk, 0:3] = blank
        padded[chunk, 3 + height : 6 + height] = blank
        padded[chunk, 3 : 3 + height] = pages[:, :, lanes].astype(F32)
        for top in range(0, height, half):
            total = jnp.broadcast_to(dwb[chunk : chunk + 1, :][None], (half, breadth, LANES))
            for sideways in range(7):
                product = None
                for vertical in range(7):
                    tap = dw[vertical, sideways : sideways + 1, lanes][None]
                    term = padded[chunk, top + vertical : top + vertical + half] * tap
                    product = term if product is None else product + term
                offset = sideways - 3
                if offset:
                    rolled = pltpu.roll(product, (-offset) % breadth, axis=1)
                    inside = (column + offset >= 0) if offset < 0 else (column + offset < breadth)
                    product = jnp.where(inside, rolled, 0.0)
                total = total + product
            conv[chunk, top * breadth : (top + half) * breadth] = total.reshape(half * breadth, LANES)
    normed = normalise([conv[chunk] for chunk in range(channels // LANES)], gain, 1e-06)
    loads[0].wait()
    product = jnp.dot(jnp.concatenate(normed, axis=1), w1[...], preferred_element_type=F32)
    hidden = []
    for chunk in range(product.shape[1] // LANES):
        pre = product[:, chunk * LANES : (chunk + 1) * LANES] + b1[chunk : chunk + 1, :]
        hidden.append((0.5 * pre * (1.0 + lax.erf(pre * 0.7071067811865476))).astype(BF))
    loads[1].wait()
    out[...] = jnp.dot(jnp.concatenate(hidden, axis=1), w2[...], preferred_element_type=F32).astype(BF)


def mlp(pages, dw, dwb, gain, w1, b1, w2):
    _, height, breadth, channels = pages.shape
    rows = height * breadth
    hbm = pl.BlockSpec(memory_space=pltpu.HBM)
    return pl.pallas_call(
        mlp_kernel,
        out_shape=jax.ShapeDtypeStruct((rows, channels), BF),
        in_specs=[vmem_spec()] * 4 + [hbm, vmem_spec(), hbm],
        out_specs=vmem_spec(),
        scratch_shapes=[
            pltpu.VMEM((channels // LANES, height + 6, breadth, LANES), F32),
            pltpu.VMEM((channels // LANES, rows, LANES), F32),
            pltpu.VMEM(w1.shape, w1.dtype),
            pltpu.VMEM(w2.shape, w2.dtype),
            pltpu.SemaphoreType.DMA((2,)),
        ],
        compiler_params=params(16),
        name="conv_mlp",
    )(pages[0], dw, lane_rows(dwb), lane_rows(gain), w1, lane_rows(b1), w2)


def block_kernel(place, parts, pages, scale, b2, gain, out):
    count, chunk, channels = parts.shape
    start = pl.multiple_of(place[0] * chunk, chunk)
    block = []
    for index in range(channels // LANES):
        lanes = slice(index * LANES, (index + 1) * LANES)
        row = slice(index, index + 1)
        total = functools.reduce(jnp.add, [parts[part, :, lanes].astype(F32) for part in range(count)])
        own = pages[pl.ds(start, chunk), lanes].astype(F32)
        block.append(own + scale[row, :] * (total + b2[row, :]))
    normed = jnp.concatenate(normalise(block, gain, 1e-05), axis=1)
    for part in range(count):
        out[part] = normed


def block_norm(place, parts, pages, scale, b2, gain):
    return pl.pallas_call(
        block_kernel,
        out_shape=jax.ShapeDtypeStruct(parts.shape, BF),
        in_specs=[smem_spec()] + [vmem_spec()] * 5,
        out_specs=vmem_spec(),
        compiler_params=params(8),
        name="block_norm",
    )(place, parts, pages, lane_rows(scale), lane_rows(b2), lane_rows(gain))


def kv_kernel(normed, wk, wv, out):
    tokens = normed[...]
    out[0, :, 0:HD] = jnp.dot(tokens, wv[...], preferred_element_type=F32).astype(BF)
    out[0, :, HD : 2 * HD] = jnp.dot(tokens, wk[...], preferred_element_type=F32).astype(BF)


def key_values(normed, wk, wv):
    rows = normed.shape[0]
    return pl.pallas_call(
        kv_kernel,
        out_shape=jax.ShapeDtypeStruct((1, rows, 2 * HD), BF),
        in_specs=[vmem_spec()] * 3,
        out_specs=vmem_spec(),
        compiler_params=params(8),
        name="key_values",
    )(normed, wk, wv)


def query_kernel(normed, wq, out):
    product = jnp.dot(normed[...], wq[...], preferred_element_type=F32) * (HD**-0.5 * LOG2E)
    for head in range(out.shape[0]):
        out[head] = product[:, head * HD : (head + 1) * HD].astype(BF)


def queries_of(normed, wq):
    rows = normed.shape[0]
    return pl.pallas_call(
        query_kernel,
        out_shape=jax.ShapeDtypeStruct((wq.shape[1] // HD, rows, HD), BF),
        in_specs=[vmem_spec()] * 2,
        out_specs=vmem_spec(),
        compiler_params=params(8),
        name="queries",
    )(normed, wq)


def attend_kernel(first, last, places, depth, sizes, *refs):
    refs = list(refs)
    valid_counts, own = refs.pop(0), refs.pop(0)
    query = refs.pop(0)
    chunks = [refs.pop(0) for _ in sizes]
    if not first:
        top_in, sums_in = refs.pop(0), refs.pop(0)
    if last:
        w_out = refs.pop(0)
        mixed = refs.pop(0)
        top_out, sums_out = refs.pop(0), refs.pop(0)
    else:
        top_out, sums_out = refs.pop(0), refs.pop(0)
    heads, rows, _ = query.shape
    here = own[0]
    here_y, here_z, here_core = lax.div(here, 2 * depth), lax.rem(lax.div(here, 2), depth), lax.rem(here, 2)
    pages = []
    for chunk, size in zip(chunks, sizes):
        for index in range(size):
            side, shift, core = places[len(pages)]
            number = (here_y ^ side) * (2 * depth) + lax.rem(here_z + shift % depth, depth) * 2 + (here_core ^ core)
            pages.append((chunk, index, valid_counts[number]))
    group_size = 4 if len(pages) % 4 == 0 else min(3, len(pages))
    tokens = chunks[0].shape[1]
    lane = lax.broadcasted_iota(jnp.int32, (1, tokens), 1)
    lane_kv = lax.broadcasted_iota(jnp.int32, (tokens, 2 * HD), 1)
    fresh = first
    for begin in range(0, len(pages), group_size):
        group = pages[begin : begin + group_size]
        keys, values, masks = [], [], []
        for chunk, index, count in group:
            both = chunk[index]
            keys.append(both[:, HD : 2 * HD])
            values.append(jnp.where(lane_kv < HD, both, jnp.ones_like(both)))
            masks.append(jnp.where(lane < count, 0.0, NEG).astype(F32))
        for head in range(heads):
            scores = [
                lax.dot_general(query[head], key, (((1,), (1,)), ((), ())), preferred_element_type=F32) + mask
                for key, mask in zip(keys, masks)
            ]
            largest = functools.reduce(jnp.maximum, scores)
            top = jnp.max(largest, axis=1, keepdims=True)
            if not fresh:
                source_top, source_sums = (top_in, sums_in) if begin == 0 else (top_out, sums_out)
                before = source_top[head][:, 0:1]
                top = jnp.maximum(top, before)
                carried = source_sums[head] * jnp.exp2(before - top)
            total = functools.reduce(
                jnp.add,
                [
                    jnp.dot(jnp.exp2(score - top).astype(BF), value, preferred_element_type=F32)
                    for score, value in zip(scores, values)
                ],
            )
            if not fresh:
                total = total + carried
            sums_out[head] = total
            top_out[head] = jnp.broadcast_to(top, (rows, HD))
        fresh = False
    if last:
        attended = jnp.concatenate(
            [(sums_out[head][:, 0:HD] / sums_out[head][:, HD : 2 * HD]).astype(BF) for head in range(heads)], axis=1
        )
        mixed[...] = jnp.dot(attended, w_out[...], preferred_element_type=F32).astype(BF)


def attend(valid_counts, own, depth, query, pieces, carry=None, w_out=None):
    heads, rows, _ = query.shape
    chunks = [piece[0] for piece in pieces]
    places = [place for piece in pieces for place in piece[1]]
    sizes = tuple(chunk.shape[0] for chunk in chunks)
    state = [jax.ShapeDtypeStruct((heads, rows, HD), F32), jax.ShapeDtypeStruct((heads, rows, 2 * HD), F32)]
    operands = [valid_counts, own, query, *chunks]
    if carry is not None:
        operands += list(carry)
    scratch = []
    if w_out is not None:
        operands.append(w_out)
        out_shape = [jax.ShapeDtypeStruct((rows, w_out.shape[1]), BF)]
        scratch = [pltpu.VMEM(one.shape, F32) for one in state]
    else:
        out_shape = state
    pairs = sum(sizes) * chunks[0].shape[1] * heads * rows
    return pl.pallas_call(
        functools.partial(attend_kernel, carry is None, w_out is not None, places, depth, sizes),
        out_shape=out_shape,
        in_specs=[smem_spec()] * 2 + [vmem_spec()] * (len(operands) - 2),
        out_specs=[vmem_spec()] * len(out_shape),
        scratch_shapes=scratch,
        cost_estimate=pl.CostEstimate(flops=pairs * 512, transcendentals=pairs, bytes_accessed=4 * 2**20),
        compiler_params=params(28),
        name="attend",
    )(*operands)


def total_kernel(parts, out):
    total = parts[0].astype(F32)
    for part in range(1, parts.shape[0]):
        total = total + parts[part].astype(F32)
    out[...] = total.astype(BF)


def total_of(parts):
    return pl.pallas_call(
        total_kernel,
        out_shape=jax.ShapeDtypeStruct(parts.shape[1:], BF),
        in_specs=[vmem_spec()],
        out_specs=vmem_spec(),
        compiler_params=params(8),
        name="total",
    )(parts)


def per_device(
    pages,
    valid_counts,
    dw_weight,
    dw_bias,
    norm1_gain,
    fc1_w,
    fc1_b,
    fc2_w,
    fc2_b,
    layer_scale,
    norm2_gain,
    w_query,
    w_key,
    w_value,
    w_out,
):
    channels = pages.shape[-1]
    rows = pages.shape[1] * pages.shape[2]
    groups = lax.axis_size("head")
    blocks = lax.axis_size("blk")
    depth = blocks // 4
    share = rows // groups

    def flip_y(array):
        return lax.ppermute(array, "blk", [(i, (i + 2 * depth) % blocks) for i in range(blocks)])

    def flip_core(array):
        return lax.ppermute(array, "blk", [(i, i ^ 1) for i in range(blocks)])

    def along_z(array, step):
        def target(i):
            return i // (2 * depth) * (2 * depth) + (i + 2 * step) % (2 * depth)

        return lax.ppermute(array, "blk", [(i, target(i)) for i in range(blocks)])

    own = lax.axis_index("blk").astype(jnp.int32)[None]
    place = lax.axis_index("head").astype(jnp.int32)[None]
    hold = lax.optimization_barrier

    partial = mlp(pages, dw_weight, dw_bias, norm1_gain, fc1_w, fc1_b, fc2_w)
    parts = lax.all_to_all(partial.reshape(groups, share, channels), "head", 0, 0, tiled=True)
    copies = block_norm(place, parts, pages.reshape(rows, channels), layer_scale, fc2_b, norm2_gain)
    normed = lax.all_to_all(copies, "head", 0, 0, tiled=True).reshape(rows, channels)

    def spots(shifts, sides, core):
        return [(side, shift, core) for side in sides for shift in shifts]

    def fold(pieces, carry=None, weight=None):
        return attend(valid_counts, own, depth, query, pieces, carry, weight)

    start = key_values(normed, w_key, w_value)
    up, down = along_z(start, 1), along_z(start, -1)
    other = flip_y(start)
    query = queries_of(normed, w_query)

    up, down, query = hold((up, down, query))
    near = jnp.concatenate([up, down])
    up, down = along_z(up, 1), along_z(down, -1)
    near_other = flip_y(near)
    crossed = flip_core(jnp.concatenate([start, other]))
    carry = fold([(start, spots((0,), (0,), 0)), (other, spots((0,), (1,), 0))])
    waiting = (crossed, spots((0,), (0, 1), 1))

    for hop in (1, 2, 3):
        up, down, carry = hold((up, down, carry))
        following = jnp.concatenate([up, down], axis=0 if hop < 3 else 1)
        if hop == 1:
            up, down = along_z(up, 1), along_z(down, -1)
        elif hop == 2:
            up, down = along_z(up[:, : rows // 2], 1), along_z(down[:, rows // 2 :], -1)
        following_other = flip_y(following)
        crossed = flip_core(jnp.concatenate([near, near_other]))
        shifts = (-hop, hop)
        carry = fold([waiting, (near, spots(shifts, (0,), 0)), (near_other, spots(shifts, (1,), 0))], carry)
        waiting = (crossed, spots(shifts, (0, 1), 1))
        near, near_other = following, following_other

    near_other, *carry = hold((near_other, *carry))
    crossed = flip_core(jnp.concatenate([near, near_other]))
    carry = fold([waiting, (near, spots((4,), (0,), 0)), (near_other, spots((4,), (1,), 0))], carry)
    (mixed,) = fold([(crossed, spots((4,), (0, 1), 1))], carry, w_out)
    parts = lax.all_to_all(mixed.reshape(groups, share, channels), "head", 0, 0, tiled=True)
    return total_of(parts)


def solution(mesh):
    in_specs = (
        P("blk", None, None, None),
        P(),
        P(),
        P(),
        P(),
        P(None, "head"),
        P("head"),
        P("head", None),
        P(),
        P(),
        P(),
        P(None, "head"),
        P(None, "head"),
        P(None, "head"),
        P("head", None),
    )
    out_specs = P(("blk", "head"), None)
    return jax.shard_map(per_device, mesh=mesh, in_specs=in_specs, out_specs=out_specs, check_vma=False)
```

time: 131 us -> 105 us (0.80)
  Pallas kernels: 41.5 us -> 24.5 us
  waiting for transfers between devices: 27.2 us -> 23.5 us
  local copies, waits for them, and re-layouts: 9.57 us -> 6.89 us
  blocking collectives: 28.4 us -> 26.1 us
  starting transfers between devices: 23.4 us -> 21.8 us
    ppermute x8, waiting for transfers between devices: 19.4 us -> 7.89 us  [along_z(): return lax.ppermute(array, 'blk', [(i, target(i)) for i in range(blocks)])]
    pallas_call x4 -> x6, Pallas kernels: 23.4 us -> 17.8 us  [attend(): pl.pallas_call(functools.partial(attend_kernel, carry is None, w_out is n...]
    ppermute x5, waiting for transfers between devices: 0.68 us -> 5.91 us  [flip_y(): lax.ppermute(array, 'blk', [(i, (i + 2 * depth) % blocks) for i in range(...]
    pallas_call x1, Pallas kernels: 9.84 us -> 5.03 us  [mlp(): pl.pallas_call(mlp_kernel, out_shape=jax.ShapeDtypeStruct((rows, channels...]
    broadcast_in_dim x6 -> x0, local copies, waits for them, and re-layouts: 4.18 us -> none  [the longest x1 1.29 us: mlp(): dwb[None]]
    unnamed x45 -> x36, local copies, waits for them, and re-layouts: 4.11 us -> 6.84 us
    all_to_all x1, waiting for transfers between devices: 7.12 us -> 9.66 us  [per_device(): lax.all_to_all(partial.reshape(groups, share, channels), 'head', 0, 0, ti...]
    pallas_call x1, Pallas kernels: 2.33 us -> 0.37 us  [queries_of(): pl.pallas_call(query_kernel, out_shape=jax.ShapeDtypeStruct((wq.shape[1]...]
  transfers between devices with their start and end apart: 19 -> 19, of which waited for: 10 -> 8; matrix products, arithmetic and copies ran while one was open for 2% -> 0% of each run, Pallas kernels for 16% -> 15%
where the time goes in v2:
time: 105 us; the launch traced here: 103 us
  blocking collectives  26.1 us (25%)
  Pallas kernels  24.5 us (23%)
  waiting for transfers between devices  23.5 us (22%)
  starting transfers between devices  21.8 us (21%)
  local copies, waits for them, and re-layouts  6.89 us (7%)
    pallas_call x6, Pallas kernels, attend(): pl.pallas_call(functools.partial(attend_kernel, carry is None, w_out is n...  17.8 us
    all_to_all x1, blocking collectives, per_device(): lax.all_to_all(mixed.reshape(groups, share, channels), 'head', 0, 0, tile...  13.4 us
    all_to_all x1, blocking collectives, per_device(): lax.all_to_all(copies, 'head', 0, 0, tiled=True).reshape(rows, channels)  12.8 us
    ppermute x8, starting transfers between devices, along_z(): return lax.ppermute(array, 'blk', [(i, target(i)) for i in range(blocks)])  10.4 us
    all_to_all x1, waiting for transfers between devices, per_device(): lax.all_to_all(partial.reshape(groups, share, channels), 'head', 0, 0, ti...  9.66 us
    ppermute x8, waiting for transfers between devices, along_z(): return lax.ppermute(array, 'blk', [(i, target(i)) for i in range(blocks)])  7.89 us
    all_to_all x1, starting transfers between devices, per_device(): lax.all_to_all(partial.reshape(groups, share, channels), 'head', 0, 0, ti...  7.07 us
    unnamed x36, local copies, waits for them, and re-layouts  6.84 us
  transfers between devices with their start and end apart: 19, of which 8 were waited for; matrix products, arithmetic and copies ran while one was open for 0% of the time, Pallas kernels for 15%

profile of v2, /device:TPU:32, one launch (start us, length us, event | category | flops | bytes accessed | tf_op | source)
XLA Modules:
  0.0 103.4 jit_solution(7798316158469317906)
XLA Ops:
  0.0 0.7 copy-done.9
  0.7 1.0 copy-done
  1.7 1.1 %copy-done.4 = bf16[768,384]{1,0:T(8,128)(2,1)S(1)} copy-done((bf16[768,384]{1,0:T(8,128)(2,1)S(1)}, bf16[768,384]{1,0:T(8,128)(2,1)}, u32[]{:S(2)}) %copy-start.4) | copy-done | bytes 589848
  2.8 1.1 %copy-done.5 = bf16[384,768]{1,0:T(8,128)(2,1)S(1)} copy-done((bf16[384,768]{1,0:T(8,128)(2,1)S(1)}, bf16[384,768]{1,0:T(8,128)(2,1)}, u32[]{:S(2)}) %copy-start.5) | copy-done | bytes 589848
  3.8 0.9 copy-done.8
  4.7 0.7 copy-done.10
  5.4 5.0 %conv_mlp.1 = bf16[256,768]{1,0:T(8,128)(2,1)} custom-call(bf16[16,16,768]{2,1,0:T(8,128)(2,1)S(1)} %bitcast.15, f32[7,7,768]{2,1,0:T(8,128)S(1)} %copy-done.8, f32[6,128]{1,0:T(8,128)S(1)} %bitcast.18, f32[6,128]{1,0:T(8,128)S(1)} %bitcast.19, bf16[768,384]{1,0:T(8,128)(2,1)S(1)} %copy-done.4, f32[3,128]{1,0:T(4,128)S(1)} %bitcast.23, ...), custom_call_target="tpu_custom_call" | custom-call | tf_op jit(solution)/shard_map/conv_mlp/pallas_call | solution.py:95
  10.5 7.1 %all-to-all-start = ((bf16[8,32,768]{2,1,0:T(8,128)(2,1)}), bf16[8,32,768]{2,1,0:T(8,128)(2,1)S(1)}, u32[]{:S(2)}, u32[]{:S(2)}) async-start(bf16[8,32,768]{2,1,0:T(8,128)(2,1)} %bitcast.6), calls=%async_computation | async-start | bytes 786432 | tf_op jit(solution)/shard_map/all_to_all | solution.py:328
  17.6 9.7 %all-to-all-done.parts = bf16[8,32,768]{2,1,0:T(8,128)(2,1)S(1)} async-done(((bf16[8,32,768]{2,1,0:T(8,128)(2,1)}), bf16[8,32,768]{2,1,0:T(8,128)(2,1)S(1)}, u32[]{:S(2)}, u32[]{:S(2)}) %all-to-all-start) | async-done | bytes 393248 | tf_op jit(solution)/shard_map/all_to_all | solution.py:328
  27.2 0.7 copy-done.12
  27.9 0.2 block_norm.1
  28.2 12.8 %all_to_all.15 = bf16[8,32,768]{2,1,0:T(8,128)(2,1)S(1)} all-to-all(bf16[8,32,768]{2,1,0:T(8,128)(2,1)S(1)} %block_norm.1), channel_id=1, replica_groups=mesh['blk'=32,'head'=8] {'head'}, dimensions={0} | all-to-all | bytes 786432 | tf_op jit(solution)/shard_map/all_to_all | solution.py:330
  41.0 0.4 key_values.1.refs_3_
  41.3 2.0 %collective-permute-start = (bf16[1,256,256]{2,1,0:T(8,128)(2,1)S(1)}, bf16[1,256,256]{2,1,0:T(8,128)(2,1)S(1)}, u32[]{:S(2)}, u32[]{:S(2)}) collective-permute-start(bf16[1,256,256]{2,1,0:T(8,128)(2,1)S(1)} %key_values.1.refs_3_), channel_id=1, source_target_pairs={{0,16},{8,24},{16,32},{24,40},{32,48},{40,56},{48,64},{56,72},{64,... | collective-permute-start | bytes 393224 | tf_op jit(solution)/shard_map/ppermute | solution.py:321
  43.3 0.1 collective-permute-start.1
  43.4 0.7 collective-permute-start.4
  44.1 0.4 queries.1.refs_2_
  44.5 1.9 %collective-permute-done = bf16[1,256,256]{2,1,0:T(8,128)(2,1)S(1)} collective-permute-done((bf16[1,256,256]{2,1,0:T(8,128)(2,1)S(1)}, bf16[1,256,256]{2,1,0:T(8,128)(2,1)S(1)}, u32[]{:S(2)}, u32[]{:S(2)}) %collective-permute-start) | collective-permute-done | bytes 131104 | tf_op jit(solution)/shard_map/ppermute | solution.py:321
  46.4 1.9 %collective-permute-done.1 = bf16[1,256,256]{2,1,0:T(8,128)(2,1)S(1)} collective-permute-done((bf16[1,256,256]{2,1,0:T(8,128)(2,1)S(1)}, bf16[1,256,256]{2,1,0:T(8,128)(2,1)S(1)}, u32[]{:S(2)}, u32[]{:S(2)}) %collective-permute-start.1) | collective-permute-done | bytes 131104 | tf_op jit(solution)/shard_map/ppermute | solution.py:321
  48.3 3.0 %collective-permute-start.2 = (bf16[1,256,256]{2,1,0:T(8,128)(2,1)S(1)}, bf16[1,256,256]{2,1,0:T(8,128)(2,1)S(1)}, u32[]{:S(2)}, u32[]{:S(2)}) collective-permute-start(bf16[1,256,256]{2,1,0:T(8,128)(2,1)S(1)} %collective-permute-done), channel_id=1, source_target_pairs={{0,16},{8,24},{16,32},{24,40},{32,48},{40,56},{48,64},{56,72},{64,... | collective-permute-start | bytes 393224 | tf_op jit(solution)/shard_map/ppermute | solution.py:321
  51.4 0.1 collective-permute-start.7
  51.5 0.8 collective-permute-start.8
  52.3 0.7 copy-done.15
  52.9 1.5 %attend.6 = (f32[4,256,128]{2,1,0:T(8,128)S(1)}, f32[4,256,256]{2,1,0:T(8,128)S(1)}) custom-call(s32[32]{0:T(128)S(1)} %copy-done.15, s32[1]{0:T(128)} %bitcast.refs_1_, bf16[4,256,128]{2,1,0:T(8,128)(2,1)S(1)} %queries.1.refs_2_, bf16[1,256,256]{2,1,0:T(8,128)(2,1)S(1)} %key_values.1.refs_3_, bf16[1,256,256]{2,1,0:T(8,128)(2,1)S(1)} %collective-permute-done.4.refs_4_), custom_call_target="tpu_custom_call" | custom-call | flops 268435456 | bytes 4194304 | tf_op jit(solution)/shard_map/attend/pallas_call | solution.py:257
  54.5 3.1 %collective-permute-done.3 = bf16[1,256,256]{2,1,0:T(8,128)(2,1)S(1)} collective-permute-done((bf16[1,256,256]{2,1,0:T(8,128)(2,1)S(1)}, bf16[1,256,256]{2,1,0:T(8,128)(2,1)S(1)}, u32[]{:S(2)}, u32[]{:S(2)}) %collective-permute-start.3) | collective-permute-done | bytes 131104 | tf_op jit(solution)/shard_map/ppermute | solution.py:321
  57.5 2.0 %collective-permute-start.5 = (bf16[1,256,256]{2,1,0:T(8,128)(2,1)S(1)}, bf16[1,256,256]{2,1,0:T(8,128)(2,1)S(1)}, u32[]{:S(2)}, u32[]{:S(2)}) collective-permute-start(bf16[1,256,256]{2,1,0:T(8,128)(2,1)S(1)} %collective-permute-done.2), channel_id=1, source_target_pairs={{0,16},{8,24},{16,32},{24,40},{32,48},{40,56},{48,64},{56,72},{64,... | collective-permute-start | bytes 393224 | tf_op jit(solution)/shard_map/ppermute | solution.py:321
  59.6 0.8 collective-permute-start.12
  60.3 3.1 %attend.7 = (f32[4,256,128]{2,1,0:T(8,128)S(1)}, f32[4,256,256]{2,1,0:T(8,128)S(1)}) custom-call(s32[32]{0:T(128)S(1)} %copy-done.15, s32[1]{0:T(128)} %bitcast.refs_1_, bf16[4,256,128]{2,1,0:T(8,128)(2,1)S(1)} %queries.1.refs_2_, bf16[2,256,256]{2,1,0:T(8,128)(2,1)S(1)} %collective-permute-done.7.refs_3_, ...), custom_call_target="tpu_custom_call" | custom-call | flops 805306368 | bytes 4194304 | tf_op jit(solution)/shard_map/attend/pallas_call | solution.py:257
  63.5 1.0 collective-permute-done.6
  64.5 0.1 pad_maximum_fusion
  64.6 0.1 collective-permute-start.11
  64.7 0.8 collective-permute-start.15
  65.5 0.6 collective-permute-done.12.refs_5_
  66.0 0.1 pad_maximum_fusion.1
  66.1 0.1 collective-permute-start.14
  66.2 3.2 %collective-permute-start.9 = (bf16[1,128,256]{2,1,0:T(8,128)(2,1)S(1)}, bf16[1,128,256]{2,1,0:T(8,128)(2,1)S(1)}, u32[]{:S(2)}, u32[]{:S(2)}) collective-permute-start(bf16[1,128,256]{2,1,0:T(8,128)(2,1)S(1)} %slice.6), channel_id=1, source_target_pairs={{0,16},{8,24},{16,32},{24,40},{32,48},{40,56},{48,64},{56,72},{64,... | collective-permute-start | bytes 196616 | tf_op jit(solution)/shard_map/ppermute | solution.py:321
  69.4 4.1 %collective-permute-done.15.refs_5_ = bf16[2,256,256]{2,1,0:T(8,128)(2,1)S(1)} collective-permute-done((bf16[2,256,256]{2,1,0:T(8,128)(2,1)S(1)}, bf16[2,256,256]{2,1,0:T(8,128)(2,1)S(1)}, u32[]{:S(2)}, u32[]{:S(2)}) %collective-permute-start.15) | collective-permute-done | bytes 262176 | tf_op jit(solution)/shard_map/ppermute | solution.py:312
  73.5 0.1 pad_maximum_fusion.2
  73.5 0.1 collective-permute-start.17
  73.7 3.9 %attend.8 = (f32[4,256,128]{2,1,0:T(8,128)S(1)}, f32[4,256,256]{2,1,0:T(8,128)S(1)}) custom-call(s32[32]{0:T(128)S(1)} %copy-done.15, s32[1]{0:T(128)} %bitcast.refs_1_, bf16[4,256,128]{2,1,0:T(8,128)(2,1)S(1)} %queries.1.refs_2_, bf16[4,256,256]{2,1,0:T(8,128)(2,1)S(1)} %collective-permute-done.11.refs_3_, ...), custom_call_target="tpu_custom_call" | custom-call | flops 1073741824 | bytes 4194304 | tf_op jit(solution)/shard_map/attend/pallas_call | solution.py:257
  77.6 1.0 collective-permute-start.13
  78.6 4.0 %attend.9 = (f32[4,256,128]{2,1,0:T(8,128)S(1)}, f32[4,256,256]{2,1,0:T(8,128)S(1)}) custom-call(s32[32]{0:T(128)S(1)} %copy-done.15, s32[1]{0:T(128)} %bitcast.refs_1_, bf16[4,256,128]{2,1,0:T(8,128)(2,1)S(1)} %queries.1.refs_2_, bf16[4,256,256]{2,1,0:T(8,128)(2,1)S(1)} %collective-permute-done.14.refs_3_, ...), custom_call_target="tpu_custom_call" | custom-call | flops 1073741824 | bytes 4194304 | tf_op jit(solution)/shard_map/attend/pallas_call | solution.py:257
  82.6 1.3 %collective-permute-done.13.refs_5_ = bf16[1,256,256]{2,1,0:T(8,128)(2,1)S(1)} collective-permute-done((bf16[1,256,256]{2,1,0:T(8,128)(2,1)S(1)}, bf16[1,256,256]{2,1,0:T(8,128)(2,1)S(1)}, u32[]{:S(2)}, u32[]{:S(2)}) %collective-permute-start.13) | collective-permute-done | bytes 131104 | tf_op jit(solution)/shard_map/ppermute | solution.py:312
  83.9 0.1 collective-permute-start.16
  84.0 3.1 %attend.10 = (f32[4,256,128]{2,1,0:T(8,128)S(1)}, f32[4,256,256]{2,1,0:T(8,128)S(1)}) custom-call(s32[32]{0:T(128)S(1)} %copy-done.15, s32[1]{0:T(128)} %bitcast.refs_1_, bf16[4,256,128]{2,1,0:T(8,128)(2,1)S(1)} %queries.1.refs_2_, bf16[4,256,256]{2,1,0:T(8,128)(2,1)S(1)} %collective-permute-done.17.refs_3_, ...), custom_call_target="tpu_custom_call" | custom-call | flops 805306368 | bytes 4194304 | tf_op jit(solution)/shard_map/attend/pallas_call | solution.py:257
  87.2 2.2 %attend.11 = bf16[256,768]{1,0:T(8,128)(2,1)S(1)} custom-call(s32[32]{0:T(128)S(1)} %copy-done.15, s32[1]{0:T(128)} %bitcast.refs_1_, bf16[4,256,128]{2,1,0:T(8,128)(2,1)S(1)} %queries.1.refs_2_, bf16[2,256,256]{2,1,0:T(8,128)(2,1)S(1)} %collective-permute-done.16.refs_3_, f32[4,256,128]{2,1,0:T(8,128)S(1)} %get-tuple-element.59.refs_4_, ...), custom_call_target="tpu_custom_call" | custom-call | flops 268435456 | bytes 4194304 | tf_op jit(solution)/shard_map/attend/pallas_call | solution.py:257
  89.4 13.4 %all_to_all.16.parts = bf16[8,32,768]{2,1,0:T(8,128)(2,1)S(1)} all-to-all(bf16[8,32,768]{2,1,0:T(8,128)(2,1)S(1)} %bitcast.17), channel_id=1, replica_groups=mesh['blk'=32,'head'=8] {'head'}, dimensions={0} | all-to-all | bytes 786432 | tf_op jit(solution)/shard_map/all_to_all | solution.py:369
  102.7 0.7 total.1
  (50 shorter events, 0.3 us)
Async XLA Ops:
  0.0 0.7 copy-start.9
  0.0 0.7 copy-start.14
  0.7 1.0 copy-start
  1.7 1.1 %copy-start.4 = (bf16[768,384]{1,0:T(8,128)(2,1)S(1)}, bf16[768,384]{1,0:T(8,128)(2,1)}, u32[]{:S(2)}) copy-start(bf16[768,384]{1,0:T(8,128)(2,1)} %w1_hbm.1) | copy-start | bytes 1769476
  2.8 1.1 %copy-start.5 = (bf16[384,768]{1,0:T(8,128)(2,1)S(1)}, bf16[384,768]{1,0:T(8,128)(2,1)}, u32[]{:S(2)}) copy-start(bf16[384,768]{1,0:T(8,128)(2,1)} %w2_hbm.1) | copy-start | bytes 1769476
  3.8 0.9 copy-start.8
  4.7 0.7 copy-start.10
  10.5 16.8 %copy-start.1 = (bf16[1,16,16,768]{3,2,1,0:T(8,128)(2,1)S(1)}, bf16[1,16,16,768]{3,2,1,0:T(8,128)(2,1)}, u32[]{:S(2)}) copy-start(bf16[1,16,16,768]{3,2,1,0:T(8,128)(2,1)} %param.15) | copy-start | bytes 1179652
  10.5 16.8 %copy-start.13 = (f32[768]{0:T(1024)S(1)}, f32[768]{0:T(1024)}, u32[]{:S(2)}) copy-start(f32[768]{0:T(1024)} %param.25) | copy-start | bytes 9220
  10.5 16.7 %all-to-all-start = ((bf16[8,32,768]{2,1,0:T(8,128)(2,1)}), bf16[8,32,768]{2,1,0:T(8,128)(2,1)S(1)}, u32[]{:S(2)}, u32[]{:S(2)}) async-start(bf16[8,32,768]{2,1,0:T(8,128)(2,1)} %bitcast.6), calls=%async_computation | async-start | bytes 786432 | tf_op jit(solution)/shard_map/all_to_all | solution.py:328
  27.2 0.7 copy-start.12
  27.2 0.7 copy-start.11
  27.9 13.0 %copy-start.6 = (bf16[768,128]{1,0:T(8,128)(2,1)S(1)}, bf16[768,128]{1,0:T(8,128)(2,1)}, u32[]{:S(2)}) copy-start(bf16[768,128]{1,0:T(8,128)(2,1)} %wk.1) | copy-start | bytes 589828
  27.9 13.0 %copy-start.7 = (bf16[768,128]{1,0:T(8,128)(2,1)S(1)}, bf16[768,128]{1,0:T(8,128)(2,1)}, u32[]{:S(2)}) copy-start(bf16[768,128]{1,0:T(8,128)(2,1)} %wv.1) | copy-start | bytes 589828
  28.2 15.9 %copy-start.2 = (bf16[768,512]{1,0:T(8,128)(2,1)S(1)}, bf16[768,512]{1,0:T(8,128)(2,1)}, u32[]{:S(2)}) copy-start(bf16[768,512]{1,0:T(8,128)(2,1)} %wq.1) | copy-start | bytes 2359300
  41.3 5.0 %collective-permute-start = (bf16[1,256,256]{2,1,0:T(8,128)(2,1)S(1)}, bf16[1,256,256]{2,1,0:T(8,128)(2,1)S(1)}, u32[]{:S(2)}, u32[]{:S(2)}) collective-permute-start(bf16[1,256,256]{2,1,0:T(8,128)(2,1)S(1)} %key_values.1.refs_3_), channel_id=1, source_target_pairs={{0,16},{8,24},{16,32},{24,40},{32,48},{40,56},{48,64},{56,72},{64,... | collective-permute-start | bytes 393224 | tf_op jit(solution)/shard_map/ppermute | solution.py:321
  43.3 5.0 %collective-permute-start.1 = (bf16[1,256,256]{2,1,0:T(8,128)(2,1)S(1)}, bf16[1,256,256]{2,1,0:T(8,128)(2,1)S(1)}, u32[]{:S(2)}, u32[]{:S(2)}) collective-permute-start(bf16[1,256,256]{2,1,0:T(8,128)(2,1)S(1)} %key_values.1.refs_3_), channel_id=1, source_target_pairs={{0,112},{8,120},{16,0},{24,8},{32,16},{40,24},{48,32},{56,40},{64,... | collective-permute-start | bytes 393224 | tf_op jit(solution)/shard_map/ppermute | solution.py:321
  43.4 7.9 %collective-permute-start.4 = (bf16[1,256,256]{2,1,0:T(8,128)(2,1)S(1)}, bf16[1,256,256]{2,1,0:T(8,128)(2,1)S(1)}, u32[]{:S(2)}, u32[]{:S(2)}) collective-permute-start(bf16[1,256,256]{2,1,0:T(8,128)(2,1)S(1)} %key_values.1.refs_3_), channel_id=1, source_target_pairs={{0,128},{8,136},{16,144},{24,152},{32,160},{40,168},{48,176},{56,1... | collective-permute-start | bytes 393224 | tf_op jit(solution)/shard_map/ppermute | solution.py:312
  48.3 6.1 %collective-permute-start.2 = (bf16[1,256,256]{2,1,0:T(8,128)(2,1)S(1)}, bf16[1,256,256]{2,1,0:T(8,128)(2,1)S(1)}, u32[]{:S(2)}, u32[]{:S(2)}) collective-permute-start(bf16[1,256,256]{2,1,0:T(8,128)(2,1)S(1)} %collective-permute-done), channel_id=1, source_target_pairs={{0,16},{8,24},{16,32},{24,40},{32,48},{40,56},{48,64},{56,72},{64,... | collective-permute-start | bytes 393224 | tf_op jit(solution)/shard_map/ppermute | solution.py:321
  51.3 6.2 %collective-permute-start.3 = (bf16[1,256,256]{2,1,0:T(8,128)(2,1)S(1)}, bf16[1,256,256]{2,1,0:T(8,128)(2,1)S(1)}, u32[]{:S(2)}, u32[]{:S(2)}) collective-permute-start(bf16[1,256,256]{2,1,0:T(8,128)(2,1)S(1)} %collective-permute-done.1), channel_id=1, source_target_pairs={{0,112},{8,120},{16,0},{24,8},{32,16},{40,24},{48,32},{56,40},{64,... | collective-permute-start | bytes 393224 | tf_op jit(solution)/shard_map/ppermute | solution.py:321
  51.4 8.9 %collective-permute-start.7 = (bf16[2,256,256]{2,1,0:T(8,128)(2,1)S(1)}, bf16[2,256,256]{2,1,0:T(8,128)(2,1)S(1)}, u32[]{:S(2)}, u32[]{:S(2)}) collective-permute-start(bf16[2,256,256]{2,1,0:T(8,128)(2,1)S(1)} %pad_maximum_fusion.3), channel_id=1, source_target_pairs={{0,8},{8,0},{16,24},{24,16},{32,40},{40,32},{48,56},{56,48},{64,72... | collective-permute-start | bytes 786440 | tf_op jit(solution)/shard_map/ppermute | solution.py:315
  51.5 8.8 %collective-permute-start.8 = (bf16[2,256,256]{2,1,0:T(8,128)(2,1)S(1)}, bf16[2,256,256]{2,1,0:T(8,128)(2,1)S(1)}, u32[]{:S(2)}, u32[]{:S(2)}) collective-permute-start(bf16[2,256,256]{2,1,0:T(8,128)(2,1)S(1)} %constant_dynamic-update-slice_fusion.refs_4_), channel_id=1, source_target_pairs={{0,128},{8,136},{16,144},{24,152},{32,160},{40,168},{48,176},{56,1... | collective-permute-start | bytes 786440 | tf_op jit(solution)/shard_map/ppermute | solution.py:312
  52.3 0.7 copy-start.15
  57.5 6.0 %collective-permute-start.5 = (bf16[1,256,256]{2,1,0:T(8,128)(2,1)S(1)}, bf16[1,256,256]{2,1,0:T(8,128)(2,1)S(1)}, u32[]{:S(2)}, u32[]{:S(2)}) collective-permute-start(bf16[1,256,256]{2,1,0:T(8,128)(2,1)S(1)} %collective-permute-done.2), channel_id=1, source_target_pairs={{0,16},{8,24},{16,32},{24,40},{32,48},{40,56},{48,64},{56,72},{64,... | collective-permute-start | bytes 393224 | tf_op jit(solution)/shard_map/ppermute | solution.py:321
  59.5 5.0 %collective-permute-start.6 = (bf16[1,256,256]{2,1,0:T(8,128)(2,1)S(1)}, bf16[1,256,256]{2,1,0:T(8,128)(2,1)S(1)}, u32[]{:S(2)}, u32[]{:S(2)}) collective-permute-start(bf16[1,256,256]{2,1,0:T(8,128)(2,1)S(1)} %collective-permute-done.3), channel_id=1, source_target_pairs={{0,112},{8,120},{16,0},{24,8},{32,16},{40,24},{48,32},{56,40},{64,... | collective-permute-start | bytes 393224 | tf_op jit(solution)/shard_map/ppermute | solution.py:321
  59.6 6.5 %collective-permute-start.12 = (bf16[2,256,256]{2,1,0:T(8,128)(2,1)S(1)}, bf16[2,256,256]{2,1,0:T(8,128)(2,1)S(1)}, u32[]{:S(2)}, u32[]{:S(2)}) collective-permute-start(bf16[2,256,256]{2,1,0:T(8,128)(2,1)S(1)} %constant_dynamic-update-slice_fusion.2.refs_4_), channel_id=1, source_target_pairs={{0,128},{8,136},{16,144},{24,152},{32,160},{40,168},{48,176},{56,1... | collective-permute-start | bytes 786440 | tf_op jit(solution)/shard_map/ppermute | solution.py:312
  64.6 9.1 %collective-permute-start.11 = (bf16[4,256,256]{2,1,0:T(8,128)(2,1)S(1)}, bf16[4,256,256]{2,1,0:T(8,128)(2,1)S(1)}, u32[]{:S(2)}, u32[]{:S(2)}) collective-permute-start(bf16[4,256,256]{2,1,0:T(8,128)(2,1)S(1)} %pad_maximum_fusion), channel_id=1, source_target_pairs={{0,8},{8,0},{16,24},{24,16},{32,40},{40,32},{48,56},{56,48},{64,72... | collective-permute-start | bytes 1572872 | tf_op jit(solution)/shard_map/ppermute | solution.py:315
  64.7 8.8 %collective-permute-start.15 = (bf16[2,256,256]{2,1,0:T(8,128)(2,1)S(1)}, bf16[2,256,256]{2,1,0:T(8,128)(2,1)S(1)}, u32[]{:S(2)}, u32[]{:S(2)}) collective-permute-start(bf16[2,256,256]{2,1,0:T(8,128)(2,1)S(1)} %constant_dynamic-update-slice_fusion.6.refs_4_), channel_id=1, source_target_pairs={{0,128},{8,136},{16,144},{24,152},{32,160},{40,168},{48,176},{56,1... | collective-permute-start | bytes 786440 | tf_op jit(solution)/shard_map/ppermute | solution.py:312
  66.1 12.5 %collective-permute-start.14 = (bf16[4,256,256]{2,1,0:T(8,128)(2,1)S(1)}, bf16[4,256,256]{2,1,0:T(8,128)(2,1)S(1)}, u32[]{:S(2)}, u32[]{:S(2)}) collective-permute-start(bf16[4,256,256]{2,1,0:T(8,128)(2,1)S(1)} %pad_maximum_fusion.1), channel_id=1, source_target_pairs={{0,8},{8,0},{16,24},{24,16},{32,40},{40,32},{48,56},{56,48},{64,72... | collective-permute-start | bytes 1572872 | tf_op jit(solution)/shard_map/ppermute | solution.py:315
  66.2 11.4 %collective-permute-start.9 = (bf16[1,128,256]{2,1,0:T(8,128)(2,1)S(1)}, bf16[1,128,256]{2,1,0:T(8,128)(2,1)S(1)}, u32[]{:S(2)}, u32[]{:S(2)}) collective-permute-start(bf16[1,128,256]{2,1,0:T(8,128)(2,1)S(1)} %slice.6), channel_id=1, source_target_pairs={{0,16},{8,24},{16,32},{24,40},{32,48},{40,56},{48,64},{56,72},{64,... | collective-permute-start | bytes 196616 | tf_op jit(solution)/shard_map/ppermute | solution.py:321
  69.4 8.2 %collective-permute-start.10 = (bf16[1,128,256]{2,1,0:T(8,128)(2,1)S(1)}, bf16[1,128,256]{2,1,0:T(8,128)(2,1)S(1)}, u32[]{:S(2)}, u32[]{:S(2)}) collective-permute-start(bf16[1,128,256]{2,1,0:T(8,128)(2,1)S(1)} %slice.7), channel_id=1, source_target_pairs={{0,112},{8,120},{16,0},{24,8},{32,16},{40,24},{48,32},{56,40},{64,... | collective-permute-start | bytes 196616 | tf_op jit(solution)/shard_map/ppermute | solution.py:321
  73.5 10.4 %collective-permute-start.17 = (bf16[4,256,256]{2,1,0:T(8,128)(2,1)S(1)}, bf16[4,256,256]{2,1,0:T(8,128)(2,1)S(1)}, u32[]{:S(2)}, u32[]{:S(2)}) collective-permute-start(bf16[4,256,256]{2,1,0:T(8,128)(2,1)S(1)} %pad_maximum_fusion.2), channel_id=1, source_target_pairs={{0,8},{8,0},{16,24},{24,16},{32,40},{40,32},{48,56},{56,48},{64,72... | collective-permute-start | bytes 1572872 | tf_op jit(solution)/shard_map/ppermute | solution.py:315
  77.6 6.2 %collective-permute-start.13 = (bf16[1,256,256]{2,1,0:T(8,128)(2,1)S(1)}, bf16[1,256,256]{2,1,0:T(8,128)(2,1)S(1)}, u32[]{:S(2)}, u32[]{:S(2)}) collective-permute-start(bf16[1,256,256]{2,1,0:T(8,128)(2,1)S(1)} %constant_dynamic-update-slice_fusion.4.refs_4_), channel_id=1, source_target_pairs={{0,128},{8,136},{16,144},{24,152},{32,160},{40,168},{48,176},{56,1... | collective-permute-start | bytes 393224 | tf_op jit(solution)/shard_map/ppermute | solution.py:312
  83.9 3.3 %copy-start.3 = (bf16[512,768]{1,0:T(8,128)(2,1)S(1)}, bf16[512,768]{1,0:T(8,128)(2,1)}, u32[]{:S(2)}) copy-start(bf16[512,768]{1,0:T(8,128)(2,1)} %refs_6_.1) | copy-start | bytes 2359300
  83.9 3.3 %collective-permute-start.16 = (bf16[2,256,256]{2,1,0:T(8,128)(2,1)S(1)}, bf16[2,256,256]{2,1,0:T(8,128)(2,1)S(1)}, u32[]{:S(2)}, u32[]{:S(2)}) collective-permute-start(bf16[2,256,256]{2,1,0:T(8,128)(2,1)S(1)} %pad_maximum_fusion.4), channel_id=1, source_target_pairs={{0,8},{8,0},{16,24},{24,16},{32,40},{40,32},{48,56},{56,48},{64,72... | collective-permute-start | bytes 786440 | tf_op jit(solution)/shard_map/ppermute | solution.py:315

commit v3 on v2

--- a/solution.py
+++ b/solution.py
@@ -42,17 +42,30 @@
     return [(piece * factor * gain[index : index + 1, :]).astype(BF) for index, piece in enumerate(centred)]
 
 
+def fixed(array):
+    return pltpu.with_memory_space_constraint(array, pltpu.HBM)
+
+
 def lane_rows(vector):
     return vector.reshape(-1, LANES)
 
 
-def mlp_kernel(pages, dw, dwb, gain, w1_hbm, b1, w2_hbm, out, padded, conv, w1, w2, arrived):
-    loads = [
-        pltpu.make_async_copy(w1_hbm, w1, arrived.at[0]),
-        pltpu.make_async_copy(w2_hbm, w2, arrived.at[1]),
-    ]
-    for load in loads:
+def mlp_kernel(pages_hbm, dw_hbm, dwb_hbm, gain_hbm, w1_hbm, b1_hbm, w2_hbm, out, *scratch):
+    padded, conv, pages, dw, dwb, gain, w1, b1, w2, arrived = scratch
+    pairs = (
+        (w1_hbm, w1),
+        (w2_hbm, w2),
+        (b1_hbm, b1),
+        (gain_hbm, gain),
+        (dwb_hbm, dwb),
+        (dw_hbm, dw),
+        (pages_hbm, pages),
+    )
+    loads = [pltpu.make_async_copy(source, target, arrived.at[index]) for index, (source, target) in enumerate(pairs)]
+    for load in reversed(loads):
         load.start()
+    for load in loads[2:]:
+        load.wait()
     height, breadth, channels = pages.shape
     half = height // 2
     column = lax.broadcasted_iota(jnp.int32, (half, breadth, LANES), 1)
@@ -91,22 +104,21 @@
 def mlp(pages, dw, dwb, gain, w1, b1, w2):
     _, height, breadth, channels = pages.shape
     rows = height * breadth
-    hbm = pl.BlockSpec(memory_space=pltpu.HBM)
+    operands = (pages[0], dw, lane_rows(dwb), lane_rows(gain), w1, lane_rows(b1), w2)
     return pl.pallas_call(
         mlp_kernel,
         out_shape=jax.ShapeDtypeStruct((rows, channels), BF),
-        in_specs=[vmem_spec()] * 4 + [hbm, vmem_spec(), hbm],
+        in_specs=[pl.BlockSpec(memory_space=pltpu.HBM)] * 7,
         out_specs=vmem_spec(),
         scratch_shapes=[
             pltpu.VMEM((channels // LANES, height + 6, breadth, LANES), F32),
             pltpu.VMEM((channels // LANES, rows, LANES), F32),
-            pltpu.VMEM(w1.shape, w1.dtype),
-            pltpu.VMEM(w2.shape, w2.dtype),
-            pltpu.SemaphoreType.DMA((2,)),
+            *[pltpu.VMEM(operand.shape, operand.dtype) for operand in operands],
+            pltpu.SemaphoreType.DMA((7,)),
         ],
         compiler_params=params(16),
         name="conv_mlp",
-    )(pages[0], dw, lane_rows(dwb), lane_rows(gain), w1, lane_rows(b1), w2)
+    )(*[fixed(operand) for operand in operands])
 
 
 def block_kernel(place, parts, pages, scale, b2, gain, out):
@@ -193,7 +205,7 @@
             side, shift, core = places[len(pages)]
             number = (here_y ^ side) * (2 * depth) + lax.rem(here_z + shift % depth, depth) * 2 + (here_core ^ core)
             pages.append((chunk, index, valid_counts[number]))
-    group_size = 4 if len(pages) % 4 == 0 else min(3, len(pages))
+    group_size = 4 if len(pages) in (4, 7, 8) else min(3, len(pages))
     tokens = chunks[0].shape[1]
     lane = lax.broadcasted_iota(jnp.int32, (1, tokens), 1)
     lane_kv = lax.broadcasted_iota(jnp.int32, (tokens, 2 * HD), 1)
@@ -260,7 +272,7 @@
         in_specs=[smem_spec()] * 2 + [vmem_spec()] * (len(operands) - 2),
         out_specs=[vmem_spec()] * len(out_shape),
         scratch_shapes=scratch,
-        cost_estimate=pl.CostEstimate(flops=pairs * 512, transcendentals=pairs, bytes_accessed=4 * 2**20),
+        cost_estimate=pl.CostEstimate(flops=pairs // 8, transcendentals=0, bytes_accessed=2**16),
         compiler_params=params(28),
         name="attend",
     )(*operands)
@@ -320,6 +332,14 @@
 
         return lax.ppermute(array, "blk", [(i, target(i)) for i in range(blocks)])
 
+    def to_side(array, step):
+        def target(i):
+            turn = 2 * step if i // 2 % 2 == 0 else -2 * step
+            return i // (2 * depth) * (2 * depth) + (i + turn) % (2 * depth)
+
+        return lax.ppermute(array, "blk", [(i, target(i)) for i in range(blocks)])
+
+    even = lax.axis_index("blk") // 2 % 2 == 0
     own = lax.axis_index("blk").astype(jnp.int32)[None]
     place = lax.axis_index("head").astype(jnp.int32)[None]
     hold = lax.optimization_barrier
@@ -339,33 +359,43 @@
     up, down = along_z(start, 1), along_z(start, -1)
     other = flip_y(start)
     query = queries_of(normed, w_query)
-
-    up, down, query = hold((up, down, query))
+    carry = fold([(start, spots((0,), (0,), 0))])
+    up, down, other, carry = hold((up, down, other, carry))
+
     near = jnp.concatenate([up, down])
     up, down = along_z(up, 1), along_z(down, -1)
     near_other = flip_y(near)
     crossed = flip_core(jnp.concatenate([start, other]))
-    carry = fold([(start, spots((0,), (0,), 0)), (other, spots((0,), (1,), 0))])
+    carry = fold([(other, spots((0,), (1,), 0)), (near, spots((-1, 1), (0,), 0))], carry)
+    up, down, near_other, crossed, carry = hold((up, down, near_other, crossed, carry))
     waiting = (crossed, spots((0,), (0, 1), 1))
 
-    for hop in (1, 2, 3):
-        up, down, carry = hold((up, down, carry))
-        following = jnp.concatenate([up, down], axis=0 if hop < 3 else 1)
-        if hop == 1:
-            up, down = along_z(up, 1), along_z(down, -1)
-        elif hop == 2:
-            up, down = along_z(up[:, : rows // 2], 1), along_z(down[:, rows // 2 :], -1)
-        following_other = flip_y(following)
-        crossed = flip_core(jnp.concatenate([near, near_other]))
-        shifts = (-hop, hop)
-        carry = fold([waiting, (near, spots(shifts, (0,), 0)), (near_other, spots(shifts, (1,), 0))], carry)
-        waiting = (crossed, spots(shifts, (0, 1), 1))
-        near, near_other = following, following_other
-
-    near_other, *carry = hold((near_other, *carry))
+    second = jnp.concatenate([up, down])
+    up, down = along_z(up, 1), along_z(down, -1)
+    second_other = flip_y(second)
     crossed = flip_core(jnp.concatenate([near, near_other]))
-    carry = fold([waiting, (near, spots((4,), (0,), 0)), (near_other, spots((4,), (1,), 0))], carry)
-    (mixed,) = fold([(crossed, spots((4,), (0, 1), 1))], carry, w_out)
+    carry = fold([waiting, (near_other, spots((-1, 1), (1,), 0)), (second, spots((-2, 2), (0,), 0))], carry)
+    up, down, second_other, crossed, carry = hold((up, down, second_other, crossed, carry))
+    waiting = (crossed, spots((-1, 1), (0, 1), 1))
+
+    third = jnp.concatenate([up, down])
+    third_other = flip_y(third)
+    far = to_side(jnp.where(even, up, down), 1)
+    far_other = to_side(jnp.where(even, second_other[0:1], second_other[1:2]), 2)
+    crossed = flip_core(jnp.concatenate([second, second_other]))
+    carry = fold([waiting, (second_other, spots((-2, 2), (1,), 0))], carry)
+    crossed, carry = hold((crossed, carry))
+    waiting = (crossed, spots((-2, 2), (0, 1), 1))
+    carry = fold([(third, spots((-3, 3), (0,), 0)), waiting], carry)
+    third_other, far, far_other, carry = hold((third_other, far, far_other, carry))
+
+    crossed = flip_core(jnp.concatenate([third, third_other, far, far_other]))
+    carry = fold(
+        [(third_other, spots((-3, 3), (1,), 0)), (far, spots((4,), (0,), 0)), (far_other, spots((4,), (1,), 0))], carry
+    )
+    crossed, carry = hold((crossed, carry))
+    waiting = (crossed, spots((-3, 3), (0, 1), 1) + spots((4,), (0, 1), 1))
+    (mixed,) = fold([waiting], carry, w_out)
     parts = lax.all_to_all(mixed.reshape(groups, share, channels), "head", 0, 0, tiled=True)
     return total_of(parts)
 

time: 105 us -> 105 us (level)
  the two profiles are of different devices: /device:TPU:32 before, /device:TPU:1 now
where the time goes in v3:
time: 105 us; the launch traced here: 104 us
  starting transfers between devices  32.5 us (31%)
  Pallas kernels  25.7 us (24%)
  blocking collectives  25.4 us (24%)
  waiting for transfers between devices  14.2 us (14%)
  local copies, waits for them, and re-layouts  3.28 us (3%)
  other arithmetic  2.86 us (3%)
    pallas_call x7, Pallas kernels, attend(): pl.pallas_call(functools.partial(attend_kernel, carry is None, w_out is n...  18.3 us
    all_to_all x1, blocking collectives, per_device(): lax.all_to_all(copies, 'head', 0, 0, tiled=True).reshape(rows, channels)  12.9 us
    all_to_all x1, blocking collectives, per_device(): lax.all_to_all(mixed.reshape(groups, share, channels), 'head', 0, 0, tile...  12.5 us
    ppermute x6, starting transfers between devices, along_z(): return lax.ppermute(array, 'blk', [(i, target(i)) for i in range(blocks)])  10.9 us
    all_to_all x1, waiting for transfers between devices, per_device(): lax.all_to_all(partial.reshape(groups, share, channels), 'head', 0, 0, ti...  7.91 us
    all_to_all x1, starting transfers between devices, per_device(): lax.all_to_all(partial.reshape(groups, share, channels), 'head', 0, 0, ti...  7.62 us
    ppermute x4, starting transfers between devices, flip_core(): return lax.ppermute(array, 'blk', [(i, i ^ 1) for i in range(blocks)])  7.45 us
    pallas_call x1, Pallas kernels, mlp(): pl.pallas_call(mlp_kernel, out_shape=jax.ShapeDtypeStruct((rows, channels...  5.75 us
  transfers between devices with their start and end apart: 17, of which 5 were waited for; matrix products, arithmetic and copies ran while one was open for 3% of the time, Pallas kernels for 15%

profile of v3, /device:TPU:1, one launch (start us, length us, event | category | flops | bytes accessed | tf_op | source)
XLA Modules:
  0.0 104.3 jit_solution(1737567968168876427)
XLA Ops:
  0.0 5.7 %conv_mlp.1 = bf16[256,768]{1,0:T(8,128)(2,1)} custom-call(bf16[16,16,768]{2,1,0:T(8,128)(2,1)} %bitcast.15, f32[7,7,768]{2,1,0:T(8,128)} %dw_hbm.1, f32[6,128]{1,0:T(8,128)} %bitcast.21, f32[6,128]{1,0:T(8,128)} %bitcast.22, bf16[768,384]{1,0:T(8,128)(2,1)} %w1_hbm.1, f32[3,128]{1,0:T(4,128)} %bitcast.23, bf16[384,768]{1,0:T(8,128)(2,1)} %w2_hbm.1), custom_call_target="tpu_custom_call" | custom-call | tf_op jit(solution)/shard_map/conv_mlp/pallas_call | solution.py:108
  5.8 0.0 copy-start
  5.8 0.0 copy-start.8
  5.8 7.6 %all-to-all-start = ((bf16[8,32,768]{2,1,0:T(8,128)(2,1)}), bf16[8,32,768]{2,1,0:T(8,128)(2,1)S(1)}, u32[]{:S(2)}, u32[]{:S(2)}) async-start(bf16[8,32,768]{2,1,0:T(8,128)(2,1)} %bitcast.6), calls=%async_computation | async-start | bytes 786432 | tf_op jit(solution)/shard_map/all_to_all | solution.py:348
  13.4 7.9 %all-to-all-done.parts = bf16[8,32,768]{2,1,0:T(8,128)(2,1)S(1)} async-done(((bf16[8,32,768]{2,1,0:T(8,128)(2,1)}), bf16[8,32,768]{2,1,0:T(8,128)(2,1)S(1)}, u32[]{:S(2)}, u32[]{:S(2)}) %all-to-all-start) | async-done | bytes 393248 | tf_op jit(solution)/shard_map/all_to_all | solution.py:348
  21.3 0.7 copy-done.7
  22.0 0.0 copy-done.6
  22.0 0.2 block_norm.1
  22.3 0.0 copy-start.1
  22.3 12.9 %all_to_all.15 = bf16[8,32,768]{2,1,0:T(8,128)(2,1)S(1)} all-to-all(bf16[8,32,768]{2,1,0:T(8,128)(2,1)S(1)} %block_norm.1), channel_id=1, replica_groups=mesh['blk'=32,'head'=8] {'head'}, dimensions={0} | all-to-all | bytes 786432 | tf_op jit(solution)/shard_map/all_to_all | solution.py:350
  35.2 0.4 key_values.1.refs_3_
  35.6 0.5 collective-permute-start.2
  36.0 5.6 %collective-permute-start.1 = (bf16[1,256,256]{2,1,0:T(8,128)(2,1)S(1)}, bf16[1,256,256]{2,1,0:T(8,128)(2,1)S(1)}, u32[]{:S(2)}, u32[]{:S(2)}) collective-permute-start(bf16[1,256,256]{2,1,0:T(8,128)(2,1)S(1)} %key_values.1.refs_3_), channel_id=1, source_target_pairs={{0,112},{8,120},{16,0},{24,8},{32,16},{40,24},{48,32},{56,40},{64,... | collective-permute-start | bytes 393224 | tf_op jit(solution)/shard_map/ppermute | solution.py:333
  41.6 0.4 queries.1.refs_2_
  42.0 0.0 copy-start.5
  42.0 0.6 copy-done.5
  42.7 1.2 %attend.7 = (f32[4,256,128]{2,1,0:T(8,128)S(1)}, f32[4,256,256]{2,1,0:T(8,128)S(1)}) custom-call(s32[32]{0:T(128)S(1)} %copy-done.5, s32[1]{0:T(128)} %bitcast.refs_1_, bf16[4,256,128]{2,1,0:T(8,128)(2,1)S(1)} %queries.1.refs_2_, bf16[1,256,256]{2,1,0:T(8,128)(2,1)S(1)} %key_values.1.refs_3_), custom_call_target="tpu_custom_call" | custom-call | flops 32768 | bytes 65536 | tf_op jit(solution)/shard_map/attend/pallas_call | solution.py:269
  43.8 0.0 collective-permute-done.2.refs_3_
  43.9 2.8 %collective-permute-done = bf16[1,256,256]{2,1,0:T(8,128)(2,1)S(1)} collective-permute-done((bf16[1,256,256]{2,1,0:T(8,128)(2,1)S(1)}, bf16[1,256,256]{2,1,0:T(8,128)(2,1)S(1)}, u32[]{:S(2)}, u32[]{:S(2)}) %collective-permute-start) | collective-permute-done | bytes 131104 | tf_op jit(solution)/shard_map/ppermute | solution.py:333
  46.7 1.2 %collective-permute-start.5 = (bf16[2,256,256]{2,1,0:T(8,128)(2,1)S(1)}, bf16[2,256,256]{2,1,0:T(8,128)(2,1)S(1)}, u32[]{:S(2)}, u32[]{:S(2)}) collective-permute-start(bf16[2,256,256]{2,1,0:T(8,128)(2,1)S(1)} %constant_dynamic-update-slice_fusion.refs_4_), channel_id=1, source_target_pairs={{0,128},{8,136},{16,144},{24,152},{32,160},{40,168},{48,176},{56,1... | collective-permute-start | bytes 786440 | tf_op jit(solution)/shard_map/ppermute | solution.py:324
  47.9 4.6 %collective-permute-start.6 = (bf16[2,256,256]{2,1,0:T(8,128)(2,1)S(1)}, bf16[2,256,256]{2,1,0:T(8,128)(2,1)S(1)}, u32[]{:S(2)}, u32[]{:S(2)}) collective-permute-start(bf16[2,256,256]{2,1,0:T(8,128)(2,1)S(1)} %pad_maximum_fusion.2), channel_id=1, source_target_pairs={{0,8},{8,0},{16,24},{24,16},{32,40},{40,32},{48,56},{56,48},{64,72... | collective-permute-start | bytes 786440 | tf_op jit(solution)/shard_map/ppermute | solution.py:327
  52.4 0.0 collective-permute-start.3
  52.4 2.7 %collective-permute-start.4 = (bf16[1,256,256]{2,1,0:T(8,128)(2,1)S(1)}, bf16[1,256,256]{2,1,0:T(8,128)(2,1)}, u32[]{:S(2)}, u32[]{:S(2)}) collective-permute-start(bf16[1,256,256]{2,1,0:T(8,128)(2,1)S(1)} %collective-permute-done.1), channel_id=1, source_target_pairs={{0,112},{8,120},{16,0},{24,8},{32,16},{40,24},{48,32},{56,40},{64,... | collective-permute-start | bytes 393224 | tf_op jit(solution)/shard_map/ppermute | solution.py:333
  55.1 2.1 %attend.8 = (f32[4,256,128]{2,1,0:T(8,128)S(1)}, f32[4,256,256]{2,1,0:T(8,128)S(1)}) custom-call(s32[32]{0:T(128)S(1)} %copy-done.5, s32[1]{0:T(128)} %bitcast.refs_1_, bf16[4,256,128]{2,1,0:T(8,128)(2,1)S(1)} %queries.1.refs_2_, bf16[1,256,256]{2,1,0:T(8,128)(2,1)S(1)} %collective-permute-done.2.refs_3_, ...), custom_call_target="tpu_custom_call" | custom-call | flops 98304 | bytes 65536 | tf_op jit(solution)/shard_map/attend/pallas_call | solution.py:269
  57.2 1.7 %collective-permute-done.3 = bf16[1,256,256]{2,1,0:T(8,128)(2,1)} collective-permute-done((bf16[1,256,256]{2,1,0:T(8,128)(2,1)S(1)}, bf16[1,256,256]{2,1,0:T(8,128)(2,1)}, u32[]{:S(2)}, u32[]{:S(2)}) %collective-permute-start.3) | collective-permute-done | bytes 131104 | tf_op jit(solution)/shard_map/ppermute | solution.py:333
  58.9 0.8 pad_maximum_fusion
  59.7 0.8 collective-permute-start.10
  60.5 0.9 constant_dynamic-update-slice_fusion.3
  61.4 0.9 constant_dynamic-update-slice_fusion.2.refs_5_
  62.4 0.5 collective-permute-start.9
  62.9 2.7 %collective-permute-start.8 = (bf16[1,256,256]{2,1,0:T(8,128)(2,1)}, bf16[1,256,256]{2,1,0:T(8,128)(2,1)}, u32[]{:S(2)}, u32[]{:S(2)}) collective-permute-start(bf16[1,256,256]{2,1,0:T(8,128)(2,1)} %collective-permute-done.4), channel_id=1, source_target_pairs={{0,112},{8,120},{16,0},{24,8},{32,16},{40,24},{48,32},{56,40},{64,... | collective-permute-start | bytes 393224 | tf_op jit(solution)/shard_map/ppermute | solution.py:333
  65.5 3.1 %attend.9 = (f32[4,256,128]{2,1,0:T(8,128)S(1)}, f32[4,256,256]{2,1,0:T(8,128)S(1)}) custom-call(s32[32]{0:T(128)S(1)} %copy-done.5, s32[1]{0:T(128)} %bitcast.refs_1_, bf16[4,256,128]{2,1,0:T(8,128)(2,1)S(1)} %queries.1.refs_2_, bf16[2,256,256]{2,1,0:T(8,128)(2,1)S(1)} %collective-permute-done.6.refs_3_, ...), custom_call_target="tpu_custom_call" | custom-call | flops 196608 | bytes 65536 | tf_op jit(solution)/shard_map/attend/pallas_call | solution.py:269
  68.6 0.5 collective-permute-done.7
  69.1 1.3 %collective-permute-done.9.refs_4_ = bf16[2,256,256]{2,1,0:T(8,128)(2,1)S(1)} collective-permute-done((bf16[2,256,256]{2,1,0:T(8,128)(2,1)S(1)}, bf16[2,256,256]{2,1,0:T(8,128)(2,1)S(1)}, u32[]{:S(2)}, u32[]{:S(2)}) %collective-permute-start.9) | collective-permute-done | bytes 262176 | tf_op jit(solution)/shard_map/ppermute | solution.py:324
  70.4 1.0 pad_maximum_fusion.1
  71.4 0.9 collective-permute-start.14
  72.3 0.9 broadcast_select_fusion
  73.3 0.5 collective-permute-start.11
  73.8 0.4 collective-permute-start.13
  74.1 3.6 %collective-permute-start.12 = (bf16[1,256,256]{2,1,0:T(8,128)(2,1)S(1)}, bf16[1,256,256]{2,1,0:T(8,128)(2,1)S(1)}, u32[]{:S(2)}, u32[]{:S(2)}) collective-permute-start(bf16[1,256,256]{2,1,0:T(8,128)(2,1)S(1)} %get-tuple-element.85), channel_id=1, source_target_pairs={{0,16},{8,24},{16,0},{24,8},{32,48},{40,56},{48,32},{56,40},{64,80... | collective-permute-start | bytes 393224 | tf_op jit(solution)/shard_map/ppermute | solution.py:340
  77.7 3.1 %attend.10 = (f32[4,256,128]{2,1,0:T(8,128)S(1)}, f32[4,256,256]{2,1,0:T(8,128)S(1)}) custom-call(s32[32]{0:T(128)S(1)} %copy-done.5, s32[1]{0:T(128)} %bitcast.refs_1_, bf16[4,256,128]{2,1,0:T(8,128)(2,1)S(1)} %queries.1.refs_2_, bf16[4,256,256]{2,1,0:T(8,128)(2,1)S(1)} %collective-permute-done.10.refs_3_, ...), custom_call_target="tpu_custom_call" | custom-call | flops 196608 | bytes 65536 | tf_op jit(solution)/shard_map/attend/pallas_call | solution.py:269
  80.8 3.1 %attend.11 = (f32[4,256,128]{2,1,0:T(8,128)S(1)}, f32[4,256,256]{2,1,0:T(8,128)S(1)}) custom-call(s32[32]{0:T(128)S(1)} %copy-done.5, s32[1]{0:T(128)} %bitcast.refs_1_, bf16[4,256,128]{2,1,0:T(8,128)(2,1)S(1)} %queries.1.refs_2_, bf16[2,256,256]{2,1,0:T(8,128)(2,1)S(1)} %get-tuple-element.87.refs_3_, ...), custom_call_target="tpu_custom_call" | custom-call | flops 196608 | bytes 65536 | tf_op jit(solution)/shard_map/attend/pallas_call | solution.py:269
  84.1 0.0 copy-start.2
  84.1 1.2 %collective-permute-start.15 = (bf16[6,256,256]{2,1,0:T(8,128)(2,1)S(1)}, bf16[6,256,256]{2,1,0:T(8,128)(2,1)S(1)}, u32[]{:S(2)}, u32[]{:S(2)}) collective-permute-start(bf16[6,256,256]{2,1,0:T(8,128)(2,1)S(1)} %constant_dynamic-update-slice_fusion.6), channel_id=1, source_target_pairs={{0,8},{8,0},{16,24},{24,16},{32,40},{40,32},{48,56},{56,48},{64,72... | collective-permute-start | bytes 2359304 | tf_op jit(solution)/shard_map/ppermute | solution.py:327
  85.3 2.5 %attend.12 = (f32[4,256,128]{2,1,0:T(8,128)S(1)}, f32[4,256,256]{2,1,0:T(8,128)S(1)}) custom-call(s32[32]{0:T(128)S(1)} %copy-done.5, s32[1]{0:T(128)} %bitcast.refs_1_, bf16[4,256,128]{2,1,0:T(8,128)(2,1)S(1)} %queries.1.refs_2_, bf16[2,256,256]{2,1,0:T(8,128)(2,1)S(1)} %collective-permute-done.11.refs_3_, ...), custom_call_target="tpu_custom_call" | custom-call | flops 131072 | bytes 65536 | tf_op jit(solution)/shard_map/attend/pallas_call | solution.py:269
  87.9 3.3 %attend.13 = bf16[256,768]{1,0:T(8,128)(2,1)S(1)} custom-call(s32[32]{0:T(128)S(1)} %copy-done.5, s32[1]{0:T(128)} %bitcast.refs_1_, bf16[4,256,128]{2,1,0:T(8,128)(2,1)S(1)} %queries.1.refs_2_, bf16[6,256,256]{2,1,0:T(8,128)(2,1)S(1)} %collective-permute-done.15.refs_3_, f32[4,256,128]{2,1,0:T(8,128)S(1)} %get-tuple-element.83.refs_4_, ...), custom_call_target="tpu_custom_call" | custom-call | flops 196608 | bytes 65536 | tf_op jit(solution)/shard_map/attend/pallas_call | solution.py:269
  91.1 12.5 %all_to_all.16.parts = bf16[8,32,768]{2,1,0:T(8,128)(2,1)S(1)} all-to-all(bf16[8,32,768]{2,1,0:T(8,128)(2,1)S(1)} %bitcast.17), channel_id=1, replica_groups=mesh['blk'=32,'head'=8] {'head'}, dimensions={0} | all-to-all | bytes 786432 | tf_op jit(solution)/shard_map/all_to_all | solution.py:399
  103.7 0.7 total.1
  (31 shorter events, 0.2 us)
Async XLA Ops:
  5.8 15.6 %copy-start = (bf16[1,16,16,768]{3,2,1,0:T(8,128)(2,1)S(1)}, bf16[1,16,16,768]{3,2,1,0:T(8,128)(2,1)}, u32[]{:S(2)}) copy-start(bf16[1,16,16,768]{3,2,1,0:T(8,128)(2,1)} %param.15) | copy-start | bytes 1179652
  5.8 15.6 %copy-start.8 = (f32[768]{0:T(1024)S(1)}, f32[768]{0:T(1024)}, u32[]{:S(2)}) copy-start(f32[768]{0:T(1024)} %param.25) | copy-start | bytes 9220
  5.8 15.5 %all-to-all-start = ((bf16[8,32,768]{2,1,0:T(8,128)(2,1)}), bf16[8,32,768]{2,1,0:T(8,128)(2,1)S(1)}, u32[]{:S(2)}, u32[]{:S(2)}) async-start(bf16[8,32,768]{2,1,0:T(8,128)(2,1)} %bitcast.6), calls=%async_computation | async-start | bytes 786432 | tf_op jit(solution)/shard_map/all_to_all | solution.py:348
  21.3 0.7 copy-start.7
  21.3 0.7 copy-start.6
  22.0 13.2 %copy-start.3 = (bf16[768,128]{1,0:T(8,128)(2,1)S(1)}, bf16[768,128]{1,0:T(8,128)(2,1)}, u32[]{:S(2)}) copy-start(bf16[768,128]{1,0:T(8,128)(2,1)} %wk.1) | copy-start | bytes 589828
  22.0 13.2 %copy-start.4 = (bf16[768,128]{1,0:T(8,128)(2,1)S(1)}, bf16[768,128]{1,0:T(8,128)(2,1)}, u32[]{:S(2)}) copy-start(bf16[768,128]{1,0:T(8,128)(2,1)} %wv.1) | copy-start | bytes 589828
  22.3 19.4 %copy-start.1 = (bf16[768,512]{1,0:T(8,128)(2,1)S(1)}, bf16[768,512]{1,0:T(8,128)(2,1)}, u32[]{:S(2)}) copy-start(bf16[768,512]{1,0:T(8,128)(2,1)} %wq.1) | copy-start | bytes 2359300
  35.6 8.3 %collective-permute-start.2 = (bf16[1,256,256]{2,1,0:T(8,128)(2,1)S(1)}, bf16[1,256,256]{2,1,0:T(8,128)(2,1)S(1)}, u32[]{:S(2)}, u32[]{:S(2)}) collective-permute-start(bf16[1,256,256]{2,1,0:T(8,128)(2,1)S(1)} %key_values.1.refs_3_), channel_id=1, source_target_pairs={{0,128},{8,136},{16,144},{24,152},{32,160},{40,168},{48,176},{56,1... | collective-permute-start | bytes 393224 | tf_op jit(solution)/shard_map/ppermute | solution.py:324
  36.0 7.8 %collective-permute-start.1 = (bf16[1,256,256]{2,1,0:T(8,128)(2,1)S(1)}, bf16[1,256,256]{2,1,0:T(8,128)(2,1)S(1)}, u32[]{:S(2)}, u32[]{:S(2)}) collective-permute-start(bf16[1,256,256]{2,1,0:T(8,128)(2,1)S(1)} %key_values.1.refs_3_), channel_id=1, source_target_pairs={{0,112},{8,120},{16,0},{24,8},{32,16},{40,24},{48,32},{56,40},{64,... | collective-permute-start | bytes 393224 | tf_op jit(solution)/shard_map/ppermute | solution.py:333
  41.6 5.0 %collective-permute-start = (bf16[1,256,256]{2,1,0:T(8,128)(2,1)S(1)}, bf16[1,256,256]{2,1,0:T(8,128)(2,1)S(1)}, u32[]{:S(2)}, u32[]{:S(2)}) collective-permute-start(bf16[1,256,256]{2,1,0:T(8,128)(2,1)S(1)} %key_values.1.refs_3_), channel_id=1, source_target_pairs={{0,16},{8,24},{16,32},{24,40},{32,48},{40,56},{48,64},{56,72},{64,... | collective-permute-start | bytes 393224 | tf_op jit(solution)/shard_map/ppermute | solution.py:333
  42.0 0.7 copy-start.5
  46.7 12.2 %collective-permute-start.5 = (bf16[2,256,256]{2,1,0:T(8,128)(2,1)S(1)}, bf16[2,256,256]{2,1,0:T(8,128)(2,1)S(1)}, u32[]{:S(2)}, u32[]{:S(2)}) collective-permute-start(bf16[2,256,256]{2,1,0:T(8,128)(2,1)S(1)} %constant_dynamic-update-slice_fusion.refs_4_), channel_id=1, source_target_pairs={{0,128},{8,136},{16,144},{24,152},{32,160},{40,168},{48,176},{56,1... | collective-permute-start | bytes 786440 | tf_op jit(solution)/shard_map/ppermute | solution.py:324
  47.9 11.0 %collective-permute-start.6 = (bf16[2,256,256]{2,1,0:T(8,128)(2,1)S(1)}, bf16[2,256,256]{2,1,0:T(8,128)(2,1)S(1)}, u32[]{:S(2)}, u32[]{:S(2)}) collective-permute-start(bf16[2,256,256]{2,1,0:T(8,128)(2,1)S(1)} %pad_maximum_fusion.2), channel_id=1, source_target_pairs={{0,8},{8,0},{16,24},{24,16},{32,40},{40,32},{48,56},{56,48},{64,72... | collective-permute-start | bytes 786440 | tf_op jit(solution)/shard_map/ppermute | solution.py:327
  52.4 6.4 %collective-permute-start.3 = (bf16[1,256,256]{2,1,0:T(8,128)(2,1)S(1)}, bf16[1,256,256]{2,1,0:T(8,128)(2,1)}, u32[]{:S(2)}, u32[]{:S(2)}) collective-permute-start(bf16[1,256,256]{2,1,0:T(8,128)(2,1)S(1)} %collective-permute-done), channel_id=1, source_target_pairs={{0,16},{8,24},{16,32},{24,40},{32,48},{40,56},{48,64},{56,72},{64,... | collective-permute-start | bytes 393224 | tf_op jit(solution)/shard_map/ppermute | solution.py:333
  52.4 6.4 %collective-permute-start.4 = (bf16[1,256,256]{2,1,0:T(8,128)(2,1)S(1)}, bf16[1,256,256]{2,1,0:T(8,128)(2,1)}, u32[]{:S(2)}, u32[]{:S(2)}) collective-permute-start(bf16[1,256,256]{2,1,0:T(8,128)(2,1)S(1)} %collective-permute-done.1), channel_id=1, source_target_pairs={{0,112},{8,120},{16,0},{24,8},{32,16},{40,24},{48,32},{56,40},{64,... | collective-permute-start | bytes 393224 | tf_op jit(solution)/shard_map/ppermute | solution.py:333
  59.7 10.6 %collective-permute-start.10 = (bf16[4,256,256]{2,1,0:T(8,128)(2,1)}, bf16[4,256,256]{2,1,0:T(8,128)(2,1)S(1)}, u32[]{:S(2)}, u32[]{:S(2)}) collective-permute-start(bf16[4,256,256]{2,1,0:T(8,128)(2,1)} %pad_maximum_fusion), channel_id=1, source_target_pairs={{0,8},{8,0},{16,24},{24,16},{32,40},{40,32},{48,56},{56,48},{64,72... | collective-permute-start | bytes 1572872 | tf_op jit(solution)/shard_map/ppermute | solution.py:327
  62.4 8.0 %collective-permute-start.9 = (bf16[2,256,256]{2,1,0:T(8,128)(2,1)S(1)}, bf16[2,256,256]{2,1,0:T(8,128)(2,1)S(1)}, u32[]{:S(2)}, u32[]{:S(2)}) collective-permute-start(bf16[2,256,256]{2,1,0:T(8,128)(2,1)S(1)} %constant_dynamic-update-slice_fusion.2.refs_5_), channel_id=1, source_target_pairs={{0,128},{8,136},{16,144},{24,152},{32,160},{40,168},{48,176},{56,1... | collective-permute-start | bytes 786440 | tf_op jit(solution)/shard_map/ppermute | solution.py:324
  62.8 6.2 %collective-permute-start.7 = (bf16[1,256,256]{2,1,0:T(8,128)(2,1)}, bf16[1,256,256]{2,1,0:T(8,128)(2,1)S(1)}, u32[]{:S(2)}, u32[]{:S(2)}) collective-permute-start(bf16[1,256,256]{2,1,0:T(8,128)(2,1)} %collective-permute-done.3), channel_id=1, source_target_pairs={{0,16},{8,24},{16,32},{24,40},{32,48},{40,56},{48,64},{56,72},{64,... | collective-permute-start | bytes 393224 | tf_op jit(solution)/shard_map/ppermute | solution.py:333
  62.9 6.2 %collective-permute-start.8 = (bf16[1,256,256]{2,1,0:T(8,128)(2,1)}, bf16[1,256,256]{2,1,0:T(8,128)(2,1)}, u32[]{:S(2)}, u32[]{:S(2)}) collective-permute-start(bf16[1,256,256]{2,1,0:T(8,128)(2,1)} %collective-permute-done.4), channel_id=1, source_target_pairs={{0,112},{8,120},{16,0},{24,8},{32,16},{40,24},{48,32},{56,40},{64,... | collective-permute-start | bytes 393224 | tf_op jit(solution)/shard_map/ppermute | solution.py:333
  71.4 9.4 %collective-permute-start.14 = (bf16[4,256,256]{2,1,0:T(8,128)(2,1)S(1)}, bf16[4,256,256]{2,1,0:T(8,128)(2,1)S(1)}, u32[]{:S(2)}, u32[]{:S(2)}) collective-permute-start(bf16[4,256,256]{2,1,0:T(8,128)(2,1)S(1)} %pad_maximum_fusion.1), channel_id=1, source_target_pairs={{0,8},{8,0},{16,24},{24,16},{32,40},{40,32},{48,56},{56,48},{64,72... | collective-permute-start | bytes 1572872 | tf_op jit(solution)/shard_map/ppermute | solution.py:327
  73.3 10.7 %collective-permute-start.11 = (bf16[2,256,256]{2,1,0:T(8,128)(2,1)S(1)}, bf16[2,256,256]{2,1,0:T(8,128)(2,1)S(1)}, u32[]{:S(2)}, u32[]{:S(2)}) collective-permute-start(bf16[2,256,256]{2,1,0:T(8,128)(2,1)S(1)} %get-tuple-element.87.refs_3_), channel_id=1, source_target_pairs={{0,128},{8,136},{16,144},{24,152},{32,160},{40,168},{48,176},{56,1... | collective-permute-start | bytes 786440 | tf_op jit(solution)/shard_map/ppermute | solution.py:324
  73.8 10.2 %collective-permute-start.13 = (bf16[1,256,256]{2,1,0:T(8,128)(2,1)S(1)}, bf16[1,256,256]{2,1,0:T(8,128)(2,1)S(1)}, u32[]{:S(2)}, u32[]{:S(2)}) collective-permute-start(bf16[1,256,256]{2,1,0:T(8,128)(2,1)S(1)} %slice_select_fusion), channel_id=1, source_target_pairs={{0,32},{8,40},{16,112},{24,120},{32,64},{40,72},{48,16},{56,24},{6... | collective-permute-start | bytes 393224 | tf_op jit(solution)/shard_map/ppermute | solution.py:340
  74.1 9.9 %collective-permute-start.12 = (bf16[1,256,256]{2,1,0:T(8,128)(2,1)S(1)}, bf16[1,256,256]{2,1,0:T(8,128)(2,1)S(1)}, u32[]{:S(2)}, u32[]{:S(2)}) collective-permute-start(bf16[1,256,256]{2,1,0:T(8,128)(2,1)S(1)} %get-tuple-element.85), channel_id=1, source_target_pairs={{0,16},{8,24},{16,0},{24,8},{32,48},{40,56},{48,32},{56,40},{64,80... | collective-permute-start | bytes 393224 | tf_op jit(solution)/shard_map/ppermute | solution.py:340
  84.1 3.8 %copy-start.2 = (bf16[512,768]{1,0:T(8,128)(2,1)S(1)}, bf16[512,768]{1,0:T(8,128)(2,1)}, u32[]{:S(2)}) copy-start(bf16[512,768]{1,0:T(8,128)(2,1)} %refs_6_.1) | copy-start | bytes 2359300
  84.1 3.8 %collective-permute-start.15 = (bf16[6,256,256]{2,1,0:T(8,128)(2,1)S(1)}, bf16[6,256,256]{2,1,0:T(8,128)(2,1)S(1)}, u32[]{:S(2)}, u32[]{:S(2)}) collective-permute-start(bf16[6,256,256]{2,1,0:T(8,128)(2,1)S(1)} %constant_dynamic-update-slice_fusion.6), channel_id=1, source_target_pairs={{0,8},{8,0},{16,24},{24,16},{32,40},{40,32},{48,56},{56,48},{64,72... | collective-permute-start | bytes 2359304 | tf_op jit(solution)/shard_map/ppermute | solution.py:327

commit v4 on v3

--- a/solution.py
+++ b/solution.py
@@ -199,11 +199,13 @@
     heads, rows, _ = query.shape
     here = own[0]
     here_y, here_z, here_core = lax.div(here, 2 * depth), lax.rem(lax.div(here, 2), depth), lax.rem(here, 2)
+    behind = 2 * here_core - 1
     pages = []
     for chunk, size in zip(chunks, sizes):
         for index in range(size):
             side, shift, core = places[len(pages)]
-            number = (here_y ^ side) * (2 * depth) + lax.rem(here_z + shift % depth, depth) * 2 + (here_core ^ core)
+            place = lax.rem(here_z + depth + shift * behind, depth)
+            number = (here_y ^ side) * (2 * depth) + place * 2 + (here_core ^ core)
             pages.append((chunk, index, valid_counts[number]))
     group_size = 4 if len(pages) in (4, 7, 8) else min(3, len(pages))
     tokens = chunks[0].shape[1]
@@ -273,7 +275,7 @@
         out_specs=[vmem_spec()] * len(out_shape),
         scratch_shapes=scratch,
         cost_estimate=pl.CostEstimate(flops=pairs // 8, transcendentals=0, bytes_accessed=2**16),
-        compiler_params=params(28),
+        compiler_params=params(14),
         name="attend",
     )(*operands)
 
@@ -320,26 +322,22 @@
     depth = blocks // 4
     share = rows // groups
 
+    def moved(array, target):
+        return lax.ppermute(array, "blk", [(i, target(i)) for i in range(blocks)])
+
     def flip_y(array):
-        return lax.ppermute(array, "blk", [(i, (i + 2 * depth) % blocks) for i in range(blocks)])
+        return moved(array, lambda i: (i + 2 * depth) % blocks)
 
     def flip_core(array):
-        return lax.ppermute(array, "blk", [(i, i ^ 1) for i in range(blocks)])
-
-    def along_z(array, step):
+        return moved(array, lambda i: i ^ 1)
+
+    def along_z(array, step=1):
         def target(i):
-            return i // (2 * depth) * (2 * depth) + (i + 2 * step) % (2 * depth)
-
-        return lax.ppermute(array, "blk", [(i, target(i)) for i in range(blocks)])
-
-    def to_side(array, step):
-        def target(i):
-            turn = 2 * step if i // 2 % 2 == 0 else -2 * step
+            turn = 2 * step if i % 2 == 0 else -2 * step
             return i // (2 * depth) * (2 * depth) + (i + turn) % (2 * depth)
 
-        return lax.ppermute(array, "blk", [(i, target(i)) for i in range(blocks)])
-
-    even = lax.axis_index("blk") // 2 % 2 == 0
+        return moved(array, target)
+
     own = lax.axis_index("blk").astype(jnp.int32)[None]
     place = lax.axis_index("head").astype(jnp.int32)[None]
     hold = lax.optimization_barrier
@@ -349,53 +347,64 @@
     copies = block_norm(place, parts, pages.reshape(rows, channels), layer_scale, fc2_b, norm2_gain)
     normed = lax.all_to_all(copies, "head", 0, 0, tiled=True).reshape(rows, channels)
 
-    def spots(shifts, sides, core):
-        return [(side, shift, core) for side in sides for shift in shifts]
-
     def fold(pieces, carry=None, weight=None):
         return attend(valid_counts, own, depth, query, pieces, carry, weight)
 
+    def mine(side, shift):
+        return [(side, shift, 0), (side, shift, 1)]
+
+    def theirs(side, shift):
+        return [(side, -shift, 1), (side, -shift, 0)]
+
     start = key_values(normed, w_key, w_value)
-    up, down = along_z(start, 1), along_z(start, -1)
-    other = flip_y(start)
+    beside = flip_core(start)
     query = queries_of(normed, w_query)
-    carry = fold([(start, spots((0,), (0,), 0))])
-    up, down, other, carry = hold((up, down, other, carry))
-
-    near = jnp.concatenate([up, down])
-    up, down = along_z(up, 1), along_z(down, -1)
-    near_other = flip_y(near)
-    crossed = flip_core(jnp.concatenate([start, other]))
-    carry = fold([(other, spots((0,), (1,), 0)), (near, spots((-1, 1), (0,), 0))], carry)
-    up, down, near_other, crossed, carry = hold((up, down, near_other, crossed, carry))
-    waiting = (crossed, spots((0,), (0, 1), 1))
-
-    second = jnp.concatenate([up, down])
-    up, down = along_z(up, 1), along_z(down, -1)
+    beside, query = hold((beside, query))
+    own_pair = jnp.concatenate([start, beside])
+
+    first = along_z(own_pair)
+    own_other = flip_y(own_pair)
+    carry = fold([(own_pair, mine(0, 0))])
+    first, own_other, carry = hold((first, own_other, carry))
+
+    second = along_z(first)
+    first_other = flip_y(first)
+    first_core = flip_core(first)
+    carry = fold([(own_other, mine(1, 0)), (first, mine(0, 1))], carry)
+    second, first_other, first_core, carry = hold((second, first_other, first_core, carry))
+
+    third = along_z(second)
     second_other = flip_y(second)
-    crossed = flip_core(jnp.concatenate([near, near_other]))
-    carry = fold([waiting, (near_other, spots((-1, 1), (1,), 0)), (second, spots((-2, 2), (0,), 0))], carry)
-    up, down, second_other, crossed, carry = hold((up, down, second_other, crossed, carry))
-    waiting = (crossed, spots((-1, 1), (0, 1), 1))
-
-    third = jnp.concatenate([up, down])
+    second_core = flip_core(second)
+    first_other_core = flip_core(first_other)
+    carry = fold([(first_core, theirs(0, 1)), (first_other, mine(1, 1)), (second, mine(0, 2))], carry)
+    third, second_other, second_core, first_other_core, carry = hold(
+        (third, second_other, second_core, first_other_core, carry)
+    )
+
     third_other = flip_y(third)
-    far = to_side(jnp.where(even, up, down), 1)
-    far_other = to_side(jnp.where(even, second_other[0:1], second_other[1:2]), 2)
-    crossed = flip_core(jnp.concatenate([second, second_other]))
-    carry = fold([waiting, (second_other, spots((-2, 2), (1,), 0))], carry)
-    crossed, carry = hold((crossed, carry))
-    waiting = (crossed, spots((-2, 2), (0, 1), 1))
-    carry = fold([(third, spots((-3, 3), (0,), 0)), waiting], carry)
+    far = along_z(third[0:1])
+    far_other = along_z(second_other[0:1], 2)
+    third_core = flip_core(third)
+    second_other_core = flip_core(second_other)
+    carry = fold(
+        [
+            (first_other_core, theirs(1, 1)),
+            (second_core, theirs(0, 2)),
+            (second_other, mine(1, 2)),
+            (third, mine(0, 3)),
+        ],
+        carry,
+    )
+    third_core, second_other_core, carry = hold((third_core, second_other_core, carry))
+    carry = fold([(third_core, theirs(0, 3)), (second_other_core, theirs(1, 2))], carry)
     third_other, far, far_other, carry = hold((third_other, far, far_other, carry))
 
-    crossed = flip_core(jnp.concatenate([third, third_other, far, far_other]))
-    carry = fold(
-        [(third_other, spots((-3, 3), (1,), 0)), (far, spots((4,), (0,), 0)), (far_other, spots((4,), (1,), 0))], carry
-    )
-    crossed, carry = hold((crossed, carry))
-    waiting = (crossed, spots((-3, 3), (0, 1), 1) + spots((4,), (0, 1), 1))
-    (mixed,) = fold([waiting], carry, w_out)
+    last = jnp.concatenate([third_other, far, far_other])
+    last_core = flip_core(last)
+    carry = fold([(last, mine(1, 3) + [(0, depth // 2, 0), (1, depth // 2, 0)])], carry)
+    last_core, carry = hold((last_core, carry))
+    (mixed,) = fold([(last_core, theirs(1, 3) + [(0, depth // 2, 1), (1, depth // 2, 1)])], carry, w_out)
     parts = lax.all_to_all(mixed.reshape(groups, share, channels), "head", 0, 0, tiled=True)
     return total_of(parts)
 

time: 105 us -> 99.3 us (0.946)
  the two profiles are of different devices: /device:TPU:1 before, /device:TPU:32 now
where the time goes in v4:
time: 99.3 us; the launch traced here: 99 us
  blocking collectives  26.5 us (27%)
  Pallas kernels  26.3 us (26%)
  starting transfers between devices  24 us (24%)
  waiting for transfers between devices  20.4 us (21%)
  local copies, waits for them, and re-layouts  1.44 us (1%)
    pallas_call x7, Pallas kernels, attend(): pl.pallas_call(functools.partial(attend_kernel, carry is None, w_out is n...  18.9 us
    ppermute x16, starting transfers between devices, moved(): return lax.ppermute(array, 'blk', [(i, target(i)) for i in range(blocks)])  16.9 us
    all_to_all x1, blocking collectives, per_device(): lax.all_to_all(mixed.reshape(groups, share, channels), 'head', 0, 0, tile...  13.8 us
    all_to_all x1, blocking collectives, per_device(): lax.all_to_all(copies, 'head', 0, 0, tiled=True).reshape(rows, channels)  12.8 us
    ppermute x16, waiting for transfers between devices, moved(): return lax.ppermute(array, 'blk', [(i, target(i)) for i in range(blocks)])  10.7 us
    all_to_all x1, waiting for transfers between devices, per_device(): lax.all_to_all(partial.reshape(groups, share, channels), 'head', 0, 0, ti...  9.66 us
    all_to_all x1, starting transfers between devices, per_device(): lax.all_to_all(partial.reshape(groups, share, channels), 'head', 0, 0, ti...  7.07 us
    pallas_call x1, Pallas kernels, mlp(): pl.pallas_call(mlp_kernel, out_shape=jax.ShapeDtypeStruct((rows, channels...  5.76 us
  transfers between devices with their start and end apart: 17, of which 6 were waited for; matrix products, arithmetic and copies ran while one was open for 0% of the time, Pallas kernels for 17%

profile of v4, /device:TPU:32, one launch (start us, length us, event | category | flops | bytes accessed | tf_op | source)
XLA Modules:
  0.0 99.0 jit_solution(15833737664169234165)
XLA Ops:
  0.0 5.8 %conv_mlp.1 = bf16[256,768]{1,0:T(8,128)(2,1)} custom-call(bf16[16,16,768]{2,1,0:T(8,128)(2,1)} %bitcast.15, f32[7,7,768]{2,1,0:T(8,128)} %dw_hbm.1, f32[6,128]{1,0:T(8,128)} %bitcast.21, f32[6,128]{1,0:T(8,128)} %bitcast.22, bf16[768,384]{1,0:T(8,128)(2,1)} %w1_hbm.1, f32[3,128]{1,0:T(4,128)} %bitcast.23, bf16[384,768]{1,0:T(8,128)(2,1)} %w2_hbm.1), custom_call_target="tpu_custom_call" | custom-call | tf_op jit(solution)/shard_map/conv_mlp/pallas_call | solution.py:108
  5.8 0.0 copy-start
  5.8 0.0 copy-start.8
  5.8 7.1 %all-to-all-start = ((bf16[8,32,768]{2,1,0:T(8,128)(2,1)}), bf16[8,32,768]{2,1,0:T(8,128)(2,1)S(1)}, u32[]{:S(2)}, u32[]{:S(2)}) async-start(bf16[8,32,768]{2,1,0:T(8,128)(2,1)} %bitcast.6), calls=%async_computation | async-start | bytes 786432 | tf_op jit(solution)/shard_map/all_to_all | solution.py:346
  12.9 9.7 %all-to-all-done.parts = bf16[8,32,768]{2,1,0:T(8,128)(2,1)S(1)} async-done(((bf16[8,32,768]{2,1,0:T(8,128)(2,1)}), bf16[8,32,768]{2,1,0:T(8,128)(2,1)S(1)}, u32[]{:S(2)}, u32[]{:S(2)}) %all-to-all-start) | async-done | bytes 393248 | tf_op jit(solution)/shard_map/all_to_all | solution.py:346
  22.5 0.7 copy-done.7
  23.2 0.0 copy-done.6
  23.2 0.2 block_norm.1
  23.5 0.0 copy-start.1
  23.5 12.8 %all_to_all.15 = bf16[8,32,768]{2,1,0:T(8,128)(2,1)S(1)} all-to-all(bf16[8,32,768]{2,1,0:T(8,128)(2,1)S(1)} %block_norm.1), channel_id=1, replica_groups=mesh['blk'=32,'head'=8] {'head'}, dimensions={0} | all-to-all | bytes 786432 | tf_op jit(solution)/shard_map/all_to_all | solution.py:348
  36.3 0.4 key_values.1
  36.6 0.1 collective-permute-start
  36.7 0.4 queries.1.refs_2_
  37.1 0.9 collective-permute-done
  38.1 0.8 collective-permute-start.2
  38.9 1.9 %collective-permute-start.1 = (bf16[2,256,256]{2,1,0:T(8,128)(2,1)S(1)}, bf16[2,256,256]{2,1,0:T(8,128)(2,1)S(1)}, u32[]{:S(2)}, u32[]{:S(2)}) collective-permute-start(bf16[2,256,256]{2,1,0:T(8,128)(2,1)S(1)} %pad_maximum_fusion.refs_3_), channel_id=1, source_target_pairs={{0,16},{8,120},{16,32},{24,8},{32,48},{40,24},{48,64},{56,40},{64,... | collective-permute-start | bytes 786440 | tf_op jit(solution)/shard_map/ppermute | solution.py:326
  40.8 0.7 copy-done.5
  41.4 1.5 %attend.7 = (f32[4,256,128]{2,1,0:T(8,128)S(1)}, f32[4,256,256]{2,1,0:T(8,128)S(1)}) custom-call(s32[32]{0:T(128)S(1)} %copy-done.5, s32[1]{0:T(128)} %bitcast.refs_1_, bf16[4,256,128]{2,1,0:T(8,128)(2,1)S(1)} %queries.1.refs_2_, bf16[2,256,256]{2,1,0:T(8,128)(2,1)S(1)} %pad_maximum_fusion.refs_3_), custom_call_target="tpu_custom_call" | custom-call | flops 65536 | bytes 65536 | tf_op jit(solution)/shard_map/attend/pallas_call | solution.py:271
  43.0 3.6 %collective-permute-done.2.refs_3_ = bf16[2,256,256]{2,1,0:T(8,128)(2,1)S(1)} collective-permute-done((bf16[2,256,256]{2,1,0:T(8,128)(2,1)S(1)}, bf16[2,256,256]{2,1,0:T(8,128)(2,1)S(1)}, u32[]{:S(2)}, u32[]{:S(2)}) %collective-permute-start.2) | collective-permute-done | bytes 262176 | tf_op jit(solution)/shard_map/ppermute | solution.py:326
  46.6 0.0 collective-permute-start.5
  46.6 0.7 collective-permute-start.4
  47.2 1.9 %collective-permute-start.3 = (bf16[2,256,256]{2,1,0:T(8,128)(2,1)S(1)}, bf16[2,256,256]{2,1,0:T(8,128)(2,1)S(1)}, u32[]{:S(2)}, u32[]{:S(2)}) collective-permute-start(bf16[2,256,256]{2,1,0:T(8,128)(2,1)S(1)} %collective-permute-done.1.refs_4_), channel_id=1, source_target_pairs={{0,16},{8,120},{16,32},{24,8},{32,48},{40,24},{48,64},{56,40},{64,... | collective-permute-start | bytes 786440 | tf_op jit(solution)/shard_map/ppermute | solution.py:326
  49.1 2.5 %attend.8 = (f32[4,256,128]{2,1,0:T(8,128)S(1)}, f32[4,256,256]{2,1,0:T(8,128)S(1)}) custom-call(s32[32]{0:T(128)S(1)} %copy-done.5, s32[1]{0:T(128)} %bitcast.refs_1_, bf16[4,256,128]{2,1,0:T(8,128)(2,1)S(1)} %queries.1.refs_2_, bf16[2,256,256]{2,1,0:T(8,128)(2,1)S(1)} %collective-permute-done.2.refs_3_, ...), custom_call_target="tpu_custom_call" | custom-call | flops 131072 | bytes 65536 | tf_op jit(solution)/shard_map/attend/pallas_call | solution.py:271
  51.7 3.6 %collective-permute-done.4.refs_4_ = bf16[2,256,256]{2,1,0:T(8,128)(2,1)S(1)} collective-permute-done((bf16[2,256,256]{2,1,0:T(8,128)(2,1)S(1)}, bf16[2,256,256]{2,1,0:T(8,128)(2,1)S(1)}, u32[]{:S(2)}, u32[]{:S(2)}) %collective-permute-start.4) | collective-permute-done | bytes 262176 | tf_op jit(solution)/shard_map/ppermute | solution.py:326
  55.3 0.0 collective-permute-done.3.refs_5_
  55.3 0.0 collective-permute-start.9
  55.3 0.5 collective-permute-start.8
  55.8 0.7 collective-permute-start.7
  56.5 1.9 %collective-permute-start.6 = (bf16[2,256,256]{2,1,0:T(8,128)(2,1)S(1)}, bf16[2,256,256]{2,1,0:T(8,128)(2,1)S(1)}, u32[]{:S(2)}, u32[]{:S(2)}) collective-permute-start(bf16[2,256,256]{2,1,0:T(8,128)(2,1)S(1)} %collective-permute-done.3.refs_5_), channel_id=1, source_target_pairs={{0,16},{8,120},{16,32},{24,8},{32,48},{40,24},{48,64},{56,40},{64,... | collective-permute-start | bytes 786440 | tf_op jit(solution)/shard_map/ppermute | solution.py:326
  58.4 3.1 %attend.9 = (f32[4,256,128]{2,1,0:T(8,128)S(1)}, f32[4,256,256]{2,1,0:T(8,128)S(1)}) custom-call(s32[32]{0:T(128)S(1)} %copy-done.5, s32[1]{0:T(128)} %bitcast.refs_1_, bf16[4,256,128]{2,1,0:T(8,128)(2,1)S(1)} %queries.1.refs_2_, bf16[2,256,256]{2,1,0:T(8,128)(2,1)S(1)} %collective-permute-done.5.refs_3_, ...), custom_call_target="tpu_custom_call" | custom-call | flops 196608 | bytes 65536 | tf_op jit(solution)/shard_map/attend/pallas_call | solution.py:271
  61.5 0.0 collective-permute-done.9.refs_3_
  61.6 2.5 %collective-permute-done.7.refs_5_ = bf16[2,256,256]{2,1,0:T(8,128)(2,1)S(1)} collective-permute-done((bf16[2,256,256]{2,1,0:T(8,128)(2,1)S(1)}, bf16[2,256,256]{2,1,0:T(8,128)(2,1)S(1)}, u32[]{:S(2)}, u32[]{:S(2)}) %collective-permute-start.7) | collective-permute-done | bytes 262176 | tf_op jit(solution)/shard_map/ppermute | solution.py:326
  64.0 0.1 collective-permute-done.6.refs_6_
  64.1 0.5 collective-permute-start.13
  64.6 0.9 collective-permute-start.10
  65.5 1.7 %collective-permute-start.11 = (bf16[1,256,256]{2,1,0:T(8,128)(2,1)S(1)}, bf16[1,256,256]{2,1,0:T(8,128)(2,1)S(1)}, u32[]{:S(2)}, u32[]{:S(2)}) collective-permute-start(bf16[1,256,256]{2,1,0:T(8,128)(2,1)S(1)} %slice.6), channel_id=1, source_target_pairs={{0,16},{8,120},{16,32},{24,8},{32,48},{40,24},{48,64},{56,40},{64,... | collective-permute-start | bytes 393224 | tf_op jit(solution)/shard_map/ppermute | solution.py:326
  67.2 5.3 %collective-permute-start.12 = (bf16[1,256,256]{2,1,0:T(8,128)(2,1)S(1)}, bf16[1,256,256]{2,1,0:T(8,128)(2,1)S(1)}, u32[]{:S(2)}, u32[]{:S(2)}) collective-permute-start(bf16[1,256,256]{2,1,0:T(8,128)(2,1)S(1)} %slice.7), channel_id=1, source_target_pairs={{0,32},{8,104},{16,48},{24,120},{32,64},{40,8},{48,80},{56,24},{64... | collective-permute-start | bytes 393224 | tf_op jit(solution)/shard_map/ppermute | solution.py:326
  72.5 3.9 %attend.10 = (f32[4,256,128]{2,1,0:T(8,128)S(1)}, f32[4,256,256]{2,1,0:T(8,128)S(1)}) custom-call(s32[32]{0:T(128)S(1)} %copy-done.5, s32[1]{0:T(128)} %bitcast.refs_1_, bf16[4,256,128]{2,1,0:T(8,128)(2,1)S(1)} %queries.1.refs_2_, bf16[2,256,256]{2,1,0:T(8,128)(2,1)S(1)} %collective-permute-done.9.refs_3_, ...), custom_call_target="tpu_custom_call" | custom-call | flops 262144 | bytes 65536 | tf_op jit(solution)/shard_map/attend/pallas_call | solution.py:271
  76.5 0.0 collective-permute-done.13.refs_3_
  76.5 2.5 %attend.11 = (f32[4,256,128]{2,1,0:T(8,128)S(1)}, f32[4,256,256]{2,1,0:T(8,128)S(1)}) custom-call(s32[32]{0:T(128)S(1)} %copy-done.5, s32[1]{0:T(128)} %bitcast.refs_1_, bf16[4,256,128]{2,1,0:T(8,128)(2,1)S(1)} %queries.1.refs_2_, bf16[2,256,256]{2,1,0:T(8,128)(2,1)S(1)} %collective-permute-done.13.refs_3_, ...), custom_call_target="tpu_custom_call" | custom-call | flops 131072 | bytes 65536 | tf_op jit(solution)/shard_map/attend/pallas_call | solution.py:271
  79.0 0.0 collective-permute-done.11
  79.1 0.0 collective-permute-done.10
  79.1 0.0 copy-start.2
  79.1 0.1 collective-permute-start.15
  79.2 2.5 %attend.12 = (f32[4,256,128]{2,1,0:T(8,128)S(1)}, f32[4,256,256]{2,1,0:T(8,128)S(1)}) custom-call(s32[32]{0:T(128)S(1)} %copy-done.5, s32[1]{0:T(128)} %bitcast.refs_1_, bf16[4,256,128]{2,1,0:T(8,128)(2,1)S(1)} %queries.1.refs_2_, bf16[4,256,256]{2,1,0:T(8,128)(2,1)S(1)} %constant_dynamic-update-slice_fusion.refs_3_, ...), custom_call_target="tpu_custom_call" | custom-call | flops 131072 | bytes 65536 | tf_op jit(solution)/shard_map/attend/pallas_call | solution.py:271
  81.8 2.7 %attend.13 = bf16[256,768]{1,0:T(8,128)(2,1)S(1)} custom-call(s32[32]{0:T(128)S(1)} %copy-done.5, s32[1]{0:T(128)} %bitcast.refs_1_, bf16[4,256,128]{2,1,0:T(8,128)(2,1)S(1)} %queries.1.refs_2_, bf16[4,256,256]{2,1,0:T(8,128)(2,1)S(1)} %collective-permute-done.15.refs_3_, f32[4,256,128]{2,1,0:T(8,128)S(1)} %get-tuple-element.85.refs_4_, ...), custom_call_target="tpu_custom_call" | custom-call | flops 131072 | bytes 65536 | tf_op jit(solution)/shard_map/attend/pallas_call | solution.py:271
  84.5 13.8 %all_to_all.16.parts = bf16[8,32,768]{2,1,0:T(8,128)(2,1)S(1)} all-to-all(bf16[8,32,768]{2,1,0:T(8,128)(2,1)S(1)} %bitcast.17), channel_id=1, replica_groups=mesh['blk'=32,'head'=8] {'head'}, dimensions={0} | all-to-all | bytes 786432 | tf_op jit(solution)/shard_map/all_to_all | solution.py:408
  98.3 0.7 total.1
  (24 shorter events, 0.1 us)
Async XLA Ops:
  5.8 16.8 %copy-start = (bf16[1,16,16,768]{3,2,1,0:T(8,128)(2,1)S(1)}, bf16[1,16,16,768]{3,2,1,0:T(8,128)(2,1)}, u32[]{:S(2)}) copy-start(bf16[1,16,16,768]{3,2,1,0:T(8,128)(2,1)} %param.15) | copy-start | bytes 1179652
  5.8 16.8 %copy-start.8 = (f32[768]{0:T(1024)S(1)}, f32[768]{0:T(1024)}, u32[]{:S(2)}) copy-start(f32[768]{0:T(1024)} %param.25) | copy-start | bytes 9220
  5.8 16.7 %all-to-all-start = ((bf16[8,32,768]{2,1,0:T(8,128)(2,1)}), bf16[8,32,768]{2,1,0:T(8,128)(2,1)S(1)}, u32[]{:S(2)}, u32[]{:S(2)}) async-start(bf16[8,32,768]{2,1,0:T(8,128)(2,1)} %bitcast.6), calls=%async_computation | async-start | bytes 786432 | tf_op jit(solution)/shard_map/all_to_all | solution.py:346
  22.5 0.7 copy-start.7
  22.5 0.7 copy-start.6
  23.2 13.0 %copy-start.3 = (bf16[768,128]{1,0:T(8,128)(2,1)S(1)}, bf16[768,128]{1,0:T(8,128)(2,1)}, u32[]{:S(2)}) copy-start(bf16[768,128]{1,0:T(8,128)(2,1)} %wk.1) | copy-start | bytes 589828
  23.2 13.0 %copy-start.4 = (bf16[768,128]{1,0:T(8,128)(2,1)S(1)}, bf16[768,128]{1,0:T(8,128)(2,1)}, u32[]{:S(2)}) copy-start(bf16[768,128]{1,0:T(8,128)(2,1)} %wv.1) | copy-start | bytes 589828
  23.5 13.3 %copy-start.1 = (bf16[768,512]{1,0:T(8,128)(2,1)S(1)}, bf16[768,512]{1,0:T(8,128)(2,1)}, u32[]{:S(2)}) copy-start(bf16[768,512]{1,0:T(8,128)(2,1)} %wq.1) | copy-start | bytes 2359300
  36.6 1.4 %collective-permute-start = (bf16[1,256,256]{2,1,0:T(8,128)(2,1)S(1)}, bf16[1,256,256]{2,1,0:T(8,128)(2,1)S(1)}, u32[]{:S(2)}, u32[]{:S(2)}) collective-permute-start(bf16[1,256,256]{2,1,0:T(8,128)(2,1)S(1)} %key_values.1), channel_id=1, source_target_pairs={{0,8},{8,0},{16,24},{24,16},{32,40},{40,32},{48,56},{56,48},{64,72... | collective-permute-start | bytes 393224 | tf_op jit(solution)/shard_map/ppermute | solution.py:326
  38.1 8.4 %collective-permute-start.2 = (bf16[2,256,256]{2,1,0:T(8,128)(2,1)S(1)}, bf16[2,256,256]{2,1,0:T(8,128)(2,1)S(1)}, u32[]{:S(2)}, u32[]{:S(2)}) collective-permute-start(bf16[2,256,256]{2,1,0:T(8,128)(2,1)S(1)} %pad_maximum_fusion.refs_3_), channel_id=1, source_target_pairs={{0,128},{8,136},{16,144},{24,152},{32,160},{40,168},{48,176},{56,1... | collective-permute-start | bytes 786440 | tf_op jit(solution)/shard_map/ppermute | solution.py:326
  38.9 7.7 %collective-permute-start.1 = (bf16[2,256,256]{2,1,0:T(8,128)(2,1)S(1)}, bf16[2,256,256]{2,1,0:T(8,128)(2,1)S(1)}, u32[]{:S(2)}, u32[]{:S(2)}) collective-permute-start(bf16[2,256,256]{2,1,0:T(8,128)(2,1)S(1)} %pad_maximum_fusion.refs_3_), channel_id=1, source_target_pairs={{0,16},{8,120},{16,32},{24,8},{32,48},{40,24},{48,64},{56,40},{64,... | collective-permute-start | bytes 786440 | tf_op jit(solution)/shard_map/ppermute | solution.py:326
  40.8 0.7 copy-start.5
  46.6 5.1 %collective-permute-start.5 = (bf16[2,256,256]{2,1,0:T(8,128)(2,1)S(1)}, bf16[2,256,256]{2,1,0:T(8,128)(2,1)S(1)}, u32[]{:S(2)}, u32[]{:S(2)}) collective-permute-start(bf16[2,256,256]{2,1,0:T(8,128)(2,1)S(1)} %collective-permute-done.1.refs_4_), channel_id=1, source_target_pairs={{0,8},{8,0},{16,24},{24,16},{32,40},{40,32},{48,56},{56,48},{64,72... | collective-permute-start | bytes 786440 | tf_op jit(solution)/shard_map/ppermute | solution.py:326
  46.6 8.7 %collective-permute-start.4 = (bf16[2,256,256]{2,1,0:T(8,128)(2,1)S(1)}, bf16[2,256,256]{2,1,0:T(8,128)(2,1)S(1)}, u32[]{:S(2)}, u32[]{:S(2)}) collective-permute-start(bf16[2,256,256]{2,1,0:T(8,128)(2,1)S(1)} %collective-permute-done.1.refs_4_), channel_id=1, source_target_pairs={{0,128},{8,136},{16,144},{24,152},{32,160},{40,168},{48,176},{56,1... | collective-permute-start | bytes 786440 | tf_op jit(solution)/shard_map/ppermute | solution.py:326
  47.2 8.0 %collective-permute-start.3 = (bf16[2,256,256]{2,1,0:T(8,128)(2,1)S(1)}, bf16[2,256,256]{2,1,0:T(8,128)(2,1)S(1)}, u32[]{:S(2)}, u32[]{:S(2)}) collective-permute-start(bf16[2,256,256]{2,1,0:T(8,128)(2,1)S(1)} %collective-permute-done.1.refs_4_), channel_id=1, source_target_pairs={{0,16},{8,120},{16,32},{24,8},{32,48},{40,24},{48,64},{56,40},{64,... | collective-permute-start | bytes 786440 | tf_op jit(solution)/shard_map/ppermute | solution.py:326
  55.3 6.3 %collective-permute-start.9 = (bf16[2,256,256]{2,1,0:T(8,128)(2,1)S(1)}, bf16[2,256,256]{2,1,0:T(8,128)(2,1)S(1)}, u32[]{:S(2)}, u32[]{:S(2)}) collective-permute-start(bf16[2,256,256]{2,1,0:T(8,128)(2,1)S(1)} %collective-permute-done.4.refs_4_), channel_id=1, source_target_pairs={{0,8},{8,0},{16,24},{24,16},{32,40},{40,32},{48,56},{56,48},{64,72... | collective-permute-start | bytes 786440 | tf_op jit(solution)/shard_map/ppermute | solution.py:326
  55.3 6.3 %collective-permute-start.8 = (bf16[2,256,256]{2,1,0:T(8,128)(2,1)S(1)}, bf16[2,256,256]{2,1,0:T(8,128)(2,1)S(1)}, u32[]{:S(2)}, u32[]{:S(2)}) collective-permute-start(bf16[2,256,256]{2,1,0:T(8,128)(2,1)S(1)} %collective-permute-done.3.refs_5_), channel_id=1, source_target_pairs={{0,8},{8,0},{16,24},{24,16},{32,40},{40,32},{48,56},{56,48},{64,72... | collective-permute-start | bytes 786440 | tf_op jit(solution)/shard_map/ppermute | solution.py:326
  55.8 8.2 %collective-permute-start.7 = (bf16[2,256,256]{2,1,0:T(8,128)(2,1)S(1)}, bf16[2,256,256]{2,1,0:T(8,128)(2,1)S(1)}, u32[]{:S(2)}, u32[]{:S(2)}) collective-permute-start(bf16[2,256,256]{2,1,0:T(8,128)(2,1)S(1)} %collective-permute-done.3.refs_5_), channel_id=1, source_target_pairs={{0,128},{8,136},{16,144},{24,152},{32,160},{40,168},{48,176},{56,1... | collective-permute-start | bytes 786440 | tf_op jit(solution)/shard_map/ppermute | solution.py:326
  56.5 7.7 %collective-permute-start.6 = (bf16[2,256,256]{2,1,0:T(8,128)(2,1)S(1)}, bf16[2,256,256]{2,1,0:T(8,128)(2,1)S(1)}, u32[]{:S(2)}, u32[]{:S(2)}) collective-permute-start(bf16[2,256,256]{2,1,0:T(8,128)(2,1)S(1)} %collective-permute-done.3.refs_5_), channel_id=1, source_target_pairs={{0,16},{8,120},{16,32},{24,8},{32,48},{40,24},{48,64},{56,40},{64,... | collective-permute-start | bytes 786440 | tf_op jit(solution)/shard_map/ppermute | solution.py:326
  64.1 12.4 %collective-permute-start.14 = (bf16[2,256,256]{2,1,0:T(8,128)(2,1)S(1)}, bf16[2,256,256]{2,1,0:T(8,128)(2,1)S(1)}, u32[]{:S(2)}, u32[]{:S(2)}) collective-permute-start(bf16[2,256,256]{2,1,0:T(8,128)(2,1)S(1)} %collective-permute-done.7.refs_5_), channel_id=1, source_target_pairs={{0,8},{8,0},{16,24},{24,16},{32,40},{40,32},{48,56},{56,48},{64,72... | collective-permute-start | bytes 786440 | tf_op jit(solution)/shard_map/ppermute | solution.py:326
  64.1 12.4 %collective-permute-start.13 = (bf16[2,256,256]{2,1,0:T(8,128)(2,1)S(1)}, bf16[2,256,256]{2,1,0:T(8,128)(2,1)S(1)}, u32[]{:S(2)}, u32[]{:S(2)}) collective-permute-start(bf16[2,256,256]{2,1,0:T(8,128)(2,1)S(1)} %collective-permute-done.6.refs_6_), channel_id=1, source_target_pairs={{0,8},{8,0},{16,24},{24,16},{32,40},{40,32},{48,56},{56,48},{64,72... | collective-permute-start | bytes 786440 | tf_op jit(solution)/shard_map/ppermute | solution.py:326
  64.6 14.4 %collective-permute-start.10 = (bf16[2,256,256]{2,1,0:T(8,128)(2,1)S(1)}, bf16[2,256,256]{2,1,0:T(8,128)(2,1)S(1)}, u32[]{:S(2)}, u32[]{:S(2)}) collective-permute-start(bf16[2,256,256]{2,1,0:T(8,128)(2,1)S(1)} %collective-permute-done.6.refs_6_), channel_id=1, source_target_pairs={{0,128},{8,136},{16,144},{24,152},{32,160},{40,168},{48,176},{56,1... | collective-permute-start | bytes 786440 | tf_op jit(solution)/shard_map/ppermute | solution.py:326
  65.5 13.5 %collective-permute-start.11 = (bf16[1,256,256]{2,1,0:T(8,128)(2,1)S(1)}, bf16[1,256,256]{2,1,0:T(8,128)(2,1)S(1)}, u32[]{:S(2)}, u32[]{:S(2)}) collective-permute-start(bf16[1,256,256]{2,1,0:T(8,128)(2,1)S(1)} %slice.6), channel_id=1, source_target_pairs={{0,16},{8,120},{16,32},{24,8},{32,48},{40,24},{48,64},{56,40},{64,... | collective-permute-start | bytes 393224 | tf_op jit(solution)/shard_map/ppermute | solution.py:326
  67.2 11.8 %collective-permute-start.12 = (bf16[1,256,256]{2,1,0:T(8,128)(2,1)S(1)}, bf16[1,256,256]{2,1,0:T(8,128)(2,1)S(1)}, u32[]{:S(2)}, u32[]{:S(2)}) collective-permute-start(bf16[1,256,256]{2,1,0:T(8,128)(2,1)S(1)} %slice.7), channel_id=1, source_target_pairs={{0,32},{8,104},{16,48},{24,120},{32,64},{40,8},{48,80},{56,24},{64... | collective-permute-start | bytes 393224 | tf_op jit(solution)/shard_map/ppermute | solution.py:326
  79.1 2.7 %copy-start.2 = (bf16[512,768]{1,0:T(8,128)(2,1)S(1)}, bf16[512,768]{1,0:T(8,128)(2,1)}, u32[]{:S(2)}) copy-start(bf16[512,768]{1,0:T(8,128)(2,1)} %refs_6_.1) | copy-start | bytes 2359300
  79.1 2.6 %collective-permute-start.15 = (bf16[4,256,256]{2,1,0:T(8,128)(2,1)S(1)}, bf16[4,256,256]{2,1,0:T(8,128)(2,1)S(1)}, u32[]{:S(2)}, u32[]{:S(2)}) collective-permute-start(bf16[4,256,256]{2,1,0:T(8,128)(2,1)S(1)} %constant_dynamic-update-slice_fusion.refs_3_), channel_id=1, source_target_pairs={{0,8},{8,0},{16,24},{24,16},{32,40},{40,32},{48,56},{56,48},{64,72... | collective-permute-start | bytes 1572872 | tf_op jit(solution)/shard_map/ppermute | solution.py:326

commit v5 on v4

--- a/solution.py
+++ b/solution.py
@@ -121,8 +121,10 @@
     )(*[fixed(operand) for operand in operands])
 
 
-def block_kernel(place, parts, pages, scale, b2, gain, out):
+def block_kernel(place, parts, pages, packed, out):
     count, chunk, channels = parts.shape
+    pieces = channels // LANES
+    scale, b2 = packed[0:pieces, :], packed[pieces : 2 * pieces, :]
     start = pl.multiple_of(place[0] * chunk, chunk)
     block = []
     for index in range(channels // LANES):
@@ -131,7 +133,7 @@
         total = functools.reduce(jnp.add, [parts[part, :, lanes].astype(F32) for part in range(count)])
         own = pages[pl.ds(start, chunk), lanes].astype(F32)
         block.append(own + scale[row, :] * (total + b2[row, :]))
-    normed = jnp.concatenate(normalise(block, gain, 1e-05), axis=1)
+    normed = jnp.concatenate(normalise(block, packed.at[2 * pieces : 3 * pieces, :], 1e-05), axis=1)
     for part in range(count):
         out[part] = normed
 
@@ -140,11 +142,11 @@
     return pl.pallas_call(
         block_kernel,
         out_shape=jax.ShapeDtypeStruct(parts.shape, BF),
-        in_specs=[smem_spec()] + [vmem_spec()] * 5,
+        in_specs=[smem_spec()] + [vmem_spec()] * 3,
         out_specs=vmem_spec(),
         compiler_params=params(8),
         name="block_norm",
-    )(place, parts, pages, lane_rows(scale), lane_rows(b2), lane_rows(gain))
+    )(place, parts, pages, jnp.concatenate([lane_rows(scale), lane_rows(b2), lane_rows(gain)]))
 
 
 def kv_kernel(normed, wk, wv, out):
@@ -165,22 +167,22 @@
     )(normed, wk, wv)
 
 
-def query_kernel(normed, wq, out):
+def query_kernel(_, normed, wq, out):
     product = jnp.dot(normed[...], wq[...], preferred_element_type=F32) * (HD**-0.5 * LOG2E)
     for head in range(out.shape[0]):
         out[head] = product[:, head * HD : (head + 1) * HD].astype(BF)
 
 
-def queries_of(normed, wq):
+def queries_of(valid_counts, normed, wq):
     rows = normed.shape[0]
     return pl.pallas_call(
         query_kernel,
         out_shape=jax.ShapeDtypeStruct((wq.shape[1] // HD, rows, HD), BF),
-        in_specs=[vmem_spec()] * 2,
+        in_specs=[smem_spec()] + [vmem_spec()] * 2,
         out_specs=vmem_spec(),
         compiler_params=params(8),
         name="queries",
-    )(normed, wq)
+    )(valid_counts, normed, wq)
 
 
 def attend_kernel(first, last, places, depth, sizes, *refs):
@@ -226,23 +228,25 @@
                 for key, mask in zip(keys, masks)
             ]
             largest = functools.reduce(jnp.maximum, scores)
-            top = jnp.max(largest, axis=1, keepdims=True)
+            top = jnp.broadcast_to(jnp.max(largest, axis=1, keepdims=True), (rows, HD))
             if not fresh:
                 source_top, source_sums = (top_in, sums_in) if begin == 0 else (top_out, sums_out)
-                before = source_top[head][:, 0:1]
+                before = source_top[head]
                 top = jnp.maximum(top, before)
-                carried = source_sums[head] * jnp.exp2(before - top)
+                factor = jnp.exp2(before - top)
+                carried = source_sums[head] * jnp.concatenate([factor, factor], axis=1)
+            wide_top = jnp.concatenate([top] * (tokens // HD), axis=1)
             total = functools.reduce(
                 jnp.add,
                 [
-                    jnp.dot(jnp.exp2(score - top).astype(BF), value, preferred_element_type=F32)
+                    jnp.dot(jnp.exp2(score - wide_top).astype(BF), value, preferred_element_type=F32)
                     for score, value in zip(scores, values)
                 ],
             )
             if not fresh:
                 total = total + carried
             sums_out[head] = total
-            top_out[head] = jnp.broadcast_to(top, (rows, HD))
+            top_out[head] = top
         fresh = False
     if last:
         attended = jnp.concatenate(
@@ -358,53 +362,63 @@
 
     start = key_values(normed, w_key, w_value)
     beside = flip_core(start)
-    query = queries_of(normed, w_query)
+    other = flip_y(start)
+    query = queries_of(valid_counts, normed, w_query)
     beside, query = hold((beside, query))
     own_pair = jnp.concatenate([start, beside])
 
     first = along_z(own_pair)
-    own_other = flip_y(own_pair)
     carry = fold([(own_pair, mine(0, 0))])
-    first, own_other, carry = hold((first, own_other, carry))
-
-    second = along_z(first)
-    first_other = flip_y(first)
+    first, other, carry = hold((first, other, carry))
+
+    second = along_z(jnp.concatenate([first, other]))
+    first_other = flip_y(first[1:2])
+    other_core = flip_core(other)
     first_core = flip_core(first)
-    carry = fold([(own_other, mine(1, 0)), (first, mine(0, 1))], carry)
-    second, first_other, first_core, carry = hold((second, first_other, first_core, carry))
+    carry = fold([(other, [(1, 0, 0)]), (first, mine(0, 1))], carry)
+    second, first_other, other_core, first_core, carry = hold((second, first_other, other_core, first_core, carry))
 
     third = along_z(second)
-    second_other = flip_y(second)
+    second_other = flip_y(second[1:2])
     second_core = flip_core(second)
     first_other_core = flip_core(first_other)
-    carry = fold([(first_core, theirs(0, 1)), (first_other, mine(1, 1)), (second, mine(0, 2))], carry)
+    carry = fold(
+        [
+            (other_core, [(1, 0, 1)]),
+            (first_core, theirs(0, 1)),
+            (first_other, [(1, 1, 1)]),
+            (second, mine(0, 2) + [(1, 1, 0)]),
+        ],
+        carry,
+    )
     third, second_other, second_core, first_other_core, carry = hold(
         (third, second_other, second_core, first_other_core, carry)
     )
 
-    third_other = flip_y(third)
-    far = along_z(third[0:1])
-    far_other = along_z(second_other[0:1], 2)
+    fourth = along_z(third[1:3])
+    third_other = flip_y(third[1:2])
+    far_other = along_z(third[2:3], 2)
     third_core = flip_core(third)
     second_other_core = flip_core(second_other)
     carry = fold(
         [
-            (first_other_core, theirs(1, 1)),
-            (second_core, theirs(0, 2)),
-            (second_other, mine(1, 2)),
-            (third, mine(0, 3)),
+            (second_core, theirs(0, 2) + [(1, -1, 1)]),
+            (first_other_core, [(1, -1, 0)]),
+            (second_other, [(1, 2, 1)]),
+            (third, mine(0, 3) + [(1, 2, 0)]),
         ],
         carry,
     )
     third_core, second_other_core, carry = hold((third_core, second_other_core, carry))
-    carry = fold([(third_core, theirs(0, 3)), (second_other_core, theirs(1, 2))], carry)
-    third_other, far, far_other, carry = hold((third_other, far, far_other, carry))
-
-    last = jnp.concatenate([third_other, far, far_other])
+    carry = fold([(third_core, theirs(0, 3) + [(1, -2, 1)]), (second_other_core, [(1, -2, 0)])], carry)
+    fourth, third_other, far_other, carry = hold((fourth, third_other, far_other, carry))
+
+    half = depth // 2
+    last = jnp.concatenate([fourth, third_other, far_other])
     last_core = flip_core(last)
-    carry = fold([(last, mine(1, 3) + [(0, depth // 2, 0), (1, depth // 2, 0)])], carry)
+    carry = fold([(last, [(0, half, 1), (1, 3, 0), (1, 3, 1), (1, half, 0)])], carry)
     last_core, carry = hold((last_core, carry))
-    (mixed,) = fold([(last_core, theirs(1, 3) + [(0, depth // 2, 1), (1, depth // 2, 1)])], carry, w_out)
+    (mixed,) = fold([(last_core, [(0, -half, 0), (1, -3, 1), (1, -3, 0), (1, -half, 1)])], carry, w_out)
     parts = lax.all_to_all(mixed.reshape(groups, share, channels), "head", 0, 0, tiled=True)
     return total_of(parts)
 

time: 99.3 us -> 97.3 us (0.980)
  waiting for transfers between devices: 20.4 us -> 17.1 us
  starting transfers between devices: 24 us -> 25.8 us
    ppermute x16 -> x17, waiting for transfers between devices: 10.7 us -> 8.19 us  [moved(): return lax.ppermute(array, 'blk', [(i, target(i)) for i in range(blocks)])]
    ppermute x16 -> x17, starting transfers between devices: 16.9 us -> 18.7 us  [moved(): return lax.ppermute(array, 'blk', [(i, target(i)) for i in range(blocks)])]
  transfers between devices with their start and end apart: 17 -> 18, of which waited for: 6 -> 7; matrix products, arithmetic and copies ran while one was open for 0% -> 0% of each run, Pallas kernels for 17% -> 17%
where the time goes in v5:
time: 97.3 us; the launch traced here: 97 us
  blocking collectives  26.8 us (28%)
  Pallas kernels  26 us (27%)
  starting transfers between devices  25.8 us (27%)
  waiting for transfers between devices  17.1 us (18%)
  local copies, waits for them, and re-layouts  1.01 us (1%)
    ppermute x17, starting transfers between devices, moved(): return lax.ppermute(array, 'blk', [(i, target(i)) for i in range(blocks)])  18.7 us
    pallas_call x7, Pallas kernels, attend(): pl.pallas_call(functools.partial(attend_kernel, carry is None, w_out is n...  18.1 us
    all_to_all x1, blocking collectives, per_device(): lax.all_to_all(mixed.reshape(groups, share, channels), 'head', 0, 0, tile...  14 us
    all_to_all x1, blocking collectives, per_device(): lax.all_to_all(copies, 'head', 0, 0, tiled=True).reshape(rows, channels)  12.8 us
    all_to_all x1, waiting for transfers between devices, per_device(): lax.all_to_all(partial.reshape(groups, share, channels), 'head', 0, 0, ti...  8.93 us
    ppermute x17, waiting for transfers between devices, moved(): return lax.ppermute(array, 'blk', [(i, target(i)) for i in range(blocks)])  8.19 us
    all_to_all x1, starting transfers between devices, per_device(): lax.all_to_all(partial.reshape(groups, share, channels), 'head', 0, 0, ti...  7.07 us
    pallas_call x1, Pallas kernels, mlp(): pl.pallas_call(mlp_kernel, out_shape=jax.ShapeDtypeStruct((rows, channels...  5.74 us
  transfers between devices with their start and end apart: 18, of which 7 were waited for; matrix products, arithmetic and copies ran while one was open for 0% of the time, Pallas kernels for 17%

profile of v5, /device:TPU:32, one launch (start us, length us, event | category | flops | bytes accessed | tf_op | source)
XLA Modules:
  0.0 97.0 jit_solution(3934871118982914931)
XLA Ops:
  0.0 5.7 %conv_mlp.1 = bf16[256,768]{1,0:T(8,128)(2,1)} custom-call(bf16[16,16,768]{2,1,0:T(8,128)(2,1)} %bitcast.15, f32[7,7,768]{2,1,0:T(8,128)} %dw_hbm.1, f32[6,128]{1,0:T(8,128)} %bitcast.18, f32[6,128]{1,0:T(8,128)} %bitcast.19, bf16[768,384]{1,0:T(8,128)(2,1)} %w1_hbm.1, f32[3,128]{1,0:T(4,128)} %bitcast.23, bf16[384,768]{1,0:T(8,128)(2,1)} %w2_hbm.1), custom_call_target="tpu_custom_call" | custom-call | tf_op jit(solution)/shard_map/conv_mlp/pallas_call | solution.py:108
  5.8 0.0 copy-start.8
  5.8 0.0 copy-start
  5.8 7.1 %all-to-all-start = ((bf16[8,32,768]{2,1,0:T(8,128)(2,1)}), bf16[8,32,768]{2,1,0:T(8,128)(2,1)S(1)}, u32[]{:S(2)}, u32[]{:S(2)}) async-start(bf16[8,32,768]{2,1,0:T(8,128)(2,1)} %bitcast.6), calls=%async_computation | async-start | bytes 786432 | tf_op jit(solution)/shard_map/all_to_all | solution.py:350
  12.9 0.0 copy-start.6
  12.9 0.7 copy-done.7
  13.5 0.0 copy-done.6
  13.6 8.9 %all-to-all-done.parts = bf16[8,32,768]{2,1,0:T(8,128)(2,1)S(1)} async-done(((bf16[8,32,768]{2,1,0:T(8,128)(2,1)}), bf16[8,32,768]{2,1,0:T(8,128)(2,1)S(1)}, u32[]{:S(2)}, u32[]{:S(2)}) %all-to-all-start) | async-done | bytes 393248 | tf_op jit(solution)/shard_map/all_to_all | solution.py:350
  22.5 0.2 block_norm.1
  22.8 0.0 copy-start.1
  22.8 12.8 %all_to_all.15 = bf16[8,32,768]{2,1,0:T(8,128)(2,1)S(1)} all-to-all(bf16[8,32,768]{2,1,0:T(8,128)(2,1)S(1)} %block_norm.1), channel_id=1, replica_groups=mesh['blk'=32,'head'=8] {'head'}, dimensions={0} | all-to-all | bytes 786432 | tf_op jit(solution)/shard_map/all_to_all | solution.py:352
  35.6 0.4 key_values.1
  35.9 0.1 collective-permute-start
  36.0 0.2 copy-done.5
  36.2 0.9 queries.1.refs_2_
  37.1 0.2 collective-permute-done
  37.4 2.0 %collective-permute-start.1 = (bf16[2,256,256]{2,1,0:T(8,128)(2,1)S(1)}, bf16[2,256,256]{2,1,0:T(8,128)(2,1)S(1)}, u32[]{:S(2)}, u32[]{:S(2)}) collective-permute-start(bf16[2,256,256]{2,1,0:T(8,128)(2,1)S(1)} %pad_maximum_fusion.1.refs_3_), channel_id=1, source_target_pairs={{0,16},{8,120},{16,32},{24,8},{32,48},{40,24},{48,64},{56,40},{64,... | collective-permute-start | bytes 786440 | tf_op jit(solution)/shard_map/ppermute | solution.py:330
  39.4 0.7 collective-permute-start.2
  40.1 1.5 %attend.7 = (f32[4,256,128]{2,1,0:T(8,128)S(1)}, f32[4,256,256]{2,1,0:T(8,128)S(1)}) custom-call(s32[32]{0:T(128)S(1)} %copy-done.5, s32[1]{0:T(128)} %bitcast.refs_1_, bf16[4,256,128]{2,1,0:T(8,128)(2,1)S(1)} %queries.1.refs_2_, bf16[2,256,256]{2,1,0:T(8,128)(2,1)S(1)} %pad_maximum_fusion.1.refs_3_), custom_call_target="tpu_custom_call" | custom-call | flops 65536 | bytes 65536 | tf_op jit(solution)/shard_map/attend/pallas_call | solution.py:275
  41.6 2.8 %collective-permute-done.2.refs_3_ = bf16[1,256,256]{2,1,0:T(8,128)(2,1)S(1)} collective-permute-done((bf16[1,256,256]{2,1,0:T(8,128)(2,1)S(1)}, bf16[1,256,256]{2,1,0:T(8,128)(2,1)S(1)}, u32[]{:S(2)}, u32[]{:S(2)}) %collective-permute-start.2) | collective-permute-done | bytes 131104 | tf_op jit(solution)/shard_map/ppermute | solution.py:330
  44.4 2.0 %collective-permute-start.3 = (bf16[3,256,256]{2,1,0:T(8,128)(2,1)S(1)}, bf16[3,256,256]{2,1,0:T(8,128)(2,1)S(1)}, u32[]{:S(2)}, u32[]{:S(2)}) collective-permute-start(bf16[3,256,256]{2,1,0:T(8,128)(2,1)S(1)} %pad_maximum_fusion), channel_id=1, source_target_pairs={{0,16},{8,120},{16,32},{24,8},{32,48},{40,24},{48,64},{56,40},{64,... | collective-permute-start | bytes 1179656 | tf_op jit(solution)/shard_map/ppermute | solution.py:330
  46.4 0.9 collective-permute-start.6
  47.3 0.8 collective-permute-start.4
  48.0 1.9 %attend.8 = (f32[4,256,128]{2,1,0:T(8,128)S(1)}, f32[4,256,256]{2,1,0:T(8,128)S(1)}) custom-call(s32[32]{0:T(128)S(1)} %copy-done.5, s32[1]{0:T(128)} %bitcast.refs_1_, bf16[4,256,128]{2,1,0:T(8,128)(2,1)S(1)} %queries.1.refs_2_, bf16[1,256,256]{2,1,0:T(8,128)(2,1)S(1)} %collective-permute-done.2.refs_3_, ...), custom_call_target="tpu_custom_call" | custom-call | flops 98304 | bytes 65536 | tf_op jit(solution)/shard_map/attend/pallas_call | solution.py:275
  50.0 2.8 %collective-permute-done.4.refs_5_ = bf16[1,256,256]{2,1,0:T(8,128)(2,1)S(1)} collective-permute-done((bf16[1,256,256]{2,1,0:T(8,128)(2,1)S(1)}, bf16[1,256,256]{2,1,0:T(8,128)(2,1)S(1)}, u32[]{:S(2)}, u32[]{:S(2)}) %collective-permute-start.4) | collective-permute-done | bytes 131104 | tf_op jit(solution)/shard_map/ppermute | solution.py:330
  52.8 0.0 collective-permute-done.5.refs_3_
  52.8 0.0 collective-permute-done.6.refs_4_
  52.8 0.9 collective-permute-done.3.refs_6_
  53.7 0.0 collective-permute-start.9
  53.7 2.2 %collective-permute-start.7 = (bf16[3,256,256]{2,1,0:T(8,128)(2,1)S(1)}, bf16[3,256,256]{2,1,0:T(8,128)(2,1)S(1)}, u32[]{:S(2)}, u32[]{:S(2)}) collective-permute-start(bf16[3,256,256]{2,1,0:T(8,128)(2,1)S(1)} %collective-permute-done.3.refs_6_), channel_id=1, source_target_pairs={{0,16},{8,120},{16,32},{24,8},{32,48},{40,24},{48,64},{56,40},{64,... | collective-permute-start | bytes 1179656 | tf_op jit(solution)/shard_map/ppermute | solution.py:330
  55.9 0.8 collective-permute-start.8
  56.7 0.9 collective-permute-start.10
  57.6 3.5 %attend.9 = (f32[4,256,128]{2,1,0:T(8,128)S(1)}, f32[4,256,256]{2,1,0:T(8,128)S(1)}) custom-call(s32[32]{0:T(128)S(1)} %copy-done.5, s32[1]{0:T(128)} %bitcast.refs_1_, bf16[4,256,128]{2,1,0:T(8,128)(2,1)S(1)} %queries.1.refs_2_, bf16[1,256,256]{2,1,0:T(8,128)(2,1)S(1)} %collective-permute-done.5.refs_3_, ...), custom_call_target="tpu_custom_call" | custom-call | flops 229376 | bytes 65536 | tf_op jit(solution)/shard_map/attend/pallas_call | solution.py:275
  61.1 1.0 %collective-permute-done.8.refs_5_ = bf16[1,256,256]{2,1,0:T(8,128)(2,1)S(1)} collective-permute-done((bf16[1,256,256]{2,1,0:T(8,128)(2,1)S(1)}, bf16[1,256,256]{2,1,0:T(8,128)(2,1)S(1)}, u32[]{:S(2)}, u32[]{:S(2)}) %collective-permute-start.8) | collective-permute-done | bytes 131104 | tf_op jit(solution)/shard_map/ppermute | solution.py:330
  62.1 0.0 collective-permute-done.10.refs_4_
  62.1 0.5 collective-permute-done.7.refs_6_
  62.7 0.6 collective-permute-start.15
  63.3 1.2 %collective-permute-start.11 = (bf16[2,256,256]{2,1,0:T(8,128)(2,1)S(1)}, bf16[2,256,256]{2,1,0:T(8,128)(2,1)S(1)}, u32[]{:S(2)}, u32[]{:S(2)}) collective-permute-start(bf16[2,256,256]{2,1,0:T(8,128)(2,1)S(1)} %slice.17), channel_id=1, source_target_pairs={{0,16},{8,120},{16,32},{24,8},{32,48},{40,24},{48,64},{56,40},{64,... | collective-permute-start | bytes 786440 | tf_op jit(solution)/shard_map/ppermute | solution.py:330
  64.5 5.8 %collective-permute-start.13 = (bf16[1,256,256]{2,1,0:T(8,128)(2,1)S(1)}, bf16[1,256,256]{2,1,0:T(8,128)(2,1)S(1)}, u32[]{:S(2)}, u32[]{:S(2)}) collective-permute-start(bf16[1,256,256]{2,1,0:T(8,128)(2,1)S(1)} %get-tuple-element.89), channel_id=1, source_target_pairs={{0,32},{8,104},{16,48},{24,120},{32,64},{40,8},{48,80},{56,24},{64... | collective-permute-start | bytes 393224 | tf_op jit(solution)/shard_map/ppermute | solution.py:330
  70.3 0.7 collective-permute-start.12
  70.9 3.8 %attend.10 = (f32[4,256,128]{2,1,0:T(8,128)S(1)}, f32[4,256,256]{2,1,0:T(8,128)S(1)}) custom-call(s32[32]{0:T(128)S(1)} %copy-done.5, s32[1]{0:T(128)} %bitcast.refs_1_, bf16[4,256,128]{2,1,0:T(8,128)(2,1)S(1)} %queries.1.refs_2_, bf16[3,256,256]{2,1,0:T(8,128)(2,1)S(1)} %collective-permute-done.9.refs_3_, ...), custom_call_target="tpu_custom_call" | custom-call | flops 262144 | bytes 65536 | tf_op jit(solution)/shard_map/attend/pallas_call | solution.py:275
  74.8 2.4 %attend.11 = (f32[4,256,128]{2,1,0:T(8,128)S(1)}, f32[4,256,256]{2,1,0:T(8,128)S(1)}) custom-call(s32[32]{0:T(128)S(1)} %copy-done.5, s32[1]{0:T(128)} %bitcast.refs_1_, bf16[4,256,128]{2,1,0:T(8,128)(2,1)S(1)} %queries.1.refs_2_, bf16[3,256,256]{2,1,0:T(8,128)(2,1)S(1)} %collective-permute-done.14.refs_3_, ...), custom_call_target="tpu_custom_call" | custom-call | flops 131072 | bytes 65536 | tf_op jit(solution)/shard_map/attend/pallas_call | solution.py:275
  77.3 0.0 copy-start.2
  77.3 0.1 collective-permute-start.16
  77.4 2.4 %attend.12 = (f32[4,256,128]{2,1,0:T(8,128)S(1)}, f32[4,256,256]{2,1,0:T(8,128)S(1)}) custom-call(s32[32]{0:T(128)S(1)} %copy-done.5, s32[1]{0:T(128)} %bitcast.refs_1_, bf16[4,256,128]{2,1,0:T(8,128)(2,1)S(1)} %queries.1.refs_2_, bf16[4,256,256]{2,1,0:T(8,128)(2,1)S(1)} %constant_dynamic-update-slice_fusion.refs_3_, ...), custom_call_target="tpu_custom_call" | custom-call | flops 131072 | bytes 65536 | tf_op jit(solution)/shard_map/attend/pallas_call | solution.py:275
  79.8 2.6 %attend.13 = bf16[256,768]{1,0:T(8,128)(2,1)S(1)} custom-call(s32[32]{0:T(128)S(1)} %copy-done.5, s32[1]{0:T(128)} %bitcast.refs_1_, bf16[4,256,128]{2,1,0:T(8,128)(2,1)S(1)} %queries.1.refs_2_, bf16[4,256,256]{2,1,0:T(8,128)(2,1)S(1)} %collective-permute-done.16.refs_3_, f32[4,256,128]{2,1,0:T(8,128)S(1)} %get-tuple-element.87.refs_4_, ...), custom_call_target="tpu_custom_call" | custom-call | flops 131072 | bytes 65536 | tf_op jit(solution)/shard_map/attend/pallas_call | solution.py:275
  82.3 14.0 %all_to_all.16.parts = bf16[8,32,768]{2,1,0:T(8,128)(2,1)S(1)} all-to-all(bf16[8,32,768]{2,1,0:T(8,128)(2,1)S(1)} %bitcast.17), channel_id=1, replica_groups=mesh['blk'=32,'head'=8] {'head'}, dimensions={0} | all-to-all | bytes 786432 | tf_op jit(solution)/shard_map/all_to_all | solution.py:422
  96.3 0.7 total.1
  (30 shorter events, 0.2 us)
Async XLA Ops:
  5.8 7.1 %copy-start.8 = (f32[768]{0:T(1024)S(1)}, f32[768]{0:T(1024)}, u32[]{:S(2)}) copy-start(f32[768]{0:T(1024)} %param.24) | copy-start | bytes 9220
  5.8 16.7 %copy-start = (bf16[1,16,16,768]{3,2,1,0:T(8,128)(2,1)S(1)}, bf16[1,16,16,768]{3,2,1,0:T(8,128)(2,1)}, u32[]{:S(2)}) copy-start(bf16[1,16,16,768]{3,2,1,0:T(8,128)(2,1)} %param.15) | copy-start | bytes 1179652
  5.8 16.7 %all-to-all-start = ((bf16[8,32,768]{2,1,0:T(8,128)(2,1)}), bf16[8,32,768]{2,1,0:T(8,128)(2,1)S(1)}, u32[]{:S(2)}, u32[]{:S(2)}) async-start(bf16[8,32,768]{2,1,0:T(8,128)(2,1)} %bitcast.6), calls=%async_computation | async-start | bytes 786432 | tf_op jit(solution)/shard_map/all_to_all | solution.py:350
  12.8 0.7 copy-start.7
  12.9 0.7 copy-start.6
  22.5 13.0 %copy-start.3 = (bf16[768,128]{1,0:T(8,128)(2,1)S(1)}, bf16[768,128]{1,0:T(8,128)(2,1)}, u32[]{:S(2)}) copy-start(bf16[768,128]{1,0:T(8,128)(2,1)} %wk.1) | copy-start | bytes 589828
  22.5 13.0 %copy-start.4 = (bf16[768,128]{1,0:T(8,128)(2,1)S(1)}, bf16[768,128]{1,0:T(8,128)(2,1)}, u32[]{:S(2)}) copy-start(bf16[768,128]{1,0:T(8,128)(2,1)} %wv.1) | copy-start | bytes 589828
  22.8 13.3 %copy-start.1 = (bf16[768,512]{1,0:T(8,128)(2,1)S(1)}, bf16[768,512]{1,0:T(8,128)(2,1)}, u32[]{:S(2)}) copy-start(bf16[768,512]{1,0:T(8,128)(2,1)} %wq.1) | copy-start | bytes 2359300
  35.6 0.7 copy-start.5
  35.9 1.4 %collective-permute-start = (bf16[1,256,256]{2,1,0:T(8,128)(2,1)S(1)}, bf16[1,256,256]{2,1,0:T(8,128)(2,1)S(1)}, u32[]{:S(2)}, u32[]{:S(2)}) collective-permute-start(bf16[1,256,256]{2,1,0:T(8,128)(2,1)S(1)} %key_values.1), channel_id=1, source_target_pairs={{0,8},{8,0},{16,24},{24,16},{32,40},{40,32},{48,56},{56,48},{64,72... | collective-permute-start | bytes 393224 | tf_op jit(solution)/shard_map/ppermute | solution.py:330
  37.4 7.0 %collective-permute-start.1 = (bf16[2,256,256]{2,1,0:T(8,128)(2,1)S(1)}, bf16[2,256,256]{2,1,0:T(8,128)(2,1)S(1)}, u32[]{:S(2)}, u32[]{:S(2)}) collective-permute-start(bf16[2,256,256]{2,1,0:T(8,128)(2,1)S(1)} %pad_maximum_fusion.1.refs_3_), channel_id=1, source_target_pairs={{0,16},{8,120},{16,32},{24,8},{32,48},{40,24},{48,64},{56,40},{64,... | collective-permute-start | bytes 786440 | tf_op jit(solution)/shard_map/ppermute | solution.py:330
  39.4 5.0 %collective-permute-start.2 = (bf16[1,256,256]{2,1,0:T(8,128)(2,1)S(1)}, bf16[1,256,256]{2,1,0:T(8,128)(2,1)S(1)}, u32[]{:S(2)}, u32[]{:S(2)}) collective-permute-start(bf16[1,256,256]{2,1,0:T(8,128)(2,1)S(1)} %key_values.1), channel_id=1, source_target_pairs={{0,128},{8,136},{16,144},{24,152},{32,160},{40,168},{48,176},{56,1... | collective-permute-start | bytes 393224 | tf_op jit(solution)/shard_map/ppermute | solution.py:330
  44.4 9.3 %collective-permute-start.3 = (bf16[3,256,256]{2,1,0:T(8,128)(2,1)S(1)}, bf16[3,256,256]{2,1,0:T(8,128)(2,1)S(1)}, u32[]{:S(2)}, u32[]{:S(2)}) collective-permute-start(bf16[3,256,256]{2,1,0:T(8,128)(2,1)S(1)} %pad_maximum_fusion), channel_id=1, source_target_pairs={{0,16},{8,120},{16,32},{24,8},{32,48},{40,24},{48,64},{56,40},{64,... | collective-permute-start | bytes 1179656 | tf_op jit(solution)/shard_map/ppermute | solution.py:330
  46.4 6.4 %collective-permute-start.6 = (bf16[2,256,256]{2,1,0:T(8,128)(2,1)S(1)}, bf16[2,256,256]{2,1,0:T(8,128)(2,1)S(1)}, u32[]{:S(2)}, u32[]{:S(2)}) collective-permute-start(bf16[2,256,256]{2,1,0:T(8,128)(2,1)S(1)} %collective-permute-done.1.refs_4_), channel_id=1, source_target_pairs={{0,8},{8,0},{16,24},{24,16},{32,40},{40,32},{48,56},{56,48},{64,72... | collective-permute-start | bytes 786440 | tf_op jit(solution)/shard_map/ppermute | solution.py:330
  47.3 5.5 %collective-permute-start.4 = (bf16[1,256,256]{2,1,0:T(8,128)(2,1)S(1)}, bf16[1,256,256]{2,1,0:T(8,128)(2,1)S(1)}, u32[]{:S(2)}, u32[]{:S(2)}) collective-permute-start(bf16[1,256,256]{2,1,0:T(8,128)(2,1)S(1)} %slice.15), channel_id=1, source_target_pairs={{0,128},{8,136},{16,144},{24,152},{32,160},{40,168},{48,176},{56,1... | collective-permute-start | bytes 393224 | tf_op jit(solution)/shard_map/ppermute | solution.py:330
  48.0 4.7 %collective-permute-start.5 = (bf16[1,256,256]{2,1,0:T(8,128)(2,1)S(1)}, bf16[1,256,256]{2,1,0:T(8,128)(2,1)S(1)}, u32[]{:S(2)}, u32[]{:S(2)}) collective-permute-start(bf16[1,256,256]{2,1,0:T(8,128)(2,1)S(1)} %collective-permute-done.2.refs_3_), channel_id=1, source_target_pairs={{0,8},{8,0},{16,24},{24,16},{32,40},{40,32},{48,56},{56,48},{64,72... | collective-permute-start | bytes 393224 | tf_op jit(solution)/shard_map/ppermute | solution.py:330
  53.7 8.5 %collective-permute-start.9 = (bf16[3,256,256]{2,1,0:T(8,128)(2,1)S(1)}, bf16[3,256,256]{2,1,0:T(8,128)(2,1)S(1)}, u32[]{:S(2)}, u32[]{:S(2)}) collective-permute-start(bf16[3,256,256]{2,1,0:T(8,128)(2,1)S(1)} %collective-permute-done.3.refs_6_), channel_id=1, source_target_pairs={{0,8},{8,0},{16,24},{24,16},{32,40},{40,32},{48,56},{56,48},{64,72... | collective-permute-start | bytes 1179656 | tf_op jit(solution)/shard_map/ppermute | solution.py:330
  53.7 9.0 %collective-permute-start.7 = (bf16[3,256,256]{2,1,0:T(8,128)(2,1)S(1)}, bf16[3,256,256]{2,1,0:T(8,128)(2,1)S(1)}, u32[]{:S(2)}, u32[]{:S(2)}) collective-permute-start(bf16[3,256,256]{2,1,0:T(8,128)(2,1)S(1)} %collective-permute-done.3.refs_6_), channel_id=1, source_target_pairs={{0,16},{8,120},{16,32},{24,8},{32,48},{40,24},{48,64},{56,40},{64,... | collective-permute-start | bytes 1179656 | tf_op jit(solution)/shard_map/ppermute | solution.py:330
  55.9 6.2 %collective-permute-start.8 = (bf16[1,256,256]{2,1,0:T(8,128)(2,1)S(1)}, bf16[1,256,256]{2,1,0:T(8,128)(2,1)S(1)}, u32[]{:S(2)}, u32[]{:S(2)}) collective-permute-start(bf16[1,256,256]{2,1,0:T(8,128)(2,1)S(1)} %slice.16), channel_id=1, source_target_pairs={{0,128},{8,136},{16,144},{24,152},{32,160},{40,168},{48,176},{56,1... | collective-permute-start | bytes 393224 | tf_op jit(solution)/shard_map/ppermute | solution.py:330
  56.7 5.4 %collective-permute-start.10 = (bf16[1,256,256]{2,1,0:T(8,128)(2,1)S(1)}, bf16[1,256,256]{2,1,0:T(8,128)(2,1)S(1)}, u32[]{:S(2)}, u32[]{:S(2)}) collective-permute-start(bf16[1,256,256]{2,1,0:T(8,128)(2,1)S(1)} %collective-permute-done.4.refs_5_), channel_id=1, source_target_pairs={{0,8},{8,0},{16,24},{24,16},{32,40},{40,32},{48,56},{56,48},{64,72... | collective-permute-start | bytes 393224 | tf_op jit(solution)/shard_map/ppermute | solution.py:330
  62.7 12.1 %collective-permute-start.14 = (bf16[3,256,256]{2,1,0:T(8,128)(2,1)S(1)}, bf16[3,256,256]{2,1,0:T(8,128)(2,1)S(1)}, u32[]{:S(2)}, u32[]{:S(2)}) collective-permute-start(bf16[3,256,256]{2,1,0:T(8,128)(2,1)S(1)} %collective-permute-done.7.refs_6_), channel_id=1, source_target_pairs={{0,8},{8,0},{16,24},{24,16},{32,40},{40,32},{48,56},{56,48},{64,72... | collective-permute-start | bytes 1179656 | tf_op jit(solution)/shard_map/ppermute | solution.py:330
  62.7 12.1 %collective-permute-start.15 = (bf16[1,256,256]{2,1,0:T(8,128)(2,1)S(1)}, bf16[1,256,256]{2,1,0:T(8,128)(2,1)S(1)}, u32[]{:S(2)}, u32[]{:S(2)}) collective-permute-start(bf16[1,256,256]{2,1,0:T(8,128)(2,1)S(1)} %collective-permute-done.8.refs_5_), channel_id=1, source_target_pairs={{0,8},{8,0},{16,24},{24,16},{32,40},{40,32},{48,56},{56,48},{64,72... | collective-permute-start | bytes 393224 | tf_op jit(solution)/shard_map/ppermute | solution.py:330
  63.3 13.9 %collective-permute-start.11 = (bf16[2,256,256]{2,1,0:T(8,128)(2,1)S(1)}, bf16[2,256,256]{2,1,0:T(8,128)(2,1)S(1)}, u32[]{:S(2)}, u32[]{:S(2)}) collective-permute-start(bf16[2,256,256]{2,1,0:T(8,128)(2,1)S(1)} %slice.17), channel_id=1, source_target_pairs={{0,16},{8,120},{16,32},{24,8},{32,48},{40,24},{48,64},{56,40},{64,... | collective-permute-start | bytes 786440 | tf_op jit(solution)/shard_map/ppermute | solution.py:330
  64.5 12.7 %collective-permute-start.13 = (bf16[1,256,256]{2,1,0:T(8,128)(2,1)S(1)}, bf16[1,256,256]{2,1,0:T(8,128)(2,1)S(1)}, u32[]{:S(2)}, u32[]{:S(2)}) collective-permute-start(bf16[1,256,256]{2,1,0:T(8,128)(2,1)S(1)} %get-tuple-element.89), channel_id=1, source_target_pairs={{0,32},{8,104},{16,48},{24,120},{32,64},{40,8},{48,80},{56,24},{64... | collective-permute-start | bytes 393224 | tf_op jit(solution)/shard_map/ppermute | solution.py:330
  70.3 6.9 %collective-permute-start.12 = (bf16[1,256,256]{2,1,0:T(8,128)(2,1)S(1)}, bf16[1,256,256]{2,1,0:T(8,128)(2,1)S(1)}, u32[]{:S(2)}, u32[]{:S(2)}) collective-permute-start(bf16[1,256,256]{2,1,0:T(8,128)(2,1)S(1)} %get-tuple-element.90), channel_id=1, source_target_pairs={{0,128},{8,136},{16,144},{24,152},{32,160},{40,168},{48,176},{56,1... | collective-permute-start | bytes 393224 | tf_op jit(solution)/shard_map/ppermute | solution.py:330
  77.3 2.5 %copy-start.2 = (bf16[512,768]{1,0:T(8,128)(2,1)S(1)}, bf16[512,768]{1,0:T(8,128)(2,1)}, u32[]{:S(2)}) copy-start(bf16[512,768]{1,0:T(8,128)(2,1)} %refs_6_.1) | copy-start | bytes 2359300
  77.3 2.5 %collective-permute-start.16 = (bf16[4,256,256]{2,1,0:T(8,128)(2,1)S(1)}, bf16[4,256,256]{2,1,0:T(8,128)(2,1)S(1)}, u32[]{:S(2)}, u32[]{:S(2)}) collective-permute-start(bf16[4,256,256]{2,1,0:T(8,128)(2,1)S(1)} %constant_dynamic-update-slice_fusion.refs_3_), channel_id=1, source_target_pairs={{0,8},{8,0},{16,24},{24,16},{32,40},{40,32},{48,56},{56,48},{64,72... | collective-permute-start | bytes 1572872 | tf_op jit(solution)/shard_map/ppermute | solution.py:330

commit v6 on v5

--- a/solution.py
+++ b/solution.py
@@ -354,11 +354,17 @@
     def fold(pieces, carry=None, weight=None):
         return attend(valid_counts, own, depth, query, pieces, carry, weight)
 
-    def mine(side, shift):
-        return [(side, shift, 0), (side, shift, 1)]
-
-    def theirs(side, shift):
-        return [(side, -shift, 1), (side, -shift, 0)]
+    def crossed(places):
+        return [(side, -shift, 1 - core) for side, shift, core in places]
+
+    def both_cores(pieces, carry, weight=None):
+        arrays = [piece[0] for piece in pieces]
+        places = [place for piece in pieces for place in piece[1]]
+        joined = arrays[0] if len(arrays) == 1 else jnp.concatenate(arrays)
+        exchanged = flip_core(joined)
+        carry = fold([(joined, places)], carry)
+        exchanged, carry = hold((exchanged, carry))
+        return fold([(exchanged, crossed(places))], carry, weight)
 
     start = key_values(normed, w_key, w_value)
     beside = flip_core(start)
@@ -367,58 +373,30 @@
     beside, query = hold((beside, query))
     own_pair = jnp.concatenate([start, beside])
 
-    first = along_z(own_pair)
-    carry = fold([(own_pair, mine(0, 0))])
-    first, other, carry = hold((first, other, carry))
-
-    second = along_z(jnp.concatenate([first, other]))
-    first_other = flip_y(first[1:2])
-    other_core = flip_core(other)
-    first_core = flip_core(first)
-    carry = fold([(other, [(1, 0, 0)]), (first, mine(0, 1))], carry)
-    second, first_other, other_core, first_core, carry = hold((second, first_other, other_core, first_core, carry))
-
-    third = along_z(second)
-    second_other = flip_y(second[1:2])
-    second_core = flip_core(second)
-    first_other_core = flip_core(first_other)
-    carry = fold(
-        [
-            (other_core, [(1, 0, 1)]),
-            (first_core, theirs(0, 1)),
-            (first_other, [(1, 1, 1)]),
-            (second, mine(0, 2) + [(1, 1, 0)]),
-        ],
-        carry,
-    )
-    third, second_other, second_core, first_other_core, carry = hold(
-        (third, second_other, second_core, first_other_core, carry)
-    )
-
-    fourth = along_z(third[1:3])
-    third_other = flip_y(third[1:2])
-    far_other = along_z(third[2:3], 2)
-    third_core = flip_core(third)
-    second_other_core = flip_core(second_other)
-    carry = fold(
-        [
-            (second_core, theirs(0, 2) + [(1, -1, 1)]),
-            (first_other_core, [(1, -1, 0)]),
-            (second_other, [(1, 2, 1)]),
-            (third, mine(0, 3) + [(1, 2, 0)]),
-        ],
-        carry,
-    )
-    third_core, second_other_core, carry = hold((third_core, second_other_core, carry))
-    carry = fold([(third_core, theirs(0, 3) + [(1, -2, 1)]), (second_other_core, [(1, -2, 0)])], carry)
-    fourth, third_other, far_other, carry = hold((fourth, third_other, far_other, carry))
+    one = along_z(own_pair)
+    carry = fold([(own_pair, [(0, 0, 0), (0, 0, 1)])])
+    one, other, carry = hold((one, other, carry))
+
+    one_other = flip_y(one[1:2])
+    joined = jnp.concatenate([one, other])
+    two = along_z(joined)
+    carry = both_cores([(joined, [(0, 1, 0), (0, 1, 1), (1, 0, 0)])], carry)
+    two, one_other, carry = hold((two, one_other, carry))
+
+    three = along_z(two)
+    two_other = flip_y(two[1:2])
+    carry = both_cores([(two, [(0, 2, 0), (0, 2, 1), (1, 1, 0)]), (one_other, [(1, 1, 1)])], carry)
+    three, two_other, carry = hold((three, two_other, carry))
 
     half = depth // 2
-    last = jnp.concatenate([fourth, third_other, far_other])
-    last_core = flip_core(last)
-    carry = fold([(last, [(0, half, 1), (1, 3, 0), (1, 3, 1), (1, half, 0)])], carry)
-    last_core, carry = hold((last_core, carry))
-    (mixed,) = fold([(last_core, [(0, -half, 0), (1, -3, 1), (1, -3, 0), (1, -half, 1)])], carry, w_out)
+    four = along_z(three[1:3])
+    three_other = flip_y(three[1:2])
+    far_other = along_z(three[2:3], 2)
+    carry = both_cores([(three, [(0, 3, 0), (0, 3, 1), (1, 2, 0)]), (two_other, [(1, 2, 1)])], carry)
+    four, three_other, far_other, carry = hold((four, three_other, far_other, carry))
+
+    pieces = [(four, [(0, half, 1), (1, 3, 0)]), (three_other, [(1, 3, 1)]), (far_other, [(1, half, 0)])]
+    (mixed,) = both_cores(pieces, carry, w_out)
     parts = lax.all_to_all(mixed.reshape(groups, share, channels), "head", 0, 0, tiled=True)
     return total_of(parts)
 

time: 97.3 us -> 95.8 us (0.985)
  starting transfers between devices: 25.8 us -> 23.2 us
  Pallas kernels: 26 us -> 27.8 us
    ppermute x17 -> x14, starting transfers between devices: 18.7 us -> 16.1 us  [moved(): return lax.ppermute(array, 'blk', [(i, target(i)) for i in range(blocks)])]
    pallas_call x7 -> x9, Pallas kernels: 18.1 us -> 19.8 us  [attend(): pl.pallas_call(functools.partial(attend_kernel, carry is None, w_out is n...]
    ppermute x17 -> x14, waiting for transfers between devices: 8.19 us -> 8 us  [moved(): return lax.ppermute(array, 'blk', [(i, target(i)) for i in range(blocks)])]
  transfers between devices with their start and end apart: 18 -> 15, of which waited for: 7 -> 7; matrix products, arithmetic and copies ran while one was open for 0% -> 0% of each run, Pallas kernels for 17% -> 19%
where the time goes in v6:
time: 95.8 us; the launch traced here: 95.5 us
  Pallas kernels  27.8 us (29%)
  blocking collectives  26.2 us (27%)
  starting transfers between devices  23.2 us (24%)
  waiting for transfers between devices  16.9 us (18%)
  local copies, waits for them, and re-layouts  1.11 us (1%)
    pallas_call x9, Pallas kernels, attend(): pl.pallas_call(functools.partial(attend_kernel, carry is None, w_out is n...  19.8 us
    ppermute x14, starting transfers between devices, moved(): return lax.ppermute(array, 'blk', [(i, target(i)) for i in range(blocks)])  16.1 us
    all_to_all x1, blocking collectives, per_device(): lax.all_to_all(mixed.reshape(groups, share, channels), 'head', 0, 0, tile...  13.4 us
    all_to_all x1, blocking collectives, per_device(): lax.all_to_all(copies, 'head', 0, 0, tiled=True).reshape(rows, channels)  12.8 us
    all_to_all x1, waiting for transfers between devices, per_device(): lax.all_to_all(partial.reshape(groups, share, channels), 'head', 0, 0, ti...  8.93 us
    ppermute x14, waiting for transfers between devices, moved(): return lax.ppermute(array, 'blk', [(i, target(i)) for i in range(blocks)])  8 us
    all_to_all x1, starting transfers between devices, per_device(): lax.all_to_all(partial.reshape(groups, share, channels), 'head', 0, 0, ti...  7.07 us
    pallas_call x1, Pallas kernels, mlp(): pl.pallas_call(mlp_kernel, out_shape=jax.ShapeDtypeStruct((rows, channels...  5.75 us
  transfers between devices with their start and end apart: 15, of which 7 were waited for; matrix products, arithmetic and copies ran while one was open for 0% of the time, Pallas kernels for 19%

profile of v6, /device:TPU:32, one launch (start us, length us, event | category | flops | bytes accessed | tf_op | source)
XLA Modules:
  0.0 95.5 jit_solution(1085489987807578780)
XLA Ops:
  0.0 5.7 %conv_mlp.1 = bf16[256,768]{1,0:T(8,128)(2,1)} custom-call(bf16[16,16,768]{2,1,0:T(8,128)(2,1)} %bitcast.15, f32[7,7,768]{2,1,0:T(8,128)} %dw_hbm.1, f32[6,128]{1,0:T(8,128)} %bitcast.18, f32[6,128]{1,0:T(8,128)} %bitcast.19, bf16[768,384]{1,0:T(8,128)(2,1)} %w1_hbm.1, f32[3,128]{1,0:T(4,128)} %bitcast.23, bf16[384,768]{1,0:T(8,128)(2,1)} %w2_hbm.1), custom_call_target="tpu_custom_call" | custom-call | tf_op jit(solution)/shard_map/conv_mlp/pallas_call | solution.py:108
  5.8 0.0 copy-start.8
  5.8 0.0 copy-start
  5.8 7.1 %all-to-all-start = ((bf16[8,32,768]{2,1,0:T(8,128)(2,1)}), bf16[8,32,768]{2,1,0:T(8,128)(2,1)S(1)}, u32[]{:S(2)}, u32[]{:S(2)}) async-start(bf16[8,32,768]{2,1,0:T(8,128)(2,1)} %bitcast.6), calls=%async_computation | async-start | bytes 786432 | tf_op jit(solution)/shard_map/all_to_all | solution.py:350
  12.9 0.0 copy-start.6
  12.9 0.7 copy-done.7
  13.5 0.0 copy-done.6
  13.6 8.9 %all-to-all-done.parts = bf16[8,32,768]{2,1,0:T(8,128)(2,1)S(1)} async-done(((bf16[8,32,768]{2,1,0:T(8,128)(2,1)}), bf16[8,32,768]{2,1,0:T(8,128)(2,1)S(1)}, u32[]{:S(2)}, u32[]{:S(2)}) %all-to-all-start) | async-done | bytes 393248 | tf_op jit(solution)/shard_map/all_to_all | solution.py:350
  22.5 0.2 block_norm.1
  22.8 0.0 copy-start.1
  22.8 12.8 %all_to_all.15 = bf16[8,32,768]{2,1,0:T(8,128)(2,1)S(1)} all-to-all(bf16[8,32,768]{2,1,0:T(8,128)(2,1)S(1)} %block_norm.1), channel_id=1, replica_groups=mesh['blk'=32,'head'=8] {'head'}, dimensions={0} | all-to-all | bytes 786432 | tf_op jit(solution)/shard_map/all_to_all | solution.py:352
  35.6 0.4 key_values.1
  35.9 0.1 collective-permute-start
  36.0 0.2 copy-done.5
  36.2 0.9 queries.1.refs_2_
  37.1 0.2 collective-permute-done
  37.4 2.0 %collective-permute-start.1 = (bf16[2,256,256]{2,1,0:T(8,128)(2,1)S(1)}, bf16[2,256,256]{2,1,0:T(8,128)(2,1)S(1)}, u32[]{:S(2)}, u32[]{:S(2)}) collective-permute-start(bf16[2,256,256]{2,1,0:T(8,128)(2,1)S(1)} %pad_maximum_fusion.refs_3_), channel_id=1, source_target_pairs={{0,16},{8,120},{16,32},{24,8},{32,48},{40,24},{48,64},{56,40},{64,... | collective-permute-start | bytes 786440 | tf_op jit(solution)/shard_map/ppermute | solution.py:330
  39.4 0.7 collective-permute-start.2
  40.1 1.5 %attend.9 = (f32[4,256,128]{2,1,0:T(8,128)S(1)}, f32[4,256,256]{2,1,0:T(8,128)S(1)}) custom-call(s32[32]{0:T(128)S(1)} %copy-done.5, s32[1]{0:T(128)} %bitcast.refs_1_, bf16[4,256,128]{2,1,0:T(8,128)(2,1)S(1)} %queries.1.refs_2_, bf16[2,256,256]{2,1,0:T(8,128)(2,1)S(1)} %pad_maximum_fusion.refs_3_), custom_call_target="tpu_custom_call" | custom-call | flops 65536 | bytes 65536 | tf_op jit(solution)/shard_map/attend/pallas_call | solution.py:275
  41.6 2.8 %collective-permute-done.2 = bf16[1,256,256]{2,1,0:T(8,128)(2,1)S(1)} collective-permute-done((bf16[1,256,256]{2,1,0:T(8,128)(2,1)S(1)}, bf16[1,256,256]{2,1,0:T(8,128)(2,1)S(1)}, u32[]{:S(2)}, u32[]{:S(2)}) %collective-permute-start.2) | collective-permute-done | bytes 131104 | tf_op jit(solution)/shard_map/ppermute | solution.py:330
  44.4 0.1 collective-permute-start.5
  44.5 2.0 %collective-permute-start.3 = (bf16[3,256,256]{2,1,0:T(8,128)(2,1)S(1)}, bf16[3,256,256]{2,1,0:T(8,128)(2,1)S(1)}, u32[]{:S(2)}, u32[]{:S(2)}) collective-permute-start(bf16[3,256,256]{2,1,0:T(8,128)(2,1)S(1)} %constant_dynamic-update-slice_fusion.refs_3_), channel_id=1, source_target_pairs={{0,16},{8,120},{16,32},{24,8},{32,48},{40,24},{48,64},{56,40},{64,... | collective-permute-start | bytes 1179656 | tf_op jit(solution)/shard_map/ppermute | solution.py:330
  46.5 0.9 collective-permute-start.4
  47.5 2.0 %attend.10 = (f32[4,256,128]{2,1,0:T(8,128)S(1)}, f32[4,256,256]{2,1,0:T(8,128)S(1)}) custom-call(s32[32]{0:T(128)S(1)} %copy-done.5, s32[1]{0:T(128)} %bitcast.refs_1_, bf16[4,256,128]{2,1,0:T(8,128)(2,1)S(1)} %queries.1.refs_2_, bf16[3,256,256]{2,1,0:T(8,128)(2,1)S(1)} %constant_dynamic-update-slice_fusion.refs_3_, ...), custom_call_target="tpu_custom_call" | custom-call | flops 98304 | bytes 65536 | tf_op jit(solution)/shard_map/attend/pallas_call | solution.py:275
  49.4 0.0 collective-permute-done.5.refs_3_
  49.4 2.0 %attend.11 = (f32[4,256,128]{2,1,0:T(8,128)S(1)}, f32[4,256,256]{2,1,0:T(8,128)S(1)}) custom-call(s32[32]{0:T(128)S(1)} %copy-done.5, s32[1]{0:T(128)} %bitcast.refs_1_, bf16[4,256,128]{2,1,0:T(8,128)(2,1)S(1)} %queries.1.refs_2_, bf16[3,256,256]{2,1,0:T(8,128)(2,1)S(1)} %collective-permute-done.5.refs_3_, f32[4,256,128]{2,1,0:T(8,128)S(1)} %get-tuple-element.63.refs_4_, ...), custom_call_target="tpu_custom_call" | custom-call | flops 98304 | bytes 65536 | tf_op jit(solution)/shard_map/attend/pallas_call | solution.py:275
  51.4 1.1 %collective-permute-done.4 = bf16[1,256,256]{2,1,0:T(8,128)(2,1)S(1)} collective-permute-done((bf16[1,256,256]{2,1,0:T(8,128)(2,1)S(1)}, bf16[1,256,256]{2,1,0:T(8,128)(2,1)S(1)}, u32[]{:S(2)}, u32[]{:S(2)}) %collective-permute-start.4) | collective-permute-done | bytes 131104 | tf_op jit(solution)/shard_map/ppermute | solution.py:330
  52.5 1.3 %collective-permute-done.3 = bf16[3,256,256]{2,1,0:T(8,128)(2,1)S(1)} collective-permute-done((bf16[3,256,256]{2,1,0:T(8,128)(2,1)S(1)}, bf16[3,256,256]{2,1,0:T(8,128)(2,1)S(1)}, u32[]{:S(2)}, u32[]{:S(2)}) %collective-permute-start.3) | collective-permute-done | bytes 393248 | tf_op jit(solution)/shard_map/ppermute | solution.py:330
  53.8 0.1 collective-permute-start.8
  53.9 1.2 %collective-permute-start.6 = (bf16[3,256,256]{2,1,0:T(8,128)(2,1)S(1)}, bf16[3,256,256]{2,1,0:T(8,128)(2,1)S(1)}, u32[]{:S(2)}, u32[]{:S(2)}) collective-permute-start(bf16[3,256,256]{2,1,0:T(8,128)(2,1)S(1)} %collective-permute-done.3), channel_id=1, source_target_pairs={{0,16},{8,120},{16,32},{24,8},{32,48},{40,24},{48,64},{56,40},{64,... | collective-permute-start | bytes 1179656 | tf_op jit(solution)/shard_map/ppermute | solution.py:330
  55.2 1.1 %collective-permute-start.7 = (bf16[1,256,256]{2,1,0:T(8,128)(2,1)S(1)}, bf16[1,256,256]{2,1,0:T(8,128)(2,1)S(1)}, u32[]{:S(2)}, u32[]{:S(2)}) collective-permute-start(bf16[1,256,256]{2,1,0:T(8,128)(2,1)S(1)} %slice.16), channel_id=1, source_target_pairs={{0,128},{8,136},{16,144},{24,152},{32,160},{40,168},{48,176},{56,1... | collective-permute-start | bytes 393224 | tf_op jit(solution)/shard_map/ppermute | solution.py:330
  56.2 2.4 %attend.12 = (f32[4,256,128]{2,1,0:T(8,128)S(1)}, f32[4,256,256]{2,1,0:T(8,128)S(1)}) custom-call(s32[32]{0:T(128)S(1)} %copy-done.5, s32[1]{0:T(128)} %bitcast.refs_1_, bf16[4,256,128]{2,1,0:T(8,128)(2,1)S(1)} %queries.1.refs_2_, bf16[4,256,256]{2,1,0:T(8,128)(2,1)S(1)} %constant_dynamic-update-slice_fusion.2.refs_3_, ...), custom_call_target="tpu_custom_call" | custom-call | flops 131072 | bytes 65536 | tf_op jit(solution)/shard_map/attend/pallas_call | solution.py:275
  58.6 0.0 collective-permute-done.8.refs_3_
  58.6 2.4 %attend.13 = (f32[4,256,128]{2,1,0:T(8,128)S(1)}, f32[4,256,256]{2,1,0:T(8,128)S(1)}) custom-call(s32[32]{0:T(128)S(1)} %copy-done.5, s32[1]{0:T(128)} %bitcast.refs_1_, bf16[4,256,128]{2,1,0:T(8,128)(2,1)S(1)} %queries.1.refs_2_, bf16[4,256,256]{2,1,0:T(8,128)(2,1)S(1)} %collective-permute-done.8.refs_3_, f32[4,256,128]{2,1,0:T(8,128)S(1)} %get-tuple-element.74.refs_4_, ...), custom_call_target="tpu_custom_call" | custom-call | flops 131072 | bytes 65536 | tf_op jit(solution)/shard_map/attend/pallas_call | solution.py:275
  61.0 2.0 %collective-permute-done.6 = bf16[3,256,256]{2,1,0:T(8,128)(2,1)S(1)} collective-permute-done((bf16[3,256,256]{2,1,0:T(8,128)(2,1)S(1)}, bf16[3,256,256]{2,1,0:T(8,128)(2,1)S(1)}, u32[]{:S(2)}, u32[]{:S(2)}) %collective-permute-start.6) | collective-permute-done | bytes 393248 | tf_op jit(solution)/shard_map/ppermute | solution.py:330
  63.0 0.1 collective-permute-start.12
  63.2 0.7 collective-permute-start.9
  63.9 6.3 %collective-permute-start.11 = (bf16[1,256,256]{2,1,0:T(8,128)(2,1)S(1)}, bf16[1,256,256]{2,1,0:T(8,128)(2,1)S(1)}, u32[]{:S(2)}, u32[]{:S(2)}) collective-permute-start(bf16[1,256,256]{2,1,0:T(8,128)(2,1)S(1)} %get-tuple-element.99), channel_id=1, source_target_pairs={{0,32},{8,104},{16,48},{24,120},{32,64},{40,8},{48,80},{56,24},{64... | collective-permute-start | bytes 393224 | tf_op jit(solution)/shard_map/ppermute | solution.py:330
  70.2 0.7 collective-permute-start.10
  70.9 2.4 %attend.14 = (f32[4,256,128]{2,1,0:T(8,128)S(1)}, f32[4,256,256]{2,1,0:T(8,128)S(1)}) custom-call(s32[32]{0:T(128)S(1)} %copy-done.5, s32[1]{0:T(128)} %bitcast.refs_1_, bf16[4,256,128]{2,1,0:T(8,128)(2,1)S(1)} %queries.1.refs_2_, bf16[4,256,256]{2,1,0:T(8,128)(2,1)S(1)} %constant_dynamic-update-slice_fusion.4.refs_3_, ...), custom_call_target="tpu_custom_call" | custom-call | flops 131072 | bytes 65536 | tf_op jit(solution)/shard_map/attend/pallas_call | solution.py:275
  73.3 2.4 %attend.15 = (f32[4,256,128]{2,1,0:T(8,128)S(1)}, f32[4,256,256]{2,1,0:T(8,128)S(1)}) custom-call(s32[32]{0:T(128)S(1)} %copy-done.5, s32[1]{0:T(128)} %bitcast.refs_1_, bf16[4,256,128]{2,1,0:T(8,128)(2,1)S(1)} %queries.1.refs_2_, bf16[4,256,256]{2,1,0:T(8,128)(2,1)S(1)} %collective-permute-done.12.refs_3_, f32[4,256,128]{2,1,0:T(8,128)S(1)} %get-tuple-element.85.refs_4_, ...), custom_call_target="tpu_custom_call" | custom-call | flops 131072 | bytes 65536 | tf_op jit(solution)/shard_map/attend/pallas_call | solution.py:275
  75.7 0.6 collective-permute-done.11
  76.4 0.0 copy-start.2
  76.4 0.1 collective-permute-start.13
  76.5 2.4 %attend.16 = (f32[4,256,128]{2,1,0:T(8,128)S(1)}, f32[4,256,256]{2,1,0:T(8,128)S(1)}) custom-call(s32[32]{0:T(128)S(1)} %copy-done.5, s32[1]{0:T(128)} %bitcast.refs_1_, bf16[4,256,128]{2,1,0:T(8,128)(2,1)S(1)} %queries.1.refs_2_, bf16[4,256,256]{2,1,0:T(8,128)(2,1)S(1)} %constant_dynamic-update-slice_fusion.6.refs_3_, ...), custom_call_target="tpu_custom_call" | custom-call | flops 131072 | bytes 65536 | tf_op jit(solution)/shard_map/attend/pallas_call | solution.py:275
  78.9 2.6 %attend.17 = bf16[256,768]{1,0:T(8,128)(2,1)S(1)} custom-call(s32[32]{0:T(128)S(1)} %copy-done.5, s32[1]{0:T(128)} %bitcast.refs_1_, bf16[4,256,128]{2,1,0:T(8,128)(2,1)S(1)} %queries.1.refs_2_, bf16[4,256,256]{2,1,0:T(8,128)(2,1)S(1)} %collective-permute-done.13.refs_3_, f32[4,256,128]{2,1,0:T(8,128)S(1)} %get-tuple-element.97.refs_4_, ...), custom_call_target="tpu_custom_call" | custom-call | flops 131072 | bytes 65536 | tf_op jit(solution)/shard_map/attend/pallas_call | solution.py:275
  81.4 13.4 %all_to_all.16.parts = bf16[8,32,768]{2,1,0:T(8,128)(2,1)S(1)} all-to-all(bf16[8,32,768]{2,1,0:T(8,128)(2,1)S(1)} %bitcast.17), channel_id=1, replica_groups=mesh['blk'=32,'head'=8] {'head'}, dimensions={0} | all-to-all | bytes 786432 | tf_op jit(solution)/shard_map/all_to_all | solution.py:400
  94.8 0.7 total.1
  (31 shorter events, 0.3 us)
Async XLA Ops:
  5.8 7.1 %copy-start.8 = (f32[768]{0:T(1024)S(1)}, f32[768]{0:T(1024)}, u32[]{:S(2)}) copy-start(f32[768]{0:T(1024)} %param.24) | copy-start | bytes 9220
  5.8 16.7 %copy-start = (bf16[1,16,16,768]{3,2,1,0:T(8,128)(2,1)S(1)}, bf16[1,16,16,768]{3,2,1,0:T(8,128)(2,1)}, u32[]{:S(2)}) copy-start(bf16[1,16,16,768]{3,2,1,0:T(8,128)(2,1)} %param.15) | copy-start | bytes 1179652
  5.8 16.7 %all-to-all-start = ((bf16[8,32,768]{2,1,0:T(8,128)(2,1)}), bf16[8,32,768]{2,1,0:T(8,128)(2,1)S(1)}, u32[]{:S(2)}, u32[]{:S(2)}) async-start(bf16[8,32,768]{2,1,0:T(8,128)(2,1)} %bitcast.6), calls=%async_computation | async-start | bytes 786432 | tf_op jit(solution)/shard_map/all_to_all | solution.py:350
  12.9 0.7 copy-start.7
  12.9 0.7 copy-start.6
  22.5 13.0 %copy-start.3 = (bf16[768,128]{1,0:T(8,128)(2,1)S(1)}, bf16[768,128]{1,0:T(8,128)(2,1)}, u32[]{:S(2)}) copy-start(bf16[768,128]{1,0:T(8,128)(2,1)} %wk.1) | copy-start | bytes 589828
  22.5 13.0 %copy-start.4 = (bf16[768,128]{1,0:T(8,128)(2,1)S(1)}, bf16[768,128]{1,0:T(8,128)(2,1)}, u32[]{:S(2)}) copy-start(bf16[768,128]{1,0:T(8,128)(2,1)} %wv.1) | copy-start | bytes 589828
  22.8 13.3 %copy-start.1 = (bf16[768,512]{1,0:T(8,128)(2,1)S(1)}, bf16[768,512]{1,0:T(8,128)(2,1)}, u32[]{:S(2)}) copy-start(bf16[768,512]{1,0:T(8,128)(2,1)} %wq.1) | copy-start | bytes 2359300
  35.6 0.7 copy-start.5
  35.9 1.4 %collective-permute-start = (bf16[1,256,256]{2,1,0:T(8,128)(2,1)S(1)}, bf16[1,256,256]{2,1,0:T(8,128)(2,1)S(1)}, u32[]{:S(2)}, u32[]{:S(2)}) collective-permute-start(bf16[1,256,256]{2,1,0:T(8,128)(2,1)S(1)} %key_values.1), channel_id=1, source_target_pairs={{0,8},{8,0},{16,24},{24,16},{32,40},{40,32},{48,56},{56,48},{64,72... | collective-permute-start | bytes 393224 | tf_op jit(solution)/shard_map/ppermute | solution.py:330
  37.4 7.0 %collective-permute-start.1 = (bf16[2,256,256]{2,1,0:T(8,128)(2,1)S(1)}, bf16[2,256,256]{2,1,0:T(8,128)(2,1)S(1)}, u32[]{:S(2)}, u32[]{:S(2)}) collective-permute-start(bf16[2,256,256]{2,1,0:T(8,128)(2,1)S(1)} %pad_maximum_fusion.refs_3_), channel_id=1, source_target_pairs={{0,16},{8,120},{16,32},{24,8},{32,48},{40,24},{48,64},{56,40},{64,... | collective-permute-start | bytes 786440 | tf_op jit(solution)/shard_map/ppermute | solution.py:330
  39.4 5.0 %collective-permute-start.2 = (bf16[1,256,256]{2,1,0:T(8,128)(2,1)S(1)}, bf16[1,256,256]{2,1,0:T(8,128)(2,1)S(1)}, u32[]{:S(2)}, u32[]{:S(2)}) collective-permute-start(bf16[1,256,256]{2,1,0:T(8,128)(2,1)S(1)} %key_values.1), channel_id=1, source_target_pairs={{0,128},{8,136},{16,144},{24,152},{32,160},{40,168},{48,176},{56,1... | collective-permute-start | bytes 393224 | tf_op jit(solution)/shard_map/ppermute | solution.py:330
  44.4 5.0 %collective-permute-start.5 = (bf16[3,256,256]{2,1,0:T(8,128)(2,1)S(1)}, bf16[3,256,256]{2,1,0:T(8,128)(2,1)S(1)}, u32[]{:S(2)}, u32[]{:S(2)}) collective-permute-start(bf16[3,256,256]{2,1,0:T(8,128)(2,1)S(1)} %constant_dynamic-update-slice_fusion.refs_3_), channel_id=1, source_target_pairs={{0,8},{8,0},{16,24},{24,16},{32,40},{40,32},{48,56},{56,48},{64,72... | collective-permute-start | bytes 1179656 | tf_op jit(solution)/shard_map/ppermute | solution.py:330
  44.5 9.3 %collective-permute-start.3 = (bf16[3,256,256]{2,1,0:T(8,128)(2,1)S(1)}, bf16[3,256,256]{2,1,0:T(8,128)(2,1)S(1)}, u32[]{:S(2)}, u32[]{:S(2)}) collective-permute-start(bf16[3,256,256]{2,1,0:T(8,128)(2,1)S(1)} %constant_dynamic-update-slice_fusion.refs_3_), channel_id=1, source_target_pairs={{0,16},{8,120},{16,32},{24,8},{32,48},{40,24},{48,64},{56,40},{64,... | collective-permute-start | bytes 1179656 | tf_op jit(solution)/shard_map/ppermute | solution.py:330
  46.5 6.0 %collective-permute-start.4 = (bf16[1,256,256]{2,1,0:T(8,128)(2,1)S(1)}, bf16[1,256,256]{2,1,0:T(8,128)(2,1)S(1)}, u32[]{:S(2)}, u32[]{:S(2)}) collective-permute-start(bf16[1,256,256]{2,1,0:T(8,128)(2,1)S(1)} %slice.15), channel_id=1, source_target_pairs={{0,128},{8,136},{16,144},{24,152},{32,160},{40,168},{48,176},{56,1... | collective-permute-start | bytes 393224 | tf_op jit(solution)/shard_map/ppermute | solution.py:330
  53.8 4.8 %collective-permute-start.8 = (bf16[4,256,256]{2,1,0:T(8,128)(2,1)S(1)}, bf16[4,256,256]{2,1,0:T(8,128)(2,1)S(1)}, u32[]{:S(2)}, u32[]{:S(2)}) collective-permute-start(bf16[4,256,256]{2,1,0:T(8,128)(2,1)S(1)} %constant_dynamic-update-slice_fusion.2.refs_3_), channel_id=1, source_target_pairs={{0,8},{8,0},{16,24},{24,16},{32,40},{40,32},{48,56},{56,48},{64,72... | collective-permute-start | bytes 1572872 | tf_op jit(solution)/shard_map/ppermute | solution.py:330
  53.9 9.1 %collective-permute-start.6 = (bf16[3,256,256]{2,1,0:T(8,128)(2,1)S(1)}, bf16[3,256,256]{2,1,0:T(8,128)(2,1)S(1)}, u32[]{:S(2)}, u32[]{:S(2)}) collective-permute-start(bf16[3,256,256]{2,1,0:T(8,128)(2,1)S(1)} %collective-permute-done.3), channel_id=1, source_target_pairs={{0,16},{8,120},{16,32},{24,8},{32,48},{40,24},{48,64},{56,40},{64,... | collective-permute-start | bytes 1179656 | tf_op jit(solution)/shard_map/ppermute | solution.py:330
  55.2 5.8 %collective-permute-start.7 = (bf16[1,256,256]{2,1,0:T(8,128)(2,1)S(1)}, bf16[1,256,256]{2,1,0:T(8,128)(2,1)S(1)}, u32[]{:S(2)}, u32[]{:S(2)}) collective-permute-start(bf16[1,256,256]{2,1,0:T(8,128)(2,1)S(1)} %slice.16), channel_id=1, source_target_pairs={{0,128},{8,136},{16,144},{24,152},{32,160},{40,168},{48,176},{56,1... | collective-permute-start | bytes 393224 | tf_op jit(solution)/shard_map/ppermute | solution.py:330
  63.0 10.3 %collective-permute-start.12 = (bf16[4,256,256]{2,1,0:T(8,128)(2,1)S(1)}, bf16[4,256,256]{2,1,0:T(8,128)(2,1)S(1)}, u32[]{:S(2)}, u32[]{:S(2)}) collective-permute-start(bf16[4,256,256]{2,1,0:T(8,128)(2,1)S(1)} %constant_dynamic-update-slice_fusion.4.refs_3_), channel_id=1, source_target_pairs={{0,8},{8,0},{16,24},{24,16},{32,40},{40,32},{48,56},{56,48},{64,72... | collective-permute-start | bytes 1572872 | tf_op jit(solution)/shard_map/ppermute | solution.py:330
  63.2 13.1 %collective-permute-start.9 = (bf16[2,256,256]{2,1,0:T(8,128)(2,1)S(1)}, bf16[2,256,256]{2,1,0:T(8,128)(2,1)S(1)}, u32[]{:S(2)}, u32[]{:S(2)}) collective-permute-start(bf16[2,256,256]{2,1,0:T(8,128)(2,1)S(1)} %slice.17), channel_id=1, source_target_pairs={{0,16},{8,120},{16,32},{24,8},{32,48},{40,24},{48,64},{56,40},{64,... | collective-permute-start | bytes 786440 | tf_op jit(solution)/shard_map/ppermute | solution.py:330
  63.9 12.4 %collective-permute-start.11 = (bf16[1,256,256]{2,1,0:T(8,128)(2,1)S(1)}, bf16[1,256,256]{2,1,0:T(8,128)(2,1)S(1)}, u32[]{:S(2)}, u32[]{:S(2)}) collective-permute-start(bf16[1,256,256]{2,1,0:T(8,128)(2,1)S(1)} %get-tuple-element.99), channel_id=1, source_target_pairs={{0,32},{8,104},{16,48},{24,120},{32,64},{40,8},{48,80},{56,24},{64... | collective-permute-start | bytes 393224 | tf_op jit(solution)/shard_map/ppermute | solution.py:330
  70.2 6.1 %collective-permute-start.10 = (bf16[1,256,256]{2,1,0:T(8,128)(2,1)S(1)}, bf16[1,256,256]{2,1,0:T(8,128)(2,1)S(1)}, u32[]{:S(2)}, u32[]{:S(2)}) collective-permute-start(bf16[1,256,256]{2,1,0:T(8,128)(2,1)S(1)} %get-tuple-element.100), channel_id=1, source_target_pairs={{0,128},{8,136},{16,144},{24,152},{32,160},{40,168},{48,176},{56,1... | collective-permute-start | bytes 393224 | tf_op jit(solution)/shard_map/ppermute | solution.py:330
  76.4 2.5 %copy-start.2 = (bf16[512,768]{1,0:T(8,128)(2,1)S(1)}, bf16[512,768]{1,0:T(8,128)(2,1)}, u32[]{:S(2)}) copy-start(bf16[512,768]{1,0:T(8,128)(2,1)} %refs_6_.1) | copy-start | bytes 2359300
  76.4 2.5 %collective-permute-start.13 = (bf16[4,256,256]{2,1,0:T(8,128)(2,1)S(1)}, bf16[4,256,256]{2,1,0:T(8,128)(2,1)S(1)}, u32[]{:S(2)}, u32[]{:S(2)}) collective-permute-start(bf16[4,256,256]{2,1,0:T(8,128)(2,1)S(1)} %constant_dynamic-update-slice_fusion.6.refs_3_), channel_id=1, source_target_pairs={{0,8},{8,0},{16,24},{24,16},{32,40},{40,32},{48,56},{56,48},{64,72... | collective-permute-start | bytes 1572872 | tf_op jit(solution)/shard_map/ppermute | solution.py:330

commit v7 on v6

--- a/solution.py
+++ b/solution.py
@@ -357,14 +357,15 @@
     def crossed(places):
         return [(side, -shift, 1 - core) for side, shift, core in places]
 
-    def both_cores(pieces, carry, weight=None):
-        arrays = [piece[0] for piece in pieces]
-        places = [place for piece in pieces for place in piece[1]]
-        joined = arrays[0] if len(arrays) == 1 else jnp.concatenate(arrays)
-        exchanged = flip_core(joined)
-        carry = fold([(joined, places)], carry)
+    def both_cores(pieces, shared, carry, weight=None):
+        exchanged = [flip_core(array) for array, _ in shared]
+        carry = fold(pieces, carry)
         exchanged, carry = hold((exchanged, carry))
-        return fold([(exchanged, crossed(places))], carry, weight)
+        return fold([(array, crossed(piece[1])) for array, piece in zip(exchanged, shared)], carry, weight)
+
+    def halves(trio, places, single, place):
+        joined = jnp.concatenate([trio[2:3], single])
+        return [(trio[0:2], places[0:2]), (joined, [places[2], place])]
 
     start = key_values(normed, w_key, w_value)
     beside = flip_core(start)
@@ -377,26 +378,34 @@
     carry = fold([(own_pair, [(0, 0, 0), (0, 0, 1)])])
     one, other, carry = hold((one, other, carry))
 
+    two = along_z(jnp.concatenate([one, other]))
     one_other = flip_y(one[1:2])
-    joined = jnp.concatenate([one, other])
-    two = along_z(joined)
-    carry = both_cores([(joined, [(0, 1, 0), (0, 1, 1), (1, 0, 0)])], carry)
+    pieces = [(one, [(0, 1, 0), (0, 1, 1)]), (other, [(1, 0, 0)])]
+    carry = both_cores(pieces, pieces, carry)
     two, one_other, carry = hold((two, one_other, carry))
 
     three = along_z(two)
     two_other = flip_y(two[1:2])
-    carry = both_cores([(two, [(0, 2, 0), (0, 2, 1), (1, 1, 0)]), (one_other, [(1, 1, 1)])], carry)
+    places, place = [(0, 2, 0), (0, 2, 1), (1, 1, 0)], (1, 1, 1)
+    carry = both_cores([(two, places), (one_other, [place])], halves(two, places, one_other, place), carry)
     three, two_other, carry = hold((three, two_other, carry))
 
-    half = depth // 2
-    four = along_z(three[1:3])
+    four = along_z(three)
     three_other = flip_y(three[1:2])
     far_other = along_z(three[2:3], 2)
-    carry = both_cores([(three, [(0, 3, 0), (0, 3, 1), (1, 2, 0)]), (two_other, [(1, 2, 1)])], carry)
+    places, place = [(0, 3, 0), (0, 3, 1), (1, 2, 0)], (1, 2, 1)
+    carry = both_cores([(three, places), (two_other, [place])], halves(three, places, two_other, place), carry)
     four, three_other, far_other, carry = hold((four, three_other, far_other, carry))
 
-    pieces = [(four, [(0, half, 1), (1, 3, 0)]), (three_other, [(1, 3, 1)]), (far_other, [(1, half, 0)])]
-    (mixed,) = both_cores(pieces, carry, w_out)
+    half = depth // 2
+    places = [(1, 3, 0), (1, 3, 1), (1, half, 0)]
+    pieces = [
+        (four, [(0, half, 0), (0, half, 1), places[0]]),
+        (three_other, [places[1]]),
+        (far_other, [places[2]]),
+    ]
+    shared = jnp.concatenate([four[2:3], three_other, far_other])
+    (mixed,) = both_cores(pieces, [(shared, places)], carry, w_out)
     parts = lax.all_to_all(mixed.reshape(groups, share, channels), "head", 0, 0, tiled=True)
     return total_of(parts)
 

time: 95.8 us -> 96.6 us (level)
  starting transfers between devices: 23.2 us -> 25.2 us
  waiting for transfers between devices: 16.9 us -> 15.7 us
    ppermute x14 -> x17, starting transfers between devices: 16.1 us -> 18.2 us  [moved(): return lax.ppermute(array, 'blk', [(i, target(i)) for i in range(blocks)])]
    ppermute x14 -> x17, waiting for transfers between devices: 8 us -> 6.73 us  [moved(): return lax.ppermute(array, 'blk', [(i, target(i)) for i in range(blocks)])]
  transfers between devices with their start and end apart: 15 -> 18, of which waited for: 7 -> 7; matrix products, arithmetic and copies ran while one was open for 0% -> 0% of each run, Pallas kernels for 19% -> 19%
where the time goes in v7:
time: 96.6 us; the launch traced here: 96.3 us
  Pallas kernels  27.8 us (29%)
  blocking collectives  26.1 us (27%)
  starting transfers between devices  25.2 us (26%)
  waiting for transfers between devices  15.7 us (16%)
  local copies, waits for them, and re-layouts  1 us (1%)
    pallas_call x9, Pallas kernels, attend(): pl.pallas_call(functools.partial(attend_kernel, carry is None, w_out is n...  19.8 us
    ppermute x17, starting transfers between devices, moved(): return lax.ppermute(array, 'blk', [(i, target(i)) for i in range(blocks)])  18.2 us
    all_to_all x1, blocking collectives, per_device(): lax.all_to_all(mixed.reshape(groups, share, channels), 'head', 0, 0, tile...  13.4 us
    all_to_all x1, blocking collectives, per_device(): lax.all_to_all(copies, 'head', 0, 0, tiled=True).reshape(rows, channels)  12.8 us
    all_to_all x1, waiting for transfers between devices, per_device(): lax.all_to_all(partial.reshape(groups, share, channels), 'head', 0, 0, ti...  8.93 us
    all_to_all x1, starting transfers between devices, per_device(): lax.all_to_all(partial.reshape(groups, share, channels), 'head', 0, 0, ti...  7.07 us
    ppermute x17, waiting for transfers between devices, moved(): return lax.ppermute(array, 'blk', [(i, target(i)) for i in range(blocks)])  6.73 us
    pallas_call x1, Pallas kernels, mlp(): pl.pallas_call(mlp_kernel, out_shape=jax.ShapeDtypeStruct((rows, channels...  5.75 us
  transfers between devices with their start and end apart: 18, of which 7 were waited for; matrix products, arithmetic and copies ran while one was open for 0% of the time, Pallas kernels for 19%

profile of v7, /device:TPU:32, one launch (start us, length us, event | category | flops | bytes accessed | tf_op | source)
XLA Modules:
  0.0 96.3 jit_solution(5310186762701850288)
XLA Ops:
  0.0 5.8 %conv_mlp.1 = bf16[256,768]{1,0:T(8,128)(2,1)} custom-call(bf16[16,16,768]{2,1,0:T(8,128)(2,1)} %bitcast.15, f32[7,7,768]{2,1,0:T(8,128)} %dw_hbm.1, f32[6,128]{1,0:T(8,128)} %bitcast.18, f32[6,128]{1,0:T(8,128)} %bitcast.19, bf16[768,384]{1,0:T(8,128)(2,1)} %w1_hbm.1, f32[3,128]{1,0:T(4,128)} %bitcast.23, bf16[384,768]{1,0:T(8,128)(2,1)} %w2_hbm.1), custom_call_target="tpu_custom_call" | custom-call | tf_op jit(solution)/shard_map/conv_mlp/pallas_call | solution.py:108
  5.8 0.0 copy-start.8
  5.8 0.0 copy-start
  5.8 7.1 %all-to-all-start = ((bf16[8,32,768]{2,1,0:T(8,128)(2,1)}), bf16[8,32,768]{2,1,0:T(8,128)(2,1)S(1)}, u32[]{:S(2)}, u32[]{:S(2)}) async-start(bf16[8,32,768]{2,1,0:T(8,128)(2,1)} %bitcast.6), calls=%async_computation | async-start | bytes 786432 | tf_op jit(solution)/shard_map/all_to_all | solution.py:350
  12.9 0.0 copy-start.6
  12.9 0.7 copy-done.7
  13.5 0.0 copy-done.6
  13.6 8.9 %all-to-all-done.parts = bf16[8,32,768]{2,1,0:T(8,128)(2,1)S(1)} async-done(((bf16[8,32,768]{2,1,0:T(8,128)(2,1)}), bf16[8,32,768]{2,1,0:T(8,128)(2,1)S(1)}, u32[]{:S(2)}, u32[]{:S(2)}) %all-to-all-start) | async-done | bytes 393248 | tf_op jit(solution)/shard_map/all_to_all | solution.py:350
  22.5 0.2 block_norm.1
  22.8 0.0 copy-start.1
  22.8 12.8 %all_to_all.15 = bf16[8,32,768]{2,1,0:T(8,128)(2,1)S(1)} all-to-all(bf16[8,32,768]{2,1,0:T(8,128)(2,1)S(1)} %block_norm.1), channel_id=1, replica_groups=mesh['blk'=32,'head'=8] {'head'}, dimensions={0} | all-to-all | bytes 786432 | tf_op jit(solution)/shard_map/all_to_all | solution.py:352
  35.6 0.4 key_values.1
  35.9 0.1 collective-permute-start
  36.0 0.2 copy-done.5
  36.2 0.9 queries.1.refs_2_
  37.1 0.2 collective-permute-done
  37.4 2.0 %collective-permute-start.1 = (bf16[2,256,256]{2,1,0:T(8,128)(2,1)S(1)}, bf16[2,256,256]{2,1,0:T(8,128)(2,1)S(1)}, u32[]{:S(2)}, u32[]{:S(2)}) collective-permute-start(bf16[2,256,256]{2,1,0:T(8,128)(2,1)S(1)} %pad_maximum_fusion.2.refs_3_), channel_id=1, source_target_pairs={{0,16},{8,120},{16,32},{24,8},{32,48},{40,24},{48,64},{56,40},{64,... | collective-permute-start | bytes 786440 | tf_op jit(solution)/shard_map/ppermute | solution.py:330
  39.4 0.7 collective-permute-start.2
  40.1 1.5 %attend.9 = (f32[4,256,128]{2,1,0:T(8,128)S(1)}, f32[4,256,256]{2,1,0:T(8,128)S(1)}) custom-call(s32[32]{0:T(128)S(1)} %copy-done.5, s32[1]{0:T(128)} %bitcast.refs_1_, bf16[4,256,128]{2,1,0:T(8,128)(2,1)S(1)} %queries.1.refs_2_, bf16[2,256,256]{2,1,0:T(8,128)(2,1)S(1)} %pad_maximum_fusion.2.refs_3_), custom_call_target="tpu_custom_call" | custom-call | flops 65536 | bytes 65536 | tf_op jit(solution)/shard_map/attend/pallas_call | solution.py:275
  41.6 2.8 %collective-permute-done.2.refs_4_ = bf16[1,256,256]{2,1,0:T(8,128)(2,1)S(1)} collective-permute-done((bf16[1,256,256]{2,1,0:T(8,128)(2,1)S(1)}, bf16[1,256,256]{2,1,0:T(8,128)(2,1)S(1)}, u32[]{:S(2)}, u32[]{:S(2)}) %collective-permute-start.2) | collective-permute-done | bytes 131104 | tf_op jit(solution)/shard_map/ppermute | solution.py:330
  44.4 2.0 %collective-permute-start.3 = (bf16[3,256,256]{2,1,0:T(8,128)(2,1)S(1)}, bf16[3,256,256]{2,1,0:T(8,128)(2,1)S(1)}, u32[]{:S(2)}, u32[]{:S(2)}) collective-permute-start(bf16[3,256,256]{2,1,0:T(8,128)(2,1)S(1)} %pad_maximum_fusion), channel_id=1, source_target_pairs={{0,16},{8,120},{16,32},{24,8},{32,48},{40,24},{48,64},{56,40},{64,... | collective-permute-start | bytes 1179656 | tf_op jit(solution)/shard_map/ppermute | solution.py:330
  46.4 0.9 collective-permute-start.5
  47.3 0.9 collective-permute-start.4
  48.2 1.9 %attend.10 = (f32[4,256,128]{2,1,0:T(8,128)S(1)}, f32[4,256,256]{2,1,0:T(8,128)S(1)}) custom-call(s32[32]{0:T(128)S(1)} %copy-done.5, s32[1]{0:T(128)} %bitcast.refs_1_, bf16[4,256,128]{2,1,0:T(8,128)(2,1)S(1)} %queries.1.refs_2_, bf16[2,256,256]{2,1,0:T(8,128)(2,1)S(1)} %collective-permute-done.1.refs_3_, ...), custom_call_target="tpu_custom_call" | custom-call | flops 98304 | bytes 65536 | tf_op jit(solution)/shard_map/attend/pallas_call | solution.py:275
  50.2 2.0 %attend.11 = (f32[4,256,128]{2,1,0:T(8,128)S(1)}, f32[4,256,256]{2,1,0:T(8,128)S(1)}) custom-call(s32[32]{0:T(128)S(1)} %copy-done.5, s32[1]{0:T(128)} %bitcast.refs_1_, bf16[4,256,128]{2,1,0:T(8,128)(2,1)S(1)} %queries.1.refs_2_, bf16[2,256,256]{2,1,0:T(8,128)(2,1)S(1)} %collective-permute-done.5.refs_3_, ...), custom_call_target="tpu_custom_call" | custom-call | flops 98304 | bytes 65536 | tf_op jit(solution)/shard_map/attend/pallas_call | solution.py:275
  52.2 1.3 %collective-permute-done.4.refs_4_ = bf16[1,256,256]{2,1,0:T(8,128)(2,1)S(1)} collective-permute-done((bf16[1,256,256]{2,1,0:T(8,128)(2,1)S(1)}, bf16[1,256,256]{2,1,0:T(8,128)(2,1)S(1)}, u32[]{:S(2)}, u32[]{:S(2)}) %collective-permute-start.4) | collective-permute-done | bytes 131104 | tf_op jit(solution)/shard_map/ppermute | solution.py:330
  53.5 0.2 collective-permute-done.3.refs_3_
  53.7 2.1 %collective-permute-start.7 = (bf16[3,256,256]{2,1,0:T(8,128)(2,1)S(1)}, bf16[3,256,256]{2,1,0:T(8,128)(2,1)S(1)}, u32[]{:S(2)}, u32[]{:S(2)}) collective-permute-start(bf16[3,256,256]{2,1,0:T(8,128)(2,1)S(1)} %collective-permute-done.3.refs_3_), channel_id=1, source_target_pairs={{0,16},{8,120},{16,32},{24,8},{32,48},{40,24},{48,64},{56,40},{64,... | collective-permute-start | bytes 1179656 | tf_op jit(solution)/shard_map/ppermute | solution.py:330
  55.8 0.1 collective-permute-start.10
  55.9 0.5 collective-permute-start.9
  56.4 0.7 collective-permute-start.8
  57.1 2.4 %attend.12 = (f32[4,256,128]{2,1,0:T(8,128)S(1)}, f32[4,256,256]{2,1,0:T(8,128)S(1)}) custom-call(s32[32]{0:T(128)S(1)} %copy-done.5, s32[1]{0:T(128)} %bitcast.refs_1_, bf16[4,256,128]{2,1,0:T(8,128)(2,1)S(1)} %queries.1.refs_2_, bf16[3,256,256]{2,1,0:T(8,128)(2,1)S(1)} %collective-permute-done.3.refs_3_, ...), custom_call_target="tpu_custom_call" | custom-call | flops 131072 | bytes 65536 | tf_op jit(solution)/shard_map/attend/pallas_call | solution.py:275
  59.5 2.4 %attend.13 = (f32[4,256,128]{2,1,0:T(8,128)S(1)}, f32[4,256,256]{2,1,0:T(8,128)S(1)}) custom-call(s32[32]{0:T(128)S(1)} %copy-done.5, s32[1]{0:T(128)} %bitcast.refs_1_, bf16[4,256,128]{2,1,0:T(8,128)(2,1)S(1)} %queries.1.refs_2_, bf16[2,256,256]{2,1,0:T(8,128)(2,1)S(1)} %collective-permute-done.9.refs_3_, ...), custom_call_target="tpu_custom_call" | custom-call | flops 131072 | bytes 65536 | tf_op jit(solution)/shard_map/attend/pallas_call | solution.py:275
  61.9 0.0 collective-permute-done.8.refs_4_
  61.9 0.7 collective-permute-done.7.refs_3_
  62.7 1.9 %collective-permute-start.11 = (bf16[3,256,256]{2,1,0:T(8,128)(2,1)S(1)}, bf16[3,256,256]{2,1,0:T(8,128)(2,1)S(1)}, u32[]{:S(2)}, u32[]{:S(2)}) collective-permute-start(bf16[3,256,256]{2,1,0:T(8,128)(2,1)S(1)} %collective-permute-done.7.refs_3_), channel_id=1, source_target_pairs={{0,16},{8,120},{16,32},{24,8},{32,48},{40,24},{48,64},{56,40},{64,... | collective-permute-start | bytes 1179656 | tf_op jit(solution)/shard_map/ppermute | solution.py:330
  64.7 0.1 collective-permute-start.15
  64.8 0.5 collective-permute-start.14
  65.3 1.3 %collective-permute-start.12 = (bf16[1,256,256]{2,1,0:T(8,128)(2,1)S(1)}, bf16[1,256,256]{2,1,0:T(8,128)(2,1)S(1)}, u32[]{:S(2)}, u32[]{:S(2)}) collective-permute-start(bf16[1,256,256]{2,1,0:T(8,128)(2,1)S(1)} %get-tuple-element.106), channel_id=1, source_target_pairs={{0,128},{8,136},{16,144},{24,152},{32,160},{40,168},{48,176},{56,1... | collective-permute-start | bytes 393224 | tf_op jit(solution)/shard_map/ppermute | solution.py:330
  66.6 4.3 %collective-permute-start.13 = (bf16[1,256,256]{2,1,0:T(8,128)(2,1)S(1)}, bf16[1,256,256]{2,1,0:T(8,128)(2,1)S(1)}, u32[]{:S(2)}, u32[]{:S(2)}) collective-permute-start(bf16[1,256,256]{2,1,0:T(8,128)(2,1)S(1)} %get-tuple-element.105), channel_id=1, source_target_pairs={{0,32},{8,104},{16,48},{24,120},{32,64},{40,8},{48,80},{56,24},{64... | collective-permute-start | bytes 393224 | tf_op jit(solution)/shard_map/ppermute | solution.py:330
  70.9 2.4 %attend.14 = (f32[4,256,128]{2,1,0:T(8,128)S(1)}, f32[4,256,256]{2,1,0:T(8,128)S(1)}) custom-call(s32[32]{0:T(128)S(1)} %copy-done.5, s32[1]{0:T(128)} %bitcast.refs_1_, bf16[4,256,128]{2,1,0:T(8,128)(2,1)S(1)} %queries.1.refs_2_, bf16[3,256,256]{2,1,0:T(8,128)(2,1)S(1)} %collective-permute-done.7.refs_3_, ...), custom_call_target="tpu_custom_call" | custom-call | flops 131072 | bytes 65536 | tf_op jit(solution)/shard_map/attend/pallas_call | solution.py:275
  73.3 2.4 %attend.15 = (f32[4,256,128]{2,1,0:T(8,128)S(1)}, f32[4,256,256]{2,1,0:T(8,128)S(1)}) custom-call(s32[32]{0:T(128)S(1)} %copy-done.5, s32[1]{0:T(128)} %bitcast.refs_1_, bf16[4,256,128]{2,1,0:T(8,128)(2,1)S(1)} %queries.1.refs_2_, bf16[2,256,256]{2,1,0:T(8,128)(2,1)S(1)} %collective-permute-done.14.refs_3_, ...), custom_call_target="tpu_custom_call" | custom-call | flops 131072 | bytes 65536 | tf_op jit(solution)/shard_map/attend/pallas_call | solution.py:275
  75.7 1.4 %collective-permute-done.13.refs_5_ = bf16[1,256,256]{2,1,0:T(8,128)(2,1)S(1)} collective-permute-done((bf16[1,256,256]{2,1,0:T(8,128)(2,1)S(1)}, bf16[1,256,256]{2,1,0:T(8,128)(2,1)S(1)}, u32[]{:S(2)}, u32[]{:S(2)}) %collective-permute-start.13) | collective-permute-done | bytes 131104 | tf_op jit(solution)/shard_map/ppermute | solution.py:330
  77.2 0.1 collective-permute-start.16
  77.3 2.8 %attend.16 = (f32[4,256,128]{2,1,0:T(8,128)S(1)}, f32[4,256,256]{2,1,0:T(8,128)S(1)}) custom-call(s32[32]{0:T(128)S(1)} %copy-done.5, s32[1]{0:T(128)} %bitcast.refs_1_, bf16[4,256,128]{2,1,0:T(8,128)(2,1)S(1)} %queries.1.refs_2_, bf16[3,256,256]{2,1,0:T(8,128)(2,1)S(1)} %collective-permute-done.11.refs_3_, ...), custom_call_target="tpu_custom_call" | custom-call | flops 163840 | bytes 65536 | tf_op jit(solution)/shard_map/attend/pallas_call | solution.py:275
  80.1 2.2 %attend.17 = bf16[256,768]{1,0:T(8,128)(2,1)S(1)} custom-call(s32[32]{0:T(128)S(1)} %copy-done.5, s32[1]{0:T(128)} %bitcast.refs_1_, bf16[4,256,128]{2,1,0:T(8,128)(2,1)S(1)} %queries.1.refs_2_, bf16[3,256,256]{2,1,0:T(8,128)(2,1)S(1)} %collective-permute-done.16.refs_3_, f32[4,256,128]{2,1,0:T(8,128)S(1)} %get-tuple-element.103.refs_4_, ...), custom_call_target="tpu_custom_call" | custom-call | flops 98304 | bytes 65536 | tf_op jit(solution)/shard_map/attend/pallas_call | solution.py:275
  82.3 13.4 %all_to_all.16.parts = bf16[8,32,768]{2,1,0:T(8,128)(2,1)S(1)} all-to-all(bf16[8,32,768]{2,1,0:T(8,128)(2,1)S(1)} %bitcast.17), channel_id=1, replica_groups=mesh['blk'=32,'head'=8] {'head'}, dimensions={0} | all-to-all | bytes 786432 | tf_op jit(solution)/shard_map/all_to_all | solution.py:409
  95.7 0.7 total.1
  (34 shorter events, 0.3 us)
Async XLA Ops:
  5.8 7.1 %copy-start.8 = (f32[768]{0:T(1024)S(1)}, f32[768]{0:T(1024)}, u32[]{:S(2)}) copy-start(f32[768]{0:T(1024)} %param.24) | copy-start | bytes 9220
  5.8 16.7 %copy-start = (bf16[1,16,16,768]{3,2,1,0:T(8,128)(2,1)S(1)}, bf16[1,16,16,768]{3,2,1,0:T(8,128)(2,1)}, u32[]{:S(2)}) copy-start(bf16[1,16,16,768]{3,2,1,0:T(8,128)(2,1)} %param.15) | copy-start | bytes 1179652
  5.8 16.7 %all-to-all-start = ((bf16[8,32,768]{2,1,0:T(8,128)(2,1)}), bf16[8,32,768]{2,1,0:T(8,128)(2,1)S(1)}, u32[]{:S(2)}, u32[]{:S(2)}) async-start(bf16[8,32,768]{2,1,0:T(8,128)(2,1)} %bitcast.6), calls=%async_computation | async-start | bytes 786432 | tf_op jit(solution)/shard_map/all_to_all | solution.py:350
  12.9 0.7 copy-start.7
  12.9 0.7 copy-start.6
  22.5 13.0 %copy-start.3 = (bf16[768,128]{1,0:T(8,128)(2,1)S(1)}, bf16[768,128]{1,0:T(8,128)(2,1)}, u32[]{:S(2)}) copy-start(bf16[768,128]{1,0:T(8,128)(2,1)} %wk.1) | copy-start | bytes 589828
  22.5 13.0 %copy-start.4 = (bf16[768,128]{1,0:T(8,128)(2,1)S(1)}, bf16[768,128]{1,0:T(8,128)(2,1)}, u32[]{:S(2)}) copy-start(bf16[768,128]{1,0:T(8,128)(2,1)} %wv.1) | copy-start | bytes 589828
  22.8 13.3 %copy-start.1 = (bf16[768,512]{1,0:T(8,128)(2,1)S(1)}, bf16[768,512]{1,0:T(8,128)(2,1)}, u32[]{:S(2)}) copy-start(bf16[768,512]{1,0:T(8,128)(2,1)} %wq.1) | copy-start | bytes 2359300
  35.6 0.7 copy-start.5
  35.9 1.4 %collective-permute-start = (bf16[1,256,256]{2,1,0:T(8,128)(2,1)S(1)}, bf16[1,256,256]{2,1,0:T(8,128)(2,1)S(1)}, u32[]{:S(2)}, u32[]{:S(2)}) collective-permute-start(bf16[1,256,256]{2,1,0:T(8,128)(2,1)S(1)} %key_values.1), channel_id=1, source_target_pairs={{0,8},{8,0},{16,24},{24,16},{32,40},{40,32},{48,56},{56,48},{64,72... | collective-permute-start | bytes 393224 | tf_op jit(solution)/shard_map/ppermute | solution.py:330
  37.4 7.0 %collective-permute-start.1 = (bf16[2,256,256]{2,1,0:T(8,128)(2,1)S(1)}, bf16[2,256,256]{2,1,0:T(8,128)(2,1)S(1)}, u32[]{:S(2)}, u32[]{:S(2)}) collective-permute-start(bf16[2,256,256]{2,1,0:T(8,128)(2,1)S(1)} %pad_maximum_fusion.2.refs_3_), channel_id=1, source_target_pairs={{0,16},{8,120},{16,32},{24,8},{32,48},{40,24},{48,64},{56,40},{64,... | collective-permute-start | bytes 786440 | tf_op jit(solution)/shard_map/ppermute | solution.py:330
  39.4 5.0 %collective-permute-start.2 = (bf16[1,256,256]{2,1,0:T(8,128)(2,1)S(1)}, bf16[1,256,256]{2,1,0:T(8,128)(2,1)S(1)}, u32[]{:S(2)}, u32[]{:S(2)}) collective-permute-start(bf16[1,256,256]{2,1,0:T(8,128)(2,1)S(1)} %key_values.1), channel_id=1, source_target_pairs={{0,128},{8,136},{16,144},{24,152},{32,160},{40,168},{48,176},{56,1... | collective-permute-start | bytes 393224 | tf_op jit(solution)/shard_map/ppermute | solution.py:330
  44.4 9.3 %collective-permute-start.3 = (bf16[3,256,256]{2,1,0:T(8,128)(2,1)S(1)}, bf16[3,256,256]{2,1,0:T(8,128)(2,1)S(1)}, u32[]{:S(2)}, u32[]{:S(2)}) collective-permute-start(bf16[3,256,256]{2,1,0:T(8,128)(2,1)S(1)} %pad_maximum_fusion), channel_id=1, source_target_pairs={{0,16},{8,120},{16,32},{24,8},{32,48},{40,24},{48,64},{56,40},{64,... | collective-permute-start | bytes 1179656 | tf_op jit(solution)/shard_map/ppermute | solution.py:330
  46.4 3.8 %collective-permute-start.5 = (bf16[2,256,256]{2,1,0:T(8,128)(2,1)S(1)}, bf16[2,256,256]{2,1,0:T(8,128)(2,1)S(1)}, u32[]{:S(2)}, u32[]{:S(2)}) collective-permute-start(bf16[2,256,256]{2,1,0:T(8,128)(2,1)S(1)} %collective-permute-done.1.refs_3_), channel_id=1, source_target_pairs={{0,8},{8,0},{16,24},{24,16},{32,40},{40,32},{48,56},{56,48},{64,72... | collective-permute-start | bytes 786440 | tf_op jit(solution)/shard_map/ppermute | solution.py:330
  47.3 2.9 %collective-permute-start.6 = (bf16[1,256,256]{2,1,0:T(8,128)(2,1)S(1)}, bf16[1,256,256]{2,1,0:T(8,128)(2,1)S(1)}, u32[]{:S(2)}, u32[]{:S(2)}) collective-permute-start(bf16[1,256,256]{2,1,0:T(8,128)(2,1)S(1)} %collective-permute-done.2.refs_4_), channel_id=1, source_target_pairs={{0,8},{8,0},{16,24},{24,16},{32,40},{40,32},{48,56},{56,48},{64,72... | collective-permute-start | bytes 393224 | tf_op jit(solution)/shard_map/ppermute | solution.py:330
  47.3 6.2 %collective-permute-start.4 = (bf16[1,256,256]{2,1,0:T(8,128)(2,1)S(1)}, bf16[1,256,256]{2,1,0:T(8,128)(2,1)S(1)}, u32[]{:S(2)}, u32[]{:S(2)}) collective-permute-start(bf16[1,256,256]{2,1,0:T(8,128)(2,1)S(1)} %slice.25), channel_id=1, source_target_pairs={{0,128},{8,136},{16,144},{24,152},{32,160},{40,168},{48,176},{56,1... | collective-permute-start | bytes 393224 | tf_op jit(solution)/shard_map/ppermute | solution.py:330
  53.7 9.0 %collective-permute-start.7 = (bf16[3,256,256]{2,1,0:T(8,128)(2,1)S(1)}, bf16[3,256,256]{2,1,0:T(8,128)(2,1)S(1)}, u32[]{:S(2)}, u32[]{:S(2)}) collective-permute-start(bf16[3,256,256]{2,1,0:T(8,128)(2,1)S(1)} %collective-permute-done.3.refs_3_), channel_id=1, source_target_pairs={{0,16},{8,120},{16,32},{24,8},{32,48},{40,24},{48,64},{56,40},{64,... | collective-permute-start | bytes 1179656 | tf_op jit(solution)/shard_map/ppermute | solution.py:330
  55.8 3.7 %collective-permute-start.10 = (bf16[2,256,256]{2,1,0:T(8,128)(2,1)S(1)}, bf16[2,256,256]{2,1,0:T(8,128)(2,1)S(1)}, u32[]{:S(2)}, u32[]{:S(2)}) collective-permute-start(bf16[2,256,256]{2,1,0:T(8,128)(2,1)S(1)} %pad_maximum_fusion.3), channel_id=1, source_target_pairs={{0,8},{8,0},{16,24},{24,16},{32,40},{40,32},{48,56},{56,48},{64,72... | collective-permute-start | bytes 786440 | tf_op jit(solution)/shard_map/ppermute | solution.py:330
  55.9 3.6 %collective-permute-start.9 = (bf16[2,256,256]{2,1,0:T(8,128)(2,1)S(1)}, bf16[2,256,256]{2,1,0:T(8,128)(2,1)S(1)}, u32[]{:S(2)}, u32[]{:S(2)}) collective-permute-start(bf16[2,256,256]{2,1,0:T(8,128)(2,1)S(1)} %slice.27), channel_id=1, source_target_pairs={{0,8},{8,0},{16,24},{24,16},{32,40},{40,32},{48,56},{56,48},{64,72... | collective-permute-start | bytes 786440 | tf_op jit(solution)/shard_map/ppermute | solution.py:330
  56.4 5.5 %collective-permute-start.8 = (bf16[1,256,256]{2,1,0:T(8,128)(2,1)S(1)}, bf16[1,256,256]{2,1,0:T(8,128)(2,1)S(1)}, u32[]{:S(2)}, u32[]{:S(2)}) collective-permute-start(bf16[1,256,256]{2,1,0:T(8,128)(2,1)S(1)} %get-tuple-element.108), channel_id=1, source_target_pairs={{0,128},{8,136},{16,144},{24,152},{32,160},{40,168},{48,176},{56,1... | collective-permute-start | bytes 393224 | tf_op jit(solution)/shard_map/ppermute | solution.py:330
  62.7 14.5 %collective-permute-start.11 = (bf16[3,256,256]{2,1,0:T(8,128)(2,1)S(1)}, bf16[3,256,256]{2,1,0:T(8,128)(2,1)S(1)}, u32[]{:S(2)}, u32[]{:S(2)}) collective-permute-start(bf16[3,256,256]{2,1,0:T(8,128)(2,1)S(1)} %collective-permute-done.7.refs_3_), channel_id=1, source_target_pairs={{0,16},{8,120},{16,32},{24,8},{32,48},{40,24},{48,64},{56,40},{64,... | collective-permute-start | bytes 1179656 | tf_op jit(solution)/shard_map/ppermute | solution.py:330
  64.7 8.6 %collective-permute-start.15 = (bf16[2,256,256]{2,1,0:T(8,128)(2,1)S(1)}, bf16[2,256,256]{2,1,0:T(8,128)(2,1)S(1)}, u32[]{:S(2)}, u32[]{:S(2)}) collective-permute-start(bf16[2,256,256]{2,1,0:T(8,128)(2,1)S(1)} %pad_maximum_fusion.4), channel_id=1, source_target_pairs={{0,8},{8,0},{16,24},{24,16},{32,40},{40,32},{48,56},{56,48},{64,72... | collective-permute-start | bytes 786440 | tf_op jit(solution)/shard_map/ppermute | solution.py:330
  64.8 8.5 %collective-permute-start.14 = (bf16[2,256,256]{2,1,0:T(8,128)(2,1)S(1)}, bf16[2,256,256]{2,1,0:T(8,128)(2,1)S(1)}, u32[]{:S(2)}, u32[]{:S(2)}) collective-permute-start(bf16[2,256,256]{2,1,0:T(8,128)(2,1)S(1)} %slice.31), channel_id=1, source_target_pairs={{0,8},{8,0},{16,24},{24,16},{32,40},{40,32},{48,56},{56,48},{64,72... | collective-permute-start | bytes 786440 | tf_op jit(solution)/shard_map/ppermute | solution.py:330
  65.3 10.4 %collective-permute-start.12 = (bf16[1,256,256]{2,1,0:T(8,128)(2,1)S(1)}, bf16[1,256,256]{2,1,0:T(8,128)(2,1)S(1)}, u32[]{:S(2)}, u32[]{:S(2)}) collective-permute-start(bf16[1,256,256]{2,1,0:T(8,128)(2,1)S(1)} %get-tuple-element.106), channel_id=1, source_target_pairs={{0,128},{8,136},{16,144},{24,152},{32,160},{40,168},{48,176},{56,1... | collective-permute-start | bytes 393224 | tf_op jit(solution)/shard_map/ppermute | solution.py:330
  66.6 10.5 %collective-permute-start.13 = (bf16[1,256,256]{2,1,0:T(8,128)(2,1)S(1)}, bf16[1,256,256]{2,1,0:T(8,128)(2,1)S(1)}, u32[]{:S(2)}, u32[]{:S(2)}) collective-permute-start(bf16[1,256,256]{2,1,0:T(8,128)(2,1)S(1)} %get-tuple-element.105), channel_id=1, source_target_pairs={{0,32},{8,104},{16,48},{24,120},{32,64},{40,8},{48,80},{56,24},{64... | collective-permute-start | bytes 393224 | tf_op jit(solution)/shard_map/ppermute | solution.py:330
  77.2 2.9 %copy-start.2 = (bf16[512,768]{1,0:T(8,128)(2,1)S(1)}, bf16[512,768]{1,0:T(8,128)(2,1)}, u32[]{:S(2)}) copy-start(bf16[512,768]{1,0:T(8,128)(2,1)} %refs_6_.1) | copy-start | bytes 2359300
  77.2 2.9 %collective-permute-start.16 = (bf16[3,256,256]{2,1,0:T(8,128)(2,1)S(1)}, bf16[3,256,256]{2,1,0:T(8,128)(2,1)S(1)}, u32[]{:S(2)}, u32[]{:S(2)}) collective-permute-start(bf16[3,256,256]{2,1,0:T(8,128)(2,1)S(1)} %pad_maximum_fusion.1), channel_id=1, source_target_pairs={{0,8},{8,0},{16,24},{24,16},{32,40},{40,32},{48,56},{56,48},{64,72... | collective-permute-start | bytes 1179656 | tf_op jit(solution)/shard_map/ppermute | solution.py:330

commit v8 on v7

--- a/solution.py
+++ b/solution.py
@@ -390,22 +390,18 @@
     carry = both_cores([(two, places), (one_other, [place])], halves(two, places, one_other, place), carry)
     three, two_other, carry = hold((three, two_other, carry))
 
-    four = along_z(three)
+    half = depth // 2
+    four = along_z(three[1:3])
     three_other = flip_y(three[1:2])
     far_other = along_z(three[2:3], 2)
-    places, place = [(0, 3, 0), (0, 3, 1), (1, 2, 0)], (1, 2, 1)
-    carry = both_cores([(three, places), (two_other, [place])], halves(three, places, two_other, place), carry)
+    joined = jnp.concatenate([three, two_other])
+    pieces = [(joined, [(0, 3, 0), (0, 3, 1), (1, 2, 0), (1, 2, 1)])]
+    carry = both_cores(pieces, pieces, carry)
     four, three_other, far_other, carry = hold((four, three_other, far_other, carry))
 
-    half = depth // 2
-    places = [(1, 3, 0), (1, 3, 1), (1, half, 0)]
-    pieces = [
-        (four, [(0, half, 0), (0, half, 1), places[0]]),
-        (three_other, [places[1]]),
-        (far_other, [places[2]]),
-    ]
-    shared = jnp.concatenate([four[2:3], three_other, far_other])
-    (mixed,) = both_cores(pieces, [(shared, places)], carry, w_out)
+    joined = jnp.concatenate([four, three_other, far_other])
+    pieces = [(joined, [(0, half, 1), (1, 3, 0), (1, 3, 1), (1, half, 0)])]
+    (mixed,) = both_cores(pieces, pieces, carry, w_out)
     parts = lax.all_to_all(mixed.reshape(groups, share, channels), "head", 0, 0, tiled=True)
     return total_of(parts)
 

time: 96.6 us -> 95.5 us (0.989)
    ppermute x17 -> x16, waiting for transfers between devices: 6.73 us -> 5.93 us  [moved(): return lax.ppermute(array, 'blk', [(i, target(i)) for i in range(blocks)])]
    ppermute x17 -> x16, starting transfers between devices: 18.2 us -> 17.8 us  [moved(): return lax.ppermute(array, 'blk', [(i, target(i)) for i in range(blocks)])]
  transfers between devices with their start and end apart: 18 -> 17, of which waited for: 7 -> 7; matrix products, arithmetic and copies ran while one was open for 0% -> 0% of each run, Pallas kernels for 19% -> 19%
where the time goes in v8:
time: 95.5 us; the launch traced here: 95.2 us
  Pallas kernels  27.8 us (29%)
  blocking collectives  26.2 us (27%)
  starting transfers between devices  24.9 us (26%)
  waiting for transfers between devices  14.9 us (16%)
  local copies, waits for them, and re-layouts  1.07 us (1%)
    pallas_call x9, Pallas kernels, attend(): pl.pallas_call(functools.partial(attend_kernel, carry is None, w_out is n...  19.8 us
    ppermute x16, starting transfers between devices, moved(): return lax.ppermute(array, 'blk', [(i, target(i)) for i in range(blocks)])  17.8 us
    all_to_all x1, blocking collectives, per_device(): lax.all_to_all(mixed.reshape(groups, share, channels), 'head', 0, 0, tile...  13.4 us
    all_to_all x1, blocking collectives, per_device(): lax.all_to_all(copies, 'head', 0, 0, tiled=True).reshape(rows, channels)  12.8 us
    all_to_all x1, waiting for transfers between devices, per_device(): lax.all_to_all(partial.reshape(groups, share, channels), 'head', 0, 0, ti...  8.93 us
    all_to_all x1, starting transfers between devices, per_device(): lax.all_to_all(partial.reshape(groups, share, channels), 'head', 0, 0, ti...  7.07 us
    ppermute x16, waiting for transfers between devices, moved(): return lax.ppermute(array, 'blk', [(i, target(i)) for i in range(blocks)])  5.93 us
    pallas_call x1, Pallas kernels, mlp(): pl.pallas_call(mlp_kernel, out_shape=jax.ShapeDtypeStruct((rows, channels...  5.75 us
  transfers between devices with their start and end apart: 17, of which 7 were waited for; matrix products, arithmetic and copies ran while one was open for 0% of the time, Pallas kernels for 19%

profile of v8, /device:TPU:32, one launch (start us, length us, event | category | flops | bytes accessed | tf_op | source)
XLA Modules:
  0.0 95.2 jit_solution(2366388106512727739)
XLA Ops:
  0.0 5.7 %conv_mlp.1 = bf16[256,768]{1,0:T(8,128)(2,1)} custom-call(bf16[16,16,768]{2,1,0:T(8,128)(2,1)} %bitcast.15, f32[7,7,768]{2,1,0:T(8,128)} %dw_hbm.1, f32[6,128]{1,0:T(8,128)} %bitcast.18, f32[6,128]{1,0:T(8,128)} %bitcast.19, bf16[768,384]{1,0:T(8,128)(2,1)} %w1_hbm.1, f32[3,128]{1,0:T(4,128)} %bitcast.23, bf16[384,768]{1,0:T(8,128)(2,1)} %w2_hbm.1), custom_call_target="tpu_custom_call" | custom-call | tf_op jit(solution)/shard_map/conv_mlp/pallas_call | solution.py:108
  5.8 0.0 copy-start.8
  5.8 0.0 copy-start
  5.8 7.1 %all-to-all-start = ((bf16[8,32,768]{2,1,0:T(8,128)(2,1)}), bf16[8,32,768]{2,1,0:T(8,128)(2,1)S(1)}, u32[]{:S(2)}, u32[]{:S(2)}) async-start(bf16[8,32,768]{2,1,0:T(8,128)(2,1)} %bitcast.6), calls=%async_computation | async-start | bytes 786432 | tf_op jit(solution)/shard_map/all_to_all | solution.py:350
  12.9 0.0 copy-start.6
  12.9 0.7 copy-done.7
  13.5 0.0 copy-done.6
  13.6 8.9 %all-to-all-done.parts = bf16[8,32,768]{2,1,0:T(8,128)(2,1)S(1)} async-done(((bf16[8,32,768]{2,1,0:T(8,128)(2,1)}), bf16[8,32,768]{2,1,0:T(8,128)(2,1)S(1)}, u32[]{:S(2)}, u32[]{:S(2)}) %all-to-all-start) | async-done | bytes 393248 | tf_op jit(solution)/shard_map/all_to_all | solution.py:350
  22.5 0.2 block_norm.1
  22.8 0.0 copy-start.1
  22.8 12.8 %all_to_all.15 = bf16[8,32,768]{2,1,0:T(8,128)(2,1)S(1)} all-to-all(bf16[8,32,768]{2,1,0:T(8,128)(2,1)S(1)} %block_norm.1), channel_id=1, replica_groups=mesh['blk'=32,'head'=8] {'head'}, dimensions={0} | all-to-all | bytes 786432 | tf_op jit(solution)/shard_map/all_to_all | solution.py:352
  35.6 0.4 key_values.1
  35.9 0.1 collective-permute-start
  36.0 0.2 copy-done.5
  36.2 0.9 queries.1.refs_2_
  37.1 0.2 collective-permute-done
  37.4 2.0 %collective-permute-start.1 = (bf16[2,256,256]{2,1,0:T(8,128)(2,1)S(1)}, bf16[2,256,256]{2,1,0:T(8,128)(2,1)S(1)}, u32[]{:S(2)}, u32[]{:S(2)}) collective-permute-start(bf16[2,256,256]{2,1,0:T(8,128)(2,1)S(1)} %pad_maximum_fusion.1.refs_3_), channel_id=1, source_target_pairs={{0,16},{8,120},{16,32},{24,8},{32,48},{40,24},{48,64},{56,40},{64,... | collective-permute-start | bytes 786440 | tf_op jit(solution)/shard_map/ppermute | solution.py:330
  39.4 0.7 collective-permute-start.2
  40.1 1.5 %attend.9 = (f32[4,256,128]{2,1,0:T(8,128)S(1)}, f32[4,256,256]{2,1,0:T(8,128)S(1)}) custom-call(s32[32]{0:T(128)S(1)} %copy-done.5, s32[1]{0:T(128)} %bitcast.refs_1_, bf16[4,256,128]{2,1,0:T(8,128)(2,1)S(1)} %queries.1.refs_2_, bf16[2,256,256]{2,1,0:T(8,128)(2,1)S(1)} %pad_maximum_fusion.1.refs_3_), custom_call_target="tpu_custom_call" | custom-call | flops 65536 | bytes 65536 | tf_op jit(solution)/shard_map/attend/pallas_call | solution.py:275
  41.6 2.8 %collective-permute-done.2.refs_4_ = bf16[1,256,256]{2,1,0:T(8,128)(2,1)S(1)} collective-permute-done((bf16[1,256,256]{2,1,0:T(8,128)(2,1)S(1)}, bf16[1,256,256]{2,1,0:T(8,128)(2,1)S(1)}, u32[]{:S(2)}, u32[]{:S(2)}) %collective-permute-start.2) | collective-permute-done | bytes 131104 | tf_op jit(solution)/shard_map/ppermute | solution.py:330
  44.4 2.0 %collective-permute-start.3 = (bf16[3,256,256]{2,1,0:T(8,128)(2,1)S(1)}, bf16[3,256,256]{2,1,0:T(8,128)(2,1)S(1)}, u32[]{:S(2)}, u32[]{:S(2)}) collective-permute-start(bf16[3,256,256]{2,1,0:T(8,128)(2,1)S(1)} %pad_maximum_fusion), channel_id=1, source_target_pairs={{0,16},{8,120},{16,32},{24,8},{32,48},{40,24},{48,64},{56,40},{64,... | collective-permute-start | bytes 1179656 | tf_op jit(solution)/shard_map/ppermute | solution.py:330
  46.4 0.9 collective-permute-start.5
  47.3 0.9 collective-permute-start.4
  48.2 1.9 %attend.10 = (f32[4,256,128]{2,1,0:T(8,128)S(1)}, f32[4,256,256]{2,1,0:T(8,128)S(1)}) custom-call(s32[32]{0:T(128)S(1)} %copy-done.5, s32[1]{0:T(128)} %bitcast.refs_1_, bf16[4,256,128]{2,1,0:T(8,128)(2,1)S(1)} %queries.1.refs_2_, bf16[2,256,256]{2,1,0:T(8,128)(2,1)S(1)} %collective-permute-done.1.refs_3_, ...), custom_call_target="tpu_custom_call" | custom-call | flops 98304 | bytes 65536 | tf_op jit(solution)/shard_map/attend/pallas_call | solution.py:275
  50.2 2.0 %attend.11 = (f32[4,256,128]{2,1,0:T(8,128)S(1)}, f32[4,256,256]{2,1,0:T(8,128)S(1)}) custom-call(s32[32]{0:T(128)S(1)} %copy-done.5, s32[1]{0:T(128)} %bitcast.refs_1_, bf16[4,256,128]{2,1,0:T(8,128)(2,1)S(1)} %queries.1.refs_2_, bf16[2,256,256]{2,1,0:T(8,128)(2,1)S(1)} %collective-permute-done.5.refs_3_, ...), custom_call_target="tpu_custom_call" | custom-call | flops 98304 | bytes 65536 | tf_op jit(solution)/shard_map/attend/pallas_call | solution.py:275
  52.2 1.3 %collective-permute-done.4.refs_4_ = bf16[1,256,256]{2,1,0:T(8,128)(2,1)S(1)} collective-permute-done((bf16[1,256,256]{2,1,0:T(8,128)(2,1)S(1)}, bf16[1,256,256]{2,1,0:T(8,128)(2,1)S(1)}, u32[]{:S(2)}, u32[]{:S(2)}) %collective-permute-start.4) | collective-permute-done | bytes 131104 | tf_op jit(solution)/shard_map/ppermute | solution.py:330
  53.5 0.2 collective-permute-done.3.refs_3_
  53.7 2.1 %collective-permute-start.7 = (bf16[3,256,256]{2,1,0:T(8,128)(2,1)S(1)}, bf16[3,256,256]{2,1,0:T(8,128)(2,1)S(1)}, u32[]{:S(2)}, u32[]{:S(2)}) collective-permute-start(bf16[3,256,256]{2,1,0:T(8,128)(2,1)S(1)} %collective-permute-done.3.refs_3_), channel_id=1, source_target_pairs={{0,16},{8,120},{16,32},{24,8},{32,48},{40,24},{48,64},{56,40},{64,... | collective-permute-start | bytes 1179656 | tf_op jit(solution)/shard_map/ppermute | solution.py:330
  55.8 0.1 collective-permute-start.10
  55.9 0.5 collective-permute-start.9
  56.4 0.7 collective-permute-start.8
  57.1 2.4 %attend.12 = (f32[4,256,128]{2,1,0:T(8,128)S(1)}, f32[4,256,256]{2,1,0:T(8,128)S(1)}) custom-call(s32[32]{0:T(128)S(1)} %copy-done.5, s32[1]{0:T(128)} %bitcast.refs_1_, bf16[4,256,128]{2,1,0:T(8,128)(2,1)S(1)} %queries.1.refs_2_, bf16[3,256,256]{2,1,0:T(8,128)(2,1)S(1)} %collective-permute-done.3.refs_3_, ...), custom_call_target="tpu_custom_call" | custom-call | flops 131072 | bytes 65536 | tf_op jit(solution)/shard_map/attend/pallas_call | solution.py:275
  59.5 2.4 %attend.13 = (f32[4,256,128]{2,1,0:T(8,128)S(1)}, f32[4,256,256]{2,1,0:T(8,128)S(1)}) custom-call(s32[32]{0:T(128)S(1)} %copy-done.5, s32[1]{0:T(128)} %bitcast.refs_1_, bf16[4,256,128]{2,1,0:T(8,128)(2,1)S(1)} %queries.1.refs_2_, bf16[2,256,256]{2,1,0:T(8,128)(2,1)S(1)} %collective-permute-done.9.refs_3_, ...), custom_call_target="tpu_custom_call" | custom-call | flops 131072 | bytes 65536 | tf_op jit(solution)/shard_map/attend/pallas_call | solution.py:275
  61.9 0.0 collective-permute-done.8
  61.9 0.7 collective-permute-done.7
  62.7 0.1 collective-permute-start.14
  62.8 2.0 %collective-permute-start.11 = (bf16[2,256,256]{2,1,0:T(8,128)(2,1)S(1)}, bf16[2,256,256]{2,1,0:T(8,128)(2,1)S(1)}, u32[]{:S(2)}, u32[]{:S(2)}) collective-permute-start(bf16[2,256,256]{2,1,0:T(8,128)(2,1)S(1)} %slice.25), channel_id=1, source_target_pairs={{0,16},{8,120},{16,32},{24,8},{32,48},{40,24},{48,64},{56,40},{64,... | collective-permute-start | bytes 786440 | tf_op jit(solution)/shard_map/ppermute | solution.py:330
  64.8 5.1 %collective-permute-start.13 = (bf16[1,256,256]{2,1,0:T(8,128)(2,1)S(1)}, bf16[1,256,256]{2,1,0:T(8,128)(2,1)S(1)}, u32[]{:S(2)}, u32[]{:S(2)}) collective-permute-start(bf16[1,256,256]{2,1,0:T(8,128)(2,1)S(1)} %get-tuple-element.103), channel_id=1, source_target_pairs={{0,32},{8,104},{16,48},{24,120},{32,64},{40,8},{48,80},{56,24},{64... | collective-permute-start | bytes 393224 | tf_op jit(solution)/shard_map/ppermute | solution.py:330
  69.9 0.7 collective-permute-start.12
  70.6 2.4 %attend.14 = (f32[4,256,128]{2,1,0:T(8,128)S(1)}, f32[4,256,256]{2,1,0:T(8,128)S(1)}) custom-call(s32[32]{0:T(128)S(1)} %copy-done.5, s32[1]{0:T(128)} %bitcast.refs_1_, bf16[4,256,128]{2,1,0:T(8,128)(2,1)S(1)} %queries.1.refs_2_, bf16[4,256,256]{2,1,0:T(8,128)(2,1)S(1)} %constant_dynamic-update-slice_fusion.refs_3_, ...), custom_call_target="tpu_custom_call" | custom-call | flops 131072 | bytes 65536 | tf_op jit(solution)/shard_map/attend/pallas_call | solution.py:275
  73.0 2.4 %attend.15 = (f32[4,256,128]{2,1,0:T(8,128)S(1)}, f32[4,256,256]{2,1,0:T(8,128)S(1)}) custom-call(s32[32]{0:T(128)S(1)} %copy-done.5, s32[1]{0:T(128)} %bitcast.refs_1_, bf16[4,256,128]{2,1,0:T(8,128)(2,1)S(1)} %queries.1.refs_2_, bf16[4,256,256]{2,1,0:T(8,128)(2,1)S(1)} %collective-permute-done.14.refs_3_, f32[4,256,128]{2,1,0:T(8,128)S(1)} %get-tuple-element.89.refs_4_, ...), custom_call_target="tpu_custom_call" | custom-call | flops 131072 | bytes 65536 | tf_op jit(solution)/shard_map/attend/pallas_call | solution.py:275
  75.3 0.6 collective-permute-done.13
  76.0 0.0 copy-start.2
  76.0 0.1 collective-permute-start.15
  76.1 2.4 %attend.16 = (f32[4,256,128]{2,1,0:T(8,128)S(1)}, f32[4,256,256]{2,1,0:T(8,128)S(1)}) custom-call(s32[32]{0:T(128)S(1)} %copy-done.5, s32[1]{0:T(128)} %bitcast.refs_1_, bf16[4,256,128]{2,1,0:T(8,128)(2,1)S(1)} %queries.1.refs_2_, bf16[4,256,256]{2,1,0:T(8,128)(2,1)S(1)} %constant_dynamic-update-slice_fusion.2.refs_3_, ...), custom_call_target="tpu_custom_call" | custom-call | flops 131072 | bytes 65536 | tf_op jit(solution)/shard_map/attend/pallas_call | solution.py:275
  78.5 2.6 %attend.17 = bf16[256,768]{1,0:T(8,128)(2,1)S(1)} custom-call(s32[32]{0:T(128)S(1)} %copy-done.5, s32[1]{0:T(128)} %bitcast.refs_1_, bf16[4,256,128]{2,1,0:T(8,128)(2,1)S(1)} %queries.1.refs_2_, bf16[4,256,256]{2,1,0:T(8,128)(2,1)S(1)} %collective-permute-done.15.refs_3_, f32[4,256,128]{2,1,0:T(8,128)S(1)} %get-tuple-element.101.refs_4_, ...), custom_call_target="tpu_custom_call" | custom-call | flops 131072 | bytes 65536 | tf_op jit(solution)/shard_map/attend/pallas_call | solution.py:275
  81.1 13.4 %all_to_all.16.parts = bf16[8,32,768]{2,1,0:T(8,128)(2,1)S(1)} all-to-all(bf16[8,32,768]{2,1,0:T(8,128)(2,1)S(1)} %bitcast.17), channel_id=1, replica_groups=mesh['blk'=32,'head'=8] {'head'}, dimensions={0} | all-to-all | bytes 786432 | tf_op jit(solution)/shard_map/all_to_all | solution.py:405
  94.5 0.7 total.1
  (34 shorter events, 0.3 us)
Async XLA Ops:
  5.8 7.1 %copy-start.8 = (f32[768]{0:T(1024)S(1)}, f32[768]{0:T(1024)}, u32[]{:S(2)}) copy-start(f32[768]{0:T(1024)} %param.24) | copy-start | bytes 9220
  5.8 16.7 %copy-start = (bf16[1,16,16,768]{3,2,1,0:T(8,128)(2,1)S(1)}, bf16[1,16,16,768]{3,2,1,0:T(8,128)(2,1)}, u32[]{:S(2)}) copy-start(bf16[1,16,16,768]{3,2,1,0:T(8,128)(2,1)} %param.15) | copy-start | bytes 1179652
  5.8 16.7 %all-to-all-start = ((bf16[8,32,768]{2,1,0:T(8,128)(2,1)}), bf16[8,32,768]{2,1,0:T(8,128)(2,1)S(1)}, u32[]{:S(2)}, u32[]{:S(2)}) async-start(bf16[8,32,768]{2,1,0:T(8,128)(2,1)} %bitcast.6), calls=%async_computation | async-start | bytes 786432 | tf_op jit(solution)/shard_map/all_to_all | solution.py:350
  12.9 0.7 copy-start.7
  12.9 0.7 copy-start.6
  22.5 13.0 %copy-start.3 = (bf16[768,128]{1,0:T(8,128)(2,1)S(1)}, bf16[768,128]{1,0:T(8,128)(2,1)}, u32[]{:S(2)}) copy-start(bf16[768,128]{1,0:T(8,128)(2,1)} %wk.1) | copy-start | bytes 589828
  22.5 13.0 %copy-start.4 = (bf16[768,128]{1,0:T(8,128)(2,1)S(1)}, bf16[768,128]{1,0:T(8,128)(2,1)}, u32[]{:S(2)}) copy-start(bf16[768,128]{1,0:T(8,128)(2,1)} %wv.1) | copy-start | bytes 589828
  22.8 13.3 %copy-start.1 = (bf16[768,512]{1,0:T(8,128)(2,1)S(1)}, bf16[768,512]{1,0:T(8,128)(2,1)}, u32[]{:S(2)}) copy-start(bf16[768,512]{1,0:T(8,128)(2,1)} %wq.1) | copy-start | bytes 2359300
  35.6 0.7 copy-start.5
  35.9 1.4 %collective-permute-start = (bf16[1,256,256]{2,1,0:T(8,128)(2,1)S(1)}, bf16[1,256,256]{2,1,0:T(8,128)(2,1)S(1)}, u32[]{:S(2)}, u32[]{:S(2)}) collective-permute-start(bf16[1,256,256]{2,1,0:T(8,128)(2,1)S(1)} %key_values.1), channel_id=1, source_target_pairs={{0,8},{8,0},{16,24},{24,16},{32,40},{40,32},{48,56},{56,48},{64,72... | collective-permute-start | bytes 393224 | tf_op jit(solution)/shard_map/ppermute | solution.py:330
  37.4 7.0 %collective-permute-start.1 = (bf16[2,256,256]{2,1,0:T(8,128)(2,1)S(1)}, bf16[2,256,256]{2,1,0:T(8,128)(2,1)S(1)}, u32[]{:S(2)}, u32[]{:S(2)}) collective-permute-start(bf16[2,256,256]{2,1,0:T(8,128)(2,1)S(1)} %pad_maximum_fusion.1.refs_3_), channel_id=1, source_target_pairs={{0,16},{8,120},{16,32},{24,8},{32,48},{40,24},{48,64},{56,40},{64,... | collective-permute-start | bytes 786440 | tf_op jit(solution)/shard_map/ppermute | solution.py:330
  39.4 5.0 %collective-permute-start.2 = (bf16[1,256,256]{2,1,0:T(8,128)(2,1)S(1)}, bf16[1,256,256]{2,1,0:T(8,128)(2,1)S(1)}, u32[]{:S(2)}, u32[]{:S(2)}) collective-permute-start(bf16[1,256,256]{2,1,0:T(8,128)(2,1)S(1)} %key_values.1), channel_id=1, source_target_pairs={{0,128},{8,136},{16,144},{24,152},{32,160},{40,168},{48,176},{56,1... | collective-permute-start | bytes 393224 | tf_op jit(solution)/shard_map/ppermute | solution.py:330
  44.4 9.3 %collective-permute-start.3 = (bf16[3,256,256]{2,1,0:T(8,128)(2,1)S(1)}, bf16[3,256,256]{2,1,0:T(8,128)(2,1)S(1)}, u32[]{:S(2)}, u32[]{:S(2)}) collective-permute-start(bf16[3,256,256]{2,1,0:T(8,128)(2,1)S(1)} %pad_maximum_fusion), channel_id=1, source_target_pairs={{0,16},{8,120},{16,32},{24,8},{32,48},{40,24},{48,64},{56,40},{64,... | collective-permute-start | bytes 1179656 | tf_op jit(solution)/shard_map/ppermute | solution.py:330
  46.4 3.8 %collective-permute-start.5 = (bf16[2,256,256]{2,1,0:T(8,128)(2,1)S(1)}, bf16[2,256,256]{2,1,0:T(8,128)(2,1)S(1)}, u32[]{:S(2)}, u32[]{:S(2)}) collective-permute-start(bf16[2,256,256]{2,1,0:T(8,128)(2,1)S(1)} %collective-permute-done.1.refs_3_), channel_id=1, source_target_pairs={{0,8},{8,0},{16,24},{24,16},{32,40},{40,32},{48,56},{56,48},{64,72... | collective-permute-start | bytes 786440 | tf_op jit(solution)/shard_map/ppermute | solution.py:330
  47.3 2.9 %collective-permute-start.6 = (bf16[1,256,256]{2,1,0:T(8,128)(2,1)S(1)}, bf16[1,256,256]{2,1,0:T(8,128)(2,1)S(1)}, u32[]{:S(2)}, u32[]{:S(2)}) collective-permute-start(bf16[1,256,256]{2,1,0:T(8,128)(2,1)S(1)} %collective-permute-done.2.refs_4_), channel_id=1, source_target_pairs={{0,8},{8,0},{16,24},{24,16},{32,40},{40,32},{48,56},{56,48},{64,72... | collective-permute-start | bytes 393224 | tf_op jit(solution)/shard_map/ppermute | solution.py:330
  47.3 6.2 %collective-permute-start.4 = (bf16[1,256,256]{2,1,0:T(8,128)(2,1)S(1)}, bf16[1,256,256]{2,1,0:T(8,128)(2,1)S(1)}, u32[]{:S(2)}, u32[]{:S(2)}) collective-permute-start(bf16[1,256,256]{2,1,0:T(8,128)(2,1)S(1)} %slice.21), channel_id=1, source_target_pairs={{0,128},{8,136},{16,144},{24,152},{32,160},{40,168},{48,176},{56,1... | collective-permute-start | bytes 393224 | tf_op jit(solution)/shard_map/ppermute | solution.py:330
  53.7 9.0 %collective-permute-start.7 = (bf16[3,256,256]{2,1,0:T(8,128)(2,1)S(1)}, bf16[3,256,256]{2,1,0:T(8,128)(2,1)S(1)}, u32[]{:S(2)}, u32[]{:S(2)}) collective-permute-start(bf16[3,256,256]{2,1,0:T(8,128)(2,1)S(1)} %collective-permute-done.3.refs_3_), channel_id=1, source_target_pairs={{0,16},{8,120},{16,32},{24,8},{32,48},{40,24},{48,64},{56,40},{64,... | collective-permute-start | bytes 1179656 | tf_op jit(solution)/shard_map/ppermute | solution.py:330
  55.8 3.7 %collective-permute-start.10 = (bf16[2,256,256]{2,1,0:T(8,128)(2,1)S(1)}, bf16[2,256,256]{2,1,0:T(8,128)(2,1)S(1)}, u32[]{:S(2)}, u32[]{:S(2)}) collective-permute-start(bf16[2,256,256]{2,1,0:T(8,128)(2,1)S(1)} %pad_maximum_fusion.2), channel_id=1, source_target_pairs={{0,8},{8,0},{16,24},{24,16},{32,40},{40,32},{48,56},{56,48},{64,72... | collective-permute-start | bytes 786440 | tf_op jit(solution)/shard_map/ppermute | solution.py:330
  55.9 3.6 %collective-permute-start.9 = (bf16[2,256,256]{2,1,0:T(8,128)(2,1)S(1)}, bf16[2,256,256]{2,1,0:T(8,128)(2,1)S(1)}, u32[]{:S(2)}, u32[]{:S(2)}) collective-permute-start(bf16[2,256,256]{2,1,0:T(8,128)(2,1)S(1)} %slice.23), channel_id=1, source_target_pairs={{0,8},{8,0},{16,24},{24,16},{32,40},{40,32},{48,56},{56,48},{64,72... | collective-permute-start | bytes 786440 | tf_op jit(solution)/shard_map/ppermute | solution.py:330
  56.4 5.5 %collective-permute-start.8 = (bf16[1,256,256]{2,1,0:T(8,128)(2,1)S(1)}, bf16[1,256,256]{2,1,0:T(8,128)(2,1)S(1)}, u32[]{:S(2)}, u32[]{:S(2)}) collective-permute-start(bf16[1,256,256]{2,1,0:T(8,128)(2,1)S(1)} %get-tuple-element.106), channel_id=1, source_target_pairs={{0,128},{8,136},{16,144},{24,152},{32,160},{40,168},{48,176},{56,1... | collective-permute-start | bytes 393224 | tf_op jit(solution)/shard_map/ppermute | solution.py:330
  62.7 10.3 %collective-permute-start.14 = (bf16[4,256,256]{2,1,0:T(8,128)(2,1)S(1)}, bf16[4,256,256]{2,1,0:T(8,128)(2,1)S(1)}, u32[]{:S(2)}, u32[]{:S(2)}) collective-permute-start(bf16[4,256,256]{2,1,0:T(8,128)(2,1)S(1)} %constant_dynamic-update-slice_fusion.refs_3_), channel_id=1, source_target_pairs={{0,8},{8,0},{16,24},{24,16},{32,40},{40,32},{48,56},{56,48},{64,72... | collective-permute-start | bytes 1572872 | tf_op jit(solution)/shard_map/ppermute | solution.py:330
  62.8 13.1 %collective-permute-start.11 = (bf16[2,256,256]{2,1,0:T(8,128)(2,1)S(1)}, bf16[2,256,256]{2,1,0:T(8,128)(2,1)S(1)}, u32[]{:S(2)}, u32[]{:S(2)}) collective-permute-start(bf16[2,256,256]{2,1,0:T(8,128)(2,1)S(1)} %slice.25), channel_id=1, source_target_pairs={{0,16},{8,120},{16,32},{24,8},{32,48},{40,24},{48,64},{56,40},{64,... | collective-permute-start | bytes 786440 | tf_op jit(solution)/shard_map/ppermute | solution.py:330
  64.8 11.2 %collective-permute-start.13 = (bf16[1,256,256]{2,1,0:T(8,128)(2,1)S(1)}, bf16[1,256,256]{2,1,0:T(8,128)(2,1)S(1)}, u32[]{:S(2)}, u32[]{:S(2)}) collective-permute-start(bf16[1,256,256]{2,1,0:T(8,128)(2,1)S(1)} %get-tuple-element.103), channel_id=1, source_target_pairs={{0,32},{8,104},{16,48},{24,120},{32,64},{40,8},{48,80},{56,24},{64... | collective-permute-start | bytes 393224 | tf_op jit(solution)/shard_map/ppermute | solution.py:330
  69.9 6.1 %collective-permute-start.12 = (bf16[1,256,256]{2,1,0:T(8,128)(2,1)S(1)}, bf16[1,256,256]{2,1,0:T(8,128)(2,1)S(1)}, u32[]{:S(2)}, u32[]{:S(2)}) collective-permute-start(bf16[1,256,256]{2,1,0:T(8,128)(2,1)S(1)} %get-tuple-element.104), channel_id=1, source_target_pairs={{0,128},{8,136},{16,144},{24,152},{32,160},{40,168},{48,176},{56,1... | collective-permute-start | bytes 393224 | tf_op jit(solution)/shard_map/ppermute | solution.py:330
  76.0 2.5 %copy-start.2 = (bf16[512,768]{1,0:T(8,128)(2,1)S(1)}, bf16[512,768]{1,0:T(8,128)(2,1)}, u32[]{:S(2)}) copy-start(bf16[512,768]{1,0:T(8,128)(2,1)} %refs_6_.1) | copy-start | bytes 2359300
  76.0 2.5 %collective-permute-start.15 = (bf16[4,256,256]{2,1,0:T(8,128)(2,1)S(1)}, bf16[4,256,256]{2,1,0:T(8,128)(2,1)S(1)}, u32[]{:S(2)}, u32[]{:S(2)}) collective-permute-start(bf16[4,256,256]{2,1,0:T(8,128)(2,1)S(1)} %constant_dynamic-update-slice_fusion.2.refs_3_), channel_id=1, source_target_pairs={{0,8},{8,0},{16,24},{24,16},{32,40},{40,32},{48,56},{56,48},{64,72... | collective-permute-start | bytes 1572872 | tf_op jit(solution)/shard_map/ppermute | solution.py:330

commit v9 on v8

--- a/solution.py
+++ b/solution.py
@@ -374,14 +374,15 @@
     beside, query = hold((beside, query))
     own_pair = jnp.concatenate([start, beside])
 
-    one = along_z(own_pair)
+    one = jnp.concatenate([along_z(start), along_z(beside), other])
     carry = fold([(own_pair, [(0, 0, 0), (0, 0, 1)])])
-    one, other, carry = hold((one, other, carry))
-
-    two = along_z(jnp.concatenate([one, other]))
+    one, carry = hold((one, carry))
+
+    two = along_z(one)
     one_other = flip_y(one[1:2])
-    pieces = [(one, [(0, 1, 0), (0, 1, 1)]), (other, [(1, 0, 0)])]
-    carry = both_cores(pieces, pieces, carry)
+    places = [(0, 1, 0), (0, 1, 1), (1, 0, 0)]
+    shared = [(one[0:2], places[0:2]), (one[2:3], places[2:3])]
+    carry = both_cores([(one, places)], shared, carry)
     two, one_other, carry = hold((two, one_other, carry))
 
     three = along_z(two)

time: 95.5 us -> 95.5 us (level)
  starting transfers between devices: 24.9 us -> 29 us
  waiting for transfers between devices: 14.9 us -> 10.8 us
    ppermute x16 -> x17, starting transfers between devices: 17.8 us -> 21.9 us  [moved(): return lax.ppermute(array, 'blk', [(i, target(i)) for i in range(blocks)])]
    ppermute x16 -> x17, waiting for transfers between devices: 5.93 us -> 1.91 us  [moved(): return lax.ppermute(array, 'blk', [(i, target(i)) for i in range(blocks)])]
  transfers between devices with their start and end apart: 17 -> 18, of which waited for: 7 -> 3; matrix products, arithmetic and copies ran while one was open for 0% -> 0% of each run, Pallas kernels for 19% -> 19%
where the time goes in v9:
time: 95.5 us; the launch traced here: 95.2 us
  starting transfers between devices  29 us (30%)
  Pallas kernels  27.8 us (29%)
  blocking collectives  26.1 us (27%)
  waiting for transfers between devices  10.8 us (11%)
    ppermute x17, starting transfers between devices, moved(): return lax.ppermute(array, 'blk', [(i, target(i)) for i in range(blocks)])  21.9 us
    pallas_call x9, Pallas kernels, attend(): pl.pallas_call(functools.partial(attend_kernel, carry is None, w_out is n...  19.8 us
    all_to_all x1, blocking collectives, per_device(): lax.all_to_all(mixed.reshape(groups, share, channels), 'head', 0, 0, tile...  13.4 us
    all_to_all x1, blocking collectives, per_device(): lax.all_to_all(copies, 'head', 0, 0, tiled=True).reshape(rows, channels)  12.8 us
    all_to_all x1, waiting for transfers between devices, per_device(): lax.all_to_all(partial.reshape(groups, share, channels), 'head', 0, 0, ti...  8.93 us
    all_to_all x1, starting transfers between devices, per_device(): lax.all_to_all(partial.reshape(groups, share, channels), 'head', 0, 0, ti...  7.07 us
    pallas_call x1, Pallas kernels, mlp(): pl.pallas_call(mlp_kernel, out_shape=jax.ShapeDtypeStruct((rows, channels...  5.76 us
  transfers between devices with their start and end apart: 18, of which 3 were waited for; matrix products, arithmetic and copies ran while one was open for 0% of the time, Pallas kernels for 19%

profile of v9, /device:TPU:32, one launch (start us, length us, event | category | flops | bytes accessed | tf_op | source)
XLA Modules:
  0.0 95.2 jit_solution(1612847304368826625)
XLA Ops:
  0.0 5.8 %conv_mlp.1 = bf16[256,768]{1,0:T(8,128)(2,1)} custom-call(bf16[16,16,768]{2,1,0:T(8,128)(2,1)} %bitcast.15, f32[7,7,768]{2,1,0:T(8,128)} %dw_hbm.1, f32[6,128]{1,0:T(8,128)} %bitcast.18, f32[6,128]{1,0:T(8,128)} %bitcast.19, bf16[768,384]{1,0:T(8,128)(2,1)} %w1_hbm.1, f32[3,128]{1,0:T(4,128)} %bitcast.23, bf16[384,768]{1,0:T(8,128)(2,1)} %w2_hbm.1), custom_call_target="tpu_custom_call" | custom-call | tf_op jit(solution)/shard_map/conv_mlp/pallas_call | solution.py:108
  5.8 0.0 copy-start.8
  5.8 0.0 copy-start
  5.8 7.1 %all-to-all-start = ((bf16[8,32,768]{2,1,0:T(8,128)(2,1)}), bf16[8,32,768]{2,1,0:T(8,128)(2,1)S(1)}, u32[]{:S(2)}, u32[]{:S(2)}) async-start(bf16[8,32,768]{2,1,0:T(8,128)(2,1)} %bitcast.6), calls=%async_computation | async-start | bytes 786432 | tf_op jit(solution)/shard_map/all_to_all | solution.py:350
  12.9 0.0 copy-start.6
  12.9 0.7 copy-done.7
  13.6 0.0 copy-done.6
  13.6 8.9 %all-to-all-done.parts = bf16[8,32,768]{2,1,0:T(8,128)(2,1)S(1)} async-done(((bf16[8,32,768]{2,1,0:T(8,128)(2,1)}), bf16[8,32,768]{2,1,0:T(8,128)(2,1)S(1)}, u32[]{:S(2)}, u32[]{:S(2)}) %all-to-all-start) | async-done | bytes 393248 | tf_op jit(solution)/shard_map/all_to_all | solution.py:350
  22.5 0.2 block_norm.1
  22.8 0.0 copy-start.1
  22.8 12.8 %all_to_all.15 = bf16[8,32,768]{2,1,0:T(8,128)(2,1)S(1)} all-to-all(bf16[8,32,768]{2,1,0:T(8,128)(2,1)S(1)} %block_norm.1), channel_id=1, replica_groups=mesh['blk'=32,'head'=8] {'head'}, dimensions={0} | all-to-all | bytes 786432 | tf_op jit(solution)/shard_map/all_to_all | solution.py:352
  35.6 0.4 key_values.1
  35.9 0.1 collective-permute-start
  36.0 0.8 collective-permute-start.3
  36.8 1.9 %collective-permute-start.1 = (bf16[1,256,256]{2,1,0:T(8,128)(2,1)S(1)}, bf16[1,256,256]{2,1,0:T(8,128)(2,1)S(1)}, u32[]{:S(2)}, u32[]{:S(2)}) collective-permute-start(bf16[1,256,256]{2,1,0:T(8,128)(2,1)S(1)} %key_values.1), channel_id=1, source_target_pairs={{0,16},{8,120},{16,32},{24,8},{32,48},{40,24},{48,64},{56,40},{64,... | collective-permute-start | bytes 393224 | tf_op jit(solution)/shard_map/ppermute | solution.py:330
  38.7 0.9 queries.1.refs_2_
  39.7 2.0 %collective-permute-start.2 = (bf16[1,256,256]{2,1,0:T(8,128)(2,1)S(1)}, bf16[1,256,256]{2,1,0:T(8,128)(2,1)S(1)}, u32[]{:S(2)}, u32[]{:S(2)}) collective-permute-start(bf16[1,256,256]{2,1,0:T(8,128)(2,1)S(1)} %collective-permute-done), channel_id=1, source_target_pairs={{0,16},{8,120},{16,32},{24,8},{32,48},{40,24},{48,64},{56,40},{64,... | collective-permute-start | bytes 393224 | tf_op jit(solution)/shard_map/ppermute | solution.py:330
  41.7 1.5 %attend.9 = (f32[4,256,128]{2,1,0:T(8,128)S(1)}, f32[4,256,256]{2,1,0:T(8,128)S(1)}) custom-call(s32[32]{0:T(128)S(1)} %copy-done.5, s32[1]{0:T(128)} %bitcast.refs_1_, bf16[4,256,128]{2,1,0:T(8,128)(2,1)S(1)} %queries.1.refs_2_, bf16[2,256,256]{2,1,0:T(8,128)(2,1)S(1)} %pad_maximum_fusion.1.refs_3_), custom_call_target="tpu_custom_call" | custom-call | flops 65536 | bytes 65536 | tf_op jit(solution)/shard_map/attend/pallas_call | solution.py:275
  43.2 0.0 collective-permute-done.3
  43.2 1.5 %collective-permute-done.2 = bf16[1,256,256]{2,1,0:T(8,128)(2,1)S(1)} collective-permute-done((bf16[1,256,256]{2,1,0:T(8,128)(2,1)S(1)}, bf16[1,256,256]{2,1,0:T(8,128)(2,1)S(1)}, u32[]{:S(2)}, u32[]{:S(2)}) %collective-permute-start.2) | collective-permute-done | bytes 131104 | tf_op jit(solution)/shard_map/ppermute | solution.py:330
  44.8 2.7 %collective-permute-start.4 = (bf16[3,256,256]{2,1,0:T(8,128)(2,1)S(1)}, bf16[3,256,256]{2,1,0:T(8,128)(2,1)S(1)}, u32[]{:S(2)}, u32[]{:S(2)}) collective-permute-start(bf16[3,256,256]{2,1,0:T(8,128)(2,1)S(1)} %pad_maximum_fusion.refs_3_), channel_id=1, source_target_pairs={{0,16},{8,120},{16,32},{24,8},{32,48},{40,24},{48,64},{56,40},{64,... | collective-permute-start | bytes 1179656 | tf_op jit(solution)/shard_map/ppermute | solution.py:330
  47.5 0.1 collective-permute-start.6
  47.6 0.6 collective-permute-start.7
  48.2 1.3 %collective-permute-start.5 = (bf16[1,256,256]{2,1,0:T(8,128)(2,1)S(1)}, bf16[1,256,256]{2,1,0:T(8,128)(2,1)S(1)}, u32[]{:S(2)}, u32[]{:S(2)}) collective-permute-start(bf16[1,256,256]{2,1,0:T(8,128)(2,1)S(1)} %get-tuple-element.106), channel_id=1, source_target_pairs={{0,128},{8,136},{16,144},{24,152},{32,160},{40,168},{48,176},{56,1... | collective-permute-start | bytes 393224 | tf_op jit(solution)/shard_map/ppermute | solution.py:330
  49.5 2.0 %attend.10 = (f32[4,256,128]{2,1,0:T(8,128)S(1)}, f32[4,256,256]{2,1,0:T(8,128)S(1)}) custom-call(s32[32]{0:T(128)S(1)} %copy-done.5, s32[1]{0:T(128)} %bitcast.refs_1_, bf16[4,256,128]{2,1,0:T(8,128)(2,1)S(1)} %queries.1.refs_2_, bf16[3,256,256]{2,1,0:T(8,128)(2,1)S(1)} %pad_maximum_fusion.refs_3_, f32[4,256,128]{2,1,0:T(8,128)S(1)} %get-tuple-element.58.refs_4_, ...), custom_call_target="tpu_custom_call" | custom-call | flops 98304 | bytes 65536 | tf_op jit(solution)/shard_map/attend/pallas_call | solution.py:275
  51.5 0.0 collective-permute-done.7.refs_4_
  51.5 2.0 %attend.11 = (f32[4,256,128]{2,1,0:T(8,128)S(1)}, f32[4,256,256]{2,1,0:T(8,128)S(1)}) custom-call(s32[32]{0:T(128)S(1)} %copy-done.5, s32[1]{0:T(128)} %bitcast.refs_1_, bf16[4,256,128]{2,1,0:T(8,128)(2,1)S(1)} %queries.1.refs_2_, bf16[2,256,256]{2,1,0:T(8,128)(2,1)S(1)} %collective-permute-done.6.refs_3_, ...), custom_call_target="tpu_custom_call" | custom-call | flops 98304 | bytes 65536 | tf_op jit(solution)/shard_map/attend/pallas_call | solution.py:275
  53.5 0.4 collective-permute-done.5.refs_4_
  53.8 2.4 %collective-permute-start.8 = (bf16[3,256,256]{2,1,0:T(8,128)(2,1)S(1)}, bf16[3,256,256]{2,1,0:T(8,128)(2,1)S(1)}, u32[]{:S(2)}, u32[]{:S(2)}) collective-permute-start(bf16[3,256,256]{2,1,0:T(8,128)(2,1)S(1)} %collective-permute-done.4.refs_3_), channel_id=1, source_target_pairs={{0,16},{8,120},{16,32},{24,8},{32,48},{40,24},{48,64},{56,40},{64,... | collective-permute-start | bytes 1179656 | tf_op jit(solution)/shard_map/ppermute | solution.py:330
  56.4 0.1 collective-permute-start.11
  56.5 0.5 collective-permute-start.10
  57.0 1.3 %collective-permute-start.9 = (bf16[1,256,256]{2,1,0:T(8,128)(2,1)S(1)}, bf16[1,256,256]{2,1,0:T(8,128)(2,1)S(1)}, u32[]{:S(2)}, u32[]{:S(2)}) collective-permute-start(bf16[1,256,256]{2,1,0:T(8,128)(2,1)S(1)} %get-tuple-element.104), channel_id=1, source_target_pairs={{0,128},{8,136},{16,144},{24,152},{32,160},{40,168},{48,176},{56,1... | collective-permute-start | bytes 393224 | tf_op jit(solution)/shard_map/ppermute | solution.py:330
  58.3 2.4 %attend.12 = (f32[4,256,128]{2,1,0:T(8,128)S(1)}, f32[4,256,256]{2,1,0:T(8,128)S(1)}) custom-call(s32[32]{0:T(128)S(1)} %copy-done.5, s32[1]{0:T(128)} %bitcast.refs_1_, bf16[4,256,128]{2,1,0:T(8,128)(2,1)S(1)} %queries.1.refs_2_, bf16[3,256,256]{2,1,0:T(8,128)(2,1)S(1)} %collective-permute-done.4.refs_3_, ...), custom_call_target="tpu_custom_call" | custom-call | flops 131072 | bytes 65536 | tf_op jit(solution)/shard_map/attend/pallas_call | solution.py:275
  60.7 0.0 collective-permute-done.11.refs_4_
  60.7 2.4 %attend.13 = (f32[4,256,128]{2,1,0:T(8,128)S(1)}, f32[4,256,256]{2,1,0:T(8,128)S(1)}) custom-call(s32[32]{0:T(128)S(1)} %copy-done.5, s32[1]{0:T(128)} %bitcast.refs_1_, bf16[4,256,128]{2,1,0:T(8,128)(2,1)S(1)} %queries.1.refs_2_, bf16[2,256,256]{2,1,0:T(8,128)(2,1)S(1)} %collective-permute-done.10.refs_3_, ...), custom_call_target="tpu_custom_call" | custom-call | flops 131072 | bytes 65536 | tf_op jit(solution)/shard_map/attend/pallas_call | solution.py:275
  63.1 0.0 collective-permute-done.8
  63.2 0.1 collective-permute-start.15
  63.3 2.3 %collective-permute-start.12 = (bf16[2,256,256]{2,1,0:T(8,128)(2,1)S(1)}, bf16[2,256,256]{2,1,0:T(8,128)(2,1)S(1)}, u32[]{:S(2)}, u32[]{:S(2)}) collective-permute-start(bf16[2,256,256]{2,1,0:T(8,128)(2,1)S(1)} %slice.33), channel_id=1, source_target_pairs={{0,16},{8,120},{16,32},{24,8},{32,48},{40,24},{48,64},{56,40},{64,... | collective-permute-start | bytes 786440 | tf_op jit(solution)/shard_map/ppermute | solution.py:330
  65.6 4.2 %collective-permute-start.14 = (bf16[1,256,256]{2,1,0:T(8,128)(2,1)S(1)}, bf16[1,256,256]{2,1,0:T(8,128)(2,1)S(1)}, u32[]{:S(2)}, u32[]{:S(2)}) collective-permute-start(bf16[1,256,256]{2,1,0:T(8,128)(2,1)S(1)} %get-tuple-element.101), channel_id=1, source_target_pairs={{0,32},{8,104},{16,48},{24,120},{32,64},{40,8},{48,80},{56,24},{64... | collective-permute-start | bytes 393224 | tf_op jit(solution)/shard_map/ppermute | solution.py:330
  69.9 1.4 %collective-permute-start.13 = (bf16[1,256,256]{2,1,0:T(8,128)(2,1)S(1)}, bf16[1,256,256]{2,1,0:T(8,128)(2,1)S(1)}, u32[]{:S(2)}, u32[]{:S(2)}) collective-permute-start(bf16[1,256,256]{2,1,0:T(8,128)(2,1)S(1)} %get-tuple-element.102), channel_id=1, source_target_pairs={{0,128},{8,136},{16,144},{24,152},{32,160},{40,168},{48,176},{56,1... | collective-permute-start | bytes 393224 | tf_op jit(solution)/shard_map/ppermute | solution.py:330
  71.2 2.4 %attend.14 = (f32[4,256,128]{2,1,0:T(8,128)S(1)}, f32[4,256,256]{2,1,0:T(8,128)S(1)}) custom-call(s32[32]{0:T(128)S(1)} %copy-done.5, s32[1]{0:T(128)} %bitcast.refs_1_, bf16[4,256,128]{2,1,0:T(8,128)(2,1)S(1)} %queries.1.refs_2_, bf16[4,256,256]{2,1,0:T(8,128)(2,1)S(1)} %constant_dynamic-update-slice_fusion.refs_3_, ...), custom_call_target="tpu_custom_call" | custom-call | flops 131072 | bytes 65536 | tf_op jit(solution)/shard_map/attend/pallas_call | solution.py:275
  73.6 2.4 %attend.15 = (f32[4,256,128]{2,1,0:T(8,128)S(1)}, f32[4,256,256]{2,1,0:T(8,128)S(1)}) custom-call(s32[32]{0:T(128)S(1)} %copy-done.5, s32[1]{0:T(128)} %bitcast.refs_1_, bf16[4,256,128]{2,1,0:T(8,128)(2,1)S(1)} %queries.1.refs_2_, bf16[4,256,256]{2,1,0:T(8,128)(2,1)S(1)} %collective-permute-done.15.refs_3_, f32[4,256,128]{2,1,0:T(8,128)S(1)} %get-tuple-element.87.refs_4_, ...), custom_call_target="tpu_custom_call" | custom-call | flops 131072 | bytes 65536 | tf_op jit(solution)/shard_map/attend/pallas_call | solution.py:275
  76.1 0.0 copy-start.2
  76.1 0.1 collective-permute-start.16
  76.2 2.4 %attend.16 = (f32[4,256,128]{2,1,0:T(8,128)S(1)}, f32[4,256,256]{2,1,0:T(8,128)S(1)}) custom-call(s32[32]{0:T(128)S(1)} %copy-done.5, s32[1]{0:T(128)} %bitcast.refs_1_, bf16[4,256,128]{2,1,0:T(8,128)(2,1)S(1)} %queries.1.refs_2_, bf16[4,256,256]{2,1,0:T(8,128)(2,1)S(1)} %constant_dynamic-update-slice_fusion.2.refs_3_, ...), custom_call_target="tpu_custom_call" | custom-call | flops 131072 | bytes 65536 | tf_op jit(solution)/shard_map/attend/pallas_call | solution.py:275
  78.6 2.6 %attend.17 = bf16[256,768]{1,0:T(8,128)(2,1)S(1)} custom-call(s32[32]{0:T(128)S(1)} %copy-done.5, s32[1]{0:T(128)} %bitcast.refs_1_, bf16[4,256,128]{2,1,0:T(8,128)(2,1)S(1)} %queries.1.refs_2_, bf16[4,256,256]{2,1,0:T(8,128)(2,1)S(1)} %collective-permute-done.16.refs_3_, f32[4,256,128]{2,1,0:T(8,128)S(1)} %get-tuple-element.99.refs_4_, ...), custom_call_target="tpu_custom_call" | custom-call | flops 131072 | bytes 65536 | tf_op jit(solution)/shard_map/attend/pallas_call | solution.py:275
  81.2 13.4 %all_to_all.16.parts = bf16[8,32,768]{2,1,0:T(8,128)(2,1)S(1)} all-to-all(bf16[8,32,768]{2,1,0:T(8,128)(2,1)S(1)} %bitcast.17), channel_id=1, replica_groups=mesh['blk'=32,'head'=8] {'head'}, dimensions={0} | all-to-all | bytes 786432 | tf_op jit(solution)/shard_map/all_to_all | solution.py:406
  94.5 0.7 total.1
  (37 shorter events, 0.3 us)
Async XLA Ops:
  5.8 7.1 %copy-start.8 = (f32[768]{0:T(1024)S(1)}, f32[768]{0:T(1024)}, u32[]{:S(2)}) copy-start(f32[768]{0:T(1024)} %param.24) | copy-start | bytes 9220
  5.8 16.7 %copy-start = (bf16[1,16,16,768]{3,2,1,0:T(8,128)(2,1)S(1)}, bf16[1,16,16,768]{3,2,1,0:T(8,128)(2,1)}, u32[]{:S(2)}) copy-start(bf16[1,16,16,768]{3,2,1,0:T(8,128)(2,1)} %param.15) | copy-start | bytes 1179652
  5.8 16.7 %all-to-all-start = ((bf16[8,32,768]{2,1,0:T(8,128)(2,1)}), bf16[8,32,768]{2,1,0:T(8,128)(2,1)S(1)}, u32[]{:S(2)}, u32[]{:S(2)}) async-start(bf16[8,32,768]{2,1,0:T(8,128)(2,1)} %bitcast.6), calls=%async_computation | async-start | bytes 786432 | tf_op jit(solution)/shard_map/all_to_all | solution.py:350
  12.9 0.7 copy-start.7
  12.9 0.7 copy-start.6
  22.5 13.0 %copy-start.3 = (bf16[768,128]{1,0:T(8,128)(2,1)S(1)}, bf16[768,128]{1,0:T(8,128)(2,1)}, u32[]{:S(2)}) copy-start(bf16[768,128]{1,0:T(8,128)(2,1)} %wk.1) | copy-start | bytes 589828
  22.5 13.0 %copy-start.4 = (bf16[768,128]{1,0:T(8,128)(2,1)S(1)}, bf16[768,128]{1,0:T(8,128)(2,1)}, u32[]{:S(2)}) copy-start(bf16[768,128]{1,0:T(8,128)(2,1)} %wv.1) | copy-start | bytes 589828
  22.8 15.9 %copy-start.1 = (bf16[768,512]{1,0:T(8,128)(2,1)S(1)}, bf16[768,512]{1,0:T(8,128)(2,1)}, u32[]{:S(2)}) copy-start(bf16[768,512]{1,0:T(8,128)(2,1)} %wq.1) | copy-start | bytes 2359300
  35.6 3.2 %copy-start.5 = (s32[32]{0:T(128)S(1)}, s32[32]{0:T(128)}, u32[]{:S(2)}) copy-start(s32[32]{0:T(128)} %refs_0_.17) | copy-start | bytes 388
  35.9 3.7 %collective-permute-start = (bf16[1,256,256]{2,1,0:T(8,128)(2,1)S(1)}, bf16[1,256,256]{2,1,0:T(8,128)(2,1)S(1)}, u32[]{:S(2)}, u32[]{:S(2)}) collective-permute-start(bf16[1,256,256]{2,1,0:T(8,128)(2,1)S(1)} %key_values.1), channel_id=1, source_target_pairs={{0,8},{8,0},{16,24},{24,16},{32,40},{40,32},{48,56},{56,48},{64,72... | collective-permute-start | bytes 393224 | tf_op jit(solution)/shard_map/ppermute | solution.py:330
  36.0 7.2 %collective-permute-start.3 = (bf16[1,256,256]{2,1,0:T(8,128)(2,1)S(1)}, bf16[1,256,256]{2,1,0:T(8,128)(2,1)S(1)}, u32[]{:S(2)}, u32[]{:S(2)}) collective-permute-start(bf16[1,256,256]{2,1,0:T(8,128)(2,1)S(1)} %key_values.1), channel_id=1, source_target_pairs={{0,128},{8,136},{16,144},{24,152},{32,160},{40,168},{48,176},{56,1... | collective-permute-start | bytes 393224 | tf_op jit(solution)/shard_map/ppermute | solution.py:330
  36.8 6.4 %collective-permute-start.1 = (bf16[1,256,256]{2,1,0:T(8,128)(2,1)S(1)}, bf16[1,256,256]{2,1,0:T(8,128)(2,1)S(1)}, u32[]{:S(2)}, u32[]{:S(2)}) collective-permute-start(bf16[1,256,256]{2,1,0:T(8,128)(2,1)S(1)} %key_values.1), channel_id=1, source_target_pairs={{0,16},{8,120},{16,32},{24,8},{32,48},{40,24},{48,64},{56,40},{64,... | collective-permute-start | bytes 393224 | tf_op jit(solution)/shard_map/ppermute | solution.py:330
  39.7 5.0 %collective-permute-start.2 = (bf16[1,256,256]{2,1,0:T(8,128)(2,1)S(1)}, bf16[1,256,256]{2,1,0:T(8,128)(2,1)S(1)}, u32[]{:S(2)}, u32[]{:S(2)}) collective-permute-start(bf16[1,256,256]{2,1,0:T(8,128)(2,1)S(1)} %collective-permute-done), channel_id=1, source_target_pairs={{0,16},{8,120},{16,32},{24,8},{32,48},{40,24},{48,64},{56,40},{64,... | collective-permute-start | bytes 393224 | tf_op jit(solution)/shard_map/ppermute | solution.py:330
  44.8 9.1 %collective-permute-start.4 = (bf16[3,256,256]{2,1,0:T(8,128)(2,1)S(1)}, bf16[3,256,256]{2,1,0:T(8,128)(2,1)S(1)}, u32[]{:S(2)}, u32[]{:S(2)}) collective-permute-start(bf16[3,256,256]{2,1,0:T(8,128)(2,1)S(1)} %pad_maximum_fusion.refs_3_), channel_id=1, source_target_pairs={{0,16},{8,120},{16,32},{24,8},{32,48},{40,24},{48,64},{56,40},{64,... | collective-permute-start | bytes 1179656 | tf_op jit(solution)/shard_map/ppermute | solution.py:330
  47.5 4.0 %collective-permute-start.6 = (bf16[2,256,256]{2,1,0:T(8,128)(2,1)S(1)}, bf16[2,256,256]{2,1,0:T(8,128)(2,1)S(1)}, u32[]{:S(2)}, u32[]{:S(2)}) collective-permute-start(bf16[2,256,256]{2,1,0:T(8,128)(2,1)S(1)} %slice.28), channel_id=1, source_target_pairs={{0,8},{8,0},{16,24},{24,16},{32,40},{40,32},{48,56},{56,48},{64,72... | collective-permute-start | bytes 786440 | tf_op jit(solution)/shard_map/ppermute | solution.py:330
  47.6 3.9 %collective-permute-start.7 = (bf16[1,256,256]{2,1,0:T(8,128)(2,1)S(1)}, bf16[1,256,256]{2,1,0:T(8,128)(2,1)S(1)}, u32[]{:S(2)}, u32[]{:S(2)}) collective-permute-start(bf16[1,256,256]{2,1,0:T(8,128)(2,1)S(1)} %get-tuple-element.105), channel_id=1, source_target_pairs={{0,8},{8,0},{16,24},{24,16},{32,40},{40,32},{48,56},{56,48},{64,72... | collective-permute-start | bytes 393224 | tf_op jit(solution)/shard_map/ppermute | solution.py:330
  48.2 5.7 %collective-permute-start.5 = (bf16[1,256,256]{2,1,0:T(8,128)(2,1)S(1)}, bf16[1,256,256]{2,1,0:T(8,128)(2,1)S(1)}, u32[]{:S(2)}, u32[]{:S(2)}) collective-permute-start(bf16[1,256,256]{2,1,0:T(8,128)(2,1)S(1)} %get-tuple-element.106), channel_id=1, source_target_pairs={{0,128},{8,136},{16,144},{24,152},{32,160},{40,168},{48,176},{56,1... | collective-permute-start | bytes 393224 | tf_op jit(solution)/shard_map/ppermute | solution.py:330
  53.8 9.3 %collective-permute-start.8 = (bf16[3,256,256]{2,1,0:T(8,128)(2,1)S(1)}, bf16[3,256,256]{2,1,0:T(8,128)(2,1)S(1)}, u32[]{:S(2)}, u32[]{:S(2)}) collective-permute-start(bf16[3,256,256]{2,1,0:T(8,128)(2,1)S(1)} %collective-permute-done.4.refs_3_), channel_id=1, source_target_pairs={{0,16},{8,120},{16,32},{24,8},{32,48},{40,24},{48,64},{56,40},{64,... | collective-permute-start | bytes 1179656 | tf_op jit(solution)/shard_map/ppermute | solution.py:330
  56.4 4.3 %collective-permute-start.11 = (bf16[2,256,256]{2,1,0:T(8,128)(2,1)S(1)}, bf16[2,256,256]{2,1,0:T(8,128)(2,1)S(1)}, u32[]{:S(2)}, u32[]{:S(2)}) collective-permute-start(bf16[2,256,256]{2,1,0:T(8,128)(2,1)S(1)} %pad_maximum_fusion.2), channel_id=1, source_target_pairs={{0,8},{8,0},{16,24},{24,16},{32,40},{40,32},{48,56},{56,48},{64,72... | collective-permute-start | bytes 786440 | tf_op jit(solution)/shard_map/ppermute | solution.py:330
  56.5 4.2 %collective-permute-start.10 = (bf16[2,256,256]{2,1,0:T(8,128)(2,1)S(1)}, bf16[2,256,256]{2,1,0:T(8,128)(2,1)S(1)}, u32[]{:S(2)}, u32[]{:S(2)}) collective-permute-start(bf16[2,256,256]{2,1,0:T(8,128)(2,1)S(1)} %slice.31), channel_id=1, source_target_pairs={{0,8},{8,0},{16,24},{24,16},{32,40},{40,32},{48,56},{56,48},{64,72... | collective-permute-start | bytes 786440 | tf_op jit(solution)/shard_map/ppermute | solution.py:330
  57.0 6.1 %collective-permute-start.9 = (bf16[1,256,256]{2,1,0:T(8,128)(2,1)S(1)}, bf16[1,256,256]{2,1,0:T(8,128)(2,1)S(1)}, u32[]{:S(2)}, u32[]{:S(2)}) collective-permute-start(bf16[1,256,256]{2,1,0:T(8,128)(2,1)S(1)} %get-tuple-element.104), channel_id=1, source_target_pairs={{0,128},{8,136},{16,144},{24,152},{32,160},{40,168},{48,176},{56,1... | collective-permute-start | bytes 393224 | tf_op jit(solution)/shard_map/ppermute | solution.py:330
  63.2 10.4 %collective-permute-start.15 = (bf16[4,256,256]{2,1,0:T(8,128)(2,1)S(1)}, bf16[4,256,256]{2,1,0:T(8,128)(2,1)S(1)}, u32[]{:S(2)}, u32[]{:S(2)}) collective-permute-start(bf16[4,256,256]{2,1,0:T(8,128)(2,1)S(1)} %constant_dynamic-update-slice_fusion.refs_3_), channel_id=1, source_target_pairs={{0,8},{8,0},{16,24},{24,16},{32,40},{40,32},{48,56},{56,48},{64,72... | collective-permute-start | bytes 1572872 | tf_op jit(solution)/shard_map/ppermute | solution.py:330
  63.3 12.7 %collective-permute-start.12 = (bf16[2,256,256]{2,1,0:T(8,128)(2,1)S(1)}, bf16[2,256,256]{2,1,0:T(8,128)(2,1)S(1)}, u32[]{:S(2)}, u32[]{:S(2)}) collective-permute-start(bf16[2,256,256]{2,1,0:T(8,128)(2,1)S(1)} %slice.33), channel_id=1, source_target_pairs={{0,16},{8,120},{16,32},{24,8},{32,48},{40,24},{48,64},{56,40},{64,... | collective-permute-start | bytes 786440 | tf_op jit(solution)/shard_map/ppermute | solution.py:330
  65.6 10.4 %collective-permute-start.14 = (bf16[1,256,256]{2,1,0:T(8,128)(2,1)S(1)}, bf16[1,256,256]{2,1,0:T(8,128)(2,1)S(1)}, u32[]{:S(2)}, u32[]{:S(2)}) collective-permute-start(bf16[1,256,256]{2,1,0:T(8,128)(2,1)S(1)} %get-tuple-element.101), channel_id=1, source_target_pairs={{0,32},{8,104},{16,48},{24,120},{32,64},{40,8},{48,80},{56,24},{64... | collective-permute-start | bytes 393224 | tf_op jit(solution)/shard_map/ppermute | solution.py:330
  69.9 6.1 %collective-permute-start.13 = (bf16[1,256,256]{2,1,0:T(8,128)(2,1)S(1)}, bf16[1,256,256]{2,1,0:T(8,128)(2,1)S(1)}, u32[]{:S(2)}, u32[]{:S(2)}) collective-permute-start(bf16[1,256,256]{2,1,0:T(8,128)(2,1)S(1)} %get-tuple-element.102), channel_id=1, source_target_pairs={{0,128},{8,136},{16,144},{24,152},{32,160},{40,168},{48,176},{56,1... | collective-permute-start | bytes 393224 | tf_op jit(solution)/shard_map/ppermute | solution.py:330
  76.1 2.5 %copy-start.2 = (bf16[512,768]{1,0:T(8,128)(2,1)S(1)}, bf16[512,768]{1,0:T(8,128)(2,1)}, u32[]{:S(2)}) copy-start(bf16[512,768]{1,0:T(8,128)(2,1)} %refs_6_.1) | copy-start | bytes 2359300
  76.1 2.5 %collective-permute-start.16 = (bf16[4,256,256]{2,1,0:T(8,128)(2,1)S(1)}, bf16[4,256,256]{2,1,0:T(8,128)(2,1)S(1)}, u32[]{:S(2)}, u32[]{:S(2)}) collective-permute-start(bf16[4,256,256]{2,1,0:T(8,128)(2,1)S(1)} %constant_dynamic-update-slice_fusion.2.refs_3_), channel_id=1, source_target_pairs={{0,8},{8,0},{16,24},{24,16},{32,40},{40,32},{48,56},{56,48},{64,72... | collective-permute-start | bytes 1572872 | tf_op jit(solution)/shard_map/ppermute | solution.py:330

commit v10 on v8

--- a/solution.py
+++ b/solution.py
@@ -52,26 +52,24 @@
 
 def mlp_kernel(pages_hbm, dw_hbm, dwb_hbm, gain_hbm, w1_hbm, b1_hbm, w2_hbm, out, *scratch):
     padded, conv, pages, dw, dwb, gain, w1, b1, w2, arrived = scratch
-    pairs = (
-        (w1_hbm, w1),
-        (w2_hbm, w2),
-        (b1_hbm, b1),
-        (gain_hbm, gain),
-        (dwb_hbm, dwb),
-        (dw_hbm, dw),
-        (pages_hbm, pages),
-    )
+    chunks = pages.shape[2] // LANES
+    pairs = [(dwb_hbm, dwb)]
+    for chunk in range(chunks):
+        lanes = slice(chunk * LANES, (chunk + 1) * LANES)
+        pairs += [(pages_hbm.at[:, :, lanes], pages.at[:, :, lanes]), (dw_hbm.at[:, :, lanes], dw.at[:, :, lanes])]
+    pairs += [(gain_hbm, gain), (b1_hbm, b1), (w1_hbm, w1), (w2_hbm, w2)]
     loads = [pltpu.make_async_copy(source, target, arrived.at[index]) for index, (source, target) in enumerate(pairs)]
-    for load in reversed(loads):
+    for load in loads:
         load.start()
-    for load in loads[2:]:
-        load.wait()
+    loads[0].wait()
     height, breadth, channels = pages.shape
     half = height // 2
     column = lax.broadcasted_iota(jnp.int32, (half, breadth, LANES), 1)
     blank = jnp.zeros((3, breadth, LANES), F32)
     for chunk in range(channels // LANES):
         lanes = slice(chunk * LANES, (chunk + 1) * LANES)
+        loads[1 + 2 * chunk].wait()
+        loads[2 + 2 * chunk].wait()
         padded[chunk, 0:3] = blank
         padded[chunk, 3 + height : 6 + height] = blank
         padded[chunk, 3 : 3 + height] = pages[:, :, lanes].astype(F32)
@@ -90,14 +88,16 @@
                     product = jnp.where(inside, rolled, 0.0)
                 total = total + product
             conv[chunk, top * breadth : (top + half) * breadth] = total.reshape(half * breadth, LANES)
+    loads[-4].wait()
     normed = normalise([conv[chunk] for chunk in range(channels // LANES)], gain, 1e-06)
-    loads[0].wait()
+    loads[-3].wait()
+    loads[-2].wait()
     product = jnp.dot(jnp.concatenate(normed, axis=1), w1[...], preferred_element_type=F32)
     hidden = []
     for chunk in range(product.shape[1] // LANES):
         pre = product[:, chunk * LANES : (chunk + 1) * LANES] + b1[chunk : chunk + 1, :]
         hidden.append((0.5 * pre * (1.0 + lax.erf(pre * 0.7071067811865476))).astype(BF))
-    loads[1].wait()
+    loads[-1].wait()
     out[...] = jnp.dot(jnp.concatenate(hidden, axis=1), w2[...], preferred_element_type=F32).astype(BF)
 
 
@@ -114,7 +114,7 @@
             pltpu.VMEM((channels // LANES, height + 6, breadth, LANES), F32),
             pltpu.VMEM((channels // LANES, rows, LANES), F32),
             *[pltpu.VMEM(operand.shape, operand.dtype) for operand in operands],
-            pltpu.SemaphoreType.DMA((7,)),
+            pltpu.SemaphoreType.DMA((2 * (channels // LANES) + 5,)),
         ],
         compiler_params=params(16),
         name="conv_mlp",
@@ -370,9 +370,9 @@
     start = key_values(normed, w_key, w_value)
     beside = flip_core(start)
     other = flip_y(start)
-    query = queries_of(valid_counts, normed, w_query)
-    beside, query = hold((beside, query))
     own_pair = jnp.concatenate([start, beside])
+    own_pair, later = hold((own_pair, normed))
+    query = queries_of(valid_counts, later, w_query)
 
     one = along_z(own_pair)
     carry = fold([(own_pair, [(0, 0, 0), (0, 0, 1)])])

time: 95.5 us -> 95.4 us (level)
  no operation moved by 1% of the time
where the time goes in v10:
time: 95.4 us; the launch traced here: 95.1 us
  Pallas kernels  27.7 us (29%)
  blocking collectives  26.2 us (27%)
  starting transfers between devices  25 us (26%)
  waiting for transfers between devices  14.3 us (15%)
  local copies, waits for them, and re-layouts  1.54 us (2%)
    pallas_call x9, Pallas kernels, attend(): pl.pallas_call(functools.partial(attend_kernel, carry is None, w_out is n...  19.9 us
    ppermute x16, starting transfers between devices, moved(): return lax.ppermute(array, 'blk', [(i, target(i)) for i in range(blocks)])  17.9 us
    all_to_all x1, blocking collectives, per_device(): lax.all_to_all(mixed.reshape(groups, share, channels), 'head', 0, 0, tile...  13.4 us
    all_to_all x1, blocking collectives, per_device(): lax.all_to_all(copies, 'head', 0, 0, tiled=True).reshape(rows, channels)  12.8 us
    all_to_all x1, waiting for transfers between devices, per_device(): lax.all_to_all(partial.reshape(groups, share, channels), 'head', 0, 0, ti...  8.92 us
    all_to_all x1, starting transfers between devices, per_device(): lax.all_to_all(partial.reshape(groups, share, channels), 'head', 0, 0, ti...  7.08 us
    pallas_call x1, Pallas kernels, mlp(): pl.pallas_call(mlp_kernel, out_shape=jax.ShapeDtypeStruct((rows, channels...  5.66 us
    ppermute x16, waiting for transfers between devices, moved(): return lax.ppermute(array, 'blk', [(i, target(i)) for i in range(blocks)])  5.34 us
  transfers between devices with their start and end apart: 17, of which 7 were waited for; matrix products, arithmetic and copies ran while one was open for 0% of the time, Pallas kernels for 19%

profile of v10, /device:TPU:32, one launch (start us, length us, event | category | flops | bytes accessed | tf_op | source)
XLA Modules:
  0.0 95.1 jit_solution(13024129755387498401)
XLA Ops:
  0.0 5.7 %conv_mlp.1 = bf16[256,768]{1,0:T(8,128)(2,1)} custom-call(bf16[16,16,768]{2,1,0:T(8,128)(2,1)} %bitcast.15, f32[7,7,768]{2,1,0:T(8,128)} %dw_hbm.1, f32[6,128]{1,0:T(8,128)} %bitcast.18, f32[6,128]{1,0:T(8,128)} %bitcast.19, bf16[768,384]{1,0:T(8,128)(2,1)} %w1_hbm.1, f32[3,128]{1,0:T(4,128)} %bitcast.23, bf16[384,768]{1,0:T(8,128)(2,1)} %w2_hbm.1), custom_call_target="tpu_custom_call" | custom-call | tf_op jit(solution)/shard_map/conv_mlp/pallas_call | solution.py:108
  5.7 0.0 copy-start.8
  5.7 0.0 copy-start
  5.7 7.1 %all-to-all-start = ((bf16[8,32,768]{2,1,0:T(8,128)(2,1)}), bf16[8,32,768]{2,1,0:T(8,128)(2,1)S(1)}, u32[]{:S(2)}, u32[]{:S(2)}) async-start(bf16[8,32,768]{2,1,0:T(8,128)(2,1)} %bitcast.6), calls=%async_computation | async-start | bytes 786432 | tf_op jit(solution)/shard_map/all_to_all | solution.py:350
  12.8 0.0 copy-start.6
  12.8 0.7 copy-done.7
  13.5 0.0 copy-done.6
  13.5 8.9 %all-to-all-done.parts = bf16[8,32,768]{2,1,0:T(8,128)(2,1)S(1)} async-done(((bf16[8,32,768]{2,1,0:T(8,128)(2,1)}), bf16[8,32,768]{2,1,0:T(8,128)(2,1)S(1)}, u32[]{:S(2)}, u32[]{:S(2)}) %all-to-all-start) | async-done | bytes 393248 | tf_op jit(solution)/shard_map/all_to_all | solution.py:350
  22.4 0.2 block_norm.1
  22.7 0.0 copy-start.3
  22.7 0.0 copy-start.4
  22.7 12.8 %all_to_all.15 = bf16[8,32,768]{2,1,0:T(8,128)(2,1)S(1)} all-to-all(bf16[8,32,768]{2,1,0:T(8,128)(2,1)S(1)} %block_norm.1), channel_id=1, replica_groups=mesh['blk'=32,'head'=8] {'head'}, dimensions={0} | all-to-all | bytes 786432 | tf_op jit(solution)/shard_map/all_to_all | solution.py:352
  35.5 0.4 key_values.1
  35.8 0.1 collective-permute-start
  35.9 1.3 %collective-permute-done = bf16[1,256,256]{2,1,0:T(8,128)(2,1)S(1)} collective-permute-done((bf16[1,256,256]{2,1,0:T(8,128)(2,1)S(1)}, bf16[1,256,256]{2,1,0:T(8,128)(2,1)S(1)}, u32[]{:S(2)}, u32[]{:S(2)}) %collective-permute-start) | collective-permute-done | bytes 131104 | tf_op jit(solution)/shard_map/ppermute | solution.py:330
  37.3 2.0 %collective-permute-start.1 = (bf16[2,256,256]{2,1,0:T(8,128)(2,1)S(1)}, bf16[2,256,256]{2,1,0:T(8,128)(2,1)S(1)}, u32[]{:S(2)}, u32[]{:S(2)}) collective-permute-start(bf16[2,256,256]{2,1,0:T(8,128)(2,1)S(1)} %pad_maximum_fusion.1.refs_3_), channel_id=1, source_target_pairs={{0,16},{8,120},{16,32},{24,8},{32,48},{40,24},{48,64},{56,40},{64,... | collective-permute-start | bytes 786440 | tf_op jit(solution)/shard_map/ppermute | solution.py:330
  39.3 0.7 collective-permute-start.2
  40.0 0.7 copy-done.5
  40.6 0.9 queries.1.refs_2_
  41.6 1.5 %attend.9 = (f32[4,256,128]{2,1,0:T(8,128)S(1)}, f32[4,256,256]{2,1,0:T(8,128)S(1)}) custom-call(s32[32]{0:T(128)S(1)} %copy-done.5, s32[1]{0:T(128)} %bitcast.refs_1_, bf16[4,256,128]{2,1,0:T(8,128)(2,1)S(1)} %queries.1.refs_2_, bf16[2,256,256]{2,1,0:T(8,128)(2,1)S(1)} %pad_maximum_fusion.1.refs_3_), custom_call_target="tpu_custom_call" | custom-call | flops 65536 | bytes 65536 | tf_op jit(solution)/shard_map/attend/pallas_call | solution.py:275
  43.1 1.2 %collective-permute-done.2.refs_4_ = bf16[1,256,256]{2,1,0:T(8,128)(2,1)S(1)} collective-permute-done((bf16[1,256,256]{2,1,0:T(8,128)(2,1)S(1)}, bf16[1,256,256]{2,1,0:T(8,128)(2,1)S(1)}, u32[]{:S(2)}, u32[]{:S(2)}) %collective-permute-start.2) | collective-permute-done | bytes 131104 | tf_op jit(solution)/shard_map/ppermute | solution.py:330
  44.3 2.0 %collective-permute-start.3 = (bf16[3,256,256]{2,1,0:T(8,128)(2,1)S(1)}, bf16[3,256,256]{2,1,0:T(8,128)(2,1)S(1)}, u32[]{:S(2)}, u32[]{:S(2)}) collective-permute-start(bf16[3,256,256]{2,1,0:T(8,128)(2,1)S(1)} %pad_maximum_fusion), channel_id=1, source_target_pairs={{0,16},{8,120},{16,32},{24,8},{32,48},{40,24},{48,64},{56,40},{64,... | collective-permute-start | bytes 1179656 | tf_op jit(solution)/shard_map/ppermute | solution.py:330
  46.3 0.9 collective-permute-start.5
  47.2 1.0 %collective-permute-start.4 = (bf16[1,256,256]{2,1,0:T(8,128)(2,1)S(1)}, bf16[1,256,256]{2,1,0:T(8,128)(2,1)S(1)}, u32[]{:S(2)}, u32[]{:S(2)}) collective-permute-start(bf16[1,256,256]{2,1,0:T(8,128)(2,1)S(1)} %slice.21), channel_id=1, source_target_pairs={{0,128},{8,136},{16,144},{24,152},{32,160},{40,168},{48,176},{56,1... | collective-permute-start | bytes 393224 | tf_op jit(solution)/shard_map/ppermute | solution.py:330
  48.2 2.0 %attend.10 = (f32[4,256,128]{2,1,0:T(8,128)S(1)}, f32[4,256,256]{2,1,0:T(8,128)S(1)}) custom-call(s32[32]{0:T(128)S(1)} %copy-done.5, s32[1]{0:T(128)} %bitcast.refs_1_, bf16[4,256,128]{2,1,0:T(8,128)(2,1)S(1)} %queries.1.refs_2_, bf16[2,256,256]{2,1,0:T(8,128)(2,1)S(1)} %collective-permute-done.1.refs_3_, ...), custom_call_target="tpu_custom_call" | custom-call | flops 98304 | bytes 65536 | tf_op jit(solution)/shard_map/attend/pallas_call | solution.py:275
  50.2 2.0 %attend.11 = (f32[4,256,128]{2,1,0:T(8,128)S(1)}, f32[4,256,256]{2,1,0:T(8,128)S(1)}) custom-call(s32[32]{0:T(128)S(1)} %copy-done.5, s32[1]{0:T(128)} %bitcast.refs_1_, bf16[4,256,128]{2,1,0:T(8,128)(2,1)S(1)} %queries.1.refs_2_, bf16[2,256,256]{2,1,0:T(8,128)(2,1)S(1)} %collective-permute-done.5.refs_3_, ...), custom_call_target="tpu_custom_call" | custom-call | flops 98304 | bytes 65536 | tf_op jit(solution)/shard_map/attend/pallas_call | solution.py:275
  52.2 1.2 %collective-permute-done.4.refs_4_ = bf16[1,256,256]{2,1,0:T(8,128)(2,1)S(1)} collective-permute-done((bf16[1,256,256]{2,1,0:T(8,128)(2,1)S(1)}, bf16[1,256,256]{2,1,0:T(8,128)(2,1)S(1)}, u32[]{:S(2)}, u32[]{:S(2)}) %collective-permute-start.4) | collective-permute-done | bytes 131104 | tf_op jit(solution)/shard_map/ppermute | solution.py:330
  53.4 0.2 collective-permute-done.3.refs_3_
  53.6 2.1 %collective-permute-start.7 = (bf16[3,256,256]{2,1,0:T(8,128)(2,1)S(1)}, bf16[3,256,256]{2,1,0:T(8,128)(2,1)S(1)}, u32[]{:S(2)}, u32[]{:S(2)}) collective-permute-start(bf16[3,256,256]{2,1,0:T(8,128)(2,1)S(1)} %collective-permute-done.3.refs_3_), channel_id=1, source_target_pairs={{0,16},{8,120},{16,32},{24,8},{32,48},{40,24},{48,64},{56,40},{64,... | collective-permute-start | bytes 1179656 | tf_op jit(solution)/shard_map/ppermute | solution.py:330
  55.7 0.1 collective-permute-start.10
  55.8 0.5 collective-permute-start.9
  56.3 0.7 collective-permute-start.8
  57.0 2.4 %attend.12 = (f32[4,256,128]{2,1,0:T(8,128)S(1)}, f32[4,256,256]{2,1,0:T(8,128)S(1)}) custom-call(s32[32]{0:T(128)S(1)} %copy-done.5, s32[1]{0:T(128)} %bitcast.refs_1_, bf16[4,256,128]{2,1,0:T(8,128)(2,1)S(1)} %queries.1.refs_2_, bf16[3,256,256]{2,1,0:T(8,128)(2,1)S(1)} %collective-permute-done.3.refs_3_, ...), custom_call_target="tpu_custom_call" | custom-call | flops 131072 | bytes 65536 | tf_op jit(solution)/shard_map/attend/pallas_call | solution.py:275
  59.4 2.4 %attend.13 = (f32[4,256,128]{2,1,0:T(8,128)S(1)}, f32[4,256,256]{2,1,0:T(8,128)S(1)}) custom-call(s32[32]{0:T(128)S(1)} %copy-done.5, s32[1]{0:T(128)} %bitcast.refs_1_, bf16[4,256,128]{2,1,0:T(8,128)(2,1)S(1)} %queries.1.refs_2_, bf16[2,256,256]{2,1,0:T(8,128)(2,1)S(1)} %collective-permute-done.9.refs_3_, ...), custom_call_target="tpu_custom_call" | custom-call | flops 131072 | bytes 65536 | tf_op jit(solution)/shard_map/attend/pallas_call | solution.py:275
  61.8 0.0 collective-permute-done.8
  61.8 0.7 collective-permute-done.7
  62.6 0.1 collective-permute-start.14
  62.7 2.0 %collective-permute-start.11 = (bf16[2,256,256]{2,1,0:T(8,128)(2,1)S(1)}, bf16[2,256,256]{2,1,0:T(8,128)(2,1)S(1)}, u32[]{:S(2)}, u32[]{:S(2)}) collective-permute-start(bf16[2,256,256]{2,1,0:T(8,128)(2,1)S(1)} %slice.25), channel_id=1, source_target_pairs={{0,16},{8,120},{16,32},{24,8},{32,48},{40,24},{48,64},{56,40},{64,... | collective-permute-start | bytes 786440 | tf_op jit(solution)/shard_map/ppermute | solution.py:330
  64.7 5.1 %collective-permute-start.13 = (bf16[1,256,256]{2,1,0:T(8,128)(2,1)S(1)}, bf16[1,256,256]{2,1,0:T(8,128)(2,1)S(1)}, u32[]{:S(2)}, u32[]{:S(2)}) collective-permute-start(bf16[1,256,256]{2,1,0:T(8,128)(2,1)S(1)} %get-tuple-element.103), channel_id=1, source_target_pairs={{0,32},{8,104},{16,48},{24,120},{32,64},{40,8},{48,80},{56,24},{64... | collective-permute-start | bytes 393224 | tf_op jit(solution)/shard_map/ppermute | solution.py:330
  69.8 0.7 collective-permute-start.12
  70.5 2.4 %attend.14 = (f32[4,256,128]{2,1,0:T(8,128)S(1)}, f32[4,256,256]{2,1,0:T(8,128)S(1)}) custom-call(s32[32]{0:T(128)S(1)} %copy-done.5, s32[1]{0:T(128)} %bitcast.refs_1_, bf16[4,256,128]{2,1,0:T(8,128)(2,1)S(1)} %queries.1.refs_2_, bf16[4,256,256]{2,1,0:T(8,128)(2,1)S(1)} %constant_dynamic-update-slice_fusion.refs_3_, ...), custom_call_target="tpu_custom_call" | custom-call | flops 131072 | bytes 65536 | tf_op jit(solution)/shard_map/attend/pallas_call | solution.py:275
  72.9 2.4 %attend.15 = (f32[4,256,128]{2,1,0:T(8,128)S(1)}, f32[4,256,256]{2,1,0:T(8,128)S(1)}) custom-call(s32[32]{0:T(128)S(1)} %copy-done.5, s32[1]{0:T(128)} %bitcast.refs_1_, bf16[4,256,128]{2,1,0:T(8,128)(2,1)S(1)} %queries.1.refs_2_, bf16[4,256,256]{2,1,0:T(8,128)(2,1)S(1)} %collective-permute-done.14.refs_3_, f32[4,256,128]{2,1,0:T(8,128)S(1)} %get-tuple-element.89.refs_4_, ...), custom_call_target="tpu_custom_call" | custom-call | flops 131072 | bytes 65536 | tf_op jit(solution)/shard_map/attend/pallas_call | solution.py:275
  75.3 0.6 collective-permute-done.13
  76.0 0.1 collective-permute-start.15
  76.1 2.4 %attend.16 = (f32[4,256,128]{2,1,0:T(8,128)S(1)}, f32[4,256,256]{2,1,0:T(8,128)S(1)}) custom-call(s32[32]{0:T(128)S(1)} %copy-done.5, s32[1]{0:T(128)} %bitcast.refs_1_, bf16[4,256,128]{2,1,0:T(8,128)(2,1)S(1)} %queries.1.refs_2_, bf16[4,256,256]{2,1,0:T(8,128)(2,1)S(1)} %constant_dynamic-update-slice_fusion.2.refs_3_, ...), custom_call_target="tpu_custom_call" | custom-call | flops 131072 | bytes 65536 | tf_op jit(solution)/shard_map/attend/pallas_call | solution.py:275
  78.5 2.6 %attend.17 = bf16[256,768]{1,0:T(8,128)(2,1)S(1)} custom-call(s32[32]{0:T(128)S(1)} %copy-done.5, s32[1]{0:T(128)} %bitcast.refs_1_, bf16[4,256,128]{2,1,0:T(8,128)(2,1)S(1)} %queries.1.refs_2_, bf16[4,256,256]{2,1,0:T(8,128)(2,1)S(1)} %collective-permute-done.15.refs_3_, f32[4,256,128]{2,1,0:T(8,128)S(1)} %get-tuple-element.101.refs_4_, ...), custom_call_target="tpu_custom_call" | custom-call | flops 131072 | bytes 65536 | tf_op jit(solution)/shard_map/attend/pallas_call | solution.py:275
  81.0 13.4 %all_to_all.16.parts = bf16[8,32,768]{2,1,0:T(8,128)(2,1)S(1)} all-to-all(bf16[8,32,768]{2,1,0:T(8,128)(2,1)S(1)} %bitcast.17), channel_id=1, replica_groups=mesh['blk'=32,'head'=8] {'head'}, dimensions={0} | all-to-all | bytes 786432 | tf_op jit(solution)/shard_map/all_to_all | solution.py:405
  94.4 0.7 total.1
  (34 shorter events, 0.3 us)
Async XLA Ops:
  5.7 7.1 %copy-start.8 = (f32[768]{0:T(1024)S(1)}, f32[768]{0:T(1024)}, u32[]{:S(2)}) copy-start(f32[768]{0:T(1024)} %param.24) | copy-start | bytes 9220
  5.7 16.7 %copy-start = (bf16[1,16,16,768]{3,2,1,0:T(8,128)(2,1)S(1)}, bf16[1,16,16,768]{3,2,1,0:T(8,128)(2,1)}, u32[]{:S(2)}) copy-start(bf16[1,16,16,768]{3,2,1,0:T(8,128)(2,1)} %param.15) | copy-start | bytes 1179652
  5.7 16.7 %all-to-all-start = ((bf16[8,32,768]{2,1,0:T(8,128)(2,1)}), bf16[8,32,768]{2,1,0:T(8,128)(2,1)S(1)}, u32[]{:S(2)}, u32[]{:S(2)}) async-start(bf16[8,32,768]{2,1,0:T(8,128)(2,1)} %bitcast.6), calls=%async_computation | async-start | bytes 786432 | tf_op jit(solution)/shard_map/all_to_all | solution.py:350
  12.8 0.7 copy-start.7
  12.8 0.7 copy-start.6
  22.7 12.8 %copy-start.3 = (bf16[768,128]{1,0:T(8,128)(2,1)S(1)}, bf16[768,128]{1,0:T(8,128)(2,1)}, u32[]{:S(2)}) copy-start(bf16[768,128]{1,0:T(8,128)(2,1)} %wk.1) | copy-start | bytes 589828
  22.7 12.8 %copy-start.4 = (bf16[768,128]{1,0:T(8,128)(2,1)S(1)}, bf16[768,128]{1,0:T(8,128)(2,1)}, u32[]{:S(2)}) copy-start(bf16[768,128]{1,0:T(8,128)(2,1)} %wv.1) | copy-start | bytes 589828
  35.5 4.5 %copy-start.1 = (bf16[768,512]{1,0:T(8,128)(2,1)S(1)}, bf16[768,512]{1,0:T(8,128)(2,1)}, u32[]{:S(2)}) copy-start(bf16[768,512]{1,0:T(8,128)(2,1)} %wq.1) | copy-start | bytes 2359300
  35.8 1.4 %collective-permute-start = (bf16[1,256,256]{2,1,0:T(8,128)(2,1)S(1)}, bf16[1,256,256]{2,1,0:T(8,128)(2,1)S(1)}, u32[]{:S(2)}, u32[]{:S(2)}) collective-permute-start(bf16[1,256,256]{2,1,0:T(8,128)(2,1)S(1)} %key_values.1), channel_id=1, source_target_pairs={{0,8},{8,0},{16,24},{24,16},{32,40},{40,32},{48,56},{56,48},{64,72... | collective-permute-start | bytes 393224 | tf_op jit(solution)/shard_map/ppermute | solution.py:330
  37.3 7.0 %collective-permute-start.1 = (bf16[2,256,256]{2,1,0:T(8,128)(2,1)S(1)}, bf16[2,256,256]{2,1,0:T(8,128)(2,1)S(1)}, u32[]{:S(2)}, u32[]{:S(2)}) collective-permute-start(bf16[2,256,256]{2,1,0:T(8,128)(2,1)S(1)} %pad_maximum_fusion.1.refs_3_), channel_id=1, source_target_pairs={{0,16},{8,120},{16,32},{24,8},{32,48},{40,24},{48,64},{56,40},{64,... | collective-permute-start | bytes 786440 | tf_op jit(solution)/shard_map/ppermute | solution.py:330
  39.3 5.0 %collective-permute-start.2 = (bf16[1,256,256]{2,1,0:T(8,128)(2,1)S(1)}, bf16[1,256,256]{2,1,0:T(8,128)(2,1)S(1)}, u32[]{:S(2)}, u32[]{:S(2)}) collective-permute-start(bf16[1,256,256]{2,1,0:T(8,128)(2,1)S(1)} %key_values.1), channel_id=1, source_target_pairs={{0,128},{8,136},{16,144},{24,152},{32,160},{40,168},{48,176},{56,1... | collective-permute-start | bytes 393224 | tf_op jit(solution)/shard_map/ppermute | solution.py:330
  40.0 0.7 copy-start.5
  44.3 9.3 %collective-permute-start.3 = (bf16[3,256,256]{2,1,0:T(8,128)(2,1)S(1)}, bf16[3,256,256]{2,1,0:T(8,128)(2,1)S(1)}, u32[]{:S(2)}, u32[]{:S(2)}) collective-permute-start(bf16[3,256,256]{2,1,0:T(8,128)(2,1)S(1)} %pad_maximum_fusion), channel_id=1, source_target_pairs={{0,16},{8,120},{16,32},{24,8},{32,48},{40,24},{48,64},{56,40},{64,... | collective-permute-start | bytes 1179656 | tf_op jit(solution)/shard_map/ppermute | solution.py:330
  46.3 3.9 %collective-permute-start.5 = (bf16[2,256,256]{2,1,0:T(8,128)(2,1)S(1)}, bf16[2,256,256]{2,1,0:T(8,128)(2,1)S(1)}, u32[]{:S(2)}, u32[]{:S(2)}) collective-permute-start(bf16[2,256,256]{2,1,0:T(8,128)(2,1)S(1)} %collective-permute-done.1.refs_3_), channel_id=1, source_target_pairs={{0,8},{8,0},{16,24},{24,16},{32,40},{40,32},{48,56},{56,48},{64,72... | collective-permute-start | bytes 786440 | tf_op jit(solution)/shard_map/ppermute | solution.py:330
  47.2 3.0 %collective-permute-start.6 = (bf16[1,256,256]{2,1,0:T(8,128)(2,1)S(1)}, bf16[1,256,256]{2,1,0:T(8,128)(2,1)S(1)}, u32[]{:S(2)}, u32[]{:S(2)}) collective-permute-start(bf16[1,256,256]{2,1,0:T(8,128)(2,1)S(1)} %collective-permute-done.2.refs_4_), channel_id=1, source_target_pairs={{0,8},{8,0},{16,24},{24,16},{32,40},{40,32},{48,56},{56,48},{64,72... | collective-permute-start | bytes 393224 | tf_op jit(solution)/shard_map/ppermute | solution.py:330
  47.2 6.2 %collective-permute-start.4 = (bf16[1,256,256]{2,1,0:T(8,128)(2,1)S(1)}, bf16[1,256,256]{2,1,0:T(8,128)(2,1)S(1)}, u32[]{:S(2)}, u32[]{:S(2)}) collective-permute-start(bf16[1,256,256]{2,1,0:T(8,128)(2,1)S(1)} %slice.21), channel_id=1, source_target_pairs={{0,128},{8,136},{16,144},{24,152},{32,160},{40,168},{48,176},{56,1... | collective-permute-start | bytes 393224 | tf_op jit(solution)/shard_map/ppermute | solution.py:330
  53.6 9.0 %collective-permute-start.7 = (bf16[3,256,256]{2,1,0:T(8,128)(2,1)S(1)}, bf16[3,256,256]{2,1,0:T(8,128)(2,1)S(1)}, u32[]{:S(2)}, u32[]{:S(2)}) collective-permute-start(bf16[3,256,256]{2,1,0:T(8,128)(2,1)S(1)} %collective-permute-done.3.refs_3_), channel_id=1, source_target_pairs={{0,16},{8,120},{16,32},{24,8},{32,48},{40,24},{48,64},{56,40},{64,... | collective-permute-start | bytes 1179656 | tf_op jit(solution)/shard_map/ppermute | solution.py:330
  55.7 3.7 %collective-permute-start.10 = (bf16[2,256,256]{2,1,0:T(8,128)(2,1)S(1)}, bf16[2,256,256]{2,1,0:T(8,128)(2,1)S(1)}, u32[]{:S(2)}, u32[]{:S(2)}) collective-permute-start(bf16[2,256,256]{2,1,0:T(8,128)(2,1)S(1)} %pad_maximum_fusion.2), channel_id=1, source_target_pairs={{0,8},{8,0},{16,24},{24,16},{32,40},{40,32},{48,56},{56,48},{64,72... | collective-permute-start | bytes 786440 | tf_op jit(solution)/shard_map/ppermute | solution.py:330
  55.8 3.6 %collective-permute-start.9 = (bf16[2,256,256]{2,1,0:T(8,128)(2,1)S(1)}, bf16[2,256,256]{2,1,0:T(8,128)(2,1)S(1)}, u32[]{:S(2)}, u32[]{:S(2)}) collective-permute-start(bf16[2,256,256]{2,1,0:T(8,128)(2,1)S(1)} %slice.23), channel_id=1, source_target_pairs={{0,8},{8,0},{16,24},{24,16},{32,40},{40,32},{48,56},{56,48},{64,72... | collective-permute-start | bytes 786440 | tf_op jit(solution)/shard_map/ppermute | solution.py:330
  56.3 5.5 %collective-permute-start.8 = (bf16[1,256,256]{2,1,0:T(8,128)(2,1)S(1)}, bf16[1,256,256]{2,1,0:T(8,128)(2,1)S(1)}, u32[]{:S(2)}, u32[]{:S(2)}) collective-permute-start(bf16[1,256,256]{2,1,0:T(8,128)(2,1)S(1)} %get-tuple-element.106), channel_id=1, source_target_pairs={{0,128},{8,136},{16,144},{24,152},{32,160},{40,168},{48,176},{56,1... | collective-permute-start | bytes 393224 | tf_op jit(solution)/shard_map/ppermute | solution.py:330
  62.6 10.3 %collective-permute-start.14 = (bf16[4,256,256]{2,1,0:T(8,128)(2,1)S(1)}, bf16[4,256,256]{2,1,0:T(8,128)(2,1)S(1)}, u32[]{:S(2)}, u32[]{:S(2)}) collective-permute-start(bf16[4,256,256]{2,1,0:T(8,128)(2,1)S(1)} %constant_dynamic-update-slice_fusion.refs_3_), channel_id=1, source_target_pairs={{0,8},{8,0},{16,24},{24,16},{32,40},{40,32},{48,56},{56,48},{64,72... | collective-permute-start | bytes 1572872 | tf_op jit(solution)/shard_map/ppermute | solution.py:330
  62.7 13.1 %collective-permute-start.11 = (bf16[2,256,256]{2,1,0:T(8,128)(2,1)S(1)}, bf16[2,256,256]{2,1,0:T(8,128)(2,1)S(1)}, u32[]{:S(2)}, u32[]{:S(2)}) collective-permute-start(bf16[2,256,256]{2,1,0:T(8,128)(2,1)S(1)} %slice.25), channel_id=1, source_target_pairs={{0,16},{8,120},{16,32},{24,8},{32,48},{40,24},{48,64},{56,40},{64,... | collective-permute-start | bytes 786440 | tf_op jit(solution)/shard_map/ppermute | solution.py:330
  64.7 11.2 %collective-permute-start.13 = (bf16[1,256,256]{2,1,0:T(8,128)(2,1)S(1)}, bf16[1,256,256]{2,1,0:T(8,128)(2,1)S(1)}, u32[]{:S(2)}, u32[]{:S(2)}) collective-permute-start(bf16[1,256,256]{2,1,0:T(8,128)(2,1)S(1)} %get-tuple-element.103), channel_id=1, source_target_pairs={{0,32},{8,104},{16,48},{24,120},{32,64},{40,8},{48,80},{56,24},{64... | collective-permute-start | bytes 393224 | tf_op jit(solution)/shard_map/ppermute | solution.py:330
  69.8 6.1 %collective-permute-start.12 = (bf16[1,256,256]{2,1,0:T(8,128)(2,1)S(1)}, bf16[1,256,256]{2,1,0:T(8,128)(2,1)S(1)}, u32[]{:S(2)}, u32[]{:S(2)}) collective-permute-start(bf16[1,256,256]{2,1,0:T(8,128)(2,1)S(1)} %get-tuple-element.104), channel_id=1, source_target_pairs={{0,128},{8,136},{16,144},{24,152},{32,160},{40,168},{48,176},{56,1... | collective-permute-start | bytes 393224 | tf_op jit(solution)/shard_map/ppermute | solution.py:330
  76.0 2.5 %copy-start.2 = (bf16[512,768]{1,0:T(8,128)(2,1)S(1)}, bf16[512,768]{1,0:T(8,128)(2,1)}, u32[]{:S(2)}) copy-start(bf16[512,768]{1,0:T(8,128)(2,1)} %refs_6_.1) | copy-start | bytes 2359300
  76.0 2.5 %collective-permute-start.15 = (bf16[4,256,256]{2,1,0:T(8,128)(2,1)S(1)}, bf16[4,256,256]{2,1,0:T(8,128)(2,1)S(1)}, u32[]{:S(2)}, u32[]{:S(2)}) collective-permute-start(bf16[4,256,256]{2,1,0:T(8,128)(2,1)S(1)} %constant_dynamic-update-slice_fusion.2.refs_3_), channel_id=1, source_target_pairs={{0,8},{8,0},{16,24},{24,16},{32,40},{40,32},{48,56},{56,48},{64,72... | collective-permute-start | bytes 1572872 | tf_op jit(solution)/shard_map/ppermute | solution.py:330

commit v11 on v10

--- a/solution.py
+++ b/solution.py
@@ -64,7 +64,7 @@
     loads[0].wait()
     height, breadth, channels = pages.shape
     half = height // 2
-    column = lax.broadcasted_iota(jnp.int32, (half, breadth, LANES), 1)
+    column = lax.broadcasted_iota(jnp.int32, (breadth, LANES), 0)
     blank = jnp.zeros((3, breadth, LANES), F32)
     for chunk in range(channels // LANES):
         lanes = slice(chunk * LANES, (chunk + 1) * LANES)
@@ -73,19 +73,22 @@
         padded[chunk, 0:3] = blank
         padded[chunk, 3 + height : 6 + height] = blank
         padded[chunk, 3 : 3 + height] = pages[:, :, lanes].astype(F32)
+        taps = []
+        for sideways in range(7):
+            offset = sideways - 3
+            inside = (column - offset >= 0) if offset > 0 else (column - offset < breadth)
+            for vertical in range(7):
+                tap = dw[vertical, sideways : sideways + 1, lanes]
+                taps.append(jnp.where(inside, tap, 0.0)[None] if offset else tap[None])
         for top in range(0, height, half):
             total = jnp.broadcast_to(dwb[chunk : chunk + 1, :][None], (half, breadth, LANES))
             for sideways in range(7):
                 product = None
                 for vertical in range(7):
-                    tap = dw[vertical, sideways : sideways + 1, lanes][None]
-                    term = padded[chunk, top + vertical : top + vertical + half] * tap
+                    term = padded[chunk, top + vertical : top + vertical + half] * taps[7 * sideways + vertical]
                     product = term if product is None else product + term
-                offset = sideways - 3
-                if offset:
-                    rolled = pltpu.roll(product, (-offset) % breadth, axis=1)
-                    inside = (column + offset >= 0) if offset < 0 else (column + offset < breadth)
-                    product = jnp.where(inside, rolled, 0.0)
+                if sideways != 3:
+                    product = pltpu.roll(product, (3 - sideways) % breadth, axis=1)
                 total = total + product
             conv[chunk, top * breadth : (top + half) * breadth] = total.reshape(half * breadth, LANES)
     loads[-4].wait()

time: 95.4 us -> 95.5 us (level)
  no operation moved by 1% of the time
where the time goes in v11:
time: 95.5 us; the launch traced here: 95.2 us
  Pallas kernels  27.8 us (29%)
  blocking collectives  26.2 us (27%)
  starting transfers between devices  25 us (26%)
  waiting for transfers between devices  14.3 us (15%)
  local copies, waits for them, and re-layouts  1.54 us (2%)
    pallas_call x9, Pallas kernels, attend(): pl.pallas_call(functools.partial(attend_kernel, carry is None, w_out is n...  19.9 us
    ppermute x16, starting transfers between devices, moved(): return lax.ppermute(array, 'blk', [(i, target(i)) for i in range(blocks)])  17.9 us
    all_to_all x1, blocking collectives, per_device(): lax.all_to_all(mixed.reshape(groups, share, channels), 'head', 0, 0, tile...  13.4 us
    all_to_all x1, blocking collectives, per_device(): lax.all_to_all(copies, 'head', 0, 0, tiled=True).reshape(rows, channels)  12.8 us
    all_to_all x1, waiting for transfers between devices, per_device(): lax.all_to_all(partial.reshape(groups, share, channels), 'head', 0, 0, ti...  8.93 us
    all_to_all x1, starting transfers between devices, per_device(): lax.all_to_all(partial.reshape(groups, share, channels), 'head', 0, 0, ti...  7.07 us
    pallas_call x1, Pallas kernels, mlp(): pl.pallas_call(mlp_kernel, out_shape=jax.ShapeDtypeStruct((rows, channels...  5.75 us
    ppermute x16, waiting for transfers between devices, moved(): return lax.ppermute(array, 'blk', [(i, target(i)) for i in range(blocks)])  5.35 us
  transfers between devices with their start and end apart: 17, of which 7 were waited for; matrix products, arithmetic and copies ran while one was open for 0% of the time, Pallas kernels for 19%

profile of v11, /device:TPU:32, one launch (start us, length us, event | category | flops | bytes accessed | tf_op | source)
XLA Modules:
  0.0 95.2 jit_solution(4688133624469004241)
XLA Ops:
  0.0 5.8 %conv_mlp.1 = bf16[256,768]{1,0:T(8,128)(2,1)} custom-call(bf16[16,16,768]{2,1,0:T(8,128)(2,1)} %bitcast.15, f32[7,7,768]{2,1,0:T(8,128)} %dw_hbm.1, f32[6,128]{1,0:T(8,128)} %bitcast.18, f32[6,128]{1,0:T(8,128)} %bitcast.19, bf16[768,384]{1,0:T(8,128)(2,1)} %w1_hbm.1, f32[3,128]{1,0:T(4,128)} %bitcast.23, bf16[384,768]{1,0:T(8,128)(2,1)} %w2_hbm.1), custom_call_target="tpu_custom_call" | custom-call | tf_op jit(solution)/shard_map/conv_mlp/pallas_call | solution.py:111
  5.8 0.0 copy-start.8
  5.8 0.0 copy-start
  5.8 7.1 %all-to-all-start = ((bf16[8,32,768]{2,1,0:T(8,128)(2,1)}), bf16[8,32,768]{2,1,0:T(8,128)(2,1)S(1)}, u32[]{:S(2)}, u32[]{:S(2)}) async-start(bf16[8,32,768]{2,1,0:T(8,128)(2,1)} %bitcast.6), calls=%async_computation | async-start | bytes 786432 | tf_op jit(solution)/shard_map/all_to_all | solution.py:353
  12.9 0.0 copy-start.6
  12.9 0.7 copy-done.7
  13.5 0.0 copy-done.6
  13.6 8.9 %all-to-all-done.parts = bf16[8,32,768]{2,1,0:T(8,128)(2,1)S(1)} async-done(((bf16[8,32,768]{2,1,0:T(8,128)(2,1)}), bf16[8,32,768]{2,1,0:T(8,128)(2,1)S(1)}, u32[]{:S(2)}, u32[]{:S(2)}) %all-to-all-start) | async-done | bytes 393248 | tf_op jit(solution)/shard_map/all_to_all | solution.py:353
  22.5 0.2 block_norm.1
  22.8 0.0 copy-start.3
  22.8 0.0 copy-start.4
  22.8 12.8 %all_to_all.15 = bf16[8,32,768]{2,1,0:T(8,128)(2,1)S(1)} all-to-all(bf16[8,32,768]{2,1,0:T(8,128)(2,1)S(1)} %block_norm.1), channel_id=1, replica_groups=mesh['blk'=32,'head'=8] {'head'}, dimensions={0} | all-to-all | bytes 786432 | tf_op jit(solution)/shard_map/all_to_all | solution.py:355
  35.6 0.4 key_values.1
  35.9 0.1 collective-permute-start
  36.0 1.3 %collective-permute-done = bf16[1,256,256]{2,1,0:T(8,128)(2,1)S(1)} collective-permute-done((bf16[1,256,256]{2,1,0:T(8,128)(2,1)S(1)}, bf16[1,256,256]{2,1,0:T(8,128)(2,1)S(1)}, u32[]{:S(2)}, u32[]{:S(2)}) %collective-permute-start) | collective-permute-done | bytes 131104 | tf_op jit(solution)/shard_map/ppermute | solution.py:333
  37.4 2.0 %collective-permute-start.1 = (bf16[2,256,256]{2,1,0:T(8,128)(2,1)S(1)}, bf16[2,256,256]{2,1,0:T(8,128)(2,1)S(1)}, u32[]{:S(2)}, u32[]{:S(2)}) collective-permute-start(bf16[2,256,256]{2,1,0:T(8,128)(2,1)S(1)} %pad_maximum_fusion.1.refs_3_), channel_id=1, source_target_pairs={{0,16},{8,120},{16,32},{24,8},{32,48},{40,24},{48,64},{56,40},{64,... | collective-permute-start | bytes 786440 | tf_op jit(solution)/shard_map/ppermute | solution.py:333
  39.4 0.7 collective-permute-start.2
  40.1 0.7 copy-done.5
  40.7 0.9 queries.1.refs_2_
  41.6 1.5 %attend.9 = (f32[4,256,128]{2,1,0:T(8,128)S(1)}, f32[4,256,256]{2,1,0:T(8,128)S(1)}) custom-call(s32[32]{0:T(128)S(1)} %copy-done.5, s32[1]{0:T(128)} %bitcast.refs_1_, bf16[4,256,128]{2,1,0:T(8,128)(2,1)S(1)} %queries.1.refs_2_, bf16[2,256,256]{2,1,0:T(8,128)(2,1)S(1)} %pad_maximum_fusion.1.refs_3_), custom_call_target="tpu_custom_call" | custom-call | flops 65536 | bytes 65536 | tf_op jit(solution)/shard_map/attend/pallas_call | solution.py:278
  43.2 1.2 %collective-permute-done.2.refs_4_ = bf16[1,256,256]{2,1,0:T(8,128)(2,1)S(1)} collective-permute-done((bf16[1,256,256]{2,1,0:T(8,128)(2,1)S(1)}, bf16[1,256,256]{2,1,0:T(8,128)(2,1)S(1)}, u32[]{:S(2)}, u32[]{:S(2)}) %collective-permute-start.2) | collective-permute-done | bytes 131104 | tf_op jit(solution)/shard_map/ppermute | solution.py:333
  44.4 2.0 %collective-permute-start.3 = (bf16[3,256,256]{2,1,0:T(8,128)(2,1)S(1)}, bf16[3,256,256]{2,1,0:T(8,128)(2,1)S(1)}, u32[]{:S(2)}, u32[]{:S(2)}) collective-permute-start(bf16[3,256,256]{2,1,0:T(8,128)(2,1)S(1)} %pad_maximum_fusion), channel_id=1, source_target_pairs={{0,16},{8,120},{16,32},{24,8},{32,48},{40,24},{48,64},{56,40},{64,... | collective-permute-start | bytes 1179656 | tf_op jit(solution)/shard_map/ppermute | solution.py:333
  46.4 0.9 collective-permute-start.5
  47.3 1.0 %collective-permute-start.4 = (bf16[1,256,256]{2,1,0:T(8,128)(2,1)S(1)}, bf16[1,256,256]{2,1,0:T(8,128)(2,1)S(1)}, u32[]{:S(2)}, u32[]{:S(2)}) collective-permute-start(bf16[1,256,256]{2,1,0:T(8,128)(2,1)S(1)} %slice.21), channel_id=1, source_target_pairs={{0,128},{8,136},{16,144},{24,152},{32,160},{40,168},{48,176},{56,1... | collective-permute-start | bytes 393224 | tf_op jit(solution)/shard_map/ppermute | solution.py:333
  48.3 2.0 %attend.10 = (f32[4,256,128]{2,1,0:T(8,128)S(1)}, f32[4,256,256]{2,1,0:T(8,128)S(1)}) custom-call(s32[32]{0:T(128)S(1)} %copy-done.5, s32[1]{0:T(128)} %bitcast.refs_1_, bf16[4,256,128]{2,1,0:T(8,128)(2,1)S(1)} %queries.1.refs_2_, bf16[2,256,256]{2,1,0:T(8,128)(2,1)S(1)} %collective-permute-done.1.refs_3_, ...), custom_call_target="tpu_custom_call" | custom-call | flops 98304 | bytes 65536 | tf_op jit(solution)/shard_map/attend/pallas_call | solution.py:278
  50.3 2.0 %attend.11 = (f32[4,256,128]{2,1,0:T(8,128)S(1)}, f32[4,256,256]{2,1,0:T(8,128)S(1)}) custom-call(s32[32]{0:T(128)S(1)} %copy-done.5, s32[1]{0:T(128)} %bitcast.refs_1_, bf16[4,256,128]{2,1,0:T(8,128)(2,1)S(1)} %queries.1.refs_2_, bf16[2,256,256]{2,1,0:T(8,128)(2,1)S(1)} %collective-permute-done.5.refs_3_, ...), custom_call_target="tpu_custom_call" | custom-call | flops 98304 | bytes 65536 | tf_op jit(solution)/shard_map/attend/pallas_call | solution.py:278
  52.3 1.2 %collective-permute-done.4.refs_4_ = bf16[1,256,256]{2,1,0:T(8,128)(2,1)S(1)} collective-permute-done((bf16[1,256,256]{2,1,0:T(8,128)(2,1)S(1)}, bf16[1,256,256]{2,1,0:T(8,128)(2,1)S(1)}, u32[]{:S(2)}, u32[]{:S(2)}) %collective-permute-start.4) | collective-permute-done | bytes 131104 | tf_op jit(solution)/shard_map/ppermute | solution.py:333
  53.5 0.2 collective-permute-done.3.refs_3_
  53.7 2.1 %collective-permute-start.7 = (bf16[3,256,256]{2,1,0:T(8,128)(2,1)S(1)}, bf16[3,256,256]{2,1,0:T(8,128)(2,1)S(1)}, u32[]{:S(2)}, u32[]{:S(2)}) collective-permute-start(bf16[3,256,256]{2,1,0:T(8,128)(2,1)S(1)} %collective-permute-done.3.refs_3_), channel_id=1, source_target_pairs={{0,16},{8,120},{16,32},{24,8},{32,48},{40,24},{48,64},{56,40},{64,... | collective-permute-start | bytes 1179656 | tf_op jit(solution)/shard_map/ppermute | solution.py:333
  55.8 0.1 collective-permute-start.10
  55.9 0.5 collective-permute-start.9
  56.4 0.7 collective-permute-start.8
  57.1 2.4 %attend.12 = (f32[4,256,128]{2,1,0:T(8,128)S(1)}, f32[4,256,256]{2,1,0:T(8,128)S(1)}) custom-call(s32[32]{0:T(128)S(1)} %copy-done.5, s32[1]{0:T(128)} %bitcast.refs_1_, bf16[4,256,128]{2,1,0:T(8,128)(2,1)S(1)} %queries.1.refs_2_, bf16[3,256,256]{2,1,0:T(8,128)(2,1)S(1)} %collective-permute-done.3.refs_3_, ...), custom_call_target="tpu_custom_call" | custom-call | flops 131072 | bytes 65536 | tf_op jit(solution)/shard_map/attend/pallas_call | solution.py:278
  59.5 2.4 %attend.13 = (f32[4,256,128]{2,1,0:T(8,128)S(1)}, f32[4,256,256]{2,1,0:T(8,128)S(1)}) custom-call(s32[32]{0:T(128)S(1)} %copy-done.5, s32[1]{0:T(128)} %bitcast.refs_1_, bf16[4,256,128]{2,1,0:T(8,128)(2,1)S(1)} %queries.1.refs_2_, bf16[2,256,256]{2,1,0:T(8,128)(2,1)S(1)} %collective-permute-done.9.refs_3_, ...), custom_call_target="tpu_custom_call" | custom-call | flops 131072 | bytes 65536 | tf_op jit(solution)/shard_map/attend/pallas_call | solution.py:278
  61.9 0.0 collective-permute-done.8
  61.9 0.7 collective-permute-done.7
  62.7 0.1 collective-permute-start.14
  62.8 2.0 %collective-permute-start.11 = (bf16[2,256,256]{2,1,0:T(8,128)(2,1)S(1)}, bf16[2,256,256]{2,1,0:T(8,128)(2,1)S(1)}, u32[]{:S(2)}, u32[]{:S(2)}) collective-permute-start(bf16[2,256,256]{2,1,0:T(8,128)(2,1)S(1)} %slice.25), channel_id=1, source_target_pairs={{0,16},{8,120},{16,32},{24,8},{32,48},{40,24},{48,64},{56,40},{64,... | collective-permute-start | bytes 786440 | tf_op jit(solution)/shard_map/ppermute | solution.py:333
  64.8 5.1 %collective-permute-start.13 = (bf16[1,256,256]{2,1,0:T(8,128)(2,1)S(1)}, bf16[1,256,256]{2,1,0:T(8,128)(2,1)S(1)}, u32[]{:S(2)}, u32[]{:S(2)}) collective-permute-start(bf16[1,256,256]{2,1,0:T(8,128)(2,1)S(1)} %get-tuple-element.103), channel_id=1, source_target_pairs={{0,32},{8,104},{16,48},{24,120},{32,64},{40,8},{48,80},{56,24},{64... | collective-permute-start | bytes 393224 | tf_op jit(solution)/shard_map/ppermute | solution.py:333
  69.9 0.7 collective-permute-start.12
  70.6 2.4 %attend.14 = (f32[4,256,128]{2,1,0:T(8,128)S(1)}, f32[4,256,256]{2,1,0:T(8,128)S(1)}) custom-call(s32[32]{0:T(128)S(1)} %copy-done.5, s32[1]{0:T(128)} %bitcast.refs_1_, bf16[4,256,128]{2,1,0:T(8,128)(2,1)S(1)} %queries.1.refs_2_, bf16[4,256,256]{2,1,0:T(8,128)(2,1)S(1)} %constant_dynamic-update-slice_fusion.refs_3_, ...), custom_call_target="tpu_custom_call" | custom-call | flops 131072 | bytes 65536 | tf_op jit(solution)/shard_map/attend/pallas_call | solution.py:278
  73.0 2.4 %attend.15 = (f32[4,256,128]{2,1,0:T(8,128)S(1)}, f32[4,256,256]{2,1,0:T(8,128)S(1)}) custom-call(s32[32]{0:T(128)S(1)} %copy-done.5, s32[1]{0:T(128)} %bitcast.refs_1_, bf16[4,256,128]{2,1,0:T(8,128)(2,1)S(1)} %queries.1.refs_2_, bf16[4,256,256]{2,1,0:T(8,128)(2,1)S(1)} %collective-permute-done.14.refs_3_, f32[4,256,128]{2,1,0:T(8,128)S(1)} %get-tuple-element.89.refs_4_, ...), custom_call_target="tpu_custom_call" | custom-call | flops 131072 | bytes 65536 | tf_op jit(solution)/shard_map/attend/pallas_call | solution.py:278
  75.4 0.6 collective-permute-done.13
  76.1 0.1 collective-permute-start.15
  76.2 2.4 %attend.16 = (f32[4,256,128]{2,1,0:T(8,128)S(1)}, f32[4,256,256]{2,1,0:T(8,128)S(1)}) custom-call(s32[32]{0:T(128)S(1)} %copy-done.5, s32[1]{0:T(128)} %bitcast.refs_1_, bf16[4,256,128]{2,1,0:T(8,128)(2,1)S(1)} %queries.1.refs_2_, bf16[4,256,256]{2,1,0:T(8,128)(2,1)S(1)} %constant_dynamic-update-slice_fusion.2.refs_3_, ...), custom_call_target="tpu_custom_call" | custom-call | flops 131072 | bytes 65536 | tf_op jit(solution)/shard_map/attend/pallas_call | solution.py:278
  78.6 2.6 %attend.17 = bf16[256,768]{1,0:T(8,128)(2,1)S(1)} custom-call(s32[32]{0:T(128)S(1)} %copy-done.5, s32[1]{0:T(128)} %bitcast.refs_1_, bf16[4,256,128]{2,1,0:T(8,128)(2,1)S(1)} %queries.1.refs_2_, bf16[4,256,256]{2,1,0:T(8,128)(2,1)S(1)} %collective-permute-done.15.refs_3_, f32[4,256,128]{2,1,0:T(8,128)S(1)} %get-tuple-element.101.refs_4_, ...), custom_call_target="tpu_custom_call" | custom-call | flops 131072 | bytes 65536 | tf_op jit(solution)/shard_map/attend/pallas_call | solution.py:278
  81.1 13.4 %all_to_all.16.parts = bf16[8,32,768]{2,1,0:T(8,128)(2,1)S(1)} all-to-all(bf16[8,32,768]{2,1,0:T(8,128)(2,1)S(1)} %bitcast.17), channel_id=1, replica_groups=mesh['blk'=32,'head'=8] {'head'}, dimensions={0} | all-to-all | bytes 786432 | tf_op jit(solution)/shard_map/all_to_all | solution.py:408
  94.5 0.7 total.1
  (34 shorter events, 0.3 us)
Async XLA Ops:
  5.8 7.1 %copy-start.8 = (f32[768]{0:T(1024)S(1)}, f32[768]{0:T(1024)}, u32[]{:S(2)}) copy-start(f32[768]{0:T(1024)} %param.24) | copy-start | bytes 9220
  5.8 16.7 %copy-start = (bf16[1,16,16,768]{3,2,1,0:T(8,128)(2,1)S(1)}, bf16[1,16,16,768]{3,2,1,0:T(8,128)(2,1)}, u32[]{:S(2)}) copy-start(bf16[1,16,16,768]{3,2,1,0:T(8,128)(2,1)} %param.15) | copy-start | bytes 1179652
  5.8 16.7 %all-to-all-start = ((bf16[8,32,768]{2,1,0:T(8,128)(2,1)}), bf16[8,32,768]{2,1,0:T(8,128)(2,1)S(1)}, u32[]{:S(2)}, u32[]{:S(2)}) async-start(bf16[8,32,768]{2,1,0:T(8,128)(2,1)} %bitcast.6), calls=%async_computation | async-start | bytes 786432 | tf_op jit(solution)/shard_map/all_to_all | solution.py:353
  12.9 0.7 copy-start.7
  12.9 0.7 copy-start.6
  22.8 12.8 %copy-start.3 = (bf16[768,128]{1,0:T(8,128)(2,1)S(1)}, bf16[768,128]{1,0:T(8,128)(2,1)}, u32[]{:S(2)}) copy-start(bf16[768,128]{1,0:T(8,128)(2,1)} %wk.1) | copy-start | bytes 589828
  22.8 12.8 %copy-start.4 = (bf16[768,128]{1,0:T(8,128)(2,1)S(1)}, bf16[768,128]{1,0:T(8,128)(2,1)}, u32[]{:S(2)}) copy-start(bf16[768,128]{1,0:T(8,128)(2,1)} %wv.1) | copy-start | bytes 589828
  35.6 4.5 %copy-start.1 = (bf16[768,512]{1,0:T(8,128)(2,1)S(1)}, bf16[768,512]{1,0:T(8,128)(2,1)}, u32[]{:S(2)}) copy-start(bf16[768,512]{1,0:T(8,128)(2,1)} %wq.1) | copy-start | bytes 2359300
  35.9 1.4 %collective-permute-start = (bf16[1,256,256]{2,1,0:T(8,128)(2,1)S(1)}, bf16[1,256,256]{2,1,0:T(8,128)(2,1)S(1)}, u32[]{:S(2)}, u32[]{:S(2)}) collective-permute-start(bf16[1,256,256]{2,1,0:T(8,128)(2,1)S(1)} %key_values.1), channel_id=1, source_target_pairs={{0,8},{8,0},{16,24},{24,16},{32,40},{40,32},{48,56},{56,48},{64,72... | collective-permute-start | bytes 393224 | tf_op jit(solution)/shard_map/ppermute | solution.py:333
  37.4 7.0 %collective-permute-start.1 = (bf16[2,256,256]{2,1,0:T(8,128)(2,1)S(1)}, bf16[2,256,256]{2,1,0:T(8,128)(2,1)S(1)}, u32[]{:S(2)}, u32[]{:S(2)}) collective-permute-start(bf16[2,256,256]{2,1,0:T(8,128)(2,1)S(1)} %pad_maximum_fusion.1.refs_3_), channel_id=1, source_target_pairs={{0,16},{8,120},{16,32},{24,8},{32,48},{40,24},{48,64},{56,40},{64,... | collective-permute-start | bytes 786440 | tf_op jit(solution)/shard_map/ppermute | solution.py:333
  39.4 5.0 %collective-permute-start.2 = (bf16[1,256,256]{2,1,0:T(8,128)(2,1)S(1)}, bf16[1,256,256]{2,1,0:T(8,128)(2,1)S(1)}, u32[]{:S(2)}, u32[]{:S(2)}) collective-permute-start(bf16[1,256,256]{2,1,0:T(8,128)(2,1)S(1)} %key_values.1), channel_id=1, source_target_pairs={{0,128},{8,136},{16,144},{24,152},{32,160},{40,168},{48,176},{56,1... | collective-permute-start | bytes 393224 | tf_op jit(solution)/shard_map/ppermute | solution.py:333
  40.1 0.7 copy-start.5
  44.4 9.3 %collective-permute-start.3 = (bf16[3,256,256]{2,1,0:T(8,128)(2,1)S(1)}, bf16[3,256,256]{2,1,0:T(8,128)(2,1)S(1)}, u32[]{:S(2)}, u32[]{:S(2)}) collective-permute-start(bf16[3,256,256]{2,1,0:T(8,128)(2,1)S(1)} %pad_maximum_fusion), channel_id=1, source_target_pairs={{0,16},{8,120},{16,32},{24,8},{32,48},{40,24},{48,64},{56,40},{64,... | collective-permute-start | bytes 1179656 | tf_op jit(solution)/shard_map/ppermute | solution.py:333
  46.4 3.9 %collective-permute-start.5 = (bf16[2,256,256]{2,1,0:T(8,128)(2,1)S(1)}, bf16[2,256,256]{2,1,0:T(8,128)(2,1)S(1)}, u32[]{:S(2)}, u32[]{:S(2)}) collective-permute-start(bf16[2,256,256]{2,1,0:T(8,128)(2,1)S(1)} %collective-permute-done.1.refs_3_), channel_id=1, source_target_pairs={{0,8},{8,0},{16,24},{24,16},{32,40},{40,32},{48,56},{56,48},{64,72... | collective-permute-start | bytes 786440 | tf_op jit(solution)/shard_map/ppermute | solution.py:333
  47.3 3.0 %collective-permute-start.6 = (bf16[1,256,256]{2,1,0:T(8,128)(2,1)S(1)}, bf16[1,256,256]{2,1,0:T(8,128)(2,1)S(1)}, u32[]{:S(2)}, u32[]{:S(2)}) collective-permute-start(bf16[1,256,256]{2,1,0:T(8,128)(2,1)S(1)} %collective-permute-done.2.refs_4_), channel_id=1, source_target_pairs={{0,8},{8,0},{16,24},{24,16},{32,40},{40,32},{48,56},{56,48},{64,72... | collective-permute-start | bytes 393224 | tf_op jit(solution)/shard_map/ppermute | solution.py:333
  47.3 6.2 %collective-permute-start.4 = (bf16[1,256,256]{2,1,0:T(8,128)(2,1)S(1)}, bf16[1,256,256]{2,1,0:T(8,128)(2,1)S(1)}, u32[]{:S(2)}, u32[]{:S(2)}) collective-permute-start(bf16[1,256,256]{2,1,0:T(8,128)(2,1)S(1)} %slice.21), channel_id=1, source_target_pairs={{0,128},{8,136},{16,144},{24,152},{32,160},{40,168},{48,176},{56,1... | collective-permute-start | bytes 393224 | tf_op jit(solution)/shard_map/ppermute | solution.py:333
  53.7 9.0 %collective-permute-start.7 = (bf16[3,256,256]{2,1,0:T(8,128)(2,1)S(1)}, bf16[3,256,256]{2,1,0:T(8,128)(2,1)S(1)}, u32[]{:S(2)}, u32[]{:S(2)}) collective-permute-start(bf16[3,256,256]{2,1,0:T(8,128)(2,1)S(1)} %collective-permute-done.3.refs_3_), channel_id=1, source_target_pairs={{0,16},{8,120},{16,32},{24,8},{32,48},{40,24},{48,64},{56,40},{64,... | collective-permute-start | bytes 1179656 | tf_op jit(solution)/shard_map/ppermute | solution.py:333
  55.8 3.7 %collective-permute-start.10 = (bf16[2,256,256]{2,1,0:T(8,128)(2,1)S(1)}, bf16[2,256,256]{2,1,0:T(8,128)(2,1)S(1)}, u32[]{:S(2)}, u32[]{:S(2)}) collective-permute-start(bf16[2,256,256]{2,1,0:T(8,128)(2,1)S(1)} %pad_maximum_fusion.2), channel_id=1, source_target_pairs={{0,8},{8,0},{16,24},{24,16},{32,40},{40,32},{48,56},{56,48},{64,72... | collective-permute-start | bytes 786440 | tf_op jit(solution)/shard_map/ppermute | solution.py:333
  55.9 3.6 %collective-permute-start.9 = (bf16[2,256,256]{2,1,0:T(8,128)(2,1)S(1)}, bf16[2,256,256]{2,1,0:T(8,128)(2,1)S(1)}, u32[]{:S(2)}, u32[]{:S(2)}) collective-permute-start(bf16[2,256,256]{2,1,0:T(8,128)(2,1)S(1)} %slice.23), channel_id=1, source_target_pairs={{0,8},{8,0},{16,24},{24,16},{32,40},{40,32},{48,56},{56,48},{64,72... | collective-permute-start | bytes 786440 | tf_op jit(solution)/shard_map/ppermute | solution.py:333
  56.4 5.5 %collective-permute-start.8 = (bf16[1,256,256]{2,1,0:T(8,128)(2,1)S(1)}, bf16[1,256,256]{2,1,0:T(8,128)(2,1)S(1)}, u32[]{:S(2)}, u32[]{:S(2)}) collective-permute-start(bf16[1,256,256]{2,1,0:T(8,128)(2,1)S(1)} %get-tuple-element.106), channel_id=1, source_target_pairs={{0,128},{8,136},{16,144},{24,152},{32,160},{40,168},{48,176},{56,1... | collective-permute-start | bytes 393224 | tf_op jit(solution)/shard_map/ppermute | solution.py:333
  62.7 10.3 %collective-permute-start.14 = (bf16[4,256,256]{2,1,0:T(8,128)(2,1)S(1)}, bf16[4,256,256]{2,1,0:T(8,128)(2,1)S(1)}, u32[]{:S(2)}, u32[]{:S(2)}) collective-permute-start(bf16[4,256,256]{2,1,0:T(8,128)(2,1)S(1)} %constant_dynamic-update-slice_fusion.refs_3_), channel_id=1, source_target_pairs={{0,8},{8,0},{16,24},{24,16},{32,40},{40,32},{48,56},{56,48},{64,72... | collective-permute-start | bytes 1572872 | tf_op jit(solution)/shard_map/ppermute | solution.py:333
  62.8 13.1 %collective-permute-start.11 = (bf16[2,256,256]{2,1,0:T(8,128)(2,1)S(1)}, bf16[2,256,256]{2,1,0:T(8,128)(2,1)S(1)}, u32[]{:S(2)}, u32[]{:S(2)}) collective-permute-start(bf16[2,256,256]{2,1,0:T(8,128)(2,1)S(1)} %slice.25), channel_id=1, source_target_pairs={{0,16},{8,120},{16,32},{24,8},{32,48},{40,24},{48,64},{56,40},{64,... | collective-permute-start | bytes 786440 | tf_op jit(solution)/shard_map/ppermute | solution.py:333
  64.8 11.2 %collective-permute-start.13 = (bf16[1,256,256]{2,1,0:T(8,128)(2,1)S(1)}, bf16[1,256,256]{2,1,0:T(8,128)(2,1)S(1)}, u32[]{:S(2)}, u32[]{:S(2)}) collective-permute-start(bf16[1,256,256]{2,1,0:T(8,128)(2,1)S(1)} %get-tuple-element.103), channel_id=1, source_target_pairs={{0,32},{8,104},{16,48},{24,120},{32,64},{40,8},{48,80},{56,24},{64... | collective-permute-start | bytes 393224 | tf_op jit(solution)/shard_map/ppermute | solution.py:333
  69.9 6.1 %collective-permute-start.12 = (bf16[1,256,256]{2,1,0:T(8,128)(2,1)S(1)}, bf16[1,256,256]{2,1,0:T(8,128)(2,1)S(1)}, u32[]{:S(2)}, u32[]{:S(2)}) collective-permute-start(bf16[1,256,256]{2,1,0:T(8,128)(2,1)S(1)} %get-tuple-element.104), channel_id=1, source_target_pairs={{0,128},{8,136},{16,144},{24,152},{32,160},{40,168},{48,176},{56,1... | collective-permute-start | bytes 393224 | tf_op jit(solution)/shard_map/ppermute | solution.py:333
  76.0 2.5 %copy-start.2 = (bf16[512,768]{1,0:T(8,128)(2,1)S(1)}, bf16[512,768]{1,0:T(8,128)(2,1)}, u32[]{:S(2)}) copy-start(bf16[512,768]{1,0:T(8,128)(2,1)} %refs_6_.1) | copy-start | bytes 2359300
  76.1 2.5 %collective-permute-start.15 = (bf16[4,256,256]{2,1,0:T(8,128)(2,1)S(1)}, bf16[4,256,256]{2,1,0:T(8,128)(2,1)S(1)}, u32[]{:S(2)}, u32[]{:S(2)}) collective-permute-start(bf16[4,256,256]{2,1,0:T(8,128)(2,1)S(1)} %constant_dynamic-update-slice_fusion.2.refs_3_), channel_id=1, source_target_pairs={{0,8},{8,0},{16,24},{24,16},{32,40},{40,32},{48,56},{56,48},{64,72... | collective-permute-start | bytes 1572872 | tf_op jit(solution)/shard_map/ppermute | solution.py:333
